TPU v7x, 32 devices: a whole 2x2x4 slice. The times are simulated.
32 devices in a mesh: src: 2 (over x), rcv: 4 (over y, core), foc: 4 (over z).
Axes of the slice: x: 2, y: 2, z: 4, core: 2. Of those that a mesh axis runs over, the one named last changes fastest.
Arguments:
- reflection: bfloat16 [2, 256, 256, 1024], P(None, 'foc', 'src', 'rcv'), may hold values from -0.1875 to 0.1875
- direct_wave: bfloat16 [2, 256, 32, 1024], P(None, None, 'foc', 'rcv'), may hold values from -6 to 6
- onset_receiver: int32 [32, 1024], P('foc', 'rcv'), may hold values from 128 to 1023
- onset_source: int32 [32, 256], P('foc', 'src'), may hold values from 128 to 1023
Outputs:
- focusing: bfloat16 [2, 256, 32, 1024], P(None, None, 'foc', 'rcv')
- muted_trace: bfloat16 [32, 256, 1024], P('foc', 'src')
Inputs may be any that keep to these rules, and one draw needn't show every extreme that they name: `onset_receiver`: onset sample of the muting window of each focal point and receiver; samples before it are kept. `onset_source`: onset sample of the muting window of each focal point and source; samples before it are kept.
All inputs are finite; a program needn't handle non-finite values.
Results may differ from a plain program's by a relative error of at most 0.029.
Values may be sent and summed in bfloat16 or wider, within the bound.
No kernel may reach another device: no remote copies, remote signals or barrier semaphores. Data moves between devices by JAX's collectives and lax.ppermute only.
A program may use at most 128 MiB of HBM per device.

v0:
```python
import math

import jax
import jax.numpy as jnp
from jax import lax
from jax.sharding import PartitionSpec as P

F = 256
NT = 1024
ITERS = 2


def basis_table():
    frequency_bins = jnp.arange(F, dtype=jnp.int32) + 1
    samples = jnp.arange(NT, dtype=jnp.int32)
    phases = frequency_bins[:, None] * samples[None, :] % NT
    angles = phases.astype(jnp.float32) * (2.0 * math.pi / NT)
    norming = math.sqrt(2.0 / NT)
    return (jnp.stack([jnp.cos(angles), -jnp.sin(angles)]) * norming).astype(jnp.bfloat16)


def mute_traces(spectrum, onsets, basis_rows):
    focal_count = spectrum.shape[2]
    samples = jnp.arange(NT, dtype=jnp.int32)

    def one_focus(focal_index, carry):
        muted_all, returned_all = carry
        one_spectrum = lax.dynamic_slice_in_dim(spectrum, focal_index, 1, 2)
        one_onset = lax.dynamic_slice_in_dim(onsets, focal_index, 1, 0)
        signal = jnp.einsum(
            "cwpr,cwt->prt", one_spectrum, basis_rows, preferred_element_type=jnp.float32
        )
        window = samples[None, None, :] < one_onset[:, :, None]
        muted_one = jnp.where(window, signal, 0.0).astype(jnp.bfloat16)
        returned = jnp.einsum(
            "prt,cwt->cwpr", muted_one, basis_rows, preferred_element_type=jnp.float32
        )
        muted_all = lax.dynamic_update_slice_in_dim(muted_all, muted_one, focal_index, 0)
        returned_all = lax.dynamic_update_slice_in_dim(returned_all, returned, focal_index, 2)
        return (muted_all, returned_all)

    initial = (
        jnp.zeros((focal_count, spectrum.shape[3], NT), jnp.bfloat16),
        jnp.zeros(spectrum.shape, jnp.float32),
    )
    return lax.fori_loop(0, focal_count, one_focus, initial)


def convolve(reflection, focusing):
    real_out = jnp.einsum(
        "wsr,wpr->wps", reflection[0], focusing[0], preferred_element_type=jnp.float32
    ) - jnp.einsum("wsr,wpr->wps", reflection[1], focusing[1], preferred_element_type=jnp.float32)
    imag_out = jnp.einsum(
        "wsr,wpr->wps", reflection[0], focusing[1], preferred_element_type=jnp.float32
    ) + jnp.einsum("wsr,wpr->wps", reflection[1], focusing[0], preferred_element_type=jnp.float32)
    return jnp.stack([real_out, imag_out])


def correlate(reflection, spectrum):
    real_out = jnp.einsum(
        "wsr,wps->wpr", reflection[0], spectrum[0], preferred_element_type=jnp.float32
    ) + jnp.einsum("wsr,wps->wpr", reflection[1], spectrum[1], preferred_element_type=jnp.float32)
    imag_out = jnp.einsum(
        "wsr,wps->wpr", reflection[0], spectrum[1], preferred_element_type=jnp.float32
    ) - jnp.einsum("wsr,wps->wpr", reflection[1], spectrum[0], preferred_element_type=jnp.float32)
    return jnp.stack([real_out, imag_out])


def renew(shares, direct_wave, onset_receiver, basis_rows, source_index):
    share_width = shares.shape[3]
    offset = source_index * share_width
    onset_share = lax.dynamic_slice_in_dim(onset_receiver, offset, share_width, 1)
    direct_share = lax.dynamic_slice_in_dim(direct_wave, offset, share_width, 3)
    unused, update = mute_traces(shares, onset_share, basis_rows)
    renewed = (direct_share.astype(jnp.float32) + update).astype(jnp.bfloat16)
    return lax.all_gather(renewed, "src", axis=3, tiled=True)


def local(reflection, direct_wave, onset_receiver, onset_source):
    basis_rows = basis_table()
    source_index = lax.axis_index("src")
    whole_reflection = lax.all_gather(reflection, "foc", axis=1, tiled=True)
    focusing = direct_wave
    muted_trace = None
    for iteration in range(ITERS):
        partial_value = convolve(whole_reflection, focusing)
        spectrum = lax.psum(partial_value.astype(jnp.bfloat16), "rcv")
        muted_trace, returned = mute_traces(spectrum, onset_source, basis_rows)
        partial_adjoint = correlate(whole_reflection, returned.astype(jnp.bfloat16))
        shares = lax.psum_scatter(
            partial_adjoint.astype(jnp.bfloat16), "src", scatter_dimension=3, tiled=True
        )
        focusing = renew(shares, direct_wave, onset_receiver, basis_rows, source_index)
    return (focusing, muted_trace)


def solution(mesh):
    in_specs = (
        P(None, "foc", "src", "rcv"),
        P(None, None, "foc", "rcv"),
        P("foc", "rcv"),
        P("foc", "src"),
    )
    out_specs = (P(None, None, "foc", "rcv"), P("foc", "src", None))
    return jax.shard_map(local, mesh=mesh, in_specs=in_specs, out_specs=out_specs, check_vma=False)
```

profile of v0, /device:TPU:0, one launch (start us, length us, event | category | flops | bytes accessed | tf_op | source)
XLA Modules:
  0.0 1451.5 jit_solution(9437227582287752656)
XLA Ops:
  8.1 565.7 %all-gather.4.cloned.1.call-done = bf16[2,256,128,256]{3,2,1,0:T(8,128)(2,1)} async-done(((bf16[2,64,128,256]{3,2,1,0:T(8,128)(2,1)}), bf16[2,256,128,256]{3,2,1,0:T(8,128)(2,1)}) %all-gather.4.cloned.1.call-update) | async-done | bytes 33554448 | tf_op jit(solution)/shard_map/all_gather | solution.py:82
  573.7 11.2 fusion.58
  584.9 11.2 fusion.57
  596.1 11.3 fusion.82
  607.4 11.0 fusion.83
  625.7 29.4 %all-reduce.3.cloned.1.call-done = bf16[2,256,8,128]{3,2,1,0:T(8,128)(2,1)} async-done(((bf16[2,256,8,128]{3,2,1,0:T(8,128)(2,1)}), bf16[2,256,8,128]{3,2,1,0:T(8,128)(2,1)}) %all-reduce.3.cloned.1.call-update) | async-done | bytes 1048592 | tf_op jit(solution)/shard_map/psum | solution.py:87
  657.5 66.9 %while.58 = (s32[]{:T(128)}, bf16[2,256,8,128]{3,2,1,0:T(8,128)(2,1)S(1)}, s32[8,128]{1,0:T(8,128)}, bf16[2,256,8,128]{3,1,0,2:T(8,128)(2,1)}, bf16[2,256,1024]{2,1,0:T(8,128)(2,1)S(1)}, /*index=5*/s32[]{:T(128)}, s32[]{:T(128)}) while((s32[]{:T(128)}, bf16[2,256,8,128]{3,2,1,0:T(8,128)(2,1)S(1)}, s32[8,128]{1,0:T(8,128)}, ...), condition=%wide.region_2.3_spmd.clone, body=%wide.region_1.2_spmd.clone.sunk | while | flops 268828672 | bytes 2885717 | solution.py:46
  660.0 5.9 dynamic_update_slice.46
  668.4 5.9 dynamic_update_slice.46
  676.7 5.9 dynamic_update_slice.46
  685.1 5.9 dynamic_update_slice.46
  693.5 5.9 dynamic_update_slice.46
  701.9 5.9 dynamic_update_slice.46
  710.2 5.9 dynamic_update_slice.46
  718.6 5.9 dynamic_update_slice.46
  724.5 7.0 fusion.56
  731.5 7.0 fusion.55
  738.4 8.1 fusion.70
  746.5 8.1 fusion.71
  754.8 23.7 %copy.33 = bf16[2,256,8,256]{2,1,0,3:T(8,128)(2,1)} copy(bf16[2,256,8,256]{3,2,1,0:T(8,128)(2,1)S(1)} %pad_maximum_fusion) | data formatting | bytes 4194304
  778.5 48.5 %reshape.210 = bf16[256,4096]{1,0:T(8,128)(2,1)} reshape(bf16[256,2,256,8]{3,2,1,0:T(8,128)(2,1)} %bitcast.276) | data formatting | bytes 4194304
  827.1 32.3 %reduce-scatter.7.cloned.1.call-done = bf16[128,4096]{1,0:T(8,128)(2,1)} async-done(((bf16[256,4096]{1,0:T(8,128)(2,1)}), bf16[128,4096]{1,0:T(8,128)(2,1)}) %reduce-scatter.7.cloned.1.call-update) | async-done | bytes 1048592
  859.4 22.0 %reshape.211 = bf16[128,2,256,8]{3,2,1,0:T(8,128)(2,1)} reshape(bf16[128,4096]{1,0:T(8,128)(2,1)} %reduce-scatter.7.cloned.1.call-done) | data formatting | bytes 2097152
  881.3 15.8 %copy.24 = bf16[2,256,8,128]{3,1,0,2:T(8,128)(2,1)S(1)} copy(bf16[2,256,8,128]{2,1,0,3:T(8,128)(2,1)} %bitcast.278) | data formatting | bytes 2097152
  898.6 72.3 %while.59 = (s32[]{:T(128)}, f32[2,256,8,128]{3,2,1,0:T(8,128)}, s32[8,128]{1,0:T(8,128)S(1)}, bf16[2,256,8,128]{3,1,0,2:T(8,128)(2,1)S(1)}, bf16[2,256,1024]{2,1,0:T(8,128)(2,1)S(1)}, /*index=5*/s32[]{:T(128)}, s32[]{:T(128)}) while((s32[]{:T(128)}, f32[2,256,8,128]{3,2,1,0:T(8,128)}, s32[8,128]{1,0:T(8,128)S(1)}, ...), condition=%wide.region_5.6_spmd.clone, body=%wide.region_4.5_spmd.clone.sunk | while | flops 268828672 | bytes 3540569 | solution.py:46
  899.4 8.2 dynamic_update_slice.47
  908.5 8.2 dynamic_update_slice.47
  917.5 8.2 dynamic_update_slice.47
  926.6 8.2 dynamic_update_slice.47
  935.6 8.2 dynamic_update_slice.47
  944.6 8.2 dynamic_update_slice.47
  953.7 8.2 dynamic_update_slice.47
  962.7 8.2 dynamic_update_slice.47
  974.2 33.0 %all-gather.6.cloned.1.call-done = bf16[2,256,8,256]{3,2,1,0:T(8,128)(2,1)} async-done(((bf16[2,256,8,128]{3,2,1,0:T(8,128)(2,1)}), bf16[2,256,8,256]{3,2,1,0:T(8,128)(2,1)}) %all-gather.6.cloned.1.call-update) | async-done | bytes 2097168 | tf_op jit(solution)/shard_map/all_gather | solution.py:76
  1007.2 11.6 fusion.54
  1018.8 11.2 fusion.53
  1030.0 11.2 fusion.84
  1041.2 11.2 fusion.85
  1055.0 36.0 %all-reduce.5.cloned.1.call-done = bf16[2,256,8,128]{3,2,1,0:T(8,128)(2,1)} async-done(((bf16[2,256,8,128]{3,2,1,0:T(8,128)(2,1)}), bf16[2,256,8,128]{3,2,1,0:T(8,128)(2,1)}) %all-reduce.5.cloned.1.call-update) | async-done | bytes 1048592 | tf_op jit(solution)/shard_map/psum | solution.py:87
  1092.7 66.2 %while.60 = (s32[]{:T(128)}, bf16[8,128,1024]{2,1,0:T(8,128)(2,1)}, bf16[2,256,8,128]{3,2,1,0:T(8,128)(2,1)S(1)}, s32[8,128]{1,0:T(8,128)}, bf16[2,256,8,128]{1,...) while((s32[]{:T(128)}, bf16[8,128,1024]{2,1,0:T(8,128)(2,1)}, ...), condition=%wide.region_8.9_spmd.clone, body=%wide.region_7.8_spmd.clone.sunk | while | flops 268828672 | bytes 3672669 | solution.py:46
  1103.3 5.9 dynamic_update_slice.49
  1111.6 5.9 dynamic_update_slice.49
  1128.1 5.9 dynamic_update_slice.49
  1136.4 5.9 dynamic_update_slice.49
  1152.9 5.9 dynamic_update_slice.49
  1158.8 7.0 fusion.52
  1165.8 7.0 fusion.51
  1172.8 8.1 fusion.72
  1180.8 8.1 fusion.73
  1189.1 23.6 %copy.35 = bf16[2,256,8,256]{2,1,0,3:T(8,128)(2,1)} copy(bf16[2,256,8,256]{3,2,1,0:T(8,128)(2,1)S(1)} %pad_maximum_fusion.1) | data formatting | bytes 4194304
  1212.7 48.5 %reshape.212 = bf16[256,4096]{1,0:T(8,128)(2,1)} reshape(bf16[256,2,256,8]{3,2,1,0:T(8,128)(2,1)} %bitcast.277) | data formatting | bytes 4194304
  1261.5 32.1 %reduce-scatter.9.cloned.1.call-done = bf16[128,4096]{1,0:T(8,128)(2,1)} async-done(((bf16[256,4096]{1,0:T(8,128)(2,1)}), bf16[128,4096]{1,0:T(8,128)(2,1)}) %reduce-scatter.9.cloned.1.call-update) | async-done | bytes 1048592
  1293.5 21.9 %reshape.213 = bf16[128,2,256,8]{3,2,1,0:T(8,128)(2,1)} reshape(bf16[128,4096]{1,0:T(8,128)(2,1)} %reduce-scatter.9.cloned.1.call-done) | data formatting | bytes 2097152
  1315.5 15.8 %copy.28 = bf16[2,256,8,128]{3,1,0,2:T(8,128)(2,1)S(1)} copy(bf16[2,256,8,128]{2,1,0,3:T(8,128)(2,1)} %bitcast.279) | data formatting | bytes 2097152
  1332.8 72.3 %while.61 = (s32[]{:T(128)}, f32[2,256,8,128]{3,2,1,0:T(8,128)}, s32[8,128]{1,0:T(8,128)S(1)}, bf16[2,256,8,128]{3,1,0,2:T(8,128)(2,1)S(1)}, bf16[2,256,1024]{2,1,0:T(8,128)(2,1)S(1)}, /*index=5*/s32[]{:T(128)}, s32[]{:T(128)}) while((s32[]{:T(128)}, f32[2,256,8,128]{3,2,1,0:T(8,128)}, s32[8,128]{1,0:T(8,128)S(1)}, ...), condition=%wide.region_11.12_spmd.clone, body=%wide.region_10.11_spmd.clone.sunk | while | flops 268828672 | bytes 3540569 | solution.py:46
  1333.6 8.2 dynamic_update_slice.50
  1342.6 8.2 dynamic_update_slice.50
  1351.7 8.2 dynamic_update_slice.50
  1360.7 8.2 dynamic_update_slice.50
  1369.7 8.2 dynamic_update_slice.50
  1378.8 8.2 dynamic_update_slice.50
  1387.8 8.2 dynamic_update_slice.50
  1396.8 8.2 dynamic_update_slice.50
  1408.1 33.2 %all-gather.8.cloned.1.call-done = bf16[2,256,8,256]{3,2,1,0:T(8,128)(2,1)} async-done(((bf16[2,256,8,128]{3,2,1,0:T(8,128)(2,1)}), bf16[2,256,8,256]{3,2,1,0:T(8,128)(2,1)}) %all-gather.8.cloned.1.call-update) | async-done | bytes 2097168 | tf_op jit(solution)/shard_map/all_gather | solution.py:76
  (154 shorter events, 96.9 us)
Async XLA Ops:
  7.2 819.9 %copy-start = (s32[8,256]{1,0:T(8,128)S(1)}, s32[8,256]{1,0:T(8,128)}, u32[]{:S(2)}) copy-start(s32[8,256]{1,0:T(8,128)} %param.14) | copy-start | bytes 24580
  7.2 566.5 %all-gather.4.cloned.1.call-start = ((), (), s32[]{:S(2)}) async-start(), calls=%async_computation.2 | async-start | bytes 41943040 | tf_op jit(solution)/shard_map/all_gather | solution.py:82
  7.9 565.8 %copy-start.2 = (bf16[2,256,8,256]{3,2,1,0:T(8,128)(2,1)S(1)}, bf16[2,256,8,256]{3,2,1,0:T(8,128)(2,1)}, u32[]{:S(2)}) copy-start(bf16[2,256,8,256]{3,2,1,0:T(8,128)(2,1)} %param.13) | copy-start | bytes 6291460
  7.9 647.2 %all-reduce.3.cloned.1.call-start = ((), (), s32[]{:S(2)}) async-start(), calls=%async_computation.3 | async-start | bytes 2097152 | tf_op jit(solution)/shard_map/psum | solution.py:87
  8.1 576.8 %copy-start.3 = (bf16[2,256,8,128]{3,2,1,0:T(8,128)(2,1)}, bf16[2,256,8,128]{3,2,1,0:T(8,128)(2,1)S(1)}, u32[]{:S(2)}) copy-start(bf16[2,256,8,128]{3,2,1,0:T(8,128)(2,1)S(1)} %fusion.101) | copy-start | bytes 3145732
  596.1 11.3 copy-start.7
  620.7 238.7 %reduce-scatter.7.cloned.1.call-start = ((), (), s32[]{:S(2)}) async-start(), calls=%async_computation.7 | async-start | bytes 3145728
  625.4 32.1 %copy-start.5 = (bf16[2,256,8,128]{3,2,1,0:T(8,128)(2,1)S(1)}, bf16[2,256,8,128]{3,2,1,0:T(8,128)(2,1)}, u32[]{:S(2)}) copy-start(bf16[2,256,8,128]{3,2,1,0:T(8,128)(2,1)} %copy-done.3) | copy-start | bytes 3145732
  827.0 180.2 %all-gather.6.cloned.1.call-start = ((), (), s32[]{:S(2)}) async-start(), calls=%async_computation.4 | async-start | bytes 3145728 | tf_op jit(solution)/shard_map/all_gather | solution.py:76
  974.0 117.0 %all-reduce.5.cloned.1.call-start = ((), (), s32[]{:S(2)}) async-start(), calls=%async_computation.5 | async-start | bytes 2097152 | tf_op jit(solution)/shard_map/psum | solution.py:87
  1007.2 11.6 copy-start.6
  1054.7 37.9 %copy-start.4 = (bf16[2,256,8,128]{3,2,1,0:T(8,128)(2,1)S(1)}, bf16[2,256,8,128]{3,2,1,0:T(8,128)(2,1)}, u32[]{:S(2)}) copy-start(bf16[2,256,8,128]{3,2,1,0:T(8,128)(2,1)} %copy-done.3) | copy-start | bytes 3145732
  1054.8 238.8 %reduce-scatter.9.cloned.1.call-start = ((), (), s32[]{:S(2)}) async-start(), calls=%async_computation.8 | async-start | bytes 3145728
  1261.2 180.2 %all-gather.8.cloned.1.call-start = ((), (), s32[]{:S(2)}) async-start(), calls=%async_computation.6 | async-start | bytes 3145728 | tf_op jit(solution)/shard_map/all_gather | solution.py:76
  1441.4 3.1 copy-start.1
Sparse Core Ops, SparseCore 0:
  9.6 564.0 all-gather.3
  620.8 34.2 all-reduce.2
  827.1 32.1 reduce-scatter.6
  974.1 33.0 all-gather.5
  1054.9 36.0 all-reduce.4
  1261.3 32.1 reduce-scatter.8
  1408.2 33.0 all-gather.7
where the time goes:
time: 1460 us; the launch traced here: 1450 us
  waiting for transfers between devices  762 us (52%)
  local copies, waits for them, and re-layouts  471 us (32%)
  matrix products  186 us (13%)
  other arithmetic  15.5 us (1%)
  between operations  14.6 us (1%)
    all_gather x1, waiting for transfers between devices, local(): whole_reflection = lax.all_gather(reflection, 'foc', axis=1, tiled=True)  566 us
    dynamic_update_slice x64, local copies, waits for them, and re-layouts, one_focus(): lax.dynamic_update_slice_in_dim(returned_all, returned, focal_index, 2)  230 us
    unnamed x27, local copies, waits for them, and re-layouts  227 us
    all_gather x2, waiting for transfers between devices, renew(): return lax.all_gather(renewed, 'src', axis=3, tiled=True)  66.3 us
    psum x2, waiting for transfers between devices, local(): spectrum = lax.psum(partial_value.astype(jnp.bfloat16), 'rcv')  65.4 us
    unnamed x9, waiting for transfers between devices  65.1 us
  transfers between devices with their start and end apart: 7, of which 7 were waited for; matrix products, arithmetic and copies ran while one was open for 0% of the time, Pallas kernels for 0%

commit v1 on v0

--- a/solution.py
+++ b/solution.py
@@ -1,13 +1,22 @@
+import functools
 import math
 
 import jax
 import jax.numpy as jnp
 from jax import lax
+from jax.experimental import pallas as pl
+from jax.experimental.pallas import tpu as pltpu
 from jax.sharding import PartitionSpec as P
 
 F = 256
 NT = 1024
 ITERS = 2
+LANES = 128
+BLOCK_W = 16
+CHUNKS = 1
+F32 = jnp.float32
+BF16 = jnp.bfloat16
+VMEM_BYTES = 48 * 1024 * 1024
 
 
 def basis_table():
@@ -76,7 +85,7 @@
     return lax.all_gather(renewed, "src", axis=3, tiled=True)
 
 
-def local(reflection, direct_wave, onset_receiver, onset_source):
+def general(reflection, direct_wave, onset_receiver, onset_source):
     basis_rows = basis_table()
     source_index = lax.axis_index("src")
     whole_reflection = lax.all_gather(reflection, "foc", axis=1, tiled=True)
@@ -94,6 +103,544 @@
     return (focusing, muted_trace)
 
 
+def swap(value, axis, mask, count):
+    return lax.ppermute(value, axis, [(i, i ^ mask) for i in range(count)])
+
+
+def ordered_basis(foc_index, foc_count, freq_count, chunk_count):
+    width = freq_count // chunk_count
+    row = jnp.arange(foc_count * 2 * freq_count, dtype=jnp.int32)
+    within = row % width
+    part = row // width % 2
+    piece = row // (2 * width) % foc_count
+    chunk = row // (2 * width * foc_count)
+    frequency = jnp.bitwise_xor(piece, foc_index) * freq_count + chunk * width + within
+    samples = jnp.arange(NT, dtype=jnp.int32)
+
+    def table(freq, quarter, sample):
+        phases = ((freq + 1) * sample + quarter * (NT // 4)) % NT
+        angles = phases.astype(F32) * (2.0 * math.pi / NT)
+        return (jnp.cos(angles) * math.sqrt(2.0 / NT)).astype(BF16)
+
+    rows = table(frequency[:, None], part[:, None], samples[None, :])
+    columns = table(frequency[None, :], part[None, :], samples[:, None])
+    return rows, columns
+
+
+def params(*semantics):
+    return pltpu.CompilerParams(dimension_semantics=semantics, vmem_limit_bytes=VMEM_BYTES)
+
+
+def split_kernel(ids, wave_ref, *refs):
+    outs, hold = refs[:-1], refs[-1]
+    width, focal = wave_ref.shape[1], wave_ref.shape[2]
+    hold[...] = wave_ref[0].astype(F32).reshape(width * focal, LANES)
+    chunk = width // len(outs)
+    for p in range(focal):
+        rows = hold[pl.ds(p, width, stride=focal), :].astype(BF16)
+        for c, out in enumerate(outs):
+            out[0, p] = rows[c * chunk : (c + 1) * chunk]
+
+
+def split_wave(ids, wave, piece, foc_count, chunk_count):
+    freq = wave.shape[1] // foc_count
+    focal = wave.shape[2]
+    chunk = freq // chunk_count
+    return pl.pallas_call(
+        split_kernel,
+        name="split_wave",
+        out_shape=[jax.ShapeDtypeStruct((2, focal, chunk, LANES), BF16)] * chunk_count,
+        grid_spec=pltpu.PrefetchScalarGridSpec(
+            num_scalar_prefetch=1,
+            grid=(2,),
+            in_specs=[
+                pl.BlockSpec((1, freq, focal, LANES), lambda c, ids: (c, ids[2] ^ piece, 0, ids[0]))
+            ],
+            out_specs=[pl.BlockSpec((1, focal, chunk, LANES), lambda c, ids: (c, 0, 0, 0))]
+            * chunk_count,
+            scratch_shapes=[pltpu.VMEM((freq * focal, LANES), F32)],
+        ),
+        compiler_params=params("arbitrary"),
+        cost_estimate=pl.CostEstimate(
+            flops=0, bytes_accessed=8 * focal * freq * LANES, transcendentals=0
+        ),
+    )(ids, wave)
+
+
+def convolve_kernel(pieces, ids, refl_ref, *refs):
+    own, other = refs[:pieces], refs[pieces : 2 * pieces]
+    keep_ref, send_ref, hold, result = refs[2 * pieces :]
+    half, me = ids[0], ids[1]
+    focal, width = own[0].shape[1], own[0].shape[2]
+    sources = refl_ref.shape[2]
+    rows = pieces * 2 * focal
+    per = 2 * focal * width
+    for place, group in ((half, own), (1 - half, other)):
+        for k in range(pieces):
+            hold[place, pl.ds(k * per, per), :] = group[k][...].astype(F32).reshape(per, LANES)
+    for w in range(width):
+        left = jnp.concatenate(
+            [hold[0, pl.ds(w, rows, stride=width), :], hold[1, pl.ds(w, rows, stride=width), :]], 1
+        ).astype(BF16)
+        right = refl_ref[:, w].reshape(2 * sources, 2 * LANES)
+        both = lax.dot_general(left, right, (((1,), (1,)), ((), ())), preferred_element_type=F32)
+        by_real = both[:, :LANES].reshape(pieces, 2, focal, LANES)
+        by_imag = both[:, LANES:].reshape(pieces, 2, focal, LANES)
+        value = jnp.stack([by_real[:, 0] - by_imag[:, 1], by_real[:, 1] + by_imag[:, 0]], 1)
+        result[pl.ds(w, rows, stride=width), :] = value.reshape(rows, LANES)
+    share = focal // 4
+    size = share * width
+    for place, out in ((0, keep_ref), (1, send_ref)):
+        for y in range(2):
+            group = (2 * y + place) ^ me
+            for k in range(pieces):
+                for c in range(2):
+                    start = ((k * 2 + c) * focal + group * share) * width
+                    block = result[pl.ds(pl.multiple_of(start, size), size), :]
+                    out[y, k, c] = block.reshape(share, width, LANES).astype(BF16)
+
+
+def convolve_chunk(ids, reflection, own, other, chunk_index):
+    pieces = len(own)
+    parts, focal, chunk, lanes = own[0].shape
+    sources = reflection.shape[2]
+    steps = chunk // BLOCK_W
+    offset = chunk_index * steps
+    share = focal // 4
+    rows = pieces * 2 * focal
+    piece_spec = pl.BlockSpec((2, focal, BLOCK_W, LANES), lambda g, ids: (0, 0, g, 0))
+    out_spec = pl.BlockSpec(
+        (2, pieces, 2, share, BLOCK_W, LANES), lambda g, ids: (0, 0, 0, 0, g, 0)
+    )
+    out = jax.ShapeDtypeStruct((2, pieces, 2, share, chunk, LANES), BF16)
+    return pl.pallas_call(
+        functools.partial(convolve_kernel, pieces),
+        name="convolve",
+        out_shape=[out, out],
+        grid_spec=pltpu.PrefetchScalarGridSpec(
+            num_scalar_prefetch=1,
+            grid=(steps,),
+            in_specs=[
+                pl.BlockSpec(
+                    (2, BLOCK_W, sources, 2 * LANES), lambda g, ids: (0, offset + g, 0, 0)
+                )
+            ]
+            + [piece_spec] * (2 * pieces),
+            out_specs=[out_spec, out_spec],
+            scratch_shapes=[
+                pltpu.VMEM((2, rows * BLOCK_W, LANES), F32),
+                pltpu.VMEM((rows * BLOCK_W, LANES), F32),
+            ],
+        ),
+        compiler_params=params("arbitrary"),
+        cost_estimate=pl.CostEstimate(
+            flops=2 * chunk * rows * 256 * 256,
+            bytes_accessed=chunk * (2 * sources * 512 + rows * 768),
+            transcendentals=0,
+        ),
+    )(ids, reflection, *own, *other)
+
+
+def correlate_kernel(pieces, ids, refl_ref, *refs):
+    sources_of = [refs[j * pieces : (j + 1) * pieces] for j in range(4)]
+    outs = refs[4 * pieces : 6 * pieces]
+    hold, result = refs[6 * pieces :]
+    half, me = ids[0], ids[1]
+    share, width = refs[0].shape[1], refs[0].shape[2]
+    focal = 4 * share
+    sources = refl_ref.shape[2]
+    rows = pieces * focal
+    size = share * width
+    for j in range(4):
+        group = j ^ me
+        for k in range(pieces):
+            start = pl.multiple_of((k * focal + group * share) * width, size)
+            for c in range(2):
+                block = sources_of[j][k][c].astype(F32).reshape(size, LANES)
+                hold[c, pl.ds(start, size), :] = block
+    for w in range(width):
+        real = hold[0, pl.ds(w, rows, stride=width), :].astype(BF16)
+        imag = hold[1, pl.ds(w, rows, stride=width), :].astype(BF16)
+        left = jnp.concatenate(
+            [jnp.concatenate([real, imag], 1), jnp.concatenate([imag, -real], 1)], 0
+        )
+        right = refl_ref[:, w].reshape(2 * sources, 2 * LANES)
+        value = lax.dot_general(left, right, (((1,), (0,)), ((), ())), preferred_element_type=F32)
+        result[0, pl.ds(w, 2 * rows, stride=width), :] = value[:, :LANES]
+        result[1, pl.ds(w, 2 * rows, stride=width), :] = value[:, LANES:]
+    size = focal * width
+    for place, group in ((half, outs[:pieces]), (1 - half, outs[pieces:])):
+        for k in range(pieces):
+            for c in range(2):
+                block = result[place, pl.ds((c * pieces + k) * size, size), :]
+                group[k][c] = block.reshape(focal, width, LANES).astype(BF16)
+
+
+def correlate_chunk(ids, reflection, parts_of, chunk_index):
+    pieces = len(parts_of[0])
+    two, share, chunk, lanes = parts_of[0][0].shape
+    focal = 4 * share
+    sources = reflection.shape[2]
+    steps = chunk // BLOCK_W
+    offset = chunk_index * steps
+    rows = pieces * 2 * focal
+    in_spec = pl.BlockSpec((2, share, BLOCK_W, LANES), lambda g, ids: (0, 0, g, 0))
+    out_spec = pl.BlockSpec((2, focal, BLOCK_W, LANES), lambda g, ids: (0, 0, g, 0))
+    out = jax.ShapeDtypeStruct((2, focal, chunk, LANES), BF16)
+    results = pl.pallas_call(
+        functools.partial(correlate_kernel, pieces),
+        name="correlate",
+        out_shape=[out] * (2 * pieces),
+        grid_spec=pltpu.PrefetchScalarGridSpec(
+            num_scalar_prefetch=1,
+            grid=(steps,),
+            in_specs=[
+                pl.BlockSpec(
+                    (2, BLOCK_W, sources, 2 * LANES), lambda g, ids: (0, offset + g, 0, 0)
+                )
+            ]
+            + [in_spec] * (4 * pieces),
+            out_specs=[out_spec] * (2 * pieces),
+            scratch_shapes=[
+                pltpu.VMEM((2, rows // 2 * BLOCK_W, LANES), F32),
+                pltpu.VMEM((2, rows * BLOCK_W, LANES), F32),
+            ],
+        ),
+        compiler_params=params("arbitrary"),
+        cost_estimate=pl.CostEstimate(
+            flops=2 * chunk * rows * 256 * 256,
+            bytes_accessed=chunk * (2 * sources * 512 + rows * 768),
+            transcendentals=0,
+        ),
+    )(ids, reflection, *[v for group in parts_of for v in group])
+    return results[:pieces], results[pieces:]
+
+
+def gather_rows(refs, index):
+    return jnp.concatenate([ref[c, index] for ref in refs for c in range(2)], 0)
+
+
+def windowed(columns_ref, rows, onsets):
+    signal = jnp.dot(columns_ref[...], rows, preferred_element_type=F32)
+    sample = lax.broadcasted_iota(jnp.int32, signal.shape, 0)
+    return jnp.where(sample < onsets, signal, 0.0).astype(BF16)
+
+
+def mute_source_kernel(count, ids, onset_ref, rows_ref, columns_ref, *refs):
+    ins, outs = refs[:count], refs[count:]
+    share, width = ins[0].shape[1], ins[0].shape[2]
+    first = ids[1] * share
+    spectrum = jnp.concatenate([gather_rows(ins, p) for p in range(share)], 1)
+    onsets = jnp.concatenate([onset_ref[pl.ds(first + p, 1), :] for p in range(share)], 1)
+    muted = windowed(columns_ref, spectrum, onsets)
+    back = jnp.dot(rows_ref[...], muted, preferred_element_type=F32).astype(BF16)
+    for i, out in enumerate(outs):
+        for c in range(2):
+            for p in range(share):
+                start = (2 * i + c) * width
+                out[c, p] = back[start : start + width, p * LANES : (p + 1) * LANES]
+
+
+def whole(shape):
+    return pl.BlockSpec(shape, lambda *index: (0,) * len(shape))
+
+
+def mute_source(ids, onset, rows, columns, pieces):
+    shape = pieces[0].shape
+    count = len(pieces)
+    return pl.pallas_call(
+        functools.partial(mute_source_kernel, count),
+        name="mute_source",
+        out_shape=[jax.ShapeDtypeStruct(shape, BF16)] * count,
+        grid_spec=pltpu.PrefetchScalarGridSpec(
+            num_scalar_prefetch=1,
+            grid=(1,),
+            in_specs=[whole(onset.shape), whole(rows.shape), whole(columns.shape)]
+            + [whole(shape)] * count,
+            out_specs=[whole(shape)] * count,
+        ),
+        compiler_params=params("arbitrary"),
+        cost_estimate=pl.CostEstimate(
+            flops=4 * NT * 2 * F * shape[1] * LANES, bytes_accessed=3 << 20, transcendentals=0
+        ),
+    )(ids, onset, rows, columns, *pieces)
+
+
+def trace_kernel(pieces, ids, onset_ref, rows_ref, *refs):
+    ins, out_ref, hold = refs[:-2], refs[-2], refs[-1]
+    share = ins[0].shape[1]
+    step = pl.program_id(0)
+    count = len(ins) // 4
+
+    @pl.when(step == 0)
+    def unpack():
+        for j in range(4):
+            for p in range(share):
+                hold[j * share + p] = gather_rows(ins[j * count : (j + 1) * count], p)
+
+    signal = lax.dot_general(
+        hold[step], rows_ref[...], (((0,), (0,)), ((), ())), preferred_element_type=F32
+    )
+    sample = lax.broadcasted_iota(jnp.int32, signal.shape, 1)
+    out_ref[0] = jnp.where(sample < onset_ref[0], signal, 0.0).astype(BF16)
+
+
+def trace_source(ids, onset, rows, parts_of):
+    focal, sources = onset.shape
+    shape = parts_of[0][0].shape
+    share = shape[1]
+    flat = [v for group in parts_of for v in group]
+
+    def place(g, ids):
+        return ((g // share) ^ ids[1]) * share + g % share, 0, 0
+
+    return pl.pallas_call(
+        functools.partial(trace_kernel, len(parts_of[0])),
+        name="trace_source",
+        out_shape=jax.ShapeDtypeStruct((focal, sources, NT), BF16),
+        grid_spec=pltpu.PrefetchScalarGridSpec(
+            num_scalar_prefetch=1,
+            grid=(focal,),
+            in_specs=[pl.BlockSpec((1, sources, 1), place), whole(rows.shape)]
+            + [whole(shape)] * len(flat),
+            out_specs=pl.BlockSpec((1, sources, NT), place),
+            scratch_shapes=[pltpu.VMEM((focal, 2 * F, LANES), BF16)],
+        ),
+        compiler_params=params("arbitrary"),
+        cost_estimate=pl.CostEstimate(
+            flops=2 * NT * 2 * F * focal * LANES, bytes_accessed=5 << 20, transcendentals=0
+        ),
+    )(ids, onset[:, :, None], rows, *flat)
+
+
+def updated(count, ids, onset_ref, rows_ref, columns_ref, refs, step, group):
+    ins, arrived, direct = refs[0], refs[1], refs[2]
+    spectra = []
+    for p in range(group):
+        parts = []
+        for i, ref in enumerate(ins):
+            for c in range(2):
+                value = ref[c, p]
+                if i in arrived:
+                    value = (value.astype(F32) + arrived[i][c, p].astype(F32)).astype(BF16)
+                parts.append(value)
+        spectra.append(jnp.concatenate(parts, 0))
+    onsets = jnp.concatenate(
+        [onset_ref[pl.ds(step * group + p, 1), :] for p in range(group)], 1
+    )
+    muted = windowed(columns_ref, jnp.concatenate(spectra, 1), onsets)
+    back = jnp.dot(rows_ref[...], muted, preferred_element_type=F32)
+    width = ins[0].shape[2]
+    for i in range(count):
+        for c in range(2):
+            for p in range(group):
+                start = (2 * i + c) * width
+                block = back[start : start + width, p * LANES : (p + 1) * LANES]
+                yield i, c, p, direct[i][c, p].astype(F32) + block
+
+
+def mute_receiver_kernel(count, own, ids, onset_ref, rows_ref, columns_ref, *refs):
+    ins, extra = refs[:count], refs[count : count + len(own)]
+    direct = refs[count + len(own) : 2 * count + len(own)]
+    outs = refs[2 * count + len(own) :]
+    group = ins[0].shape[1]
+    state = (ins, dict(zip(own, extra)), direct)
+    step = pl.program_id(0)
+    for i, c, p, value in updated(
+        count, ids, onset_ref, rows_ref, columns_ref, state, step, group
+    ):
+        outs[i][c, p] = value.astype(BF16)
+
+
+def mute_receiver_last_kernel(
+    count, own, pieces, ids, onset_ref, rows_ref, columns_ref, *refs
+):
+    ins, extra = refs[:count], refs[count : count + len(own)]
+    direct = refs[count + len(own) : 2 * count + len(own)]
+    out_ref, hold = refs[2 * count + len(own) :]
+    group, width = ins[0].shape[1], ins[0].shape[2]
+    focal = out_ref.shape[2]
+    chunks = count // pieces
+    state = (ins, dict(zip(own, extra)), direct)
+    step = pl.program_id(0)
+    for i, c, p, value in updated(
+        count, ids, onset_ref, rows_ref, columns_ref, state, step, group
+    ):
+        chunk, k = i // pieces, i % pieces
+        first = c * F + ((k ^ ids[2]) * chunks + chunk) * width
+        hold[pl.ds(first * focal + step * group + p, width, stride=focal), :] = value
+
+    @pl.when(step == pl.num_programs(0) - 1)
+    def flush():
+        out_ref[...] = hold[...].astype(BF16).reshape(out_ref.shape)
+
+
+def mute_receiver(ids, onset, rows, columns, pieces, arrived, direct, last, piece_count):
+    shape = pieces[0].shape
+    focal = shape[1]
+    count = len(pieces)
+    own = sorted(arrived)
+    group = 2
+    steps = focal // group
+    spec = pl.BlockSpec((2, group) + shape[2:], lambda g, ids: (0, g, 0, 0))
+    common = dict(
+        num_scalar_prefetch=1,
+        grid=(steps,),
+        in_specs=[
+            pl.BlockSpec((focal, LANES), lambda g, ids: (0, ids[0])),
+            whole(rows.shape),
+            whole(columns.shape),
+        ]
+        + [spec] * (2 * count + len(own)),
+    )
+    if last:
+        kernel = functools.partial(mute_receiver_last_kernel, count, own, piece_count)
+        out_shape = jax.ShapeDtypeStruct((2, F, focal, LANES), BF16)
+        grid_spec = pltpu.PrefetchScalarGridSpec(
+            out_specs=whole(out_shape.shape),
+            scratch_shapes=[pltpu.VMEM((2 * F * focal, LANES), F32)],
+            **common,
+        )
+    else:
+        kernel = functools.partial(mute_receiver_kernel, count, own)
+        out_shape = [jax.ShapeDtypeStruct(shape, BF16)] * count
+        grid_spec = pltpu.PrefetchScalarGridSpec(out_specs=[spec] * count, **common)
+    return pl.pallas_call(
+        kernel,
+        name="mute_receiver",
+        out_shape=out_shape,
+        grid_spec=grid_spec,
+        compiler_params=params("arbitrary"),
+        cost_estimate=pl.CostEstimate(
+            flops=4 * NT * 2 * F * focal * LANES, bytes_accessed=5 << 20, transcendentals=0
+        ),
+    )(ids, onset, rows, columns, *pieces, *[arrived[i] for i in own], *direct)
+
+
+def join_kernel(ids, own_ref, other_ref, out_ref):
+    half = ids[0]
+    out_ref[:, :, :, pl.ds(pl.multiple_of(half * LANES, LANES), LANES)] = own_ref[...]
+    out_ref[:, :, :, pl.ds(pl.multiple_of((1 - half) * LANES, LANES), LANES)] = other_ref[...]
+
+
+def join_halves(ids, own, other):
+    two, freq, focal, lanes = own.shape
+    step = freq // 4
+    spec = pl.BlockSpec((1, step, focal, lanes), lambda c, g, ids: (c, g, 0, 0))
+    return pl.pallas_call(
+        join_kernel,
+        name="join_halves",
+        out_shape=jax.ShapeDtypeStruct((two, freq, focal, 2 * lanes), BF16),
+        grid_spec=pltpu.PrefetchScalarGridSpec(
+            num_scalar_prefetch=1,
+            grid=(two, 4),
+            in_specs=[spec, spec],
+            out_specs=pl.BlockSpec((1, step, focal, 2 * lanes), lambda c, g, ids: (c, g, 0, 0)),
+        ),
+        compiler_params=params("arbitrary", "arbitrary"),
+        cost_estimate=pl.CostEstimate(
+            flops=0, bytes_accessed=8 * two * freq * focal * lanes, transcendentals=0
+        ),
+    )(ids, own, other)
+
+
+def add(left, right):
+    return (left.astype(F32) + right.astype(F32)).astype(BF16)
+
+
+def resident(counts, reflection, direct_wave, onset_receiver, onset_source):
+    src_count, rcv_count, foc_count = counts
+    ids = jnp.stack([lax.axis_index("src"), lax.axis_index("rcv"), lax.axis_index("foc")])
+    ids = ids.astype(jnp.int32)
+    freq = reflection.shape[1]
+    pieces = range(foc_count)
+    order = [k for k in (2, 3, 1, 0) if k < foc_count]
+    chunks = range(CHUNKS)
+
+    def to_foc(value, k):
+        return value if k == 0 else swap(value, "foc", k, foc_count)
+
+    def to_src(value):
+        return swap(value, "src", 1, src_count)
+
+    def to_core(value):
+        return swap(value, "rcv", 1, rcv_count)
+
+    def to_y(value):
+        return swap(value, "rcv", 2, rcv_count)
+
+    direct = [[None] * foc_count for c in chunks]
+    for k in order:
+        for c, value in enumerate(split_wave(ids, direct_wave, k, foc_count, CHUNKS)):
+            direct[c][k] = value
+    rows, columns = ordered_basis(ids[2], foc_count, freq, CHUNKS)
+    focusing = direct
+    muted_trace = None
+    for iteration in range(ITERS):
+        last = iteration == ITERS - 1
+        spectrum = []
+        for c in chunks:
+            own = [to_foc(focusing[c][k], k) for k in pieces]
+            other = [to_src(value) for value in own]
+            keep, send = convolve_chunk(ids, reflection, own, other, c)
+            got = to_core(send)
+            beyond = to_y(add(keep[1], got[1]))
+            total = (
+                keep[0].astype(F32) + got[0].astype(F32) + beyond.astype(F32)
+            ).astype(BF16)
+            spectrum += [to_foc(total[k], k) for k in pieces]
+        returned = mute_source(ids, onset_source, rows, columns, spectrum)
+        kept = [[None] * foc_count for c in chunks]
+        arrived = {}
+        ready = [[None] * foc_count for c in chunks]
+        for c in chunks:
+            mine = [to_foc(returned[c * foc_count + k], k) for k in pieces]
+            across = [to_y(value) for value in mine]
+            groups = [mine, [to_core(v) for v in mine], across, [to_core(v) for v in across]]
+            own, other = correlate_chunk(ids, reflection, groups, c)
+            for k in order:
+                got = to_src(other[k])
+                if k == 0:
+                    ready[c][k] = own[k]
+                    arrived[c * foc_count] = got
+                else:
+                    ready[c][k] = to_foc(add(own[k], got), k)
+        flat = [v for group in ready for v in group]
+        flat_direct = [v for group in direct for v in group]
+        renewed = mute_receiver(
+            ids, onset_receiver, rows, columns, flat, arrived, flat_direct, last, foc_count
+        )
+        if last:
+            across = [to_y(value) for value in spectrum]
+            groups = [
+                spectrum,
+                [to_core(v) for v in spectrum],
+                across,
+                [to_core(v) for v in across],
+            ]
+            muted_trace = trace_source(ids, onset_source, rows, groups)
+            return join_halves(ids, renewed, to_src(renewed)), muted_trace
+        focusing = [renewed[c * foc_count : (c + 1) * foc_count] for c in chunks]
+
+
+def local(counts, reflection, direct_wave, onset_receiver, onset_source):
+    src_count, rcv_count, foc_count = counts
+    two, freq, sources, receivers = reflection.shape
+    focal = direct_wave.shape[2]
+    fits = (
+        (src_count, rcv_count) == (2, 4)
+        and foc_count in (2, 4)
+        and sources == LANES
+        and receivers == 2 * LANES
+        and focal == 8
+        and freq % (CHUNKS * BLOCK_W) == 0
+        and freq * foc_count == F
+    )
+    if fits:
+        return resident(counts, reflection, direct_wave, onset_receiver, onset_source)
+    return general(reflection, direct_wave, onset_receiver, onset_source)
+
+
 def solution(mesh):
     in_specs = (
         P(None, "foc", "src", "rcv"),
@@ -102,4 +649,11 @@
         P("foc", "src"),
     )
     out_specs = (P(None, None, "foc", "rcv"), P("foc", "src", None))
-    return jax.shard_map(local, mesh=mesh, in_specs=in_specs, out_specs=out_specs, check_vma=False)
+    counts = (mesh.shape["src"], mesh.shape["rcv"], mesh.shape["foc"])
+    return jax.shard_map(
+        functools.partial(local, counts),
+        mesh=mesh,
+        in_specs=in_specs,
+        out_specs=out_specs,
+        check_vma=False,
+    )

time: 1460 us -> 299 us (0.20)
  waiting for transfers between devices: 762 us -> 143 us
  local copies, waits for them, and re-layouts: 471 us -> 1.86 us
  matrix products: 186 us -> 0 us
  starting transfers between devices: 1.39 us -> 75.1 us
  Pallas kernels: 0 us -> 56.4 us
    all_gather x3 -> x0, waiting for transfers between devices: 632 us -> none  [the longest x1 566 us: local(): whole_reflection = lax.all_gather(reflection, 'foc', axis=1, tiled=True)]
    dynamic_update_slice x64 -> x0, local copies, waits for them, and re-layouts: 230 us -> none  [one_focus(): lax.dynamic_update_slice_in_dim(returned_all, returned, focal_index, 2)]
    unnamed x27 -> x6, local copies, waits for them, and re-layouts: 227 us -> 1.6 us
    dot_general x56 -> x0, matrix products: 186 us -> none  [the longest x32 27.6 us: one_focus(): jnp.einsum('prt,cwt->cwpr', muted_one, basis_rows, preferred_element_type...]
    ppermute x0 -> x81, waiting for transfers between devices: none -> 143 us  [swap(): return lax.ppermute(value, axis, [(i, i ^ mask) for i in range(count)])]
    ppermute x0 -> x81, starting transfers between devices: none -> 75.1 us  [swap(): return lax.ppermute(value, axis, [(i, i ^ mask) for i in range(count)])]
    psum x2 -> x0, waiting for transfers between devices: 65.4 us -> none  [local(): spectrum = lax.psum(partial_value.astype(jnp.bfloat16), 'rcv')]
    unnamed x9 -> x0, waiting for transfers between devices: 65.1 us -> none
  transfers between devices with their start and end apart: 7 -> 81, of which waited for: 7 -> 43; matrix products, arithmetic and copies ran while one was open for 0% -> 6% of each run, Pallas kernels for 0% -> 3%
where the time goes in v1:
time: 299 us; the launch traced here: 295 us
  waiting for transfers between devices  143 us (48%)
  starting transfers between devices  75.1 us (25%)
  Pallas kernels  56.4 us (19%)
  other arithmetic  17.6 us (6%)
    ppermute x81, waiting for transfers between devices, swap(): return lax.ppermute(value, axis, [(i, i ^ mask) for i in range(count)])  143 us
    ppermute x81, starting transfers between devices, swap(): return lax.ppermute(value, axis, [(i, i ^ mask) for i in range(count)])  75.1 us
    convert_element_type x2, other arithmetic, table(): return (jnp.cos(angles) * math.sqrt(2.0 / NT)).astype(BF16)  16.7 us
    pallas_call x2, Pallas kernels, convolve_chunk(): pl.pallas_call(functools.partial(convolve_kernel, pieces), name='convolve...  13.4 us
    pallas_call x2, Pallas kernels, correlate_chunk(): pl.pallas_call(functools.partial(correlate_kernel, pieces), name='correla...  13.2 us
    pallas_call x2, Pallas kernels, mute_receiver(): pl.pallas_call(kernel, name='mute_receiver', out_shape=out_shape, grid_sp...  11.1 us
    pallas_call x1, Pallas kernels, trace_source(): pl.pallas_call(functools.partial(trace_kernel, len(parts_of[0])), name='t...  6.18 us
    pallas_call x1, Pallas kernels, join_halves(): pl.pallas_call(join_kernel, name='join_halves', out_shape=jax.ShapeDtypeS...  6.05 us
  transfers between devices with their start and end apart: 81, of which 43 were waited for; matrix products, arithmetic and copies ran while one was open for 6% of the time, Pallas kernels for 3%

profile of v1, /device:TPU:0, one launch (start us, length us, event | category | flops | bytes accessed | tf_op | source)
XLA Modules:
  0.0 294.9 jit_solution(13308431834893428841)
XLA Ops:
  0.7 1.6 copy-done
  3.1 3.1 %collective-permute-start = (bf16[2,8,64,128]{3,2,1,0:T(8,128)(2,1)S(1)}, bf16[2,8,64,128]{3,2,1,0:T(8,128)(2,1)S(1)}, u32[]{:S(2)}, u32[]{:S(2)}) collective-permute-start(bf16[2,8,64,128]{3,2,1,0:T(8,128)(2,1)S(1)} %split_wave.5.refs_6_), channel_id=1, source_target_pairs={{0,1},{1,0},{2,3},{3,2},{4,5},{5,4},{6,7},{7,6},{8,9},{9,8},{10,11... | collective-permute-start | bytes 786440 | tf_op jit(solution)/shard_map/ppermute | solution.py:107
  7.0 2.7 collective-permute-start.1
  11.2 1.8 collective-permute-start.3
  13.0 3.9 %collective-permute-done.refs_1_ = bf16[2,8,64,128]{3,2,1,0:T(8,128)(2,1)S(1)} collective-permute-done((bf16[2,8,64,128]{3,2,1,0:T(8,128)(2,1)S(1)}, bf16[2,8,64,128]{3,2,1,0:T(8,128)(2,1)S(1)}, u32[]{:S(2)}, u32[]{:S(2)}) %collective-permute-start) | collective-permute-done | bytes 262176 | tf_op jit(solution)/shard_map/ppermute | solution.py:107
  16.9 1.7 collective-permute-start.4
  18.6 9.8 %collective-permute-done.1.refs_2_ = bf16[2,8,64,128]{3,2,1,0:T(8,128)(2,1)S(1)} collective-permute-done((bf16[2,8,64,128]{3,2,1,0:T(8,128)(2,1)S(1)}, bf16[2,8,64,128]{3,2,1,0:T(8,128)(2,1)S(1)}, u32[]{:S(2)}, u32[]{:S(2)}) %collective-permute-start.1) | collective-permute-done | bytes 262176 | tf_op jit(solution)/shard_map/ppermute | solution.py:107
  28.4 1.5 collective-permute-start.5
  30.4 4.3 %collective-permute-done.5.refs_6_ = bf16[2,8,64,128]{3,2,1,0:T(8,128)(2,1)S(1)} collective-permute-done((bf16[2,8,64,128]{3,2,1,0:T(8,128)(2,1)S(1)}, bf16[2,8,64,128]{3,2,1,0:T(8,128)(2,1)S(1)}, u32[]{:S(2)}, u32[]{:S(2)}) %collective-permute-start.5) | collective-permute-done | bytes 262176 | tf_op jit(solution)/shard_map/ppermute | solution.py:107
  34.8 2.8 collective-permute-done.6.refs_7_
  37.6 6.6 %convolve.2 = (bf16[2,4,2,2,64,128]{5,4,3,2,1,0:T(8,128)(2,1)S(1)}, bf16[2,4,2,2,64,128]{5,4,3,2,1,0:T(8,128)(2,1)S(1)}) custom-call(s32[3]{0:T(128)S(1)} %pad_add_fusion.ids, bf16[2,64,128,256]{3,2,1,0:T(8,128)(2,1)} %refl_ref.7, bf16[2,8,64,128]{3,2,1,0:T(8,128)(2,1)S(1)} %split_wave.4.refs_0_.refs_5_, ...), custom_call_target="tpu_custom_call" | custom-call | flops 536870912 | bytes 11534336 | tf_op jit(solution)/shard_map/convolve/pallas_call | solution.py:216
  44.3 1.9 collective-permute-done.7
  46.2 1.6 collective-permute-start.8
  47.8 8.7 %fusion.5.rows_ref = bf16[512,1024]{1,0:T(8,128)(2,1)S(1)} fusion(s32[512]{0:T(512)S(1)} %get-tuple-element.75, s32[512]{0:T(512)S(1)} %get-tuple-element.74), kind=kLoop, calls=%fused_computation.11 | loop fusion | flops 8912896 | bytes 1052672 | tf_op jit(solution)/shard_map/convert_element_type | solution.py:123
  56.7 2.5 collective-permute-start.9
  59.2 2.5 collective-permute-start.10
  61.7 8.0 %fusion.11.columns_ref = bf16[1024,512]{1,0:T(8,128)(2,1)S(1)} fusion(s32[512]{0:T(512)S(1)} %get-tuple-element.75, s32[512]{0:T(512)S(1)} %get-tuple-element.74), kind=kLoop, calls=%fused_computation.17 | loop fusion | flops 8912896 | bytes 1052672 | tf_op jit(solution)/shard_map/convert_element_type | solution.py:123
  69.8 1.7 mute_source.2
  72.6 3.4 %collective-permute-start.13 = (bf16[2,2,64,128]{3,2,1,0:T(8,128)(2,1)S(1)}, bf16[2,2,64,128]{3,2,1,0:T(8,128)(2,1)S(1)}, u32[]{:S(2)}, u32[]{:S(2)}) collective-permute-start(bf16[2,2,64,128]{3,2,1,0:T(8,128)(2,1)S(1)} %get-tuple-element.38), channel_id=1, source_target_pairs={{0,2},{1,3},{2,0},{3,1},{4,6},{5,7},{6,4},{7,5},{8,10},{9,11},{10,... | collective-permute-start | bytes 196616 | tf_op jit(solution)/shard_map/ppermute | solution.py:107
  76.7 3.1 %collective-permute-done.13.refs_2_ = bf16[2,2,64,128]{3,2,1,0:T(8,128)(2,1)S(1)} collective-permute-done((bf16[2,2,64,128]{3,2,1,0:T(8,128)(2,1)S(1)}, bf16[2,2,64,128]{3,2,1,0:T(8,128)(2,1)S(1)}, u32[]{:S(2)}, u32[]{:S(2)}) %collective-permute-start.13) | collective-permute-done | bytes 65568 | tf_op jit(solution)/shard_map/ppermute | solution.py:107
  79.8 2.3 collective-permute-done.14.refs_3_
  82.5 1.5 collective-permute-start.21
  89.6 6.6 %correlate.2 = (bf16[2,8,64,128]{3,2,1,0:T(8,128)(2,1)S(1)}, bf16[2,8,64,128]{3,2,1,0:T(8,128)(2,1)S(1)}, bf16[2,8,64,128]{3,2,1,0:T(8,128)(2,1)S(1)}, bf16[2,8,...) custom-call(s32[3]{0:T(128)S(1)} %pad_add_fusion.ids, ...), custom_call_target="tpu_custom_call" | custom-call | flops 536870912 | bytes 11534336 | tf_op jit(solution)/shard_map/correlate/pallas_call | solution.py:290
  96.2 1.6 collective-permute-start.27
  98.3 1.5 collective-permute-start.31
  100.3 5.1 %collective-permute-done.27 = bf16[2,8,64,128]{3,2,1,0:T(8,128)(2,1)S(1)} collective-permute-done((bf16[2,8,64,128]{3,2,1,0:T(8,128)(2,1)S(1)}, bf16[2,8,64,128]{3,2,1,0:T(8,128)(2,1)S(1)}, u32[]{:S(2)}, u32[]{:S(2)}) %collective-permute-start.27) | collective-permute-done | bytes 262176 | tf_op jit(solution)/shard_map/ppermute | solution.py:107
  105.6 5.5 %collective-permute-done.29 = bf16[2,8,64,128]{3,2,1,0:T(8,128)(2,1)S(1)} collective-permute-done((bf16[2,8,64,128]{3,2,1,0:T(8,128)(2,1)S(1)}, bf16[2,8,64,128]{3,2,1,0:T(8,128)(2,1)S(1)}, u32[]{:S(2)}, u32[]{:S(2)}) %collective-permute-start.29) | collective-permute-done | bytes 262176 | tf_op jit(solution)/shard_map/ppermute | solution.py:107
  111.8 4.8 %collective-permute-done.31 = bf16[2,8,64,128]{3,2,1,0:T(8,128)(2,1)S(1)} collective-permute-done((bf16[2,8,64,128]{3,2,1,0:T(8,128)(2,1)S(1)}, bf16[2,8,64,128]{3,2,1,0:T(8,128)(2,1)S(1)}, u32[]{:S(2)}, u32[]{:S(2)}) %collective-permute-start.31) | collective-permute-done | bytes 262176 | tf_op jit(solution)/shard_map/ppermute | solution.py:107
  116.7 2.0 collective-permute-start.32
  118.7 2.8 collective-permute-done.33.refs_4_
  121.5 7.9 %collective-permute-done.30.refs_2_ = bf16[2,8,64,128]{3,2,1,0:T(8,128)(2,1)S(1)} collective-permute-done((bf16[2,8,64,128]{3,2,1,0:T(8,128)(2,1)S(1)}, bf16[2,8,64,128]{3,2,1,0:T(8,128)(2,1)S(1)}, u32[]{:S(2)}, u32[]{:S(2)}) %collective-permute-start.30) | collective-permute-done | bytes 262176 | tf_op jit(solution)/shard_map/ppermute | solution.py:107
  129.4 5.6 %mute_receiver.2 = (bf16[2,8,64,128]{3,2,1,0:T(8,128)(2,1)S(1)}, bf16[2,8,64,128]{3,2,1,0:T(8,128)(2,1)S(1)}, bf16[2,8,64,128]{3,2,1,0:T(8,128)(2,1)S(1)}, bf16[2,8,64,128]{3,2,1,0:T(8,128)(2,1)S(1)}) custom-call(s32[3]{0:T(128)S(1)} %pad_add_fusion.ids, s32[8,256]{1,0:T(8,128)S(1)} %copy-done.2, bf16[512,1024]{1,0:T(8,128)(2,1)S(1)} %fusion.5.rows_ref, ...), custom_call_target="tpu_custom_call" | custom-call | flops 2147483648 | bytes 5242880 | tf_op jit(solution)/shard_map/mute_receiver/pallas_call | solution.py:508
  135.0 6.1 %collective-permute-start.34 = (bf16[2,8,64,128]{3,2,1,0:T(8,128)(2,1)S(1)}, bf16[2,8,64,128]{3,2,1,0:T(8,128)(2,1)S(1)}, u32[]{:S(2)}, u32[]{:S(2)}) collective-permute-start(bf16[2,8,64,128]{3,2,1,0:T(8,128)(2,1)S(1)} %get-tuple-element.49), channel_id=1, source_target_pairs={{0,1},{1,0},{2,3},{3,2},{4,5},{5,4},{6,7},{7,6},{8,9},{9,8},{10,11... | collective-permute-start | bytes 786440 | tf_op jit(solution)/shard_map/ppermute | solution.py:107
  142.1 1.5 collective-permute-start.36
  143.6 1.5 collective-permute-start.37
  145.1 7.4 %collective-permute-done.34.refs_1_ = bf16[2,8,64,128]{3,2,1,0:T(8,128)(2,1)S(1)} collective-permute-done((bf16[2,8,64,128]{3,2,1,0:T(8,128)(2,1)S(1)}, bf16[2,8,64,128]{3,2,1,0:T(8,128)(2,1)S(1)}, u32[]{:S(2)}, u32[]{:S(2)}) %collective-permute-start.34) | collective-permute-done | bytes 262176 | tf_op jit(solution)/shard_map/ppermute | solution.py:107
  154.0 8.5 %collective-permute-done.35.refs_2_ = bf16[2,8,64,128]{3,2,1,0:T(8,128)(2,1)S(1)} collective-permute-done((bf16[2,8,64,128]{3,2,1,0:T(8,128)(2,1)S(1)}, bf16[2,8,64,128]{3,2,1,0:T(8,128)(2,1)S(1)}, u32[]{:S(2)}, u32[]{:S(2)}) %collective-permute-start.35) | collective-permute-done | bytes 262176 | tf_op jit(solution)/shard_map/ppermute | solution.py:107
  162.5 1.5 collective-permute-start.39
  164.5 4.3 %collective-permute-done.39.refs_6_ = bf16[2,8,64,128]{3,2,1,0:T(8,128)(2,1)S(1)} collective-permute-done((bf16[2,8,64,128]{3,2,1,0:T(8,128)(2,1)S(1)}, bf16[2,8,64,128]{3,2,1,0:T(8,128)(2,1)S(1)}, u32[]{:S(2)}, u32[]{:S(2)}) %collective-permute-start.39) | collective-permute-done | bytes 262176 | tf_op jit(solution)/shard_map/ppermute | solution.py:107
  168.8 2.8 collective-permute-done.40.refs_7_
  171.7 6.8 %convolve.3 = (bf16[2,4,2,2,64,128]{5,4,3,2,1,0:T(8,128)(2,1)S(1)}, bf16[2,4,2,2,64,128]{5,4,3,2,1,0:T(8,128)(2,1)S(1)}) custom-call(s32[3]{0:T(128)S(1)} %pad_add_fusion.ids, bf16[2,64,128,256]{3,2,1,0:T(8,128)(2,1)} %refl_ref.7, bf16[2,8,64,128]{3,2,1,0:T(8,128)(2,1)S(1)} %get-tuple-element.48.refs_0_, ...), custom_call_target="tpu_custom_call" | custom-call | flops 536870912 | bytes 11534336 | tf_op jit(solution)/shard_map/convolve/pallas_call | solution.py:216
  178.5 1.9 collective-permute-done.41
  181.2 7.7 %collective-permute-done.42 = bf16[4,2,2,64,128]{4,3,2,1,0:T(8,128)(2,1)S(1)} collective-permute-done((bf16[4,2,2,64,128]{4,3,2,1,0:T(8,128)(2,1)S(1)}, bf16[4,2,2,64,128]{4,3,2,1,0:T(8,128)(2,1)S(1)}, u32[]{:S(2)}, u32[]{:S(2)}) %collective-permute-start.42) | collective-permute-done | bytes 262176 | tf_op jit(solution)/shard_map/ppermute | solution.py:107
  189.1 3.0 %collective-permute-start.43 = (bf16[2,2,64,128]{3,2,1,0:T(8,128)(2,1)S(1)}, bf16[2,2,64,128]{3,2,1,0:T(8,128)(2,1)S(1)}, u32[]{:S(2)}, u32[]{:S(2)}) collective-permute-start(bf16[2,2,64,128]{3,2,1,0:T(8,128)(2,1)S(1)} %get-tuple-element.68), channel_id=1, source_target_pairs={{0,1},{1,0},{2,3},{3,2},{4,5},{5,4},{6,7},{7,6},{8,9},{9,8},{10,11... | collective-permute-start | bytes 196616 | tf_op jit(solution)/shard_map/ppermute | solution.py:107
  193.0 1.5 collective-permute-start.45
  194.5 5.0 %collective-permute-done.44.refs_2_ = bf16[2,2,64,128]{3,2,1,0:T(8,128)(2,1)S(1)} collective-permute-done((bf16[2,2,64,128]{3,2,1,0:T(8,128)(2,1)S(1)}, bf16[2,2,64,128]{3,2,1,0:T(8,128)(2,1)S(1)}, u32[]{:S(2)}, u32[]{:S(2)}) %collective-permute-start.44) | collective-permute-done | bytes 65568 | tf_op jit(solution)/shard_map/ppermute | solution.py:107
  199.5 1.7 mute_source.3
  203.9 1.7 collective-permute-start.48
  206.5 2.2 collective-permute-done.47.refs_2_
  217.6 6.6 %correlate.3 = (bf16[2,8,64,128]{3,2,1,0:T(8,128)(2,1)S(1)}, bf16[2,8,64,128]{3,2,1,0:T(8,128)(2,1)S(1)}, bf16[2,8,64,128]{3,2,1,0:T(8,128)(2,1)S(1)}, bf16[2,8,...) custom-call(s32[3]{0:T(128)S(1)} %pad_add_fusion.ids, ...), custom_call_target="tpu_custom_call" | custom-call | flops 536870912 | bytes 11534336 | tf_op jit(solution)/shard_map/correlate/pallas_call | solution.py:290
  224.2 1.5 collective-permute-start.61
  228.4 5.1 %collective-permute-done.61 = bf16[2,8,64,128]{3,2,1,0:T(8,128)(2,1)S(1)} collective-permute-done((bf16[2,8,64,128]{3,2,1,0:T(8,128)(2,1)S(1)}, bf16[2,8,64,128]{3,2,1,0:T(8,128)(2,1)S(1)}, u32[]{:S(2)}, u32[]{:S(2)}) %collective-permute-start.61) | collective-permute-done | bytes 262176 | tf_op jit(solution)/shard_map/ppermute | solution.py:107
  234.2 4.8 %collective-permute-done.63 = bf16[2,8,64,128]{3,2,1,0:T(8,128)(2,1)S(1)} collective-permute-done((bf16[2,8,64,128]{3,2,1,0:T(8,128)(2,1)S(1)}, bf16[2,8,64,128]{3,2,1,0:T(8,128)(2,1)S(1)}, u32[]{:S(2)}, u32[]{:S(2)}) %collective-permute-start.63) | collective-permute-done | bytes 262176 | tf_op jit(solution)/shard_map/ppermute | solution.py:107
  240.5 4.2 %collective-permute-done.65 = bf16[2,8,64,128]{3,2,1,0:T(8,128)(2,1)S(1)} collective-permute-done((bf16[2,8,64,128]{3,2,1,0:T(8,128)(2,1)S(1)}, bf16[2,8,64,128]{3,2,1,0:T(8,128)(2,1)S(1)}, u32[]{:S(2)}, u32[]{:S(2)}) %collective-permute-start.65) | collective-permute-done | bytes 262176 | tf_op jit(solution)/shard_map/ppermute | solution.py:107
  244.8 1.9 collective-permute-start.66
  246.6 2.9 collective-permute-done.67.refs_4_
  249.5 8.7 %collective-permute-done.64.refs_2_ = bf16[2,8,64,128]{3,2,1,0:T(8,128)(2,1)S(1)} collective-permute-done((bf16[2,8,64,128]{3,2,1,0:T(8,128)(2,1)S(1)}, bf16[2,8,64,128]{3,2,1,0:T(8,128)(2,1)S(1)}, u32[]{:S(2)}, u32[]{:S(2)}) %collective-permute-start.64) | collective-permute-done | bytes 262176 | tf_op jit(solution)/shard_map/ppermute | solution.py:107
  258.3 5.6 %mute_receiver.3.own_ref = bf16[2,256,8,128]{3,2,1,0:T(8,128)(2,1)S(1)} custom-call(s32[3]{0:T(128)S(1)} %pad_add_fusion.ids, s32[8,256]{1,0:T(8,128)S(1)} %copy-done.2, bf16[512,1024]{1,0:T(8,128)(2,1)S(1)} %fusion.5.rows_ref, bf16[1024,512]{1,0:T(8,128)(2,1)S(1)} %fusion.11.columns_ref, bf16[2,8,64,128]{3,2,1,0:T(8,128)(2,1)S(1)} %get-tuple-element.58.refs_0_, ...), custom_call_target="tpu_custom_call" | custom-call | flops 2147483648 | bytes 5242880 | tf_op jit(solution)/shard_map/mute_receiver/pallas_call | solution.py:508
  263.8 1.5 collective-permute-start.68
  266.8 3.1 %collective-permute-done.73.refs_8_ = bf16[2,2,64,128]{3,2,1,0:T(8,128)(2,1)S(1)} collective-permute-done((bf16[2,2,64,128]{3,2,1,0:T(8,128)(2,1)S(1)}, bf16[2,2,64,128]{3,2,1,0:T(8,128)(2,1)S(1)}, u32[]{:S(2)}, u32[]{:S(2)}) %collective-permute-start.73) | collective-permute-done | bytes 65568 | tf_op jit(solution)/shard_map/ppermute | solution.py:107
  272.6 2.3 collective-permute-done.74.refs_9_
  277.9 6.2 %trace_source.1 = bf16[8,128,1024]{2,1,0:T(8,128)(2,1)} custom-call(s32[3]{0:T(128)S(1)} %pad_add_fusion.ids, s32[8,128,1]{2,1,0:T(8,128)S(1)} %copy.6.onset_ref, bf16[512,1024]{1,0:T(8,128)(2,1)S(1)} %fusion.5.rows_ref, bf16[2,2,64,128]{3,2,1,0:T(8,128)(2,1)S(1)} %get-tuple-element.69.refs_0_, bf16[2,2,64,128]{3,2,1,0:T(8,128)(2,1)S(1)} %collective-permute-done.43.refs_1_, ...), custom_call_target="tpu_custom_call" | custom-call | flops 1073741824 | bytes 5242880 | tf_op jit(solution)/shard_map/trace_source/pallas_call | solution.py:397
  284.1 4.7 %collective-permute-done.68.other_ref = bf16[2,256,8,128]{3,2,1,0:T(8,128)(2,1)} collective-permute-done((bf16[2,256,8,128]{3,2,1,0:T(8,128)(2,1)S(1)}, bf16[2,256,8,128]{3,2,1,0:T(8,128)(2,1)}, u32[]{:S(2)}, u32[]{:S(2)}) %collective-permute-start.68) | collective-permute-done | bytes 1048608 | tf_op jit(solution)/shard_map/ppermute | solution.py:107
  288.9 6.1 %join_halves.1 = bf16[2,256,8,256]{3,2,1,0:T(8,128)(2,1)} custom-call(s32[3]{0:T(128)S(1)} %pad_add_fusion.ids, bf16[2,256,8,128]{3,2,1,0:T(8,128)(2,1)S(1)} %mute_receiver.3.own_ref, bf16[2,256,8,128]{3,2,1,0:T(8,128)(2,1)} %collective-permute-done.68.other_ref), custom_call_target="tpu_custom_call" | custom-call | bytes 4194304 | tf_op jit(solution)/shard_map/join_halves/pallas_call | solution.py:530
  (135 shorter events, 43.4 us)
Async XLA Ops:
  3.1 13.8 %collective-permute-start = (bf16[2,8,64,128]{3,2,1,0:T(8,128)(2,1)S(1)}, bf16[2,8,64,128]{3,2,1,0:T(8,128)(2,1)S(1)}, u32[]{:S(2)}, u32[]{:S(2)}) collective-permute-start(bf16[2,8,64,128]{3,2,1,0:T(8,128)(2,1)S(1)} %split_wave.5.refs_6_), channel_id=1, source_target_pairs={{0,1},{1,0},{2,3},{3,2},{4,5},{5,4},{6,7},{7,6},{8,9},{9,8},{10,11... | collective-permute-start | bytes 786440 | tf_op jit(solution)/shard_map/ppermute | solution.py:107
  7.0 21.4 %collective-permute-start.1 = (bf16[2,8,64,128]{3,2,1,0:T(8,128)(2,1)S(1)}, bf16[2,8,64,128]{3,2,1,0:T(8,128)(2,1)S(1)}, u32[]{:S(2)}, u32[]{:S(2)}) collective-permute-start(bf16[2,8,64,128]{3,2,1,0:T(8,128)(2,1)S(1)} %split_wave.6.refs_7_), channel_id=1, source_target_pairs={{0,2},{1,3},{2,0},{3,1},{4,6},{5,7},{6,4},{7,5},{8,10},{9,11},{10,... | collective-permute-start | bytes 786440 | tf_op jit(solution)/shard_map/ppermute | solution.py:107
  10.4 19.5 %collective-permute-start.2 = (bf16[2,8,64,128]{3,2,1,0:T(8,128)(2,1)S(1)}, bf16[2,8,64,128]{3,2,1,0:T(8,128)(2,1)S(1)}, u32[]{:S(2)}, u32[]{:S(2)}) collective-permute-start(bf16[2,8,64,128]{3,2,1,0:T(8,128)(2,1)S(1)} %split_wave.7.refs_8_), channel_id=1, source_target_pairs={{0,3},{1,2},{2,1},{3,0},{4,7},{5,6},{6,5},{7,4},{8,11},{9,10},{10,... | collective-permute-start | bytes 786440 | tf_op jit(solution)/shard_map/ppermute | solution.py:107
  11.2 19.2 %collective-permute-start.3 = (bf16[2,8,64,128]{3,2,1,0:T(8,128)(2,1)S(1)}, bf16[2,8,64,128]{3,2,1,0:T(8,128)(2,1)S(1)}, u32[]{:S(2)}, u32[]{:S(2)}) collective-permute-start(bf16[2,8,64,128]{3,2,1,0:T(8,128)(2,1)S(1)} %split_wave.4.refs_0_.refs_5_), channel_id=1, source_target_pairs={{0,16},{16,0},{1,17},{17,1},{2,18},{18,2},{3,19},{19,3},{4,20},{20... | collective-permute-start | bytes 786440 | tf_op jit(solution)/shard_map/ppermute | solution.py:107
  16.9 13.5 %collective-permute-start.4 = (bf16[2,8,64,128]{3,2,1,0:T(8,128)(2,1)S(1)}, bf16[2,8,64,128]{3,2,1,0:T(8,128)(2,1)S(1)}, u32[]{:S(2)}, u32[]{:S(2)}) collective-permute-start(bf16[2,8,64,128]{3,2,1,0:T(8,128)(2,1)S(1)} %collective-permute-done.refs_1_), channel_id=1, source_target_pairs={{0,16},{16,0},{1,17},{17,1},{2,18},{18,2},{3,19},{19,3},{4,20},{20... | collective-permute-start | bytes 786440 | tf_op jit(solution)/shard_map/ppermute | solution.py:107
  28.4 6.4 %collective-permute-start.5 = (bf16[2,8,64,128]{3,2,1,0:T(8,128)(2,1)S(1)}, bf16[2,8,64,128]{3,2,1,0:T(8,128)(2,1)S(1)}, u32[]{:S(2)}, u32[]{:S(2)}) collective-permute-start(bf16[2,8,64,128]{3,2,1,0:T(8,128)(2,1)S(1)} %collective-permute-done.1.refs_2_), channel_id=1, source_target_pairs={{0,16},{16,0},{1,17},{17,1},{2,18},{18,2},{3,19},{19,3},{4,20},{20... | collective-permute-start | bytes 786440 | tf_op jit(solution)/shard_map/ppermute | solution.py:107
  29.9 7.7 %collective-permute-start.6 = (bf16[2,8,64,128]{3,2,1,0:T(8,128)(2,1)S(1)}, bf16[2,8,64,128]{3,2,1,0:T(8,128)(2,1)S(1)}, u32[]{:S(2)}, u32[]{:S(2)}) collective-permute-start(bf16[2,8,64,128]{3,2,1,0:T(8,128)(2,1)S(1)} %collective-permute-done.2.refs_3_), channel_id=1, source_target_pairs={{0,16},{16,0},{1,17},{17,1},{2,18},{18,2},{3,19},{19,3},{4,20},{20... | collective-permute-start | bytes 786440 | tf_op jit(solution)/shard_map/ppermute | solution.py:107
  46.2 10.3 %collective-permute-start.8 = (bf16[4,2,2,64,128]{4,3,2,1,0:T(8,128)(2,1)S(1)}, bf16[4,2,2,64,128]{4,3,2,1,0:T(8,128)(2,1)S(1)}, u32[]{:S(2)}, u32[]{:S(2)}) collective-permute-start(bf16[4,2,2,64,128]{4,3,2,1,0:T(8,128)(2,1)S(1)} %fusion.14), channel_id=1, source_target_pairs={{0,8},{4,12},{8,0},{12,4},{1,9},{5,13},{9,1},{13,5},{2,10},{6,14},... | collective-permute-start | bytes 786440 | tf_op jit(solution)/shard_map/ppermute | solution.py:107
  56.7 13.1 %collective-permute-start.9 = (bf16[2,2,64,128]{3,2,1,0:T(8,128)(2,1)S(1)}, bf16[2,2,64,128]{3,2,1,0:T(8,128)(2,1)S(1)}, u32[]{:S(2)}, u32[]{:S(2)}) collective-permute-start(bf16[2,2,64,128]{3,2,1,0:T(8,128)(2,1)S(1)} %get-tuple-element.72), channel_id=1, source_target_pairs={{0,1},{1,0},{2,3},{3,2},{4,5},{5,4},{6,7},{7,6},{8,9},{9,8},{10,11... | collective-permute-start | bytes 196616 | tf_op jit(solution)/shard_map/ppermute | solution.py:107
  59.2 10.5 %collective-permute-start.10 = (bf16[2,2,64,128]{3,2,1,0:T(8,128)(2,1)S(1)}, bf16[2,2,64,128]{3,2,1,0:T(8,128)(2,1)S(1)}, u32[]{:S(2)}, u32[]{:S(2)}) collective-permute-start(bf16[2,2,64,128]{3,2,1,0:T(8,128)(2,1)S(1)} %get-tuple-element.71), channel_id=1, source_target_pairs={{0,2},{1,3},{2,0},{3,1},{4,6},{5,7},{6,4},{7,5},{8,10},{9,11},{10,... | collective-permute-start | bytes 196616 | tf_op jit(solution)/shard_map/ppermute | solution.py:107
  61.7 8.1 %collective-permute-start.11 = (bf16[2,2,64,128]{3,2,1,0:T(8,128)(2,1)S(1)}, bf16[2,2,64,128]{3,2,1,0:T(8,128)(2,1)S(1)}, u32[]{:S(2)}, u32[]{:S(2)}) collective-permute-start(bf16[2,2,64,128]{3,2,1,0:T(8,128)(2,1)S(1)} %get-tuple-element.70), channel_id=1, source_target_pairs={{0,3},{1,2},{2,1},{3,0},{4,7},{5,6},{6,5},{7,4},{8,11},{9,10},{10,... | collective-permute-start | bytes 196616 | tf_op jit(solution)/shard_map/ppermute | solution.py:107
  71.5 5.0 %collective-permute-start.12 = (bf16[2,2,64,128]{3,2,1,0:T(8,128)(2,1)S(1)}, bf16[2,2,64,128]{3,2,1,0:T(8,128)(2,1)S(1)}, u32[]{:S(2)}, u32[]{:S(2)}) collective-permute-start(bf16[2,2,64,128]{3,2,1,0:T(8,128)(2,1)S(1)} %get-tuple-element.37), channel_id=1, source_target_pairs={{0,1},{1,0},{2,3},{3,2},{4,5},{5,4},{6,7},{7,6},{8,9},{9,8},{10,11... | collective-permute-start | bytes 196616 | tf_op jit(solution)/shard_map/ppermute | solution.py:107
  72.6 7.2 %collective-permute-start.13 = (bf16[2,2,64,128]{3,2,1,0:T(8,128)(2,1)S(1)}, bf16[2,2,64,128]{3,2,1,0:T(8,128)(2,1)S(1)}, u32[]{:S(2)}, u32[]{:S(2)}) collective-permute-start(bf16[2,2,64,128]{3,2,1,0:T(8,128)(2,1)S(1)} %get-tuple-element.38), channel_id=1, source_target_pairs={{0,2},{1,3},{2,0},{3,1},{4,6},{5,7},{6,4},{7,5},{8,10},{9,11},{10,... | collective-permute-start | bytes 196616 | tf_op jit(solution)/shard_map/ppermute | solution.py:107
  76.0 6.1 %collective-permute-start.14 = (bf16[2,2,64,128]{3,2,1,0:T(8,128)(2,1)S(1)}, bf16[2,2,64,128]{3,2,1,0:T(8,128)(2,1)S(1)}, u32[]{:S(2)}, u32[]{:S(2)}) collective-permute-start(bf16[2,2,64,128]{3,2,1,0:T(8,128)(2,1)S(1)} %get-tuple-element.39), channel_id=1, source_target_pairs={{0,3},{1,2},{2,1},{3,0},{4,7},{5,6},{6,5},{7,4},{8,11},{9,10},{10,... | collective-permute-start | bytes 196616 | tf_op jit(solution)/shard_map/ppermute | solution.py:107
  76.0 6.6 %collective-permute-start.15 = (bf16[2,2,64,128]{3,2,1,0:T(8,128)(2,1)S(1)}, bf16[2,2,64,128]{3,2,1,0:T(8,128)(2,1)S(1)}, u32[]{:S(2)}, u32[]{:S(2)}) collective-permute-start(bf16[2,2,64,128]{3,2,1,0:T(8,128)(2,1)S(1)} %get-tuple-element.36.refs_0_), channel_id=1, source_target_pairs={{0,4},{4,0},{8,12},{12,8},{1,5},{5,1},{9,13},{13,9},{2,6},{6,2},{1... | collective-permute-start | bytes 196616 | tf_op jit(solution)/shard_map/ppermute | solution.py:107
  76.0 8.1 %collective-permute-start.19 = (bf16[2,2,64,128]{3,2,1,0:T(8,128)(2,1)S(1)}, bf16[2,2,64,128]{3,2,1,0:T(8,128)(2,1)S(1)}, u32[]{:S(2)}, u32[]{:S(2)}) collective-permute-start(bf16[2,2,64,128]{3,2,1,0:T(8,128)(2,1)S(1)} %get-tuple-element.36.refs_0_), channel_id=1, source_target_pairs={{0,8},{4,12},{8,0},{12,4},{1,9},{5,13},{9,1},{13,5},{2,10},{6,14},... | collective-permute-start | bytes 196616 | tf_op jit(solution)/shard_map/ppermute | solution.py:107
  76.5 8.1 %collective-permute-start.16 = (bf16[2,2,64,128]{3,2,1,0:T(8,128)(2,1)S(1)}, bf16[2,2,64,128]{3,2,1,0:T(8,128)(2,1)S(1)}, u32[]{:S(2)}, u32[]{:S(2)}) collective-permute-start(bf16[2,2,64,128]{3,2,1,0:T(8,128)(2,1)S(1)} %collective-permute-done.12.refs_1_), channel_id=1, source_target_pairs={{0,4},{4,0},{8,12},{12,8},{1,5},{5,1},{9,13},{13,9},{2,6},{6,2},{1... | collective-permute-start | bytes 196616 | tf_op jit(solution)/shard_map/ppermute | solution.py:107
  79.8 4.8 %collective-permute-start.17 = (bf16[2,2,64,128]{3,2,1,0:T(8,128)(2,1)S(1)}, bf16[2,2,64,128]{3,2,1,0:T(8,128)(2,1)S(1)}, u32[]{:S(2)}, u32[]{:S(2)}) collective-permute-start(bf16[2,2,64,128]{3,2,1,0:T(8,128)(2,1)S(1)} %collective-permute-done.13.refs_2_), channel_id=1, source_target_pairs={{0,4},{4,0},{8,12},{12,8},{1,5},{5,1},{9,13},{13,9},{2,6},{6,2},{1... | collective-permute-start | bytes 196616 | tf_op jit(solution)/shard_map/ppermute | solution.py:107
  82.0 4.3 %collective-permute-start.20 = (bf16[2,2,64,128]{3,2,1,0:T(8,128)(2,1)S(1)}, bf16[2,2,64,128]{3,2,1,0:T(8,128)(2,1)S(1)}, u32[]{:S(2)}, u32[]{:S(2)}) collective-permute-start(bf16[2,2,64,128]{3,2,1,0:T(8,128)(2,1)S(1)} %collective-permute-done.12.refs_1_), channel_id=1, source_target_pairs={{0,8},{4,12},{8,0},{12,4},{1,9},{5,13},{9,1},{13,5},{2,10},{6,14},... | collective-permute-start | bytes 196616 | tf_op jit(solution)/shard_map/ppermute | solution.py:107
  82.5 4.5 %collective-permute-start.21 = (bf16[2,2,64,128]{3,2,1,0:T(8,128)(2,1)S(1)}, bf16[2,2,64,128]{3,2,1,0:T(8,128)(2,1)S(1)}, u32[]{:S(2)}, u32[]{:S(2)}) collective-permute-start(bf16[2,2,64,128]{3,2,1,0:T(8,128)(2,1)S(1)} %collective-permute-done.13.refs_2_), channel_id=1, source_target_pairs={{0,8},{4,12},{8,0},{12,4},{1,9},{5,13},{9,1},{13,5},{2,10},{6,14},... | collective-permute-start | bytes 196616 | tf_op jit(solution)/shard_map/ppermute | solution.py:107
  84.1 4.3 %collective-permute-start.22 = (bf16[2,2,64,128]{3,2,1,0:T(8,128)(2,1)S(1)}, bf16[2,2,64,128]{3,2,1,0:T(8,128)(2,1)S(1)}, u32[]{:S(2)}, u32[]{:S(2)}) collective-permute-start(bf16[2,2,64,128]{3,2,1,0:T(8,128)(2,1)S(1)} %collective-permute-done.14.refs_3_), channel_id=1, source_target_pairs={{0,8},{4,12},{8,0},{12,4},{1,9},{5,13},{9,1},{13,5},{2,10},{6,14},... | collective-permute-start | bytes 196616 | tf_op jit(solution)/shard_map/ppermute | solution.py:107
  96.2 9.2 %collective-permute-start.27 = (bf16[2,8,64,128]{3,2,1,0:T(8,128)(2,1)S(1)}, bf16[2,8,64,128]{3,2,1,0:T(8,128)(2,1)S(1)}, u32[]{:S(2)}, u32[]{:S(2)}) collective-permute-start(bf16[2,8,64,128]{3,2,1,0:T(8,128)(2,1)S(1)} %get-tuple-element.42), channel_id=1, source_target_pairs={{0,16},{16,0},{1,17},{17,1},{2,18},{18,2},{3,19},{19,3},{4,20},{20... | collective-permute-start | bytes 786440 | tf_op jit(solution)/shard_map/ppermute | solution.py:107
  97.7 13.3 %collective-permute-start.29 = (bf16[2,8,64,128]{3,2,1,0:T(8,128)(2,1)S(1)}, bf16[2,8,64,128]{3,2,1,0:T(8,128)(2,1)S(1)}, u32[]{:S(2)}, u32[]{:S(2)}) collective-permute-start(bf16[2,8,64,128]{3,2,1,0:T(8,128)(2,1)S(1)} %get-tuple-element.44), channel_id=1, source_target_pairs={{0,16},{16,0},{1,17},{17,1},{2,18},{18,2},{3,19},{19,3},{4,20},{20... | collective-permute-start | bytes 786440 | tf_op jit(solution)/shard_map/ppermute | solution.py:107
  98.3 18.4 %collective-permute-start.31 = (bf16[2,8,64,128]{3,2,1,0:T(8,128)(2,1)S(1)}, bf16[2,8,64,128]{3,2,1,0:T(8,128)(2,1)S(1)}, u32[]{:S(2)}, u32[]{:S(2)}) collective-permute-start(bf16[2,8,64,128]{3,2,1,0:T(8,128)(2,1)S(1)} %get-tuple-element.46), channel_id=1, source_target_pairs={{0,16},{16,0},{1,17},{17,1},{2,18},{18,2},{3,19},{19,3},{4,20},{20... | collective-permute-start | bytes 786440 | tf_op jit(solution)/shard_map/ppermute | solution.py:107
  99.8 21.7 %collective-permute-start.33 = (bf16[2,8,64,128]{3,2,1,0:T(8,128)(2,1)S(1)}, bf16[2,8,64,128]{3,2,1,0:T(8,128)(2,1)S(1)}, u32[]{:S(2)}, u32[]{:S(2)}) collective-permute-start(bf16[2,8,64,128]{3,2,1,0:T(8,128)(2,1)S(1)} %get-tuple-element.47), channel_id=1, source_target_pairs={{0,16},{16,0},{1,17},{17,1},{2,18},{18,2},{3,19},{19,3},{4,20},{20... | collective-permute-start | bytes 786440 | tf_op jit(solution)/shard_map/ppermute | solution.py:107
  105.5 16.0 %collective-permute-start.28 = (bf16[2,8,64,128]{3,2,1,0:T(8,128)(2,1)S(1)}, bf16[2,8,64,128]{3,2,1,0:T(8,128)(2,1)S(1)}, u32[]{:S(2)}, u32[]{:S(2)}) collective-permute-start(bf16[2,8,64,128]{3,2,1,0:T(8,128)(2,1)S(1)} %add_convert_fusion.6), channel_id=1, source_target_pairs={{0,1},{1,0},{2,3},{3,2},{4,5},{5,4},{6,7},{7,6},{8,9},{9,8},{10,11... | collective-permute-start | bytes 786440 | tf_op jit(solution)/shard_map/ppermute | solution.py:107
  111.1 18.3 %collective-permute-start.30 = (bf16[2,8,64,128]{3,2,1,0:T(8,128)(2,1)S(1)}, bf16[2,8,64,128]{3,2,1,0:T(8,128)(2,1)S(1)}, u32[]{:S(2)}, u32[]{:S(2)}) collective-permute-start(bf16[2,8,64,128]{3,2,1,0:T(8,128)(2,1)S(1)} %add_convert_fusion.5), channel_id=1, source_target_pairs={{0,2},{1,3},{2,0},{3,1},{4,6},{5,7},{6,4},{7,5},{8,10},{9,11},{10,... | collective-permute-start | bytes 786440 | tf_op jit(solution)/shard_map/ppermute | solution.py:107
  116.7 12.7 %collective-permute-start.32 = (bf16[2,8,64,128]{3,2,1,0:T(8,128)(2,1)S(1)}, bf16[2,8,64,128]{3,2,1,0:T(8,128)(2,1)S(1)}, u32[]{:S(2)}, u32[]{:S(2)}) collective-permute-start(bf16[2,8,64,128]{3,2,1,0:T(8,128)(2,1)S(1)} %add_convert_fusion.4), channel_id=1, source_target_pairs={{0,3},{1,2},{2,1},{3,0},{4,7},{5,6},{6,5},{7,4},{8,11},{9,10},{10,... | collective-permute-start | bytes 786440 | tf_op jit(solution)/shard_map/ppermute | solution.py:107
  135.0 17.5 %collective-permute-start.34 = (bf16[2,8,64,128]{3,2,1,0:T(8,128)(2,1)S(1)}, bf16[2,8,64,128]{3,2,1,0:T(8,128)(2,1)S(1)}, u32[]{:S(2)}, u32[]{:S(2)}) collective-permute-start(bf16[2,8,64,128]{3,2,1,0:T(8,128)(2,1)S(1)} %get-tuple-element.49), channel_id=1, source_target_pairs={{0,1},{1,0},{2,3},{3,2},{4,5},{5,4},{6,7},{7,6},{8,9},{9,8},{10,11... | collective-permute-start | bytes 786440 | tf_op jit(solution)/shard_map/ppermute | solution.py:107
  141.1 21.3 %collective-permute-start.35 = (bf16[2,8,64,128]{3,2,1,0:T(8,128)(2,1)S(1)}, bf16[2,8,64,128]{3,2,1,0:T(8,128)(2,1)S(1)}, u32[]{:S(2)}, u32[]{:S(2)}) collective-permute-start(bf16[2,8,64,128]{3,2,1,0:T(8,128)(2,1)S(1)} %get-tuple-element.50), channel_id=1, source_target_pairs={{0,2},{1,3},{2,0},{3,1},{4,6},{5,7},{6,4},{7,5},{8,10},{9,11},{10,... | collective-permute-start | bytes 786440 | tf_op jit(solution)/shard_map/ppermute | solution.py:107
  142.1 21.9 %collective-permute-start.36 = (bf16[2,8,64,128]{3,2,1,0:T(8,128)(2,1)S(1)}, bf16[2,8,64,128]{3,2,1,0:T(8,128)(2,1)S(1)}, u32[]{:S(2)}, u32[]{:S(2)}) collective-permute-start(bf16[2,8,64,128]{3,2,1,0:T(8,128)(2,1)S(1)} %get-tuple-element.51), channel_id=1, source_target_pairs={{0,3},{1,2},{2,1},{3,0},{4,7},{5,6},{6,5},{7,4},{8,11},{9,10},{10,... | collective-permute-start | bytes 786440 | tf_op jit(solution)/shard_map/ppermute | solution.py:107
  143.6 20.9 %collective-permute-start.37 = (bf16[2,8,64,128]{3,2,1,0:T(8,128)(2,1)S(1)}, bf16[2,8,64,128]{3,2,1,0:T(8,128)(2,1)S(1)}, u32[]{:S(2)}, u32[]{:S(2)}) collective-permute-start(bf16[2,8,64,128]{3,2,1,0:T(8,128)(2,1)S(1)} %get-tuple-element.48.refs_0_), channel_id=1, source_target_pairs={{0,16},{16,0},{1,17},{17,1},{2,18},{18,2},{3,19},{19,3},{4,20},{20... | collective-permute-start | bytes 786440 | tf_op jit(solution)/shard_map/ppermute | solution.py:107
  152.5 12.0 %collective-permute-start.38 = (bf16[2,8,64,128]{3,2,1,0:T(8,128)(2,1)S(1)}, bf16[2,8,64,128]{3,2,1,0:T(8,128)(2,1)S(1)}, u32[]{:S(2)}, u32[]{:S(2)}) collective-permute-start(bf16[2,8,64,128]{3,2,1,0:T(8,128)(2,1)S(1)} %collective-permute-done.34.refs_1_), channel_id=1, source_target_pairs={{0,16},{16,0},{1,17},{17,1},{2,18},{18,2},{3,19},{19,3},{4,20},{20... | collective-permute-start | bytes 786440 | tf_op jit(solution)/shard_map/ppermute | solution.py:107
  162.5 6.4 %collective-permute-start.39 = (bf16[2,8,64,128]{3,2,1,0:T(8,128)(2,1)S(1)}, bf16[2,8,64,128]{3,2,1,0:T(8,128)(2,1)S(1)}, u32[]{:S(2)}, u32[]{:S(2)}) collective-permute-start(bf16[2,8,64,128]{3,2,1,0:T(8,128)(2,1)S(1)} %collective-permute-done.35.refs_2_), channel_id=1, source_target_pairs={{0,16},{16,0},{1,17},{17,1},{2,18},{18,2},{3,19},{19,3},{4,20},{20... | collective-permute-start | bytes 786440 | tf_op jit(solution)/shard_map/ppermute | solution.py:107
  164.0 7.7 %collective-permute-start.40 = (bf16[2,8,64,128]{3,2,1,0:T(8,128)(2,1)S(1)}, bf16[2,8,64,128]{3,2,1,0:T(8,128)(2,1)S(1)}, u32[]{:S(2)}, u32[]{:S(2)}) collective-permute-start(bf16[2,8,64,128]{3,2,1,0:T(8,128)(2,1)S(1)} %collective-permute-done.36.refs_3_), channel_id=1, source_target_pairs={{0,16},{16,0},{1,17},{17,1},{2,18},{18,2},{3,19},{19,3},{4,20},{20... | collective-permute-start | bytes 786440 | tf_op jit(solution)/shard_map/ppermute | solution.py:107
  180.5 8.4 %collective-permute-start.42 = (bf16[4,2,2,64,128]{4,3,2,1,0:T(8,128)(2,1)S(1)}, bf16[4,2,2,64,128]{4,3,2,1,0:T(8,128)(2,1)S(1)}, u32[]{:S(2)}, u32[]{:S(2)}) collective-permute-start(bf16[4,2,2,64,128]{4,3,2,1,0:T(8,128)(2,1)S(1)} %fusion.15), channel_id=1, source_target_pairs={{0,8},{4,12},{8,0},{12,4},{1,9},{5,13},{9,1},{13,5},{2,10},{6,14},... | collective-permute-start | bytes 786440 | tf_op jit(solution)/shard_map/ppermute | solution.py:107
  189.1 5.4 %collective-permute-start.43 = (bf16[2,2,64,128]{3,2,1,0:T(8,128)(2,1)S(1)}, bf16[2,2,64,128]{3,2,1,0:T(8,128)(2,1)S(1)}, u32[]{:S(2)}, u32[]{:S(2)}) collective-permute-start(bf16[2,2,64,128]{3,2,1,0:T(8,128)(2,1)S(1)} %get-tuple-element.68), channel_id=1, source_target_pairs={{0,1},{1,0},{2,3},{3,2},{4,5},{5,4},{6,7},{7,6},{8,9},{9,8},{10,11... | collective-permute-start | bytes 196616 | tf_op jit(solution)/shard_map/ppermute | solution.py:107
  192.0 7.4 %collective-permute-start.44 = (bf16[2,2,64,128]{3,2,1,0:T(8,128)(2,1)S(1)}, bf16[2,2,64,128]{3,2,1,0:T(8,128)(2,1)S(1)}, u32[]{:S(2)}, u32[]{:S(2)}) collective-permute-start(bf16[2,2,64,128]{3,2,1,0:T(8,128)(2,1)S(1)} %get-tuple-element.67), channel_id=1, source_target_pairs={{0,2},{1,3},{2,0},{3,1},{4,6},{5,7},{6,4},{7,5},{8,10},{9,11},{10,... | collective-permute-start | bytes 196616 | tf_op jit(solution)/shard_map/ppermute | solution.py:107
  193.0 6.5 %collective-permute-start.45 = (bf16[2,2,64,128]{3,2,1,0:T(8,128)(2,1)S(1)}, bf16[2,2,64,128]{3,2,1,0:T(8,128)(2,1)S(1)}, u32[]{:S(2)}, u32[]{:S(2)}) collective-permute-start(bf16[2,2,64,128]{3,2,1,0:T(8,128)(2,1)S(1)} %get-tuple-element.66), channel_id=1, source_target_pairs={{0,3},{1,2},{2,1},{3,0},{4,7},{5,6},{6,5},{7,4},{8,11},{9,10},{10,... | collective-permute-start | bytes 196616 | tf_op jit(solution)/shard_map/ppermute | solution.py:107
  201.2 5.1 %collective-permute-start.46 = (bf16[2,2,64,128]{3,2,1,0:T(8,128)(2,1)S(1)}, bf16[2,2,64,128]{3,2,1,0:T(8,128)(2,1)S(1)}, u32[]{:S(2)}, u32[]{:S(2)}) collective-permute-start(bf16[2,2,64,128]{3,2,1,0:T(8,128)(2,1)S(1)} %get-tuple-element.55), channel_id=1, source_target_pairs={{0,1},{1,0},{2,3},{3,2},{4,5},{5,4},{6,7},{7,6},{8,9},{9,8},{10,11... | collective-permute-start | bytes 196616 | tf_op jit(solution)/shard_map/ppermute | solution.py:107
  202.5 6.2 %collective-permute-start.47 = (bf16[2,2,64,128]{3,2,1,0:T(8,128)(2,1)S(1)}, bf16[2,2,64,128]{3,2,1,0:T(8,128)(2,1)S(1)}, u32[]{:S(2)}, u32[]{:S(2)}) collective-permute-start(bf16[2,2,64,128]{3,2,1,0:T(8,128)(2,1)S(1)} %get-tuple-element.56), channel_id=1, source_target_pairs={{0,2},{1,3},{2,0},{3,1},{4,6},{5,7},{6,4},{7,5},{8,10},{9,11},{10,... | collective-permute-start | bytes 196616 | tf_op jit(solution)/shard_map/ppermute | solution.py:107
  203.9 6.2 %collective-permute-start.48 = (bf16[2,2,64,128]{3,2,1,0:T(8,128)(2,1)S(1)}, bf16[2,2,64,128]{3,2,1,0:T(8,128)(2,1)S(1)}, u32[]{:S(2)}, u32[]{:S(2)}) collective-permute-start(bf16[2,2,64,128]{3,2,1,0:T(8,128)(2,1)S(1)} %get-tuple-element.57), channel_id=1, source_target_pairs={{0,3},{1,2},{2,1},{3,0},{4,7},{5,6},{6,5},{7,4},{8,11},{9,10},{10,... | collective-permute-start | bytes 196616 | tf_op jit(solution)/shard_map/ppermute | solution.py:107
  205.6 5.2 %collective-permute-start.49 = (bf16[2,2,64,128]{3,2,1,0:T(8,128)(2,1)S(1)}, bf16[2,2,64,128]{3,2,1,0:T(8,128)(2,1)S(1)}, u32[]{:S(2)}, u32[]{:S(2)}) collective-permute-start(bf16[2,2,64,128]{3,2,1,0:T(8,128)(2,1)S(1)} %get-tuple-element.54.refs_0_), channel_id=1, source_target_pairs={{0,4},{4,0},{8,12},{12,8},{1,5},{5,1},{9,13},{13,9},{2,6},{6,2},{1... | collective-permute-start | bytes 196616 | tf_op jit(solution)/shard_map/ppermute | solution.py:107
  205.6 6.5 %collective-permute-start.53 = (bf16[2,2,64,128]{3,2,1,0:T(8,128)(2,1)S(1)}, bf16[2,2,64,128]{3,2,1,0:T(8,128)(2,1)S(1)}, u32[]{:S(2)}, u32[]{:S(2)}) collective-permute-start(bf16[2,2,64,128]{3,2,1,0:T(8,128)(2,1)S(1)} %get-tuple-element.54.refs_0_), channel_id=1, source_target_pairs={{0,8},{4,12},{8,0},{12,4},{1,9},{5,13},{9,1},{13,5},{2,10},{6,14},... | collective-permute-start | bytes 196616 | tf_op jit(solution)/shard_map/ppermute | solution.py:107
  206.3 6.5 %collective-permute-start.50 = (bf16[2,2,64,128]{3,2,1,0:T(8,128)(2,1)S(1)}, bf16[2,2,64,128]{3,2,1,0:T(8,128)(2,1)S(1)}, u32[]{:S(2)}, u32[]{:S(2)}) collective-permute-start(bf16[2,2,64,128]{3,2,1,0:T(8,128)(2,1)S(1)} %collective-permute-done.46.refs_1_), channel_id=1, source_target_pairs={{0,4},{4,0},{8,12},{12,8},{1,5},{5,1},{9,13},{13,9},{2,6},{6,2},{1... | collective-permute-start | bytes 196616 | tf_op jit(solution)/shard_map/ppermute | solution.py:107
  210.1 4.6 %collective-permute-start.54 = (bf16[2,2,64,128]{3,2,1,0:T(8,128)(2,1)S(1)}, bf16[2,2,64,128]{3,2,1,0:T(8,128)(2,1)S(1)}, u32[]{:S(2)}, u32[]{:S(2)}) collective-permute-start(bf16[2,2,64,128]{3,2,1,0:T(8,128)(2,1)S(1)} %collective-permute-done.46.refs_1_), channel_id=1, source_target_pairs={{0,8},{4,12},{8,0},{12,4},{1,9},{5,13},{9,1},{13,5},{2,10},{6,14},... | collective-permute-start | bytes 196616 | tf_op jit(solution)/shard_map/ppermute | solution.py:107
  210.8 4.7 %collective-permute-start.55 = (bf16[2,2,64,128]{3,2,1,0:T(8,128)(2,1)S(1)}, bf16[2,2,64,128]{3,2,1,0:T(8,128)(2,1)S(1)}, u32[]{:S(2)}, u32[]{:S(2)}) collective-permute-start(bf16[2,2,64,128]{3,2,1,0:T(8,128)(2,1)S(1)} %collective-permute-done.47.refs_2_), channel_id=1, source_target_pairs={{0,8},{4,12},{8,0},{12,4},{1,9},{5,13},{9,1},{13,5},{2,10},{6,14},... | collective-permute-start | bytes 196616 | tf_op jit(solution)/shard_map/ppermute | solution.py:107
  212.1 4.3 %collective-permute-start.56 = (bf16[2,2,64,128]{3,2,1,0:T(8,128)(2,1)S(1)}, bf16[2,2,64,128]{3,2,1,0:T(8,128)(2,1)S(1)}, u32[]{:S(2)}, u32[]{:S(2)}) collective-permute-start(bf16[2,2,64,128]{3,2,1,0:T(8,128)(2,1)S(1)} %collective-permute-done.48.refs_3_), channel_id=1, source_target_pairs={{0,8},{4,12},{8,0},{12,4},{1,9},{5,13},{9,1},{13,5},{2,10},{6,14},... | collective-permute-start | bytes 196616 | tf_op jit(solution)/shard_map/ppermute | solution.py:107
  224.2 9.2 %collective-permute-start.61 = (bf16[2,8,64,128]{3,2,1,0:T(8,128)(2,1)S(1)}, bf16[2,8,64,128]{3,2,1,0:T(8,128)(2,1)S(1)}, u32[]{:S(2)}, u32[]{:S(2)}) collective-permute-start(bf16[2,8,64,128]{3,2,1,0:T(8,128)(2,1)S(1)} %get-tuple-element.60), channel_id=1, source_target_pairs={{0,16},{16,0},{1,17},{17,1},{2,18},{18,2},{3,19},{19,3},{4,20},{20... | collective-permute-start | bytes 786440 | tf_op jit(solution)/shard_map/ppermute | solution.py:107
  225.8 13.3 %collective-permute-start.63 = (bf16[2,8,64,128]{3,2,1,0:T(8,128)(2,1)S(1)}, bf16[2,8,64,128]{3,2,1,0:T(8,128)(2,1)S(1)}, u32[]{:S(2)}, u32[]{:S(2)}) collective-permute-start(bf16[2,8,64,128]{3,2,1,0:T(8,128)(2,1)S(1)} %get-tuple-element.62), channel_id=1, source_target_pairs={{0,16},{16,0},{1,17},{17,1},{2,18},{18,2},{3,19},{19,3},{4,20},{20... | collective-permute-start | bytes 786440 | tf_op jit(solution)/shard_map/ppermute | solution.py:107
  226.3 18.4 %collective-permute-start.65 = (bf16[2,8,64,128]{3,2,1,0:T(8,128)(2,1)S(1)}, bf16[2,8,64,128]{3,2,1,0:T(8,128)(2,1)S(1)}, u32[]{:S(2)}, u32[]{:S(2)}) collective-permute-start(bf16[2,8,64,128]{3,2,1,0:T(8,128)(2,1)S(1)} %get-tuple-element.64), channel_id=1, source_target_pairs={{0,16},{16,0},{1,17},{17,1},{2,18},{18,2},{3,19},{19,3},{4,20},{20... | collective-permute-start | bytes 786440 | tf_op jit(solution)/shard_map/ppermute | solution.py:107
  227.8 21.7 %collective-permute-start.67 = (bf16[2,8,64,128]{3,2,1,0:T(8,128)(2,1)S(1)}, bf16[2,8,64,128]{3,2,1,0:T(8,128)(2,1)S(1)}, u32[]{:S(2)}, u32[]{:S(2)}) collective-permute-start(bf16[2,8,64,128]{3,2,1,0:T(8,128)(2,1)S(1)} %get-tuple-element.65), channel_id=1, source_target_pairs={{0,16},{16,0},{1,17},{17,1},{2,18},{18,2},{3,19},{19,3},{4,20},{20... | collective-permute-start | bytes 786440 | tf_op jit(solution)/shard_map/ppermute | solution.py:107
  233.5 16.0 %collective-permute-start.62 = (bf16[2,8,64,128]{3,2,1,0:T(8,128)(2,1)S(1)}, bf16[2,8,64,128]{3,2,1,0:T(8,128)(2,1)S(1)}, u32[]{:S(2)}, u32[]{:S(2)}) collective-permute-start(bf16[2,8,64,128]{3,2,1,0:T(8,128)(2,1)S(1)} %add_convert_fusion.2), channel_id=1, source_target_pairs={{0,1},{1,0},{2,3},{3,2},{4,5},{5,4},{6,7},{7,6},{8,9},{9,8},{10,11... | collective-permute-start | bytes 786440 | tf_op jit(solution)/shard_map/ppermute | solution.py:107
  239.2 19.1 %collective-permute-start.64 = (bf16[2,8,64,128]{3,2,1,0:T(8,128)(2,1)S(1)}, bf16[2,8,64,128]{3,2,1,0:T(8,128)(2,1)S(1)}, u32[]{:S(2)}, u32[]{:S(2)}) collective-permute-start(bf16[2,8,64,128]{3,2,1,0:T(8,128)(2,1)S(1)} %add_convert_fusion.1), channel_id=1, source_target_pairs={{0,2},{1,3},{2,0},{3,1},{4,6},{5,7},{6,4},{7,5},{8,10},{9,11},{10,... | collective-permute-start | bytes 786440 | tf_op jit(solution)/shard_map/ppermute | solution.py:107
  244.8 13.5 %collective-permute-start.66 = (bf16[2,8,64,128]{3,2,1,0:T(8,128)(2,1)S(1)}, bf16[2,8,64,128]{3,2,1,0:T(8,128)(2,1)S(1)}, u32[]{:S(2)}, u32[]{:S(2)}) collective-permute-start(bf16[2,8,64,128]{3,2,1,0:T(8,128)(2,1)S(1)} %add_convert_fusion), channel_id=1, source_target_pairs={{0,3},{1,2},{2,1},{3,0},{4,7},{5,6},{6,5},{7,4},{8,11},{9,10},{10,... | collective-permute-start | bytes 786440 | tf_op jit(solution)/shard_map/ppermute | solution.py:107
  263.8 25.0 %collective-permute-start.68 = (bf16[2,256,8,128]{3,2,1,0:T(8,128)(2,1)S(1)}, bf16[2,256,8,128]{3,2,1,0:T(8,128)(2,1)}, u32[]{:S(2)}, u32[]{:S(2)}) collective-permute-start(bf16[2,256,8,128]{3,2,1,0:T(8,128)(2,1)S(1)} %mute_receiver.3.own_ref), channel_id=1, source_target_pairs={{0,16},{16,0},{1,17},{17,1},{2,18},{18,2},{3,19},{19,3},{4,20},{20... | collective-permute-start | bytes 3145736 | tf_op jit(solution)/shard_map/ppermute | solution.py:107
  265.4 4.5 %collective-permute-start.73 = (bf16[2,2,64,128]{3,2,1,0:T(8,128)(2,1)S(1)}, bf16[2,2,64,128]{3,2,1,0:T(8,128)(2,1)S(1)}, u32[]{:S(2)}, u32[]{:S(2)}) collective-permute-start(bf16[2,2,64,128]{3,2,1,0:T(8,128)(2,1)S(1)} %get-tuple-element.69.refs_0_), channel_id=1, source_target_pairs={{0,8},{4,12},{8,0},{12,4},{1,9},{5,13},{9,1},{13,5},{2,10},{6,14},... | collective-permute-start | bytes 196616 | tf_op jit(solution)/shard_map/ppermute | solution.py:107
  266.1 4.5 %collective-permute-start.70 = (bf16[2,2,64,128]{3,2,1,0:T(8,128)(2,1)S(1)}, bf16[2,2,64,128]{3,2,1,0:T(8,128)(2,1)S(1)}, u32[]{:S(2)}, u32[]{:S(2)}) collective-permute-start(bf16[2,2,64,128]{3,2,1,0:T(8,128)(2,1)S(1)} %collective-permute-done.43.refs_1_), channel_id=1, source_target_pairs={{0,4},{4,0},{8,12},{12,8},{1,5},{5,1},{9,13},{13,9},{2,6},{6,2},{1... | collective-permute-start | bytes 196616 | tf_op jit(solution)/shard_map/ppermute | solution.py:107
  266.3 5.6 %collective-permute-start.71 = (bf16[2,2,64,128]{3,2,1,0:T(8,128)(2,1)S(1)}, bf16[2,2,64,128]{3,2,1,0:T(8,128)(2,1)S(1)}, u32[]{:S(2)}, u32[]{:S(2)}) collective-permute-start(bf16[2,2,64,128]{3,2,1,0:T(8,128)(2,1)S(1)} %collective-permute-done.44.refs_2_), channel_id=1, source_target_pairs={{0,4},{4,0},{8,12},{12,8},{1,5},{5,1},{9,13},{13,9},{2,6},{6,2},{1... | collective-permute-start | bytes 196616 | tf_op jit(solution)/shard_map/ppermute | solution.py:107
  266.7 6.0 %collective-permute-start.72 = (bf16[2,2,64,128]{3,2,1,0:T(8,128)(2,1)S(1)}, bf16[2,2,64,128]{3,2,1,0:T(8,128)(2,1)S(1)}, u32[]{:S(2)}, u32[]{:S(2)}) collective-permute-start(bf16[2,2,64,128]{3,2,1,0:T(8,128)(2,1)S(1)} %collective-permute-done.45.refs_3_), channel_id=1, source_target_pairs={{0,4},{4,0},{8,12},{12,8},{1,5},{5,1},{9,13},{13,9},{2,6},{6,2},{1... | collective-permute-start | bytes 196616 | tf_op jit(solution)/shard_map/ppermute | solution.py:107
  269.9 5.0 %collective-permute-start.74 = (bf16[2,2,64,128]{3,2,1,0:T(8,128)(2,1)S(1)}, bf16[2,2,64,128]{3,2,1,0:T(8,128)(2,1)S(1)}, u32[]{:S(2)}, u32[]{:S(2)}) collective-permute-start(bf16[2,2,64,128]{3,2,1,0:T(8,128)(2,1)S(1)} %collective-permute-done.43.refs_1_), channel_id=1, source_target_pairs={{0,8},{4,12},{8,0},{12,4},{1,9},{5,13},{9,1},{13,5},{2,10},{6,14},... | collective-permute-start | bytes 196616 | tf_op jit(solution)/shard_map/ppermute | solution.py:107
  270.6 5.2 %collective-permute-start.75 = (bf16[2,2,64,128]{3,2,1,0:T(8,128)(2,1)S(1)}, bf16[2,2,64,128]{3,2,1,0:T(8,128)(2,1)S(1)}, u32[]{:S(2)}, u32[]{:S(2)}) collective-permute-start(bf16[2,2,64,128]{3,2,1,0:T(8,128)(2,1)S(1)} %collective-permute-done.44.refs_2_), channel_id=1, source_target_pairs={{0,8},{4,12},{8,0},{12,4},{1,9},{5,13},{9,1},{13,5},{2,10},{6,14},... | collective-permute-start | bytes 196616 | tf_op jit(solution)/shard_map/ppermute | solution.py:107
  271.9 4.6 %collective-permute-start.76 = (bf16[2,2,64,128]{3,2,1,0:T(8,128)(2,1)S(1)}, bf16[2,2,64,128]{3,2,1,0:T(8,128)(2,1)S(1)}, u32[]{:S(2)}, u32[]{:S(2)}) collective-permute-start(bf16[2,2,64,128]{3,2,1,0:T(8,128)(2,1)S(1)} %collective-permute-done.45.refs_3_), channel_id=1, source_target_pairs={{0,8},{4,12},{8,0},{12,4},{1,9},{5,13},{9,1},{13,5},{2,10},{6,14},... | collective-permute-start | bytes 196616 | tf_op jit(solution)/shard_map/ppermute | solution.py:107
  272.6 4.1 %collective-permute-start.77 = (bf16[2,2,64,128]{3,2,1,0:T(8,128)(2,1)S(1)}, bf16[2,2,64,128]{3,2,1,0:T(8,128)(2,1)S(1)}, u32[]{:S(2)}, u32[]{:S(2)}) collective-permute-start(bf16[2,2,64,128]{3,2,1,0:T(8,128)(2,1)S(1)} %collective-permute-done.73.refs_8_), channel_id=1, source_target_pairs={{0,4},{4,0},{8,12},{12,8},{1,5},{5,1},{9,13},{13,9},{2,6},{6,2},{1... | collective-permute-start | bytes 196616 | tf_op jit(solution)/shard_map/ppermute | solution.py:107
  (20 other events, 95.9 us)

commit v2 on v0

--- a/solution.py
+++ b/solution.py
@@ -1,13 +1,22 @@
+import functools
 import math
 
 import jax
 import jax.numpy as jnp
 from jax import lax
+from jax.experimental import pallas as pl
+from jax.experimental.pallas import tpu as pltpu
 from jax.sharding import PartitionSpec as P
 
 F = 256
 NT = 1024
 ITERS = 2
+LANES = 128
+BLOCK_W = 16
+HALVES = 2
+F32 = jnp.float32
+BF16 = jnp.bfloat16
+VMEM_BYTES = 24 * 1024 * 1024
 
 
 def basis_table():
@@ -76,7 +85,7 @@
     return lax.all_gather(renewed, "src", axis=3, tiled=True)
 
 
-def local(reflection, direct_wave, onset_receiver, onset_source):
+def general(reflection, direct_wave, onset_receiver, onset_source):
     basis_rows = basis_table()
     source_index = lax.axis_index("src")
     whole_reflection = lax.all_gather(reflection, "foc", axis=1, tiled=True)
@@ -94,6 +103,557 @@
     return (focusing, muted_trace)
 
 
+VMEM_SPEC = pl.BlockSpec(memory_space=pltpu.VMEM)
+SMEM_SPEC = pl.BlockSpec(memory_space=pltpu.SMEM)
+
+
+def swap(value, axis, mask, count):
+    return lax.ppermute(value, axis, [(i, i ^ mask) for i in range(count)])
+
+
+def call(kernel, name, out_shape, flops, size, operands, scratch=()):
+    many = isinstance(out_shape, list)
+    return pl.pallas_call(
+        kernel,
+        name=name,
+        out_shape=out_shape,
+        in_specs=[SMEM_SPEC] + [VMEM_SPEC] * (len(operands) - 1),
+        out_specs=[VMEM_SPEC] * len(out_shape) if many else VMEM_SPEC,
+        scratch_shapes=list(scratch),
+        compiler_params=pltpu.CompilerParams(vmem_limit_bytes=VMEM_BYTES),
+        cost_estimate=pl.CostEstimate(flops=flops, bytes_accessed=size, transcendentals=0),
+    )(*operands)
+
+
+def table(frequency, part, sample):
+    phase = ((frequency + 1) * sample + part * (NT // 4)) & (NT - 1)
+    x = (jnp.abs(phase - NT // 2) - NT // 4).astype(F32) * (4.0 / NT)
+    square = x * x
+    total = jnp.zeros_like(x)
+    for order in (11, 9, 7, 5, 3, 1):
+        sign = -1.0 if order % 4 == 3 else 1.0
+        total = total * square + sign * (math.pi / 2) ** order / math.factorial(order)
+    return (total * x * math.sqrt(2.0 / NT)).astype(BF16)
+
+
+def basis_kernel(ids, rows_ref, columns_ref):
+    size = rows_ref.shape[0]
+    freq = BLOCK_W * 4
+    pieces = size // (2 * freq)
+    for k in range(pieces):
+        first = (k ^ ids[2]) * freq
+        for c in range(2):
+            frequency = lax.broadcasted_iota(jnp.int32, (freq, NT), 0) + first
+            sample = lax.broadcasted_iota(jnp.int32, (freq, NT), 1)
+            start = (2 * k + c) * freq
+            rows_ref[start : start + freq, :] = table(frequency, c, sample)
+        lane = lax.broadcasted_iota(jnp.int32, (NT, 2 * freq), 1)
+        sample = lax.broadcasted_iota(jnp.int32, (NT, 2 * freq), 0)
+        part = (lane >= freq).astype(jnp.int32)
+        start = 2 * k * freq
+        columns_ref[:, start : start + 2 * freq] = table(lane - part * freq + first, part, sample)
+
+
+def basis(ids):
+    size = 2 * F
+    return call(
+        basis_kernel,
+        "basis",
+        [jax.ShapeDtypeStruct((size, NT), BF16), jax.ShapeDtypeStruct((NT, size), BF16)],
+        40 * size * NT,
+        4 * size * NT,
+        (ids,),
+    )
+
+
+def split_kernel(both, ids, wave_ref, out_ref, hold):
+    width, focal = wave_ref.shape[1], wave_ref.shape[2]
+    for place in range(2 if both else 1):
+        lanes = slice(place * LANES, (place + 1) * LANES)
+        hold[...] = wave_ref[0, :, :, lanes].astype(F32).reshape(width * focal, LANES)
+        for p in range(focal):
+            rows = hold[pl.ds(p, width, stride=focal), :].astype(BF16)
+            if both:
+                out_ref[place, 0, p] = rows
+            else:
+                out_ref[0, p] = rows
+
+
+def split_wave(ids, wave, piece, foc_count, both):
+    freq = wave.shape[1] // foc_count
+    focal = wave.shape[2]
+    if both:
+        shape = (2, 2, focal, freq, LANES)
+        in_spec = pl.BlockSpec(
+            (1, freq, focal, 2 * LANES), lambda c, ids: (c, ids[2] ^ piece, 0, 0)
+        )
+        out_spec = pl.BlockSpec((2, 1, focal, freq, LANES), lambda c, ids: (0, c, 0, 0, 0))
+    else:
+        shape = (2, focal, freq, LANES)
+        in_spec = pl.BlockSpec(
+            (1, freq, focal, LANES), lambda c, ids: (c, ids[2] ^ piece, 0, ids[0])
+        )
+        out_spec = pl.BlockSpec((1, focal, freq, LANES), lambda c, ids: (c, 0, 0, 0))
+    return pl.pallas_call(
+        functools.partial(split_kernel, both),
+        name="split_wave",
+        out_shape=jax.ShapeDtypeStruct(shape, BF16),
+        grid_spec=pltpu.PrefetchScalarGridSpec(
+            num_scalar_prefetch=1,
+            grid=(2,),
+            in_specs=[in_spec],
+            out_specs=out_spec,
+            scratch_shapes=[pltpu.VMEM((freq * focal, LANES), F32)],
+        ),
+        compiler_params=pltpu.CompilerParams(vmem_limit_bytes=VMEM_BYTES),
+        cost_estimate=pl.CostEstimate(
+            flops=0, bytes_accessed=8 * focal * freq * LANES, transcendentals=0
+        ),
+    )(ids, wave)
+
+
+def convolve_kernel(plan, pieces, focal, ids, refl_ref, *refs):
+    ins = refs[: len(plan)]
+    keep_ref, send_ref, hold, result = refs[len(plan) :]
+    half, me = ids[0], ids[1]
+    sources = refl_ref.shape[2]
+    rows = pieces * 2 * focal
+    share = focal // 4
+
+    def block(b, carry):
+        first = pl.multiple_of(b * BLOCK_W, BLOCK_W)
+        window = pl.ds(first, BLOCK_W)
+
+        def put(place, k, c, start, value):
+            size = value.shape[0] * BLOCK_W
+            at = ((k * 2 + c) * focal + start) * BLOCK_W
+            hold[place, at : at + size, :] = value.astype(F32).reshape(size, LANES)
+
+        for ref, (kind, k, start) in zip(ins, plan):
+            for c in range(2):
+                if kind == "both":
+                    put(0, k, c, start, ref[0, c, :, window, :])
+                    put(1, k, c, start, ref[1, c, :, window, :])
+                elif kind == "own":
+                    put(half, k, c, start, ref[c, :, window, :])
+                else:
+                    put(1 - half, k, c, start, ref[c, :, window, :])
+        for w in range(BLOCK_W):
+            step = pl.ds(w, rows, stride=BLOCK_W)
+            left = jnp.concatenate([hold[0, step, :], hold[1, step, :]], 1).astype(BF16)
+            right = refl_ref[:, first + w].reshape(2 * sources, 2 * LANES)
+            both = lax.dot_general(
+                left, right, (((1,), (1,)), ((), ())), preferred_element_type=F32
+            )
+            by_real = both[:, :LANES].reshape(pieces, 2, focal, LANES)
+            by_imag = both[:, LANES:].reshape(pieces, 2, focal, LANES)
+            value = jnp.stack(
+                [by_real[:, 0] - by_imag[:, 1], by_real[:, 1] + by_imag[:, 0]], 1
+            )
+            result[step, :] = value.reshape(rows, LANES)
+        size = share * BLOCK_W
+        for place, out in ((0, keep_ref), (1, send_ref)):
+            for y in range(2):
+                group = (2 * y + place) ^ me
+                for k in range(pieces):
+                    for c in range(2):
+                        start = ((k * 2 + c) * focal + group * share) * BLOCK_W
+                        part = result[pl.ds(pl.multiple_of(start, size), size), :]
+                        out[y, k, c, :, window, :] = part.reshape(
+                            share, BLOCK_W, LANES
+                        ).astype(BF16)
+        return carry
+
+    lax.fori_loop(0, refl_ref.shape[1] // BLOCK_W, block, 0)
+
+
+def convolve_pieces(ids, reflection, plan, arrays, pieces, focal):
+    two, freq, sources, receivers = reflection.shape
+    rows = pieces * 2 * focal
+    out = jax.ShapeDtypeStruct((2, pieces, 2, focal // 4, freq, LANES), BF16)
+    return call(
+        functools.partial(convolve_kernel, plan, pieces, focal),
+        "convolve",
+        [out, out],
+        2 * freq * rows * 256 * 256,
+        freq * (2 * sources * 512 + rows * 768),
+        (ids, reflection, *arrays),
+        [
+            pltpu.VMEM((2, rows * BLOCK_W, LANES), F32),
+            pltpu.VMEM((rows * BLOCK_W, LANES), F32),
+        ],
+    )
+
+
+def correlate_kernel(pieces, ids, refl_ref, *refs):
+    ins = [refs[j * pieces : (j + 1) * pieces] for j in range(4)]
+    outs = refs[4 * pieces : -2]
+    hold, result = refs[-2:]
+    half, me = ids[0], ids[1]
+    share = ins[0][0].shape[1]
+    focal = 4 * share
+    sources = refl_ref.shape[2]
+    rows = pieces * focal
+    part_size = focal // HALVES
+
+    def block(b, carry):
+        first = pl.multiple_of(b * BLOCK_W, BLOCK_W)
+        window = pl.ds(first, BLOCK_W)
+        size = share * BLOCK_W
+        for j in range(4):
+            group = j ^ me
+            for k in range(pieces):
+                start = pl.multiple_of((k * focal + group * share) * BLOCK_W, size)
+                for c in range(2):
+                    value = ins[j][k][c, :, window, :].astype(F32).reshape(size, LANES)
+                    hold[c, pl.ds(start, size), :] = value
+        for w in range(BLOCK_W):
+            step = pl.ds(w, rows, stride=BLOCK_W)
+            real = hold[0, step, :].astype(BF16)
+            imag = hold[1, step, :].astype(BF16)
+            left = jnp.concatenate(
+                [jnp.concatenate([real, imag], 1), jnp.concatenate([imag, -real], 1)], 0
+            )
+            right = refl_ref[:, first + w].reshape(2 * sources, 2 * LANES)
+            value = lax.dot_general(
+                left, right, (((1,), (0,)), ((), ())), preferred_element_type=F32
+            )
+            step = pl.ds(w, 2 * rows, stride=BLOCK_W)
+            result[0, step, :] = value[:, :LANES]
+            result[1, step, :] = value[:, LANES:]
+        size = part_size * BLOCK_W
+        index = 0
+        for place in (half, 1 - half):
+            for q in range(HALVES):
+                for group in PAIRS:
+                    for i, k in enumerate(group):
+                        for c in range(2):
+                            at = ((c * pieces + k) * focal + q * part_size) * BLOCK_W
+                            part = result[place, at : at + size, :]
+                            outs[index][i, c, :, window, :] = part.reshape(
+                                part_size, BLOCK_W, LANES
+                            ).astype(BF16)
+                    index += 1
+        return carry
+
+    lax.fori_loop(0, refl_ref.shape[1] // BLOCK_W, block, 0)
+
+
+PAIRS = ((2, 3), (1, 0))
+
+
+def correlate_pieces(ids, reflection, groups):
+    pieces = len(groups[0])
+    two, share, freq, lanes = groups[0][0].shape
+    focal = 4 * share
+    sources = reflection.shape[2]
+    rows = pieces * 2 * focal
+    out = jax.ShapeDtypeStruct((2, 2, focal // HALVES, freq, LANES), BF16)
+    count = HALVES * len(PAIRS)
+    results = call(
+        functools.partial(correlate_kernel, pieces),
+        "correlate",
+        [out] * (2 * count),
+        2 * freq * rows * 256 * 256,
+        freq * (2 * sources * 512 + rows * 768),
+        (ids, reflection, *[v for group in groups for v in group]),
+        [
+            pltpu.VMEM((2, rows // 2 * BLOCK_W, LANES), F32),
+            pltpu.VMEM((2, rows * BLOCK_W, LANES), F32),
+        ],
+    )
+    return results[:count], results[count:]
+
+
+def windowed(columns_ref, rows, onsets):
+    signal = jnp.dot(columns_ref[...], rows, preferred_element_type=F32)
+    sample = lax.broadcasted_iota(jnp.int32, signal.shape, 0)
+    return jnp.where(sample < onsets, signal, 0.0).astype(BF16)
+
+
+def mute_source_kernel(copy, ids, onset_ref, rows_ref, columns_ref, *refs):
+    pieces = (len(refs) - copy) // 2
+    ins, outs = refs[:pieces], refs[pieces : 2 * pieces]
+    share, width = ins[0].shape[1], ins[0].shape[2]
+    first = ids[1] * share
+    if copy:
+        for k in range(pieces):
+            refs[-1][k] = ins[k][...]
+    spectrum = jnp.concatenate(
+        [
+            jnp.concatenate([ref[c, p] for ref in ins for c in range(2)], 0)
+            for p in range(share)
+        ],
+        1,
+    )
+    onsets = jnp.concatenate([onset_ref[pl.ds(first + p, 1), :] for p in range(share)], 1)
+    muted = windowed(columns_ref, spectrum, onsets)
+    back = jnp.dot(rows_ref[...], muted, preferred_element_type=F32).astype(BF16)
+    for i, out in enumerate(outs):
+        for c in range(2):
+            for p in range(share):
+                start = (2 * i + c) * width
+                out[c, p] = back[start : start + width, p * LANES : (p + 1) * LANES]
+
+
+def mute_source(ids, onset, rows, columns, pieces, copy):
+    shape = pieces[0].shape
+    outs = [jax.ShapeDtypeStruct(shape, BF16)] * len(pieces)
+    if copy:
+        outs = outs + [jax.ShapeDtypeStruct((len(pieces),) + shape, BF16)]
+    return call(
+        functools.partial(mute_source_kernel, int(copy)),
+        "mute_source",
+        outs,
+        4 * NT * 2 * F * shape[1] * LANES,
+        3 << 20,
+        (ids, onset, rows, columns, *pieces),
+    )
+
+
+def trace_kernel(ids, onset_ref, rows_ref, *refs):
+    ins, out_ref = refs[:4], refs[4]
+    pieces, two, share = ins[0].shape[:3]
+    step = pl.program_id(0)
+    for j in range(4):
+
+        @pl.when(step // share == j)
+        def one():
+            p = step % share
+            spectrum = jnp.concatenate(
+                [ins[j][k, c, p] for k in range(pieces) for c in range(2)], 0
+            )
+            signal = lax.dot_general(
+                spectrum, rows_ref[...], (((0,), (0,)), ((), ())), preferred_element_type=F32
+            )
+            sample = lax.broadcasted_iota(jnp.int32, signal.shape, 1)
+            out_ref[0] = jnp.where(sample < onset_ref[0], signal, 0.0).astype(BF16)
+
+
+def trace_source(ids, onset, rows, groups):
+    focal, sources = onset.shape
+    share = groups[0].shape[2]
+
+    def place(g, ids):
+        return ((g // share) ^ ids[1]) * share + g % share, 0, 0
+
+    return pl.pallas_call(
+        trace_kernel,
+        name="trace_source",
+        out_shape=jax.ShapeDtypeStruct((focal, sources, NT), BF16),
+        grid_spec=pltpu.PrefetchScalarGridSpec(
+            num_scalar_prefetch=1,
+            grid=(focal,),
+            in_specs=[pl.BlockSpec((1, sources, 1), place)] + [VMEM_SPEC] * 5,
+            out_specs=pl.BlockSpec((1, sources, NT), place),
+        ),
+        compiler_params=pltpu.CompilerParams(vmem_limit_bytes=VMEM_BYTES),
+        cost_estimate=pl.CostEstimate(
+            flops=2 * NT * 2 * F * focal * LANES, bytes_accessed=5 << 20, transcendentals=0
+        ),
+    )(ids, onset[:, :, None], rows, *groups)
+
+
+def mute_receiver_kernel(first, both, last, ids, onset_ref, rows_ref, columns_ref, *refs):
+    near, extra, one, two, three = refs[:5]
+    pieces = 4
+    direct = refs[5 : 5 + pieces]
+    outs = refs[5 + pieces :]
+    half = ids[0]
+    count, width = one.shape[1], one.shape[2]
+    lanes = pl.ds(pl.multiple_of(half * LANES, LANES), LANES)
+
+    def part(k, c, p):
+        if k == 0:
+            return (near[1, c, p].astype(F32) + extra[1, c, p].astype(F32)).astype(BF16)
+        return (None, one, two, three)[k][c, p]
+
+    step = 2
+    for start in range(0, count, step):
+        group = range(start, start + step)
+        spectrum = jnp.concatenate(
+            [
+                jnp.concatenate([part(k, c, p) for k in range(pieces) for c in range(2)], 0)
+                for p in group
+            ],
+            1,
+        )
+        onsets = jnp.concatenate(
+            [onset_ref[first + p : first + p + 1, lanes] for p in group], 1
+        )
+        muted = windowed(columns_ref, spectrum, onsets)
+        back = jnp.dot(rows_ref[...], muted, preferred_element_type=F32)
+        for k in range(pieces):
+            for c in range(2):
+                for i, p in enumerate(group):
+                    at = (2 * k + c) * width
+                    block = back[at : at + width, i * LANES : (i + 1) * LANES]
+                    if k in both:
+                        wave = direct[k][half, c, first + p]
+                    else:
+                        wave = direct[k][c, first + p]
+                    value = (wave.astype(F32) + block).astype(BF16)
+                    if last:
+                        outs[0][c, k ^ ids[2], p] = value
+                    else:
+                        outs[k][c, p] = value
+
+
+def mute_receiver(ids, onset, rows, columns, arrays, direct, first, both, last):
+    shape = arrays[2].shape
+    count, freq = shape[1], shape[2]
+    if last:
+        outs = jax.ShapeDtypeStruct((2, 4, count, freq, LANES), BF16)
+    else:
+        outs = [jax.ShapeDtypeStruct(shape, BF16)] * 4
+    return call(
+        functools.partial(mute_receiver_kernel, first, both, last),
+        "mute_receiver",
+        outs,
+        4 * NT * 2 * F * count * LANES,
+        4 << 20,
+        (ids, onset, rows, columns, *arrays, *direct),
+    )
+
+
+def join_kernel(ids, *refs):
+    ins, out_ref, hold = refs[:HALVES], refs[-2], refs[-1]
+    two, one, count, width, lanes = ins[0].shape
+    focal = HALVES * count
+    for c in range(2):
+        for q, ref in enumerate(ins):
+            for p in range(count):
+                hold[pl.ds(c * width * focal + q * count + p, width, stride=focal), :] = ref[
+                    c, 0, p
+                ].astype(F32)
+    out_ref[...] = hold[...].astype(BF16).reshape(out_ref.shape)
+
+
+def join_halves(ids, parts, mask, into=None):
+    two, foc_count, count, freq, lanes = parts[0].shape
+    focal = HALVES * count
+    spec = pl.BlockSpec((two, 1, count, freq, lanes), lambda g, ids: (0, g, 0, 0, 0))
+    extra = [] if into is None else [into]
+    return pl.pallas_call(
+        join_kernel,
+        name="join_halves",
+        out_shape=jax.ShapeDtypeStruct((two, foc_count * freq, focal, 2 * lanes), BF16),
+        grid_spec=pltpu.PrefetchScalarGridSpec(
+            num_scalar_prefetch=1,
+            grid=(foc_count,),
+            in_specs=[spec] * HALVES + [pl.BlockSpec(memory_space=pl.ANY)] * len(extra),
+            out_specs=pl.BlockSpec(
+                (two, freq, focal, lanes), lambda g, ids: (0, g, 0, ids[0] ^ mask)
+            ),
+            scratch_shapes=[pltpu.VMEM((two * freq * focal, lanes), F32)],
+        ),
+        input_output_aliases={1 + HALVES: 0} if extra else {},
+        compiler_params=pltpu.CompilerParams(vmem_limit_bytes=VMEM_BYTES),
+        cost_estimate=pl.CostEstimate(
+            flops=0, bytes_accessed=8 * foc_count * freq * focal * lanes, transcendentals=0
+        ),
+    )(ids, *parts, *extra)
+
+
+def add(left, right):
+    return (left.astype(F32) + right.astype(F32)).astype(BF16)
+
+
+def resident(counts, reflection, direct_wave, onset_receiver, onset_source):
+    src_count, rcv_count, foc_count = counts
+    ids = jnp.stack([lax.axis_index("src"), lax.axis_index("rcv"), lax.axis_index("foc")])
+    ids = ids.astype(jnp.int32)
+    focal = direct_wave.shape[2]
+    pieces = range(foc_count)
+    near = (0, 1)
+
+    def to_foc(value, k):
+        return value if k == 0 else swap(value, "foc", k, foc_count)
+
+    def to_src(value):
+        return swap(value, "src", 1, src_count)
+
+    def to_core(value):
+        return swap(value, "rcv", 1, rcv_count)
+
+    def to_y(value):
+        return swap(value, "rcv", 2, rcv_count)
+
+    direct = [None] * foc_count
+    for k in (2, 3, 1, 0):
+        direct[k] = split_wave(ids, direct_wave, k, foc_count, k in near)
+    rows, columns = basis(ids)
+    plan, arrays = [("both", 0, 0)], [direct[0]]
+    for k in (2, 3, 1):
+        got = to_foc(direct[k], k)
+        if k in near:
+            plan, arrays = plan + [("both", k, 0)], arrays + [got]
+        else:
+            plan = plan + [("own", k, 0), ("other", k, 0)]
+            arrays = arrays + [got, to_src(got)]
+    arrays[0], rows, columns = lax.optimization_barrier((arrays[0], rows, columns))
+    for iteration in range(ITERS):
+        last = iteration == ITERS - 1
+        keep, send = convolve_pieces(ids, reflection, tuple(plan), arrays, foc_count, focal)
+        got = to_core(send)
+        beyond = to_y(add(keep[1], got[1]))
+        total = (keep[0].astype(F32) + got[0].astype(F32) + beyond.astype(F32)).astype(BF16)
+        spectrum = [to_foc(total[k], k) for k in pieces]
+        returned = mute_source(ids, onset_source, rows, columns, spectrum, last)
+        mine = [to_foc(returned[k], k) for k in pieces]
+        across = [to_y(value) for value in mine]
+        groups = [mine, [to_core(v) for v in mine], across, [to_core(v) for v in across]]
+        own, other = correlate_pieces(ids, reflection, groups)
+        renewed = []
+        plan, arrays = [], []
+        count = focal // HALVES
+        for q in range(HALVES):
+            far, close = 2 * q, 2 * q + 1
+            got_far, got_close = to_src(other[far]), to_src(other[close])
+            ready = (
+                own[close],
+                got_close,
+                to_foc(add(own[close][0], got_close[0]), 1),
+                to_foc(add(own[far][0], got_far[0]), 2),
+                to_foc(add(own[far][1], got_far[1]), 3),
+            )
+            fresh = mute_receiver(
+                ids, onset_receiver, rows, columns, ready, direct, q * count, near, last
+            )
+            if last:
+                renewed.append(fresh)
+                continue
+            for k in (2, 3, 1, 0):
+                value = to_foc(fresh[k], k)
+                plan += [("own", k, q * count), ("other", k, q * count)]
+                arrays += [value, to_src(value)]
+        if last:
+            crossed = [to_src(value) for value in renewed]
+            mine = returned[-1]
+            across = to_y(mine)
+            groups = [mine, to_core(mine), across, to_core(across)]
+            muted_trace = trace_source(ids, onset_source, rows, groups)
+            partly = join_halves(ids, renewed, 0)
+            return join_halves(ids, crossed, 1, partly), muted_trace
+
+
+def local(counts, reflection, direct_wave, onset_receiver, onset_source):
+    src_count, rcv_count, foc_count = counts
+    two, freq, sources, receivers = reflection.shape
+    focal = direct_wave.shape[2]
+    fits = (
+        (src_count, rcv_count, foc_count) == (2, 4, 4)
+        and sources == LANES
+        and receivers == 2 * LANES
+        and focal == 8
+        and freq == 4 * BLOCK_W
+        and freq * foc_count == F
+    )
+    if fits:
+        return resident(counts, reflection, direct_wave, onset_receiver, onset_source)
+    return general(reflection, direct_wave, onset_receiver, onset_source)
+
+
 def solution(mesh):
     in_specs = (
         P(None, "foc", "src", "rcv"),
@@ -102,4 +662,11 @@
         P("foc", "src"),
     )
     out_specs = (P(None, None, "foc", "rcv"), P("foc", "src", None))
-    return jax.shard_map(local, mesh=mesh, in_specs=in_specs, out_specs=out_specs, check_vma=False)
+    counts = (mesh.shape["src"], mesh.shape["rcv"], mesh.shape["foc"])
+    return jax.shard_map(
+        functools.partial(local, counts),
+        mesh=mesh,
+        in_specs=in_specs,
+        out_specs=out_specs,
+        check_vma=False,
+    )

time: 1460 us -> 266 us (0.18)
  waiting for transfers between devices: 762 us -> 130 us
  local copies, waits for them, and re-layouts: 471 us -> 1.87 us
  matrix products: 186 us -> 0 us
  starting transfers between devices: 1.39 us -> 83.3 us
  Pallas kernels: 0 us -> 48.5 us
    all_gather x3 -> x0, waiting for transfers between devices: 632 us -> none  [the longest x1 566 us: local(): whole_reflection = lax.all_gather(reflection, 'foc', axis=1, tiled=True)]
    dynamic_update_slice x64 -> x0, local copies, waits for them, and re-layouts: 230 us -> none  [one_focus(): lax.dynamic_update_slice_in_dim(returned_all, returned, focal_index, 2)]
    unnamed x27 -> x8, local copies, waits for them, and re-layouts: 227 us -> 1.61 us
    dot_general x56 -> x0, matrix products: 186 us -> none  [the longest x32 27.6 us: one_focus(): jnp.einsum('prt,cwt->cwpr', muted_one, basis_rows, preferred_element_type...]
    ppermute x0 -> x84, waiting for transfers between devices: none -> 130 us  [swap(): return lax.ppermute(value, axis, [(i, i ^ mask) for i in range(count)])]
    ppermute x0 -> x84, starting transfers between devices: none -> 83.3 us  [swap(): return lax.ppermute(value, axis, [(i, i ^ mask) for i in range(count)])]
    psum x2 -> x0, waiting for transfers between devices: 65.4 us -> none  [local(): spectrum = lax.psum(partial_value.astype(jnp.bfloat16), 'rcv')]
    unnamed x9 -> x0, waiting for transfers between devices: 65.1 us -> none
  transfers between devices with their start and end apart: 7 -> 84, of which waited for: 7 -> 44; matrix products, arithmetic and copies ran while one was open for 0% -> 0% of each run, Pallas kernels for 0% -> 9%
where the time goes in v2:
time: 266 us
  waiting for transfers between devices  130 us (49%)
  starting transfers between devices  83.3 us (31%)
  Pallas kernels  48.5 us (18%)
    ppermute x84, waiting for transfers between devices, swap(): return lax.ppermute(value, axis, [(i, i ^ mask) for i in range(count)])  130 us
    ppermute x84, starting transfers between devices, swap(): return lax.ppermute(value, axis, [(i, i ^ mask) for i in range(count)])  83.3 us
    pallas_call x11, Pallas kernels, call(): pl.pallas_call(kernel, name=name, out_shape=out_shape, in_specs=[SMEM_SPE...  32.4 us
    pallas_call x2, Pallas kernels, join_halves(): pl.pallas_call(join_kernel, name='join_halves', out_shape=jax.ShapeDtypeS...  6.56 us
    pallas_call x1, Pallas kernels, trace_source(): pl.pallas_call(trace_kernel, name='trace_source', out_shape=jax.ShapeDtyp...  6.27 us
  transfers between devices with their start and end apart: 84, of which 44 were waited for; matrix products, arithmetic and copies ran while one was open for 0% of the time, Pallas kernels for 9%

profile of v2, /device:TPU:0, one launch (start us, length us, event | category | flops | bytes accessed | tf_op | source)
XLA Modules:
  0.0 265.5 jit_solution(13433227499876576525)
XLA Ops:
  0.7 1.6 copy-done.1
  3.1 4.1 %collective-permute-start = (bf16[2,8,64,128]{3,2,1,0:T(8,128)(2,1)S(1)}, bf16[2,8,64,128]{3,2,1,0:T(8,128)(2,1)S(1)}, u32[]{:S(2)}, u32[]{:S(2)}) collective-permute-start(bf16[2,8,64,128]{3,2,1,0:T(8,128)(2,1)S(1)} %split_wave.5.refs_7_), channel_id=1, source_target_pairs={{0,2},{1,3},{2,0},{3,1},{4,6},{5,7},{6,4},{7,5},{8,10},{9,11},{10,... | collective-permute-start | bytes 786440 | tf_op jit(solution)/shard_map/ppermute | solution.py:111
  10.6 15.0 %collective-permute-done.refs_1_ = bf16[2,8,64,128]{3,2,1,0:T(8,128)(2,1)S(1)} collective-permute-done((bf16[2,8,64,128]{3,2,1,0:T(8,128)(2,1)S(1)}, bf16[2,8,64,128]{3,2,1,0:T(8,128)(2,1)S(1)}, u32[]{:S(2)}, u32[]{:S(2)}) %collective-permute-start) | collective-permute-done | bytes 262176 | tf_op jit(solution)/shard_map/ppermute | solution.py:111
  25.6 1.8 collective-permute-start.1
  28.5 4.1 %basis.1 = (bf16[512,1024]{1,0:T(8,128)(2,1)S(1)}, bf16[1024,512]{1,0:T(8,128)(2,1)S(1)}) custom-call(s32[3]{0:T(128)S(1)} %pad_add_fusion.ids), custom_call_target="tpu_custom_call" | custom-call | flops 20971520 | bytes 2097152 | tf_op jit(solution)/shard_map/basis/pallas_call | solution.py:116
  32.6 2.2 collective-permute-done.1.refs_2_
  34.8 3.0 %collective-permute-done.3.refs_4_ = bf16[2,8,64,128]{3,2,1,0:T(8,128)(2,1)S(1)} collective-permute-done((bf16[2,8,64,128]{3,2,1,0:T(8,128)(2,1)S(1)}, bf16[2,8,64,128]{3,2,1,0:T(8,128)(2,1)S(1)}, u32[]{:S(2)}, u32[]{:S(2)}) %collective-permute-start.3) | collective-permute-done | bytes 262176 | tf_op jit(solution)/shard_map/ppermute | solution.py:111
  37.9 4.0 %convolve.2 = (bf16[2,4,2,2,64,128]{5,4,3,2,1,0:T(8,128)(2,1)S(1)}, bf16[2,4,2,2,64,128]{5,4,3,2,1,0:T(8,128)(2,1)S(1)}) custom-call(s32[3]{0:T(128)S(1)} %pad_add_fusion.ids, bf16[2,64,128,256]{3,2,1,0:T(8,128)(2,1)S(1)} %copy-done, bf16[2,2,8,64,128]{4,3,2,1,0:T(8,128)(2,1)S(1)} %split_wave.4.refs_0_.refs_5_, ...), custom_call_target="tpu_custom_call" | custom-call | flops 536870912 | bytes 11534336 | tf_op jit(solution)/shard_map/convolve/pallas_call | solution.py:116
  42.0 1.9 collective-permute-done.5
  45.4 7.1 %collective-permute-done.6 = bf16[4,2,2,64,128]{4,3,2,1,0:T(8,128)(2,1)S(1)} collective-permute-done((bf16[4,2,2,64,128]{4,3,2,1,0:T(8,128)(2,1)S(1)}, bf16[4,2,2,64,128]{4,3,2,1,0:T(8,128)(2,1)S(1)}, u32[]{:S(2)}, u32[]{:S(2)}) %collective-permute-start.6) | collective-permute-done | bytes 262176 | tf_op jit(solution)/shard_map/ppermute | solution.py:111
  52.6 1.5 collective-permute-start.7
  54.1 3.4 %collective-permute-start.8 = (bf16[2,2,64,128]{3,2,1,0:T(8,128)(2,1)S(1)}, bf16[2,2,64,128]{3,2,1,0:T(8,128)(2,1)S(1)}, u32[]{:S(2)}, u32[]{:S(2)}) collective-permute-start(bf16[2,2,64,128]{3,2,1,0:T(8,128)(2,1)S(1)} %get-tuple-element.99), channel_id=1, source_target_pairs={{0,2},{1,3},{2,0},{3,1},{4,6},{5,7},{6,4},{7,5},{8,10},{9,11},{10,... | collective-permute-start | bytes 196616 | tf_op jit(solution)/shard_map/ppermute | solution.py:111
  57.5 4.1 %collective-permute-done.8.refs_2_ = bf16[2,2,64,128]{3,2,1,0:T(8,128)(2,1)S(1)} collective-permute-done((bf16[2,2,64,128]{3,2,1,0:T(8,128)(2,1)S(1)}, bf16[2,2,64,128]{3,2,1,0:T(8,128)(2,1)S(1)}, u32[]{:S(2)}, u32[]{:S(2)}) %collective-permute-start.8) | collective-permute-done | bytes 65568 | tf_op jit(solution)/shard_map/ppermute | solution.py:111
  61.6 1.9 collective-permute-done.9.refs_3_
  63.5 1.7 mute_source.2
  65.3 1.9 collective-permute-start.11
  67.2 2.4 collective-permute-start.12
  69.7 1.5 collective-permute-start.17
  71.7 1.6 collective-permute-done.12.refs_3_
  75.4 1.5 collective-permute-start.20
  81.1 3.9 %correlate.2 = (bf16[2,2,4,64,128]{4,3,2,1,0:T(8,128)(2,1)S(1)}, bf16[2,2,4,64,128]{4,3,2,1,0:T(8,128)(2,1)S(1)}, bf16[2,2,4,64,128]{4,3,2,1,0:T(8,128)(2,1)S(1)...) custom-call(s32[3]{0:T(128)S(1)} %pad_add_fusion.ids, ...), custom_call_target="tpu_custom_call" | custom-call | flops 536870912 | bytes 11534336 | tf_op jit(solution)/shard_map/correlate/pallas_call | solution.py:116
  85.0 1.6 collective-permute-start.25
  89.2 5.1 %collective-permute-done.25.refs_1_ = bf16[2,2,4,64,128]{4,3,2,1,0:T(8,128)(2,1)S(1)} collective-permute-done((bf16[2,2,4,64,128]{4,3,2,1,0:T(8,128)(2,1)S(1)}, bf16[2,2,4,64,128]{4,3,2,1,0:T(8,128)(2,1)S(1)}, u32[]{:S(2)}, u32[]{:S(2)}) %collective-permute-start.25) | collective-permute-done | bytes 262176 | tf_op jit(solution)/shard_map/ppermute | solution.py:111
  94.8 5.1 %collective-permute-done.27 = bf16[2,2,4,64,128]{4,3,2,1,0:T(8,128)(2,1)S(1)} collective-permute-done((bf16[2,2,4,64,128]{4,3,2,1,0:T(8,128)(2,1)S(1)}, bf16[2,2,4,64,128]{4,3,2,1,0:T(8,128)(2,1)S(1)}, u32[]{:S(2)}, u32[]{:S(2)}) %collective-permute-start.27) | collective-permute-done | bytes 262176 | tf_op jit(solution)/shard_map/ppermute | solution.py:111
  100.6 2.3 collective-permute-start.29
  102.8 2.7 %collective-permute-done.37.refs_1_ = bf16[2,2,4,64,128]{4,3,2,1,0:T(8,128)(2,1)S(1)} collective-permute-done((bf16[2,2,4,64,128]{4,3,2,1,0:T(8,128)(2,1)S(1)}, bf16[2,2,4,64,128]{4,3,2,1,0:T(8,128)(2,1)S(1)}, u32[]{:S(2)}, u32[]{:S(2)}) %collective-permute-start.37) | collective-permute-done | bytes 262176 | tf_op jit(solution)/shard_map/ppermute | solution.py:111
  106.1 4.3 %collective-permute-done.39 = bf16[2,2,4,64,128]{4,3,2,1,0:T(8,128)(2,1)S(1)} collective-permute-done((bf16[2,2,4,64,128]{4,3,2,1,0:T(8,128)(2,1)S(1)}, bf16[2,2,4,64,128]{4,3,2,1,0:T(8,128)(2,1)S(1)}, u32[]{:S(2)}, u32[]{:S(2)}) %collective-permute-start.39) | collective-permute-done | bytes 262176 | tf_op jit(solution)/shard_map/ppermute | solution.py:111
  111.0 2.3 collective-permute-start.41
  113.3 2.3 mute_receiver.4
  115.6 1.7 collective-permute-start.30
  119.1 8.3 %collective-permute-done.40.refs_3_ = bf16[2,4,64,128]{3,2,1,0:T(8,128)(2,1)S(1)} collective-permute-done((bf16[2,4,64,128]{3,2,1,0:T(8,128)(2,1)S(1)}, bf16[2,4,64,128]{3,2,1,0:T(8,128)(2,1)S(1)}, u32[]{:S(2)}, u32[]{:S(2)}) %collective-permute-start.40) | collective-permute-done | bytes 131104 | tf_op jit(solution)/shard_map/ppermute | solution.py:111
  128.9 2.2 mute_receiver.5
  131.1 2.1 collective-permute-start.42
  133.2 2.2 collective-permute-start.44
  138.4 5.9 %collective-permute-done.42.refs_8_ = bf16[2,4,64,128]{3,2,1,0:T(8,128)(2,1)S(1)} collective-permute-done((bf16[2,4,64,128]{3,2,1,0:T(8,128)(2,1)S(1)}, bf16[2,4,64,128]{3,2,1,0:T(8,128)(2,1)S(1)}, u32[]{:S(2)}, u32[]{:S(2)}) %collective-permute-start.42) | collective-permute-done | bytes 131104 | tf_op jit(solution)/shard_map/ppermute | solution.py:111
  150.6 2.8 %collective-permute-done.35.refs_5_ = bf16[2,4,64,128]{3,2,1,0:T(8,128)(2,1)S(1)} collective-permute-done((bf16[2,4,64,128]{3,2,1,0:T(8,128)(2,1)S(1)}, bf16[2,4,64,128]{3,2,1,0:T(8,128)(2,1)S(1)}, u32[]{:S(2)}, u32[]{:S(2)}) %collective-permute-start.35) | collective-permute-done | bytes 131104 | tf_op jit(solution)/shard_map/ppermute | solution.py:111
  153.4 2.8 %collective-permute-done.43.refs_9_ = bf16[2,4,64,128]{3,2,1,0:T(8,128)(2,1)S(1)} collective-permute-done((bf16[2,4,64,128]{3,2,1,0:T(8,128)(2,1)S(1)}, bf16[2,4,64,128]{3,2,1,0:T(8,128)(2,1)S(1)}, u32[]{:S(2)}, u32[]{:S(2)}) %collective-permute-start.43) | collective-permute-done | bytes 131104 | tf_op jit(solution)/shard_map/ppermute | solution.py:111
  156.3 2.8 %collective-permute-done.45.refs_11_ = bf16[2,4,64,128]{3,2,1,0:T(8,128)(2,1)S(1)} collective-permute-done((bf16[2,4,64,128]{3,2,1,0:T(8,128)(2,1)S(1)}, bf16[2,4,64,128]{3,2,1,0:T(8,128)(2,1)S(1)}, u32[]{:S(2)}, u32[]{:S(2)}) %collective-permute-start.45) | collective-permute-done | bytes 131104 | tf_op jit(solution)/shard_map/ppermute | solution.py:111
  159.1 1.8 collective-permute-done.47.refs_13_
  160.9 4.0 %convolve.3 = (bf16[2,4,2,2,64,128]{5,4,3,2,1,0:T(8,128)(2,1)S(1)}, bf16[2,4,2,2,64,128]{5,4,3,2,1,0:T(8,128)(2,1)S(1)}) custom-call(s32[3]{0:T(128)S(1)} %pad_add_fusion.ids, bf16[2,64,128,256]{3,2,1,0:T(8,128)(2,1)S(1)} %copy-done, bf16[2,4,64,128]{3,2,1,0:T(8,128)(2,1)S(1)} %collective-permute-done.30.refs_0_, ...), custom_call_target="tpu_custom_call" | custom-call | flops 536870912 | bytes 11534336 | tf_op jit(solution)/shard_map/convolve/pallas_call | solution.py:116
  165.0 1.9 collective-permute-done.49
  168.2 7.1 %collective-permute-done.50 = bf16[4,2,2,64,128]{4,3,2,1,0:T(8,128)(2,1)S(1)} collective-permute-done((bf16[4,2,2,64,128]{4,3,2,1,0:T(8,128)(2,1)S(1)}, bf16[4,2,2,64,128]{4,3,2,1,0:T(8,128)(2,1)S(1)}, u32[]{:S(2)}, u32[]{:S(2)}) %collective-permute-start.50) | collective-permute-done | bytes 262176 | tf_op jit(solution)/shard_map/ppermute | solution.py:111
  176.1 2.0 collective-permute-start.52
  178.1 1.9 collective-permute-start.53
  180.1 3.0 %collective-permute-done.52.refs_2_ = bf16[2,2,64,128]{3,2,1,0:T(8,128)(2,1)S(1)} collective-permute-done((bf16[2,2,64,128]{3,2,1,0:T(8,128)(2,1)S(1)}, bf16[2,2,64,128]{3,2,1,0:T(8,128)(2,1)S(1)}, u32[]{:S(2)}, u32[]{:S(2)}) %collective-permute-start.52) | collective-permute-done | bytes 65568 | tf_op jit(solution)/shard_map/ppermute | solution.py:111
  184.3 1.7 mute_source.3
  186.8 1.7 collective-permute-start.55
  188.5 2.0 collective-permute-start.56
  190.4 1.6 collective-permute-start.61
  192.9 1.7 collective-permute-done.56.refs_3_
  202.1 4.0 %correlate.3 = (bf16[2,2,4,64,128]{4,3,2,1,0:T(8,128)(2,1)S(1)}, bf16[2,2,4,64,128]{4,3,2,1,0:T(8,128)(2,1)S(1)}, bf16[2,2,4,64,128]{4,3,2,1,0:T(8,128)(2,1)S(1)...) custom-call(s32[3]{0:T(128)S(1)} %pad_add_fusion.ids, ...), custom_call_target="tpu_custom_call" | custom-call | flops 536870912 | bytes 11534336 | tf_op jit(solution)/shard_map/correlate/pallas_call | solution.py:116
  210.2 5.1 %collective-permute-done.69.refs_1_ = bf16[2,2,4,64,128]{4,3,2,1,0:T(8,128)(2,1)S(1)} collective-permute-done((bf16[2,2,4,64,128]{4,3,2,1,0:T(8,128)(2,1)S(1)}, bf16[2,2,4,64,128]{4,3,2,1,0:T(8,128)(2,1)S(1)}, u32[]{:S(2)}, u32[]{:S(2)}) %collective-permute-start.69) | collective-permute-done | bytes 262176 | tf_op jit(solution)/shard_map/ppermute | solution.py:111
  215.8 5.1 %collective-permute-done.71 = bf16[2,2,4,64,128]{4,3,2,1,0:T(8,128)(2,1)S(1)} collective-permute-done((bf16[2,2,4,64,128]{4,3,2,1,0:T(8,128)(2,1)S(1)}, bf16[2,2,4,64,128]{4,3,2,1,0:T(8,128)(2,1)S(1)}, u32[]{:S(2)}, u32[]{:S(2)}) %collective-permute-start.71) | collective-permute-done | bytes 262176 | tf_op jit(solution)/shard_map/ppermute | solution.py:111
  221.4 2.3 collective-permute-start.73
  223.8 2.8 %collective-permute-done.75.refs_1_ = bf16[2,2,4,64,128]{4,3,2,1,0:T(8,128)(2,1)S(1)} collective-permute-done((bf16[2,2,4,64,128]{4,3,2,1,0:T(8,128)(2,1)S(1)}, bf16[2,2,4,64,128]{4,3,2,1,0:T(8,128)(2,1)S(1)}, u32[]{:S(2)}, u32[]{:S(2)}) %collective-permute-start.75) | collective-permute-done | bytes 262176 | tf_op jit(solution)/shard_map/ppermute | solution.py:111
  227.0 4.4 %collective-permute-done.77 = bf16[2,2,4,64,128]{4,3,2,1,0:T(8,128)(2,1)S(1)} collective-permute-done((bf16[2,2,4,64,128]{4,3,2,1,0:T(8,128)(2,1)S(1)}, bf16[2,2,4,64,128]{4,3,2,1,0:T(8,128)(2,1)S(1)}, u32[]{:S(2)}, u32[]{:S(2)}) %collective-permute-start.77) | collective-permute-done | bytes 262176 | tf_op jit(solution)/shard_map/ppermute | solution.py:111
  231.9 2.3 collective-permute-start.79
  235.3 2.2 mute_receiver.6.refs_0_
  238.4 4.3 %collective-permute-done.78.refs_3_ = bf16[2,4,64,128]{3,2,1,0:T(8,128)(2,1)S(1)} collective-permute-done((bf16[2,4,64,128]{3,2,1,0:T(8,128)(2,1)S(1)}, bf16[2,4,64,128]{3,2,1,0:T(8,128)(2,1)S(1)}, u32[]{:S(2)}, u32[]{:S(2)}) %collective-permute-start.78) | collective-permute-done | bytes 131104 | tf_op jit(solution)/shard_map/ppermute | solution.py:111
  242.7 2.2 mute_receiver.7.refs_1_
  248.1 6.3 %trace_source.1 = bf16[8,128,1024]{2,1,0:T(8,128)(2,1)} custom-call(s32[3]{0:T(128)S(1)} %pad_add_fusion.ids, s32[8,128,1]{2,1,0:T(8,128)S(1)} %copy.7.onset_ref, bf16[512,1024]{1,0:T(8,128)(2,1)S(1)} %get-tuple-element.46.rows_ref, bf16[4,2,2,64,128]{4,3,2,1,0:T(8,128)(2,1)S(1)} %get-tuple-element.85.refs_0_, ...), custom_call_target="tpu_custom_call" | custom-call | flops 1073741824 | bytes 5242880 | tf_op jit(solution)/shard_map/trace_source/pallas_call | solution.py:440
  254.4 2.5 join_halves.2.refs_2_
  256.9 4.6 %collective-permute-done.80.refs_1_ = bf16[2,4,4,64,128]{4,3,2,1,0:T(8,128)(2,1)} collective-permute-done((bf16[2,4,4,64,128]{4,3,2,1,0:T(8,128)(2,1)S(1)}, bf16[2,4,4,64,128]{4,3,2,1,0:T(8,128)(2,1)}, u32[]{:S(2)}, u32[]{:S(2)}) %collective-permute-start.80) | collective-permute-done | bytes 524320 | tf_op jit(solution)/shard_map/ppermute | solution.py:111
  261.5 4.1 %join_halves.3 = bf16[2,256,8,256]{3,2,1,0:T(8,128)(2,1)} custom-call(s32[3]{0:T(128)S(1)} %pad_add_fusion.ids, bf16[2,4,4,64,128]{4,3,2,1,0:T(8,128)(2,1)S(1)} %collective-permute-done.74.refs_0_, bf16[2,4,4,64,128]{4,3,2,1,0:T(8,128)(2,1)} %collective-permute-done.80.refs_1_, ...), custom_call_target="tpu_custom_call", output_to_operand_aliasing={{}: (3, {})} | custom-call | bytes 2097152 | tf_op jit(solution)/shard_map/join_halves/pallas_call | solution.py:537
  (146 shorter events, 55.2 us)
Async XLA Ops:
  3.1 22.5 %collective-permute-start = (bf16[2,8,64,128]{3,2,1,0:T(8,128)(2,1)S(1)}, bf16[2,8,64,128]{3,2,1,0:T(8,128)(2,1)S(1)}, u32[]{:S(2)}, u32[]{:S(2)}) collective-permute-start(bf16[2,8,64,128]{3,2,1,0:T(8,128)(2,1)S(1)} %split_wave.5.refs_7_), channel_id=1, source_target_pairs={{0,2},{1,3},{2,0},{3,1},{4,6},{5,7},{6,4},{7,5},{8,10},{9,11},{10,... | collective-permute-start | bytes 786440 | tf_op jit(solution)/shard_map/ppermute | solution.py:111
  8.0 19.5 %collective-permute-start.2 = (bf16[2,8,64,128]{3,2,1,0:T(8,128)(2,1)S(1)}, bf16[2,8,64,128]{3,2,1,0:T(8,128)(2,1)S(1)}, u32[]{:S(2)}, u32[]{:S(2)}) collective-permute-start(bf16[2,8,64,128]{3,2,1,0:T(8,128)(2,1)S(1)} %split_wave.6.refs_8_), channel_id=1, source_target_pairs={{0,3},{1,2},{2,1},{3,0},{4,7},{5,6},{6,5},{7,4},{8,11},{9,10},{10,... | collective-permute-start | bytes 786440 | tf_op jit(solution)/shard_map/ppermute | solution.py:111
  10.2 27.6 %collective-permute-start.4 = (bf16[2,2,8,64,128]{4,3,2,1,0:T(8,128)(2,1)S(1)}, bf16[2,2,8,64,128]{4,3,2,1,0:T(8,128)(2,1)S(1)}, u32[]{:S(2)}, u32[]{:S(2)}) collective-permute-start(bf16[2,2,8,64,128]{4,3,2,1,0:T(8,128)(2,1)S(1)} %split_wave.7.refs_6_), channel_id=1, source_target_pairs={{0,1},{1,0},{2,3},{3,2},{4,5},{5,4},{6,7},{7,6},{8,9},{9,8},{10,11... | collective-permute-start | bytes 1572872 | tf_op jit(solution)/shard_map/ppermute | solution.py:111
  25.6 9.2 %collective-permute-start.1 = (bf16[2,8,64,128]{3,2,1,0:T(8,128)(2,1)S(1)}, bf16[2,8,64,128]{3,2,1,0:T(8,128)(2,1)S(1)}, u32[]{:S(2)}, u32[]{:S(2)}) collective-permute-start(bf16[2,8,64,128]{3,2,1,0:T(8,128)(2,1)S(1)} %collective-permute-done.refs_1_), channel_id=1, source_target_pairs={{0,16},{16,0},{1,17},{17,1},{2,18},{18,2},{3,19},{19,3},{4,20},{20... | collective-permute-start | bytes 786440 | tf_op jit(solution)/shard_map/ppermute | solution.py:111
  27.4 10.4 %collective-permute-start.3 = (bf16[2,8,64,128]{3,2,1,0:T(8,128)(2,1)S(1)}, bf16[2,8,64,128]{3,2,1,0:T(8,128)(2,1)S(1)}, u32[]{:S(2)}, u32[]{:S(2)}) collective-permute-start(bf16[2,8,64,128]{3,2,1,0:T(8,128)(2,1)S(1)} %collective-permute-done.2.refs_3_), channel_id=1, source_target_pairs={{0,16},{16,0},{1,17},{17,1},{2,18},{18,2},{3,19},{19,3},{4,20},{20... | collective-permute-start | bytes 786440 | tf_op jit(solution)/shard_map/ppermute | solution.py:111
  44.0 8.4 %collective-permute-start.6 = (bf16[4,2,2,64,128]{4,3,2,1,0:T(8,128)(2,1)S(1)}, bf16[4,2,2,64,128]{4,3,2,1,0:T(8,128)(2,1)S(1)}, u32[]{:S(2)}, u32[]{:S(2)}) collective-permute-start(bf16[4,2,2,64,128]{4,3,2,1,0:T(8,128)(2,1)S(1)} %fusion.2), channel_id=1, source_target_pairs={{0,8},{4,12},{8,0},{12,4},{1,9},{5,13},{9,1},{13,5},{2,10},{6,14},... | collective-permute-start | bytes 786440 | tf_op jit(solution)/shard_map/ppermute | solution.py:111
  52.6 4.9 %collective-permute-start.7 = (bf16[2,2,64,128]{3,2,1,0:T(8,128)(2,1)S(1)}, bf16[2,2,64,128]{3,2,1,0:T(8,128)(2,1)S(1)}, u32[]{:S(2)}, u32[]{:S(2)}) collective-permute-start(bf16[2,2,64,128]{3,2,1,0:T(8,128)(2,1)S(1)} %get-tuple-element.100), channel_id=1, source_target_pairs={{0,1},{1,0},{2,3},{3,2},{4,5},{5,4},{6,7},{7,6},{8,9},{9,8},{10,11... | collective-permute-start | bytes 196616 | tf_op jit(solution)/shard_map/ppermute | solution.py:111
  54.1 7.5 %collective-permute-start.8 = (bf16[2,2,64,128]{3,2,1,0:T(8,128)(2,1)S(1)}, bf16[2,2,64,128]{3,2,1,0:T(8,128)(2,1)S(1)}, u32[]{:S(2)}, u32[]{:S(2)}) collective-permute-start(bf16[2,2,64,128]{3,2,1,0:T(8,128)(2,1)S(1)} %get-tuple-element.99), channel_id=1, source_target_pairs={{0,2},{1,3},{2,0},{3,1},{4,6},{5,7},{6,4},{7,5},{8,10},{9,11},{10,... | collective-permute-start | bytes 196616 | tf_op jit(solution)/shard_map/ppermute | solution.py:111
  57.5 6.1 %collective-permute-start.9 = (bf16[2,2,64,128]{3,2,1,0:T(8,128)(2,1)S(1)}, bf16[2,2,64,128]{3,2,1,0:T(8,128)(2,1)S(1)}, u32[]{:S(2)}, u32[]{:S(2)}) collective-permute-start(bf16[2,2,64,128]{3,2,1,0:T(8,128)(2,1)S(1)} %get-tuple-element.98), channel_id=1, source_target_pairs={{0,3},{1,2},{2,1},{3,0},{4,7},{5,6},{6,5},{7,4},{8,11},{9,10},{10,... | collective-permute-start | bytes 196616 | tf_op jit(solution)/shard_map/ppermute | solution.py:111
  65.2 6.0 %collective-permute-start.10 = (bf16[2,2,64,128]{3,2,1,0:T(8,128)(2,1)S(1)}, bf16[2,2,64,128]{3,2,1,0:T(8,128)(2,1)S(1)}, u32[]{:S(2)}, u32[]{:S(2)}) collective-permute-start(bf16[2,2,64,128]{3,2,1,0:T(8,128)(2,1)S(1)} %get-tuple-element.52), channel_id=1, source_target_pairs={{0,1},{1,0},{2,3},{3,2},{4,5},{5,4},{6,7},{7,6},{8,9},{9,8},{10,11... | collective-permute-start | bytes 196616 | tf_op jit(solution)/shard_map/ppermute | solution.py:111
  65.3 6.1 %collective-permute-start.11 = (bf16[2,2,64,128]{3,2,1,0:T(8,128)(2,1)S(1)}, bf16[2,2,64,128]{3,2,1,0:T(8,128)(2,1)S(1)}, u32[]{:S(2)}, u32[]{:S(2)}) collective-permute-start(bf16[2,2,64,128]{3,2,1,0:T(8,128)(2,1)S(1)} %get-tuple-element.53), channel_id=1, source_target_pairs={{0,2},{1,3},{2,0},{3,1},{4,6},{5,7},{6,4},{7,5},{8,10},{9,11},{10,... | collective-permute-start | bytes 196616 | tf_op jit(solution)/shard_map/ppermute | solution.py:111
  67.2 6.1 %collective-permute-start.12 = (bf16[2,2,64,128]{3,2,1,0:T(8,128)(2,1)S(1)}, bf16[2,2,64,128]{3,2,1,0:T(8,128)(2,1)S(1)}, u32[]{:S(2)}, u32[]{:S(2)}) collective-permute-start(bf16[2,2,64,128]{3,2,1,0:T(8,128)(2,1)S(1)} %get-tuple-element.54), channel_id=1, source_target_pairs={{0,3},{1,2},{2,1},{3,0},{4,7},{5,6},{6,5},{7,4},{8,11},{9,10},{10,... | collective-permute-start | bytes 196616 | tf_op jit(solution)/shard_map/ppermute | solution.py:111
  69.7 5.2 %collective-permute-start.13 = (bf16[2,2,64,128]{3,2,1,0:T(8,128)(2,1)S(1)}, bf16[2,2,64,128]{3,2,1,0:T(8,128)(2,1)S(1)}, u32[]{:S(2)}, u32[]{:S(2)}) collective-permute-start(bf16[2,2,64,128]{3,2,1,0:T(8,128)(2,1)S(1)} %get-tuple-element.51.refs_0_), channel_id=1, source_target_pairs={{0,4},{4,0},{8,12},{12,8},{1,5},{5,1},{9,13},{13,9},{2,6},{6,2},{1... | collective-permute-start | bytes 196616 | tf_op jit(solution)/shard_map/ppermute | solution.py:111
  69.7 5.7 %collective-permute-start.17 = (bf16[2,2,64,128]{3,2,1,0:T(8,128)(2,1)S(1)}, bf16[2,2,64,128]{3,2,1,0:T(8,128)(2,1)S(1)}, u32[]{:S(2)}, u32[]{:S(2)}) collective-permute-start(bf16[2,2,64,128]{3,2,1,0:T(8,128)(2,1)S(1)} %get-tuple-element.51.refs_0_), channel_id=1, source_target_pairs={{0,8},{4,12},{8,0},{12,4},{1,9},{5,13},{9,1},{13,5},{2,10},{6,14},... | collective-permute-start | bytes 196616 | tf_op jit(solution)/shard_map/ppermute | solution.py:111
  71.2 5.7 %collective-permute-start.14 = (bf16[2,2,64,128]{3,2,1,0:T(8,128)(2,1)S(1)}, bf16[2,2,64,128]{3,2,1,0:T(8,128)(2,1)S(1)}, u32[]{:S(2)}, u32[]{:S(2)}) collective-permute-start(bf16[2,2,64,128]{3,2,1,0:T(8,128)(2,1)S(1)} %collective-permute-done.10.refs_1_), channel_id=1, source_target_pairs={{0,4},{4,0},{8,12},{12,8},{1,5},{5,1},{9,13},{13,9},{2,6},{6,2},{1... | collective-permute-start | bytes 196616 | tf_op jit(solution)/shard_map/ppermute | solution.py:111
  71.5 5.4 %collective-permute-start.15 = (bf16[2,2,64,128]{3,2,1,0:T(8,128)(2,1)S(1)}, bf16[2,2,64,128]{3,2,1,0:T(8,128)(2,1)S(1)}, u32[]{:S(2)}, u32[]{:S(2)}) collective-permute-start(bf16[2,2,64,128]{3,2,1,0:T(8,128)(2,1)S(1)} %collective-permute-done.11.refs_2_), channel_id=1, source_target_pairs={{0,4},{4,0},{8,12},{12,8},{1,5},{5,1},{9,13},{13,9},{2,6},{6,2},{1... | collective-permute-start | bytes 196616 | tf_op jit(solution)/shard_map/ppermute | solution.py:111
  73.3 4.6 %collective-permute-start.18 = (bf16[2,2,64,128]{3,2,1,0:T(8,128)(2,1)S(1)}, bf16[2,2,64,128]{3,2,1,0:T(8,128)(2,1)S(1)}, u32[]{:S(2)}, u32[]{:S(2)}) collective-permute-start(bf16[2,2,64,128]{3,2,1,0:T(8,128)(2,1)S(1)} %collective-permute-done.10.refs_1_), channel_id=1, source_target_pairs={{0,8},{4,12},{8,0},{12,4},{1,9},{5,13},{9,1},{13,5},{2,10},{6,14},... | collective-permute-start | bytes 196616 | tf_op jit(solution)/shard_map/ppermute | solution.py:111
  85.0 9.2 %collective-permute-start.25 = (bf16[2,2,4,64,128]{4,3,2,1,0:T(8,128)(2,1)S(1)}, bf16[2,2,4,64,128]{4,3,2,1,0:T(8,128)(2,1)S(1)}, u32[]{:S(2)}, u32[]{:S(2)}) collective-permute-start(bf16[2,2,4,64,128]{4,3,2,1,0:T(8,128)(2,1)S(1)} %get-tuple-element.56), channel_id=1, source_target_pairs={{0,16},{16,0},{1,17},{17,1},{2,18},{18,2},{3,19},{19,3},{4,20},{20... | collective-permute-start | bytes 786440 | tf_op jit(solution)/shard_map/ppermute | solution.py:111
  86.6 13.3 %collective-permute-start.27 = (bf16[2,2,4,64,128]{4,3,2,1,0:T(8,128)(2,1)S(1)}, bf16[2,2,4,64,128]{4,3,2,1,0:T(8,128)(2,1)S(1)}, u32[]{:S(2)}, u32[]{:S(2)}) collective-permute-start(bf16[2,2,4,64,128]{4,3,2,1,0:T(8,128)(2,1)S(1)} %get-tuple-element.58), channel_id=1, source_target_pairs={{0,16},{16,0},{1,17},{17,1},{2,18},{18,2},{3,19},{19,3},{4,20},{20... | collective-permute-start | bytes 786440 | tf_op jit(solution)/shard_map/ppermute | solution.py:111
  87.1 18.4 %collective-permute-start.37 = (bf16[2,2,4,64,128]{4,3,2,1,0:T(8,128)(2,1)S(1)}, bf16[2,2,4,64,128]{4,3,2,1,0:T(8,128)(2,1)S(1)}, u32[]{:S(2)}, u32[]{:S(2)}) collective-permute-start(bf16[2,2,4,64,128]{4,3,2,1,0:T(8,128)(2,1)S(1)} %get-tuple-element.64), channel_id=1, source_target_pairs={{0,16},{16,0},{1,17},{17,1},{2,18},{18,2},{3,19},{19,3},{4,20},{20... | collective-permute-start | bytes 786440 | tf_op jit(solution)/shard_map/ppermute | solution.py:111
  88.6 21.7 %collective-permute-start.39 = (bf16[2,2,4,64,128]{4,3,2,1,0:T(8,128)(2,1)S(1)}, bf16[2,2,4,64,128]{4,3,2,1,0:T(8,128)(2,1)S(1)}, u32[]{:S(2)}, u32[]{:S(2)}) collective-permute-start(bf16[2,2,4,64,128]{4,3,2,1,0:T(8,128)(2,1)S(1)} %get-tuple-element.66), channel_id=1, source_target_pairs={{0,16},{16,0},{1,17},{17,1},{2,18},{18,2},{3,19},{19,3},{4,20},{20... | collective-permute-start | bytes 786440 | tf_op jit(solution)/shard_map/ppermute | solution.py:111
  94.3 16.7 %collective-permute-start.26 = (bf16[2,4,64,128]{3,2,1,0:T(8,128)(2,1)S(1)}, bf16[2,4,64,128]{3,2,1,0:T(8,128)(2,1)S(1)}, u32[]{:S(2)}, u32[]{:S(2)}) collective-permute-start(bf16[2,4,64,128]{3,2,1,0:T(8,128)(2,1)S(1)} %fusion.4), channel_id=1, source_target_pairs={{0,1},{1,0},{2,3},{3,2},{4,5},{5,4},{6,7},{7,6},{8,9},{9,8},{10,11... | collective-permute-start | bytes 393224 | tf_op jit(solution)/shard_map/ppermute | solution.py:111
  100.0 13.3 %collective-permute-start.28 = (bf16[2,4,64,128]{3,2,1,0:T(8,128)(2,1)S(1)}, bf16[2,4,64,128]{3,2,1,0:T(8,128)(2,1)S(1)}, u32[]{:S(2)}, u32[]{:S(2)}) collective-permute-start(bf16[2,4,64,128]{3,2,1,0:T(8,128)(2,1)S(1)} %get-tuple-element.93), channel_id=1, source_target_pairs={{0,2},{1,3},{2,0},{3,1},{4,6},{5,7},{6,4},{7,5},{8,10},{9,11},{10,... | collective-permute-start | bytes 393224 | tf_op jit(solution)/shard_map/ppermute | solution.py:111
  100.6 12.7 %collective-permute-start.29 = (bf16[2,4,64,128]{3,2,1,0:T(8,128)(2,1)S(1)}, bf16[2,4,64,128]{3,2,1,0:T(8,128)(2,1)S(1)}, u32[]{:S(2)}, u32[]{:S(2)}) collective-permute-start(bf16[2,4,64,128]{3,2,1,0:T(8,128)(2,1)S(1)} %get-tuple-element.92), channel_id=1, source_target_pairs={{0,3},{1,2},{2,1},{3,0},{4,7},{5,6},{6,5},{7,4},{8,11},{9,10},{10,... | collective-permute-start | bytes 393224 | tf_op jit(solution)/shard_map/ppermute | solution.py:111
  105.5 13.1 %collective-permute-start.38 = (bf16[2,4,64,128]{3,2,1,0:T(8,128)(2,1)S(1)}, bf16[2,4,64,128]{3,2,1,0:T(8,128)(2,1)S(1)}, u32[]{:S(2)}, u32[]{:S(2)}) collective-permute-start(bf16[2,4,64,128]{3,2,1,0:T(8,128)(2,1)S(1)} %fusion.7), channel_id=1, source_target_pairs={{0,1},{1,0},{2,3},{3,2},{4,5},{5,4},{6,7},{7,6},{8,9},{9,8},{10,11... | collective-permute-start | bytes 393224 | tf_op jit(solution)/shard_map/ppermute | solution.py:111
  110.4 17.0 %collective-permute-start.40 = (bf16[2,4,64,128]{3,2,1,0:T(8,128)(2,1)S(1)}, bf16[2,4,64,128]{3,2,1,0:T(8,128)(2,1)S(1)}, u32[]{:S(2)}, u32[]{:S(2)}) collective-permute-start(bf16[2,4,64,128]{3,2,1,0:T(8,128)(2,1)S(1)} %get-tuple-element.91), channel_id=1, source_target_pairs={{0,2},{1,3},{2,0},{3,1},{4,6},{5,7},{6,4},{7,5},{8,10},{9,11},{10,... | collective-permute-start | bytes 393224 | tf_op jit(solution)/shard_map/ppermute | solution.py:111
  111.0 17.9 %collective-permute-start.41 = (bf16[2,4,64,128]{3,2,1,0:T(8,128)(2,1)S(1)}, bf16[2,4,64,128]{3,2,1,0:T(8,128)(2,1)S(1)}, u32[]{:S(2)}, u32[]{:S(2)}) collective-permute-start(bf16[2,4,64,128]{3,2,1,0:T(8,128)(2,1)S(1)} %get-tuple-element.90), channel_id=1, source_target_pairs={{0,3},{1,2},{2,1},{3,0},{4,7},{5,6},{6,5},{7,4},{8,11},{9,10},{10,... | collective-permute-start | bytes 393224 | tf_op jit(solution)/shard_map/ppermute | solution.py:111
  115.6 17.7 %collective-permute-start.30 = (bf16[2,4,64,128]{3,2,1,0:T(8,128)(2,1)S(1)}, bf16[2,4,64,128]{3,2,1,0:T(8,128)(2,1)S(1)}, u32[]{:S(2)}, u32[]{:S(2)}) collective-permute-start(bf16[2,4,64,128]{3,2,1,0:T(8,128)(2,1)S(1)} %get-tuple-element.59), channel_id=1, source_target_pairs={{0,2},{1,3},{2,0},{3,1},{4,6},{5,7},{6,4},{7,5},{8,10},{9,11},{10,... | collective-permute-start | bytes 393224 | tf_op jit(solution)/shard_map/ppermute | solution.py:111
  117.3 18.2 %collective-permute-start.32 = (bf16[2,4,64,128]{3,2,1,0:T(8,128)(2,1)S(1)}, bf16[2,4,64,128]{3,2,1,0:T(8,128)(2,1)S(1)}, u32[]{:S(2)}, u32[]{:S(2)}) collective-permute-start(bf16[2,4,64,128]{3,2,1,0:T(8,128)(2,1)S(1)} %get-tuple-element.60), channel_id=1, source_target_pairs={{0,3},{1,2},{2,1},{3,0},{4,7},{5,6},{6,5},{7,4},{8,11},{9,10},{10,... | collective-permute-start | bytes 393224 | tf_op jit(solution)/shard_map/ppermute | solution.py:111
  118.7 17.7 %collective-permute-start.34 = (bf16[2,4,64,128]{3,2,1,0:T(8,128)(2,1)S(1)}, bf16[2,4,64,128]{3,2,1,0:T(8,128)(2,1)S(1)}, u32[]{:S(2)}, u32[]{:S(2)}) collective-permute-start(bf16[2,4,64,128]{3,2,1,0:T(8,128)(2,1)S(1)} %get-tuple-element.61), channel_id=1, source_target_pairs={{0,1},{1,0},{2,3},{3,2},{4,5},{5,4},{6,7},{7,6},{8,9},{9,8},{10,11... | collective-permute-start | bytes 393224 | tf_op jit(solution)/shard_map/ppermute | solution.py:111
  127.4 10.5 %collective-permute-start.36 = (bf16[2,4,64,128]{3,2,1,0:T(8,128)(2,1)S(1)}, bf16[2,4,64,128]{3,2,1,0:T(8,128)(2,1)S(1)}, u32[]{:S(2)}, u32[]{:S(2)}) collective-permute-start(bf16[2,4,64,128]{3,2,1,0:T(8,128)(2,1)S(1)} %get-tuple-element.62.refs_6_), channel_id=1, source_target_pairs={{0,16},{16,0},{1,17},{17,1},{2,18},{18,2},{3,19},{19,3},{4,20},{20... | collective-permute-start | bytes 393224 | tf_op jit(solution)/shard_map/ppermute | solution.py:111
  131.1 13.1 %collective-permute-start.42 = (bf16[2,4,64,128]{3,2,1,0:T(8,128)(2,1)S(1)}, bf16[2,4,64,128]{3,2,1,0:T(8,128)(2,1)S(1)}, u32[]{:S(2)}, u32[]{:S(2)}) collective-permute-start(bf16[2,4,64,128]{3,2,1,0:T(8,128)(2,1)S(1)} %get-tuple-element.67), channel_id=1, source_target_pairs={{0,2},{1,3},{2,0},{3,1},{4,6},{5,7},{6,4},{7,5},{8,10},{9,11},{10,... | collective-permute-start | bytes 393224 | tf_op jit(solution)/shard_map/ppermute | solution.py:111
  133.2 12.5 %collective-permute-start.44 = (bf16[2,4,64,128]{3,2,1,0:T(8,128)(2,1)S(1)}, bf16[2,4,64,128]{3,2,1,0:T(8,128)(2,1)S(1)}, u32[]{:S(2)}, u32[]{:S(2)}) collective-permute-start(bf16[2,4,64,128]{3,2,1,0:T(8,128)(2,1)S(1)} %get-tuple-element.68), channel_id=1, source_target_pairs={{0,3},{1,2},{2,1},{3,0},{4,7},{5,6},{6,5},{7,4},{8,11},{9,10},{10,... | collective-permute-start | bytes 393224 | tf_op jit(solution)/shard_map/ppermute | solution.py:111
  135.4 10.9 %collective-permute-start.46 = (bf16[2,4,64,128]{3,2,1,0:T(8,128)(2,1)S(1)}, bf16[2,4,64,128]{3,2,1,0:T(8,128)(2,1)S(1)}, u32[]{:S(2)}, u32[]{:S(2)}) collective-permute-start(bf16[2,4,64,128]{3,2,1,0:T(8,128)(2,1)S(1)} %get-tuple-element.69), channel_id=1, source_target_pairs={{0,1},{1,0},{2,3},{3,2},{4,5},{5,4},{6,7},{7,6},{8,9},{9,8},{10,11... | collective-permute-start | bytes 393224 | tf_op jit(solution)/shard_map/ppermute | solution.py:111
  136.4 11.5 %collective-permute-start.48 = (bf16[2,4,64,128]{3,2,1,0:T(8,128)(2,1)S(1)}, bf16[2,4,64,128]{3,2,1,0:T(8,128)(2,1)S(1)}, u32[]{:S(2)}, u32[]{:S(2)}) collective-permute-start(bf16[2,4,64,128]{3,2,1,0:T(8,128)(2,1)S(1)} %get-tuple-element.70.refs_14_), channel_id=1, source_target_pairs={{0,16},{16,0},{1,17},{17,1},{2,18},{18,2},{3,19},{19,3},{4,20},{20... | collective-permute-start | bytes 393224 | tf_op jit(solution)/shard_map/ppermute | solution.py:111
  137.9 10.5 %collective-permute-start.31 = (bf16[2,4,64,128]{3,2,1,0:T(8,128)(2,1)S(1)}, bf16[2,4,64,128]{3,2,1,0:T(8,128)(2,1)S(1)}, u32[]{:S(2)}, u32[]{:S(2)}) collective-permute-start(bf16[2,4,64,128]{3,2,1,0:T(8,128)(2,1)S(1)} %collective-permute-done.30.refs_0_), channel_id=1, source_target_pairs={{0,16},{16,0},{1,17},{17,1},{2,18},{18,2},{3,19},{19,3},{4,20},{20... | collective-permute-start | bytes 393224 | tf_op jit(solution)/shard_map/ppermute | solution.py:111
  144.3 6.4 %collective-permute-start.33 = (bf16[2,4,64,128]{3,2,1,0:T(8,128)(2,1)S(1)}, bf16[2,4,64,128]{3,2,1,0:T(8,128)(2,1)S(1)}, u32[]{:S(2)}, u32[]{:S(2)}) collective-permute-start(bf16[2,4,64,128]{3,2,1,0:T(8,128)(2,1)S(1)} %collective-permute-done.32.refs_2_), channel_id=1, source_target_pairs={{0,16},{16,0},{1,17},{17,1},{2,18},{18,2},{3,19},{19,3},{4,20},{20... | collective-permute-start | bytes 393224 | tf_op jit(solution)/shard_map/ppermute | solution.py:111
  145.8 7.7 %collective-permute-start.35 = (bf16[2,4,64,128]{3,2,1,0:T(8,128)(2,1)S(1)}, bf16[2,4,64,128]{3,2,1,0:T(8,128)(2,1)S(1)}, u32[]{:S(2)}, u32[]{:S(2)}) collective-permute-start(bf16[2,4,64,128]{3,2,1,0:T(8,128)(2,1)S(1)} %collective-permute-done.34.refs_4_), channel_id=1, source_target_pairs={{0,16},{16,0},{1,17},{17,1},{2,18},{18,2},{3,19},{19,3},{4,20},{20... | collective-permute-start | bytes 393224 | tf_op jit(solution)/shard_map/ppermute | solution.py:111
  146.3 9.9 %collective-permute-start.43 = (bf16[2,4,64,128]{3,2,1,0:T(8,128)(2,1)S(1)}, bf16[2,4,64,128]{3,2,1,0:T(8,128)(2,1)S(1)}, u32[]{:S(2)}, u32[]{:S(2)}) collective-permute-start(bf16[2,4,64,128]{3,2,1,0:T(8,128)(2,1)S(1)} %collective-permute-done.42.refs_8_), channel_id=1, source_target_pairs={{0,16},{16,0},{1,17},{17,1},{2,18},{18,2},{3,19},{19,3},{4,20},{20... | collective-permute-start | bytes 393224 | tf_op jit(solution)/shard_map/ppermute | solution.py:111
  147.8 11.2 %collective-permute-start.45 = (bf16[2,4,64,128]{3,2,1,0:T(8,128)(2,1)S(1)}, bf16[2,4,64,128]{3,2,1,0:T(8,128)(2,1)S(1)}, u32[]{:S(2)}, u32[]{:S(2)}) collective-permute-start(bf16[2,4,64,128]{3,2,1,0:T(8,128)(2,1)S(1)} %collective-permute-done.44.refs_10_), channel_id=1, source_target_pairs={{0,16},{16,0},{1,17},{17,1},{2,18},{18,2},{3,19},{19,3},{4,20},{20... | collective-permute-start | bytes 393224 | tf_op jit(solution)/shard_map/ppermute | solution.py:111
  148.4 12.5 %collective-permute-start.47 = (bf16[2,4,64,128]{3,2,1,0:T(8,128)(2,1)S(1)}, bf16[2,4,64,128]{3,2,1,0:T(8,128)(2,1)S(1)}, u32[]{:S(2)}, u32[]{:S(2)}) collective-permute-start(bf16[2,4,64,128]{3,2,1,0:T(8,128)(2,1)S(1)} %collective-permute-done.46.refs_12_), channel_id=1, source_target_pairs={{0,16},{16,0},{1,17},{17,1},{2,18},{18,2},{3,19},{19,3},{4,20},{20... | collective-permute-start | bytes 393224 | tf_op jit(solution)/shard_map/ppermute | solution.py:111
  166.9 8.4 %collective-permute-start.50 = (bf16[4,2,2,64,128]{4,3,2,1,0:T(8,128)(2,1)S(1)}, bf16[4,2,2,64,128]{4,3,2,1,0:T(8,128)(2,1)S(1)}, u32[]{:S(2)}, u32[]{:S(2)}) collective-permute-start(bf16[4,2,2,64,128]{4,3,2,1,0:T(8,128)(2,1)S(1)} %fusion.3), channel_id=1, source_target_pairs={{0,8},{4,12},{8,0},{12,4},{1,9},{5,13},{9,1},{13,5},{2,10},{6,14},... | collective-permute-start | bytes 786440 | tf_op jit(solution)/shard_map/ppermute | solution.py:111
  176.1 6.9 %collective-permute-start.52 = (bf16[2,2,64,128]{3,2,1,0:T(8,128)(2,1)S(1)}, bf16[2,2,64,128]{3,2,1,0:T(8,128)(2,1)S(1)}, u32[]{:S(2)}, u32[]{:S(2)}) collective-permute-start(bf16[2,2,64,128]{3,2,1,0:T(8,128)(2,1)S(1)} %get-tuple-element.95), channel_id=1, source_target_pairs={{0,2},{1,3},{2,0},{3,1},{4,6},{5,7},{6,4},{7,5},{8,10},{9,11},{10,... | collective-permute-start | bytes 196616 | tf_op jit(solution)/shard_map/ppermute | solution.py:111
  178.1 6.2 %collective-permute-start.53 = (bf16[2,2,64,128]{3,2,1,0:T(8,128)(2,1)S(1)}, bf16[2,2,64,128]{3,2,1,0:T(8,128)(2,1)S(1)}, u32[]{:S(2)}, u32[]{:S(2)}) collective-permute-start(bf16[2,2,64,128]{3,2,1,0:T(8,128)(2,1)S(1)} %get-tuple-element.94), channel_id=1, source_target_pairs={{0,3},{1,2},{2,1},{3,0},{4,7},{5,6},{6,5},{7,4},{8,11},{9,10},{10,... | collective-permute-start | bytes 196616 | tf_op jit(solution)/shard_map/ppermute | solution.py:111
  186.0 6.1 %collective-permute-start.54 = (bf16[2,2,64,128]{3,2,1,0:T(8,128)(2,1)S(1)}, bf16[2,2,64,128]{3,2,1,0:T(8,128)(2,1)S(1)}, u32[]{:S(2)}, u32[]{:S(2)}) collective-permute-start(bf16[2,2,64,128]{3,2,1,0:T(8,128)(2,1)S(1)} %get-tuple-element.74), channel_id=1, source_target_pairs={{0,1},{1,0},{2,3},{3,2},{4,5},{5,4},{6,7},{7,6},{8,9},{9,8},{10,11... | collective-permute-start | bytes 196616 | tf_op jit(solution)/shard_map/ppermute | solution.py:111
  186.8 6.1 %collective-permute-start.55 = (bf16[2,2,64,128]{3,2,1,0:T(8,128)(2,1)S(1)}, bf16[2,2,64,128]{3,2,1,0:T(8,128)(2,1)S(1)}, u32[]{:S(2)}, u32[]{:S(2)}) collective-permute-start(bf16[2,2,64,128]{3,2,1,0:T(8,128)(2,1)S(1)} %get-tuple-element.75), channel_id=1, source_target_pairs={{0,2},{1,3},{2,0},{3,1},{4,6},{5,7},{6,4},{7,5},{8,10},{9,11},{10,... | collective-permute-start | bytes 196616 | tf_op jit(solution)/shard_map/ppermute | solution.py:111
  188.5 6.1 %collective-permute-start.56 = (bf16[2,2,64,128]{3,2,1,0:T(8,128)(2,1)S(1)}, bf16[2,2,64,128]{3,2,1,0:T(8,128)(2,1)S(1)}, u32[]{:S(2)}, u32[]{:S(2)}) collective-permute-start(bf16[2,2,64,128]{3,2,1,0:T(8,128)(2,1)S(1)} %get-tuple-element.76), channel_id=1, source_target_pairs={{0,3},{1,2},{2,1},{3,0},{4,7},{5,6},{6,5},{7,4},{8,11},{9,10},{10,... | collective-permute-start | bytes 196616 | tf_op jit(solution)/shard_map/ppermute | solution.py:111
  190.4 5.3 %collective-permute-start.57 = (bf16[2,2,64,128]{3,2,1,0:T(8,128)(2,1)S(1)}, bf16[2,2,64,128]{3,2,1,0:T(8,128)(2,1)S(1)}, u32[]{:S(2)}, u32[]{:S(2)}) collective-permute-start(bf16[2,2,64,128]{3,2,1,0:T(8,128)(2,1)S(1)} %get-tuple-element.73.refs_0_), channel_id=1, source_target_pairs={{0,4},{4,0},{8,12},{12,8},{1,5},{5,1},{9,13},{13,9},{2,6},{6,2},{1... | collective-permute-start | bytes 196616 | tf_op jit(solution)/shard_map/ppermute | solution.py:111
  190.4 6.1 %collective-permute-start.61 = (bf16[2,2,64,128]{3,2,1,0:T(8,128)(2,1)S(1)}, bf16[2,2,64,128]{3,2,1,0:T(8,128)(2,1)S(1)}, u32[]{:S(2)}, u32[]{:S(2)}) collective-permute-start(bf16[2,2,64,128]{3,2,1,0:T(8,128)(2,1)S(1)} %get-tuple-element.73.refs_0_), channel_id=1, source_target_pairs={{0,8},{4,12},{8,0},{12,4},{1,9},{5,13},{9,1},{13,5},{2,10},{6,14},... | collective-permute-start | bytes 196616 | tf_op jit(solution)/shard_map/ppermute | solution.py:111
  192.1 5.7 %collective-permute-start.58 = (bf16[2,2,64,128]{3,2,1,0:T(8,128)(2,1)S(1)}, bf16[2,2,64,128]{3,2,1,0:T(8,128)(2,1)S(1)}, u32[]{:S(2)}, u32[]{:S(2)}) collective-permute-start(bf16[2,2,64,128]{3,2,1,0:T(8,128)(2,1)S(1)} %collective-permute-done.54.refs_1_), channel_id=1, source_target_pairs={{0,4},{4,0},{8,12},{12,8},{1,5},{5,1},{9,13},{13,9},{2,6},{6,2},{1... | collective-permute-start | bytes 196616 | tf_op jit(solution)/shard_map/ppermute | solution.py:111
  192.9 5.0 %collective-permute-start.59 = (bf16[2,2,64,128]{3,2,1,0:T(8,128)(2,1)S(1)}, bf16[2,2,64,128]{3,2,1,0:T(8,128)(2,1)S(1)}, u32[]{:S(2)}, u32[]{:S(2)}) collective-permute-start(bf16[2,2,64,128]{3,2,1,0:T(8,128)(2,1)S(1)} %collective-permute-done.55.refs_2_), channel_id=1, source_target_pairs={{0,4},{4,0},{8,12},{12,8},{1,5},{5,1},{9,13},{13,9},{2,6},{6,2},{1... | collective-permute-start | bytes 196616 | tf_op jit(solution)/shard_map/ppermute | solution.py:111
  206.1 9.2 %collective-permute-start.69 = (bf16[2,2,4,64,128]{4,3,2,1,0:T(8,128)(2,1)S(1)}, bf16[2,2,4,64,128]{4,3,2,1,0:T(8,128)(2,1)S(1)}, u32[]{:S(2)}, u32[]{:S(2)}) collective-permute-start(bf16[2,2,4,64,128]{4,3,2,1,0:T(8,128)(2,1)S(1)} %get-tuple-element.78), channel_id=1, source_target_pairs={{0,16},{16,0},{1,17},{17,1},{2,18},{18,2},{3,19},{19,3},{4,20},{20... | collective-permute-start | bytes 786440 | tf_op jit(solution)/shard_map/ppermute | solution.py:111
  207.5 13.4 %collective-permute-start.71 = (bf16[2,2,4,64,128]{4,3,2,1,0:T(8,128)(2,1)S(1)}, bf16[2,2,4,64,128]{4,3,2,1,0:T(8,128)(2,1)S(1)}, u32[]{:S(2)}, u32[]{:S(2)}) collective-permute-start(bf16[2,2,4,64,128]{4,3,2,1,0:T(8,128)(2,1)S(1)} %get-tuple-element.80), channel_id=1, source_target_pairs={{0,16},{16,0},{1,17},{17,1},{2,18},{18,2},{3,19},{19,3},{4,20},{20... | collective-permute-start | bytes 786440 | tf_op jit(solution)/shard_map/ppermute | solution.py:111
  208.2 18.4 %collective-permute-start.75 = (bf16[2,2,4,64,128]{4,3,2,1,0:T(8,128)(2,1)S(1)}, bf16[2,2,4,64,128]{4,3,2,1,0:T(8,128)(2,1)S(1)}, u32[]{:S(2)}, u32[]{:S(2)}) collective-permute-start(bf16[2,2,4,64,128]{4,3,2,1,0:T(8,128)(2,1)S(1)} %get-tuple-element.82), channel_id=1, source_target_pairs={{0,16},{16,0},{1,17},{17,1},{2,18},{18,2},{3,19},{19,3},{4,20},{20... | collective-permute-start | bytes 786440 | tf_op jit(solution)/shard_map/ppermute | solution.py:111
  209.6 21.8 %collective-permute-start.77 = (bf16[2,2,4,64,128]{4,3,2,1,0:T(8,128)(2,1)S(1)}, bf16[2,2,4,64,128]{4,3,2,1,0:T(8,128)(2,1)S(1)}, u32[]{:S(2)}, u32[]{:S(2)}) collective-permute-start(bf16[2,2,4,64,128]{4,3,2,1,0:T(8,128)(2,1)S(1)} %get-tuple-element.84), channel_id=1, source_target_pairs={{0,16},{16,0},{1,17},{17,1},{2,18},{18,2},{3,19},{19,3},{4,20},{20... | collective-permute-start | bytes 786440 | tf_op jit(solution)/shard_map/ppermute | solution.py:111
  215.3 16.6 %collective-permute-start.70 = (bf16[2,4,64,128]{3,2,1,0:T(8,128)(2,1)S(1)}, bf16[2,4,64,128]{3,2,1,0:T(8,128)(2,1)S(1)}, u32[]{:S(2)}, u32[]{:S(2)}) collective-permute-start(bf16[2,4,64,128]{3,2,1,0:T(8,128)(2,1)S(1)} %fusion.10), channel_id=1, source_target_pairs={{0,1},{1,0},{2,3},{3,2},{4,5},{5,4},{6,7},{7,6},{8,9},{9,8},{10,11... | collective-permute-start | bytes 393224 | tf_op jit(solution)/shard_map/ppermute | solution.py:111
  221.0 13.2 %collective-permute-start.72 = (bf16[2,4,64,128]{3,2,1,0:T(8,128)(2,1)S(1)}, bf16[2,4,64,128]{3,2,1,0:T(8,128)(2,1)S(1)}, u32[]{:S(2)}, u32[]{:S(2)}) collective-permute-start(bf16[2,4,64,128]{3,2,1,0:T(8,128)(2,1)S(1)} %get-tuple-element.89), channel_id=1, source_target_pairs={{0,2},{1,3},{2,0},{3,1},{4,6},{5,7},{6,4},{7,5},{8,10},{9,11},{10,... | collective-permute-start | bytes 393224 | tf_op jit(solution)/shard_map/ppermute | solution.py:111
  221.4 13.9 %collective-permute-start.73 = (bf16[2,4,64,128]{3,2,1,0:T(8,128)(2,1)S(1)}, bf16[2,4,64,128]{3,2,1,0:T(8,128)(2,1)S(1)}, u32[]{:S(2)}, u32[]{:S(2)}) collective-permute-start(bf16[2,4,64,128]{3,2,1,0:T(8,128)(2,1)S(1)} %get-tuple-element.88), channel_id=1, source_target_pairs={{0,3},{1,2},{2,1},{3,0},{4,7},{5,6},{6,5},{7,4},{8,11},{9,10},{10,... | collective-permute-start | bytes 393224 | tf_op jit(solution)/shard_map/ppermute | solution.py:111
  226.6 11.8 %collective-permute-start.76 = (bf16[2,4,64,128]{3,2,1,0:T(8,128)(2,1)S(1)}, bf16[2,4,64,128]{3,2,1,0:T(8,128)(2,1)S(1)}, u32[]{:S(2)}, u32[]{:S(2)}) collective-permute-start(bf16[2,4,64,128]{3,2,1,0:T(8,128)(2,1)S(1)} %fusion.13), channel_id=1, source_target_pairs={{0,1},{1,0},{2,3},{3,2},{4,5},{5,4},{6,7},{7,6},{8,9},{9,8},{10,11... | collective-permute-start | bytes 393224 | tf_op jit(solution)/shard_map/ppermute | solution.py:111
  231.4 11.2 %collective-permute-start.78 = (bf16[2,4,64,128]{3,2,1,0:T(8,128)(2,1)S(1)}, bf16[2,4,64,128]{3,2,1,0:T(8,128)(2,1)S(1)}, u32[]{:S(2)}, u32[]{:S(2)}) collective-permute-start(bf16[2,4,64,128]{3,2,1,0:T(8,128)(2,1)S(1)} %get-tuple-element.87), channel_id=1, source_target_pairs={{0,2},{1,3},{2,0},{3,1},{4,6},{5,7},{6,4},{7,5},{8,10},{9,11},{10,... | collective-permute-start | bytes 393224 | tf_op jit(solution)/shard_map/ppermute | solution.py:111
  231.9 10.8 %collective-permute-start.79 = (bf16[2,4,64,128]{3,2,1,0:T(8,128)(2,1)S(1)}, bf16[2,4,64,128]{3,2,1,0:T(8,128)(2,1)S(1)}, u32[]{:S(2)}, u32[]{:S(2)}) collective-permute-start(bf16[2,4,64,128]{3,2,1,0:T(8,128)(2,1)S(1)} %get-tuple-element.86), channel_id=1, source_target_pairs={{0,3},{1,2},{2,1},{3,0},{4,7},{5,6},{6,5},{7,4},{8,11},{9,10},{10,... | collective-permute-start | bytes 393224 | tf_op jit(solution)/shard_map/ppermute | solution.py:111
  234.2 11.6 %collective-permute-start.82 = (bf16[4,2,2,64,128]{4,3,2,1,0:T(8,128)(2,1)S(1)}, bf16[4,2,2,64,128]{4,3,2,1,0:T(8,128)(2,1)}, u32[]{:S(2)}, u32[]{:S(2)}) collective-permute-start(bf16[4,2,2,64,128]{4,3,2,1,0:T(8,128)(2,1)S(1)} %get-tuple-element.85.refs_0_), channel_id=1, source_target_pairs={{0,8},{4,12},{8,0},{12,4},{1,9},{5,13},{9,1},{13,5},{2,10},{6,14},... | collective-permute-start | bytes 786440 | tf_op jit(solution)/shard_map/ppermute | solution.py:111
  237.6 19.3 %collective-permute-start.74 = (bf16[2,4,4,64,128]{4,3,2,1,0:T(8,128)(2,1)S(1)}, bf16[2,4,4,64,128]{4,3,2,1,0:T(8,128)(2,1)S(1)}, u32[]{:S(2)}, u32[]{:S(2)}) collective-permute-start(bf16[2,4,4,64,128]{4,3,2,1,0:T(8,128)(2,1)S(1)} %mute_receiver.6.refs_0_), channel_id=1, source_target_pairs={{0,16},{16,0},{1,17},{17,1},{2,18},{18,2},{3,19},{19,3},{4,20},{20... | collective-permute-start | bytes 1572872 | tf_op jit(solution)/shard_map/ppermute | solution.py:111
  244.9 16.6 %collective-permute-start.80 = (bf16[2,4,4,64,128]{4,3,2,1,0:T(8,128)(2,1)S(1)}, bf16[2,4,4,64,128]{4,3,2,1,0:T(8,128)(2,1)}, u32[]{:S(2)}, u32[]{:S(2)}) collective-permute-start(bf16[2,4,4,64,128]{4,3,2,1,0:T(8,128)(2,1)S(1)} %mute_receiver.7.refs_1_), channel_id=1, source_target_pairs={{0,16},{16,0},{1,17},{17,1},{2,18},{18,2},{3,19},{19,3},{4,20},{20... | collective-permute-start | bytes 1572872 | tf_op jit(solution)/shard_map/ppermute | solution.py:111
  (24 other events, 142.2 us)

commit v3 on v2

--- a/solution.py
+++ b/solution.py
@@ -455,7 +455,7 @@
 
 
 def mute_receiver_kernel(first, both, last, ids, onset_ref, rows_ref, columns_ref, *refs):
-    near, extra, one, two, three = refs[:5]
+    two, three, one, near, extra = refs[:5]
     pieces = 4
     direct = refs[5 : 5 + pieces]
     outs = refs[5 + pieces :]
@@ -518,13 +518,14 @@
 
 def join_kernel(ids, *refs):
     ins, out_ref, hold = refs[:HALVES], refs[-2], refs[-1]
-    two, one, count, width, lanes = ins[0].shape
+    two, foc_count, count, width, lanes = ins[0].shape
     focal = HALVES * count
+    step = pl.program_id(0)
     for c in range(2):
         for q, ref in enumerate(ins):
             for p in range(count):
                 hold[pl.ds(c * width * focal + q * count + p, width, stride=focal), :] = ref[
-                    c, 0, p
+                    c, step, p
                 ].astype(F32)
     out_ref[...] = hold[...].astype(BF16).reshape(out_ref.shape)
 
@@ -532,7 +533,6 @@
 def join_halves(ids, parts, mask, into=None):
     two, foc_count, count, freq, lanes = parts[0].shape
     focal = HALVES * count
-    spec = pl.BlockSpec((two, 1, count, freq, lanes), lambda g, ids: (0, g, 0, 0, 0))
     extra = [] if into is None else [into]
     return pl.pallas_call(
         join_kernel,
@@ -541,7 +541,7 @@
         grid_spec=pltpu.PrefetchScalarGridSpec(
             num_scalar_prefetch=1,
             grid=(foc_count,),
-            in_specs=[spec] * HALVES + [pl.BlockSpec(memory_space=pl.ANY)] * len(extra),
+            in_specs=[VMEM_SPEC] * HALVES + [pl.BlockSpec(memory_space=pl.ANY)] * len(extra),
             out_specs=pl.BlockSpec(
                 (two, freq, focal, lanes), lambda g, ids: (0, g, 0, ids[0] ^ mask)
             ),
@@ -580,9 +580,13 @@
         return swap(value, "rcv", 2, rcv_count)
 
     direct = [None] * foc_count
-    for k in (2, 3, 1, 0):
-        direct[k] = split_wave(ids, direct_wave, k, foc_count, k in near)
+    direct[2] = split_wave(ids, direct_wave, 2, foc_count, False)
     rows, columns = basis(ids)
+    later, rows, columns = lax.optimization_barrier((ids, rows, columns))
+    direct[3] = split_wave(later, direct_wave, 3, foc_count, False)
+    later, direct[3] = lax.optimization_barrier((ids, direct[3]))
+    direct[1] = split_wave(later, direct_wave, 1, foc_count, True)
+    direct[0] = split_wave(later, direct_wave, 0, foc_count, True)
     plan, arrays = [("both", 0, 0)], [direct[0]]
     for k in (2, 3, 1):
         got = to_foc(direct[k], k)
@@ -591,7 +595,6 @@
         else:
             plan = plan + [("own", k, 0), ("other", k, 0)]
             arrays = arrays + [got, to_src(got)]
-    arrays[0], rows, columns = lax.optimization_barrier((arrays[0], rows, columns))
     for iteration in range(ITERS):
         last = iteration == ITERS - 1
         keep, send = convolve_pieces(ids, reflection, tuple(plan), arrays, foc_count, focal)
@@ -605,28 +608,39 @@
         groups = [mine, [to_core(v) for v in mine], across, [to_core(v) for v in across]]
         own, other = correlate_pieces(ids, reflection, groups)
         renewed = []
+        early = []
         plan, arrays = [], []
         count = focal // HALVES
         for q in range(HALVES):
             far, close = 2 * q, 2 * q + 1
             got_far, got_close = to_src(other[far]), to_src(other[close])
+            if q == 1:
+                got_close, fresh = lax.optimization_barrier((got_close, fresh))
             ready = (
+                to_foc(add(own[far][0], got_far[0]), 2),
+                to_foc(add(own[far][1], got_far[1]), 3),
+                to_foc(add(own[close][0], got_close[0]), 1),
                 own[close],
                 got_close,
-                to_foc(add(own[close][0], got_close[0]), 1),
-                to_foc(add(own[far][0], got_far[0]), 2),
-                to_foc(add(own[far][1], got_far[1]), 3),
-            )
+            )
+            if q == 1:
+                ready, early = lax.optimization_barrier((ready, early))
             fresh = mute_receiver(
                 ids, onset_receiver, rows, columns, ready, direct, q * count, near, last
             )
             if last:
                 renewed.append(fresh)
                 continue
-            for k in (2, 3, 1, 0):
-                value = to_foc(fresh[k], k)
-                plan += [("own", k, q * count), ("other", k, q * count)]
-                arrays += [value, to_src(value)]
+            moved = [to_foc(fresh[k], k) for k in (2, 3, 1, 0)]
+            if q == 0 and not last:
+                before, early = moved, [to_src(moved[3])]
+                continue
+            before[:2], moved[2] = lax.optimization_barrier((before[:2], moved[2]))
+            crossed = [to_src(before[0]), to_src(before[1]), to_src(before[2])] + early
+            after = [to_src(moved[3]), to_src(moved[2])]
+            after = [to_src(moved[0]), to_src(moved[1]), after[1], after[0]]
+            arrays = before + crossed + moved + after
+            plan = [(kind, k, start * count) for start in range(2) for kind in ("own", "other") for k in (2, 3, 1, 0)]
         if last:
             crossed = [to_src(value) for value in renewed]
             mine = returned[-1]

time: 266 us -> 255 us (0.959)
  waiting for transfers between devices: 130 us -> 117 us
  starting transfers between devices: 83.3 us -> 86.6 us
    ppermute x84, waiting for transfers between devices: 130 us -> 117 us  [swap(): return lax.ppermute(value, axis, [(i, i ^ mask) for i in range(count)])]
    ppermute x84, starting transfers between devices: 83.3 us -> 86.6 us  [swap(): return lax.ppermute(value, axis, [(i, i ^ mask) for i in range(count)])]
  transfers between devices with their start and end apart: 84 -> 84, of which waited for: 44 -> 41; matrix products, arithmetic and copies ran while one was open for 0% -> 0% of each run, Pallas kernels for 9% -> 10%
where the time goes in v3:
time: 255 us
  waiting for transfers between devices  117 us (46%)
  starting transfers between devices  86.6 us (34%)
  Pallas kernels  47.8 us (19%)
    ppermute x84, waiting for transfers between devices, swap(): return lax.ppermute(value, axis, [(i, i ^ mask) for i in range(count)])  117 us
    ppermute x84, starting transfers between devices, swap(): return lax.ppermute(value, axis, [(i, i ^ mask) for i in range(count)])  86.6 us
    pallas_call x11, Pallas kernels, call(): pl.pallas_call(kernel, name=name, out_shape=out_shape, in_specs=[SMEM_SPE...  32.5 us
    pallas_call x1, Pallas kernels, trace_source(): pl.pallas_call(trace_kernel, name='trace_source', out_shape=jax.ShapeDtyp...  6.28 us
    pallas_call x2, Pallas kernels, join_halves(): pl.pallas_call(join_kernel, name='join_halves', out_shape=jax.ShapeDtypeS...  5.85 us
  transfers between devices with their start and end apart: 84, of which 41 were waited for; matrix products, arithmetic and copies ran while one was open for 0% of the time, Pallas kernels for 10%

profile of v3, /device:TPU:0, one launch (start us, length us, event | category | flops | bytes accessed | tf_op | source)
XLA Modules:
  0.0 254.8 jit_solution(15423997094473088696)
XLA Ops:
  0.7 1.6 copy-done.1
  3.1 4.1 %collective-permute-start = (bf16[2,8,64,128]{3,2,1,0:T(8,128)(2,1)S(1)}, bf16[2,8,64,128]{3,2,1,0:T(8,128)(2,1)S(1)}, u32[]{:S(2)}, u32[]{:S(2)}) collective-permute-start(bf16[2,8,64,128]{3,2,1,0:T(8,128)(2,1)S(1)} %split_wave.6.refs_7_), channel_id=1, source_target_pairs={{0,2},{1,3},{2,0},{3,1},{4,6},{5,7},{6,4},{7,5},{8,10},{9,11},{10,... | collective-permute-start | bytes 786440 | tf_op jit(solution)/shard_map/ppermute | solution.py:111
  7.2 4.1 %basis.1 = (bf16[512,1024]{1,0:T(8,128)(2,1)S(1)}, bf16[1024,512]{1,0:T(8,128)(2,1)S(1)}) custom-call(s32[3]{0:T(128)S(1)} %pad_add_fusion.ids), custom_call_target="tpu_custom_call" | custom-call | flops 20971520 | bytes 2097152 | tf_op jit(solution)/shard_map/basis/pallas_call | solution.py:116
  14.7 10.9 %collective-permute-done.refs_1_ = bf16[2,8,64,128]{3,2,1,0:T(8,128)(2,1)S(1)} collective-permute-done((bf16[2,8,64,128]{3,2,1,0:T(8,128)(2,1)S(1)}, bf16[2,8,64,128]{3,2,1,0:T(8,128)(2,1)S(1)}, u32[]{:S(2)}, u32[]{:S(2)}) %collective-permute-start) | collective-permute-done | bytes 262176 | tf_op jit(solution)/shard_map/ppermute | solution.py:111
  25.6 1.8 collective-permute-start.1
  28.5 6.3 %collective-permute-done.1.refs_2_ = bf16[2,8,64,128]{3,2,1,0:T(8,128)(2,1)S(1)} collective-permute-done((bf16[2,8,64,128]{3,2,1,0:T(8,128)(2,1)S(1)}, bf16[2,8,64,128]{3,2,1,0:T(8,128)(2,1)S(1)}, u32[]{:S(2)}, u32[]{:S(2)}) %collective-permute-start.1) | collective-permute-done | bytes 262176 | tf_op jit(solution)/shard_map/ppermute | solution.py:111
  34.8 3.0 %collective-permute-done.3.refs_4_ = bf16[2,8,64,128]{3,2,1,0:T(8,128)(2,1)S(1)} collective-permute-done((bf16[2,8,64,128]{3,2,1,0:T(8,128)(2,1)S(1)}, bf16[2,8,64,128]{3,2,1,0:T(8,128)(2,1)S(1)}, u32[]{:S(2)}, u32[]{:S(2)}) %collective-permute-start.3) | collective-permute-done | bytes 262176 | tf_op jit(solution)/shard_map/ppermute | solution.py:111
  37.9 4.0 %convolve.2 = (bf16[2,4,2,2,64,128]{5,4,3,2,1,0:T(8,128)(2,1)S(1)}, bf16[2,4,2,2,64,128]{5,4,3,2,1,0:T(8,128)(2,1)S(1)}) custom-call(s32[3]{0:T(128)S(1)} %pad_add_fusion.ids, bf16[2,64,128,256]{3,2,1,0:T(8,128)(2,1)S(1)} %copy-done, bf16[2,2,8,64,128]{4,3,2,1,0:T(8,128)(2,1)S(1)} %split_wave.5.refs_0_.refs_5_, ...), custom_call_target="tpu_custom_call" | custom-call | flops 536870912 | bytes 11534336 | tf_op jit(solution)/shard_map/convolve/pallas_call | solution.py:116
  42.0 1.9 collective-permute-done.5
  45.4 7.1 %collective-permute-done.6 = bf16[4,2,2,64,128]{4,3,2,1,0:T(8,128)(2,1)S(1)} collective-permute-done((bf16[4,2,2,64,128]{4,3,2,1,0:T(8,128)(2,1)S(1)}, bf16[4,2,2,64,128]{4,3,2,1,0:T(8,128)(2,1)S(1)}, u32[]{:S(2)}, u32[]{:S(2)}) %collective-permute-start.6) | collective-permute-done | bytes 262176 | tf_op jit(solution)/shard_map/ppermute | solution.py:111
  54.1 3.4 %collective-permute-start.8 = (bf16[2,2,64,128]{3,2,1,0:T(8,128)(2,1)S(1)}, bf16[2,2,64,128]{3,2,1,0:T(8,128)(2,1)S(1)}, u32[]{:S(2)}, u32[]{:S(2)}) collective-permute-start(bf16[2,2,64,128]{3,2,1,0:T(8,128)(2,1)S(1)} %get-tuple-element.135), channel_id=1, source_target_pairs={{0,2},{1,3},{2,0},{3,1},{4,6},{5,7},{6,4},{7,5},{8,10},{9,11},{10,... | collective-permute-start | bytes 196616 | tf_op jit(solution)/shard_map/ppermute | solution.py:111
  57.5 4.1 %collective-permute-done.8.refs_2_ = bf16[2,2,64,128]{3,2,1,0:T(8,128)(2,1)S(1)} collective-permute-done((bf16[2,2,64,128]{3,2,1,0:T(8,128)(2,1)S(1)}, bf16[2,2,64,128]{3,2,1,0:T(8,128)(2,1)S(1)}, u32[]{:S(2)}, u32[]{:S(2)}) %collective-permute-start.8) | collective-permute-done | bytes 65568 | tf_op jit(solution)/shard_map/ppermute | solution.py:111
  61.6 1.9 collective-permute-done.9.refs_3_
  63.5 1.7 mute_source.2
  65.3 1.9 collective-permute-start.11
  67.2 2.4 collective-permute-start.12
  69.7 1.5 collective-permute-start.17
  71.7 1.6 collective-permute-done.12.refs_3_
  75.4 1.5 collective-permute-start.20
  81.1 3.9 %correlate.2 = (bf16[2,2,4,64,128]{4,3,2,1,0:T(8,128)(2,1)S(1)}, bf16[2,2,4,64,128]{4,3,2,1,0:T(8,128)(2,1)S(1)}, bf16[2,2,4,64,128]{4,3,2,1,0:T(8,128)(2,1)S(1)...) custom-call(s32[3]{0:T(128)S(1)} %pad_add_fusion.ids, ...), custom_call_target="tpu_custom_call" | custom-call | flops 536870912 | bytes 11534336 | tf_op jit(solution)/shard_map/correlate/pallas_call | solution.py:116
  85.0 1.6 collective-permute-start.25
  89.2 5.1 %collective-permute-done.25 = bf16[2,2,4,64,128]{4,3,2,1,0:T(8,128)(2,1)S(1)} collective-permute-done((bf16[2,2,4,64,128]{4,3,2,1,0:T(8,128)(2,1)S(1)}, bf16[2,2,4,64,128]{4,3,2,1,0:T(8,128)(2,1)S(1)}, u32[]{:S(2)}, u32[]{:S(2)}) %collective-permute-start.25) | collective-permute-done | bytes 262176 | tf_op jit(solution)/shard_map/ppermute | solution.py:111
  94.9 2.3 collective-permute-start.27
  97.2 2.7 %collective-permute-done.28.refs_4_ = bf16[2,2,4,64,128]{4,3,2,1,0:T(8,128)(2,1)S(1)} collective-permute-done((bf16[2,2,4,64,128]{4,3,2,1,0:T(8,128)(2,1)S(1)}, bf16[2,2,4,64,128]{4,3,2,1,0:T(8,128)(2,1)S(1)}, u32[]{:S(2)}, u32[]{:S(2)}) %collective-permute-start.28) | collective-permute-done | bytes 262176 | tf_op jit(solution)/shard_map/ppermute | solution.py:111
  100.4 5.1 %collective-permute-done.32 = bf16[2,2,4,64,128]{4,3,2,1,0:T(8,128)(2,1)S(1)} collective-permute-done((bf16[2,2,4,64,128]{4,3,2,1,0:T(8,128)(2,1)S(1)}, bf16[2,2,4,64,128]{4,3,2,1,0:T(8,128)(2,1)S(1)}, u32[]{:S(2)}, u32[]{:S(2)}) %collective-permute-start.32) | collective-permute-done | bytes 262176 | tf_op jit(solution)/shard_map/ppermute | solution.py:111
  106.2 2.3 collective-permute-start.34
  108.5 2.3 mute_receiver.4
  114.4 1.9 collective-permute-done.33.refs_0_
  116.3 2.1 collective-permute-start.31
  118.9 2.2 mute_receiver.5
  126.0 3.1 %collective-permute-done.30.refs_0_ = bf16[2,4,64,128]{3,2,1,0:T(8,128)(2,1)S(1)} collective-permute-done((bf16[2,4,64,128]{3,2,1,0:T(8,128)(2,1)S(1)}, bf16[2,4,64,128]{3,2,1,0:T(8,128)(2,1)S(1)}, u32[]{:S(2)}, u32[]{:S(2)}) %collective-permute-start.30) | collective-permute-done | bytes 131104 | tf_op jit(solution)/shard_map/ppermute | solution.py:111
  129.1 2.0 collective-permute-start.44
  134.5 4.8 %collective-permute-done.43.refs_8_ = bf16[2,4,64,128]{3,2,1,0:T(8,128)(2,1)S(1)} collective-permute-done((bf16[2,4,64,128]{3,2,1,0:T(8,128)(2,1)S(1)}, bf16[2,4,64,128]{3,2,1,0:T(8,128)(2,1)S(1)}, u32[]{:S(2)}, u32[]{:S(2)}) %collective-permute-start.43) | collective-permute-done | bytes 131104 | tf_op jit(solution)/shard_map/ppermute | solution.py:111
  142.4 3.3 %collective-permute-done.45.refs_12_ = bf16[2,4,64,128]{3,2,1,0:T(8,128)(2,1)S(1)} collective-permute-done((bf16[2,4,64,128]{3,2,1,0:T(8,128)(2,1)S(1)}, bf16[2,4,64,128]{3,2,1,0:T(8,128)(2,1)S(1)}, u32[]{:S(2)}, u32[]{:S(2)}) %collective-permute-start.45) | collective-permute-done | bytes 131104 | tf_op jit(solution)/shard_map/ppermute | solution.py:111
  145.6 2.2 collective-permute-done.46.refs_13_
  149.3 4.0 %convolve.3 = (bf16[2,4,2,2,64,128]{5,4,3,2,1,0:T(8,128)(2,1)S(1)}, bf16[2,4,2,2,64,128]{5,4,3,2,1,0:T(8,128)(2,1)S(1)}) custom-call(s32[3]{0:T(128)S(1)} %pad_add_fusion.ids, bf16[2,64,128,256]{3,2,1,0:T(8,128)(2,1)S(1)} %copy-done, bf16[2,4,64,128]{3,2,1,0:T(8,128)(2,1)S(1)} %collective-permute-done.30.refs_0_, ...), custom_call_target="tpu_custom_call" | custom-call | flops 536870912 | bytes 11534336 | tf_op jit(solution)/shard_map/convolve/pallas_call | solution.py:116
  153.4 1.9 collective-permute-done.49
  156.5 7.2 %collective-permute-done.50 = bf16[4,2,2,64,128]{4,3,2,1,0:T(8,128)(2,1)S(1)} collective-permute-done((bf16[4,2,2,64,128]{4,3,2,1,0:T(8,128)(2,1)S(1)}, bf16[4,2,2,64,128]{4,3,2,1,0:T(8,128)(2,1)S(1)}, u32[]{:S(2)}, u32[]{:S(2)}) %collective-permute-start.50) | collective-permute-done | bytes 262176 | tf_op jit(solution)/shard_map/ppermute | solution.py:111
  163.9 6.2 %collective-permute-start.51 = (bf16[2,2,64,128]{3,2,1,0:T(8,128)(2,1)S(1)}, bf16[2,2,64,128]{3,2,1,0:T(8,128)(2,1)S(1)}, u32[]{:S(2)}, u32[]{:S(2)}) collective-permute-start(bf16[2,2,64,128]{3,2,1,0:T(8,128)(2,1)S(1)} %get-tuple-element.132), channel_id=1, source_target_pairs={{0,1},{1,0},{2,3},{3,2},{4,5},{5,4},{6,7},{7,6},{8,9},{9,8},{10,11... | collective-permute-start | bytes 196616 | tf_op jit(solution)/shard_map/ppermute | solution.py:111
  170.2 2.4 collective-permute-start.53
  172.6 4.6 %collective-permute-done.52.refs_2_ = bf16[2,2,64,128]{3,2,1,0:T(8,128)(2,1)S(1)} collective-permute-done((bf16[2,2,64,128]{3,2,1,0:T(8,128)(2,1)S(1)}, bf16[2,2,64,128]{3,2,1,0:T(8,128)(2,1)S(1)}, u32[]{:S(2)}, u32[]{:S(2)}) %collective-permute-start.52) | collective-permute-done | bytes 65568 | tf_op jit(solution)/shard_map/ppermute | solution.py:111
  177.2 1.7 mute_source.3
  178.9 1.6 collective-permute-start.54
  181.1 2.3 collective-permute-start.56
  184.2 3.8 %collective-permute-done.55.refs_2_ = bf16[2,2,64,128]{3,2,1,0:T(8,128)(2,1)S(1)} collective-permute-done((bf16[2,2,64,128]{3,2,1,0:T(8,128)(2,1)S(1)}, bf16[2,2,64,128]{3,2,1,0:T(8,128)(2,1)S(1)}, u32[]{:S(2)}, u32[]{:S(2)}) %collective-permute-start.55) | collective-permute-done | bytes 65568 | tf_op jit(solution)/shard_map/ppermute | solution.py:111
  191.2 1.7 collective-permute-done.62.refs_9_
  196.6 4.0 %correlate.3 = (bf16[2,2,4,64,128]{4,3,2,1,0:T(8,128)(2,1)S(1)}, bf16[2,2,4,64,128]{4,3,2,1,0:T(8,128)(2,1)S(1)}, bf16[2,2,4,64,128]{4,3,2,1,0:T(8,128)(2,1)S(1)...) custom-call(s32[3]{0:T(128)S(1)} %pad_add_fusion.ids, ...), custom_call_target="tpu_custom_call" | custom-call | flops 536870912 | bytes 11534336 | tf_op jit(solution)/shard_map/correlate/pallas_call | solution.py:116
  200.6 1.8 collective-permute-start.69
  202.6 1.7 collective-permute-start.75
  204.7 5.1 %collective-permute-done.69 = bf16[2,2,4,64,128]{4,3,2,1,0:T(8,128)(2,1)S(1)} collective-permute-done((bf16[2,2,4,64,128]{4,3,2,1,0:T(8,128)(2,1)S(1)}, bf16[2,2,4,64,128]{4,3,2,1,0:T(8,128)(2,1)S(1)}, u32[]{:S(2)}, u32[]{:S(2)}) %collective-permute-start.69) | collective-permute-done | bytes 262176 | tf_op jit(solution)/shard_map/ppermute | solution.py:111
  210.1 2.4 collective-permute-start.71
  212.5 2.9 %collective-permute-done.72.refs_4_ = bf16[2,2,4,64,128]{4,3,2,1,0:T(8,128)(2,1)S(1)} collective-permute-done((bf16[2,2,4,64,128]{4,3,2,1,0:T(8,128)(2,1)S(1)}, bf16[2,2,4,64,128]{4,3,2,1,0:T(8,128)(2,1)S(1)}, u32[]{:S(2)}, u32[]{:S(2)}) %collective-permute-start.72) | collective-permute-done | bytes 262176 | tf_op jit(solution)/shard_map/ppermute | solution.py:111
  215.7 5.3 %collective-permute-done.75 = bf16[2,2,4,64,128]{4,3,2,1,0:T(8,128)(2,1)S(1)} collective-permute-done((bf16[2,2,4,64,128]{4,3,2,1,0:T(8,128)(2,1)S(1)}, bf16[2,2,4,64,128]{4,3,2,1,0:T(8,128)(2,1)S(1)}, u32[]{:S(2)}, u32[]{:S(2)}) %collective-permute-start.75) | collective-permute-done | bytes 262176 | tf_op jit(solution)/shard_map/ppermute | solution.py:111
  221.4 2.4 collective-permute-start.77
  223.8 2.2 mute_receiver.6.refs_0_
  227.7 1.6 collective-permute-start.74
  229.3 2.3 collective-permute-done.76.refs_0_
  231.6 2.6 %collective-permute-done.79.refs_2_ = bf16[2,4,64,128]{3,2,1,0:T(8,128)(2,1)S(1)} collective-permute-done((bf16[2,4,64,128]{3,2,1,0:T(8,128)(2,1)S(1)}, bf16[2,4,64,128]{3,2,1,0:T(8,128)(2,1)S(1)}, u32[]{:S(2)}, u32[]{:S(2)}) %collective-permute-start.79) | collective-permute-done | bytes 131104 | tf_op jit(solution)/shard_map/ppermute | solution.py:111
  234.2 2.2 mute_receiver.7.refs_1_
  236.4 1.8 collective-permute-start.80
  240.4 6.3 %trace_source.1 = bf16[8,128,1024]{2,1,0:T(8,128)(2,1)} custom-call(s32[3]{0:T(128)S(1)} %pad_add_fusion.ids, s32[8,128,1]{2,1,0:T(8,128)S(1)} %copy.7.onset_ref, bf16[512,1024]{1,0:T(8,128)(2,1)S(1)} %get-tuple-element.64.rows_ref, bf16[4,2,2,64,128]{4,3,2,1,0:T(8,128)(2,1)S(1)} %get-tuple-element.121.refs_0_, ...), custom_call_target="tpu_custom_call" | custom-call | flops 1073741824 | bytes 5242880 | tf_op jit(solution)/shard_map/trace_source/pallas_call | solution.py:440
  246.7 2.4 join_halves.2.refs_2_
  249.1 2.2 collective-permute-done.80.refs_1_
  251.3 3.4 %join_halves.3 = bf16[2,256,8,256]{3,2,1,0:T(8,128)(2,1)} custom-call(s32[3]{0:T(128)S(1)} %pad_add_fusion.ids, bf16[2,4,4,64,128]{4,3,2,1,0:T(8,128)(2,1)S(1)} %collective-permute-done.74.refs_0_, bf16[2,4,4,64,128]{4,3,2,1,0:T(8,128)(2,1)} %collective-permute-done.80.refs_1_, ...), custom_call_target="tpu_custom_call", output_to_operand_aliasing={{}: (3, {})} | custom-call | bytes 2097152 | tf_op jit(solution)/shard_map/join_halves/pallas_call | solution.py:537
  (146 shorter events, 52.0 us)
Async XLA Ops:
  3.1 22.5 %collective-permute-start = (bf16[2,8,64,128]{3,2,1,0:T(8,128)(2,1)S(1)}, bf16[2,8,64,128]{3,2,1,0:T(8,128)(2,1)S(1)}, u32[]{:S(2)}, u32[]{:S(2)}) collective-permute-start(bf16[2,8,64,128]{3,2,1,0:T(8,128)(2,1)S(1)} %split_wave.6.refs_7_), channel_id=1, source_target_pairs={{0,2},{1,3},{2,0},{3,1},{4,6},{5,7},{6,4},{7,5},{8,10},{9,11},{10,... | collective-permute-start | bytes 786440 | tf_op jit(solution)/shard_map/ppermute | solution.py:111
  12.1 15.3 %collective-permute-start.2 = (bf16[2,8,64,128]{3,2,1,0:T(8,128)(2,1)S(1)}, bf16[2,8,64,128]{3,2,1,0:T(8,128)(2,1)S(1)}, u32[]{:S(2)}, u32[]{:S(2)}) collective-permute-start(bf16[2,8,64,128]{3,2,1,0:T(8,128)(2,1)S(1)} %split_wave.4.refs_8_), channel_id=1, source_target_pairs={{0,3},{1,2},{2,1},{3,0},{4,7},{5,6},{6,5},{7,4},{8,11},{9,10},{10,... | collective-permute-start | bytes 786440 | tf_op jit(solution)/shard_map/ppermute | solution.py:111
  14.4 23.5 %collective-permute-start.4 = (bf16[2,2,8,64,128]{4,3,2,1,0:T(8,128)(2,1)S(1)}, bf16[2,2,8,64,128]{4,3,2,1,0:T(8,128)(2,1)S(1)}, u32[]{:S(2)}, u32[]{:S(2)}) collective-permute-start(bf16[2,2,8,64,128]{4,3,2,1,0:T(8,128)(2,1)S(1)} %split_wave.7.refs_6_), channel_id=1, source_target_pairs={{0,1},{1,0},{2,3},{3,2},{4,5},{5,4},{6,7},{7,6},{8,9},{9,8},{10,11... | collective-permute-start | bytes 1572872 | tf_op jit(solution)/shard_map/ppermute | solution.py:111
  25.6 9.2 %collective-permute-start.1 = (bf16[2,8,64,128]{3,2,1,0:T(8,128)(2,1)S(1)}, bf16[2,8,64,128]{3,2,1,0:T(8,128)(2,1)S(1)}, u32[]{:S(2)}, u32[]{:S(2)}) collective-permute-start(bf16[2,8,64,128]{3,2,1,0:T(8,128)(2,1)S(1)} %collective-permute-done.refs_1_), channel_id=1, source_target_pairs={{0,16},{16,0},{1,17},{17,1},{2,18},{18,2},{3,19},{19,3},{4,20},{20... | collective-permute-start | bytes 786440 | tf_op jit(solution)/shard_map/ppermute | solution.py:111
  27.4 10.4 %collective-permute-start.3 = (bf16[2,8,64,128]{3,2,1,0:T(8,128)(2,1)S(1)}, bf16[2,8,64,128]{3,2,1,0:T(8,128)(2,1)S(1)}, u32[]{:S(2)}, u32[]{:S(2)}) collective-permute-start(bf16[2,8,64,128]{3,2,1,0:T(8,128)(2,1)S(1)} %collective-permute-done.2.refs_3_), channel_id=1, source_target_pairs={{0,16},{16,0},{1,17},{17,1},{2,18},{18,2},{3,19},{19,3},{4,20},{20... | collective-permute-start | bytes 786440 | tf_op jit(solution)/shard_map/ppermute | solution.py:111
  44.0 8.4 %collective-permute-start.6 = (bf16[4,2,2,64,128]{4,3,2,1,0:T(8,128)(2,1)S(1)}, bf16[4,2,2,64,128]{4,3,2,1,0:T(8,128)(2,1)S(1)}, u32[]{:S(2)}, u32[]{:S(2)}) collective-permute-start(bf16[4,2,2,64,128]{4,3,2,1,0:T(8,128)(2,1)S(1)} %fusion.2), channel_id=1, source_target_pairs={{0,8},{4,12},{8,0},{12,4},{1,9},{5,13},{9,1},{13,5},{2,10},{6,14},... | collective-permute-start | bytes 786440 | tf_op jit(solution)/shard_map/ppermute | solution.py:111
  54.1 7.5 %collective-permute-start.8 = (bf16[2,2,64,128]{3,2,1,0:T(8,128)(2,1)S(1)}, bf16[2,2,64,128]{3,2,1,0:T(8,128)(2,1)S(1)}, u32[]{:S(2)}, u32[]{:S(2)}) collective-permute-start(bf16[2,2,64,128]{3,2,1,0:T(8,128)(2,1)S(1)} %get-tuple-element.135), channel_id=1, source_target_pairs={{0,2},{1,3},{2,0},{3,1},{4,6},{5,7},{6,4},{7,5},{8,10},{9,11},{10,... | collective-permute-start | bytes 196616 | tf_op jit(solution)/shard_map/ppermute | solution.py:111
  57.5 6.1 %collective-permute-start.9 = (bf16[2,2,64,128]{3,2,1,0:T(8,128)(2,1)S(1)}, bf16[2,2,64,128]{3,2,1,0:T(8,128)(2,1)S(1)}, u32[]{:S(2)}, u32[]{:S(2)}) collective-permute-start(bf16[2,2,64,128]{3,2,1,0:T(8,128)(2,1)S(1)} %get-tuple-element.134), channel_id=1, source_target_pairs={{0,3},{1,2},{2,1},{3,0},{4,7},{5,6},{6,5},{7,4},{8,11},{9,10},{10,... | collective-permute-start | bytes 196616 | tf_op jit(solution)/shard_map/ppermute | solution.py:111
  65.2 6.0 %collective-permute-start.10 = (bf16[2,2,64,128]{3,2,1,0:T(8,128)(2,1)S(1)}, bf16[2,2,64,128]{3,2,1,0:T(8,128)(2,1)S(1)}, u32[]{:S(2)}, u32[]{:S(2)}) collective-permute-start(bf16[2,2,64,128]{3,2,1,0:T(8,128)(2,1)S(1)} %get-tuple-element.72), channel_id=1, source_target_pairs={{0,1},{1,0},{2,3},{3,2},{4,5},{5,4},{6,7},{7,6},{8,9},{9,8},{10,11... | collective-permute-start | bytes 196616 | tf_op jit(solution)/shard_map/ppermute | solution.py:111
  65.3 6.1 %collective-permute-start.11 = (bf16[2,2,64,128]{3,2,1,0:T(8,128)(2,1)S(1)}, bf16[2,2,64,128]{3,2,1,0:T(8,128)(2,1)S(1)}, u32[]{:S(2)}, u32[]{:S(2)}) collective-permute-start(bf16[2,2,64,128]{3,2,1,0:T(8,128)(2,1)S(1)} %get-tuple-element.73), channel_id=1, source_target_pairs={{0,2},{1,3},{2,0},{3,1},{4,6},{5,7},{6,4},{7,5},{8,10},{9,11},{10,... | collective-permute-start | bytes 196616 | tf_op jit(solution)/shard_map/ppermute | solution.py:111
  67.2 6.1 %collective-permute-start.12 = (bf16[2,2,64,128]{3,2,1,0:T(8,128)(2,1)S(1)}, bf16[2,2,64,128]{3,2,1,0:T(8,128)(2,1)S(1)}, u32[]{:S(2)}, u32[]{:S(2)}) collective-permute-start(bf16[2,2,64,128]{3,2,1,0:T(8,128)(2,1)S(1)} %get-tuple-element.74), channel_id=1, source_target_pairs={{0,3},{1,2},{2,1},{3,0},{4,7},{5,6},{6,5},{7,4},{8,11},{9,10},{10,... | collective-permute-start | bytes 196616 | tf_op jit(solution)/shard_map/ppermute | solution.py:111
  69.7 5.2 %collective-permute-start.13 = (bf16[2,2,64,128]{3,2,1,0:T(8,128)(2,1)S(1)}, bf16[2,2,64,128]{3,2,1,0:T(8,128)(2,1)S(1)}, u32[]{:S(2)}, u32[]{:S(2)}) collective-permute-start(bf16[2,2,64,128]{3,2,1,0:T(8,128)(2,1)S(1)} %get-tuple-element.71.refs_0_), channel_id=1, source_target_pairs={{0,4},{4,0},{8,12},{12,8},{1,5},{5,1},{9,13},{13,9},{2,6},{6,2},{1... | collective-permute-start | bytes 196616 | tf_op jit(solution)/shard_map/ppermute | solution.py:111
  69.7 5.7 %collective-permute-start.17 = (bf16[2,2,64,128]{3,2,1,0:T(8,128)(2,1)S(1)}, bf16[2,2,64,128]{3,2,1,0:T(8,128)(2,1)S(1)}, u32[]{:S(2)}, u32[]{:S(2)}) collective-permute-start(bf16[2,2,64,128]{3,2,1,0:T(8,128)(2,1)S(1)} %get-tuple-element.71.refs_0_), channel_id=1, source_target_pairs={{0,8},{4,12},{8,0},{12,4},{1,9},{5,13},{9,1},{13,5},{2,10},{6,14},... | collective-permute-start | bytes 196616 | tf_op jit(solution)/shard_map/ppermute | solution.py:111
  71.2 5.7 %collective-permute-start.14 = (bf16[2,2,64,128]{3,2,1,0:T(8,128)(2,1)S(1)}, bf16[2,2,64,128]{3,2,1,0:T(8,128)(2,1)S(1)}, u32[]{:S(2)}, u32[]{:S(2)}) collective-permute-start(bf16[2,2,64,128]{3,2,1,0:T(8,128)(2,1)S(1)} %collective-permute-done.10.refs_1_), channel_id=1, source_target_pairs={{0,4},{4,0},{8,12},{12,8},{1,5},{5,1},{9,13},{13,9},{2,6},{6,2},{1... | collective-permute-start | bytes 196616 | tf_op jit(solution)/shard_map/ppermute | solution.py:111
  71.5 5.4 %collective-permute-start.15 = (bf16[2,2,64,128]{3,2,1,0:T(8,128)(2,1)S(1)}, bf16[2,2,64,128]{3,2,1,0:T(8,128)(2,1)S(1)}, u32[]{:S(2)}, u32[]{:S(2)}) collective-permute-start(bf16[2,2,64,128]{3,2,1,0:T(8,128)(2,1)S(1)} %collective-permute-done.11.refs_2_), channel_id=1, source_target_pairs={{0,4},{4,0},{8,12},{12,8},{1,5},{5,1},{9,13},{13,9},{2,6},{6,2},{1... | collective-permute-start | bytes 196616 | tf_op jit(solution)/shard_map/ppermute | solution.py:111
  85.0 9.2 %collective-permute-start.25 = (bf16[2,2,4,64,128]{4,3,2,1,0:T(8,128)(2,1)S(1)}, bf16[2,2,4,64,128]{4,3,2,1,0:T(8,128)(2,1)S(1)}, u32[]{:S(2)}, u32[]{:S(2)}) collective-permute-start(bf16[2,2,4,64,128]{4,3,2,1,0:T(8,128)(2,1)S(1)} %get-tuple-element.76), channel_id=1, source_target_pairs={{0,16},{16,0},{1,17},{17,1},{2,18},{18,2},{3,19},{19,3},{4,20},{20... | collective-permute-start | bytes 786440 | tf_op jit(solution)/shard_map/ppermute | solution.py:111
  86.6 13.3 %collective-permute-start.28 = (bf16[2,2,4,64,128]{4,3,2,1,0:T(8,128)(2,1)S(1)}, bf16[2,2,4,64,128]{4,3,2,1,0:T(8,128)(2,1)S(1)}, u32[]{:S(2)}, u32[]{:S(2)}) collective-permute-start(bf16[2,2,4,64,128]{4,3,2,1,0:T(8,128)(2,1)S(1)} %get-tuple-element.78), channel_id=1, source_target_pairs={{0,16},{16,0},{1,17},{17,1},{2,18},{18,2},{3,19},{19,3},{4,20},{20... | collective-permute-start | bytes 786440 | tf_op jit(solution)/shard_map/ppermute | solution.py:111
  87.1 18.4 %collective-permute-start.32 = (bf16[2,2,4,64,128]{4,3,2,1,0:T(8,128)(2,1)S(1)}, bf16[2,2,4,64,128]{4,3,2,1,0:T(8,128)(2,1)S(1)}, u32[]{:S(2)}, u32[]{:S(2)}) collective-permute-start(bf16[2,2,4,64,128]{4,3,2,1,0:T(8,128)(2,1)S(1)} %get-tuple-element.82), channel_id=1, source_target_pairs={{0,16},{16,0},{1,17},{17,1},{2,18},{18,2},{3,19},{19,3},{4,20},{20... | collective-permute-start | bytes 786440 | tf_op jit(solution)/shard_map/ppermute | solution.py:111
  88.6 22.1 %collective-permute-start.35 = (bf16[2,2,4,64,128]{4,3,2,1,0:T(8,128)(2,1)S(1)}, bf16[2,2,4,64,128]{4,3,2,1,0:T(8,128)(2,1)S(1)}, u32[]{:S(2)}, u32[]{:S(2)}) collective-permute-start(bf16[2,2,4,64,128]{4,3,2,1,0:T(8,128)(2,1)S(1)} %get-tuple-element.84), channel_id=1, source_target_pairs={{0,16},{16,0},{1,17},{17,1},{2,18},{18,2},{3,19},{19,3},{4,20},{20... | collective-permute-start | bytes 786440 | tf_op jit(solution)/shard_map/ppermute | solution.py:111
  94.3 11.8 %collective-permute-start.26 = (bf16[2,4,64,128]{3,2,1,0:T(8,128)(2,1)S(1)}, bf16[2,4,64,128]{3,2,1,0:T(8,128)(2,1)S(1)}, u32[]{:S(2)}, u32[]{:S(2)}) collective-permute-start(bf16[2,4,64,128]{3,2,1,0:T(8,128)(2,1)S(1)} %get-tuple-element.129), channel_id=1, source_target_pairs={{0,2},{1,3},{2,0},{3,1},{4,6},{5,7},{6,4},{7,5},{8,10},{9,11},{10,... | collective-permute-start | bytes 393224 | tf_op jit(solution)/shard_map/ppermute | solution.py:111
  94.9 13.5 %collective-permute-start.27 = (bf16[2,4,64,128]{3,2,1,0:T(8,128)(2,1)S(1)}, bf16[2,4,64,128]{3,2,1,0:T(8,128)(2,1)S(1)}, u32[]{:S(2)}, u32[]{:S(2)}) collective-permute-start(bf16[2,4,64,128]{3,2,1,0:T(8,128)(2,1)S(1)} %get-tuple-element.128), channel_id=1, source_target_pairs={{0,3},{1,2},{2,1},{3,0},{4,7},{5,6},{6,5},{7,4},{8,11},{9,10},{10,... | collective-permute-start | bytes 393224 | tf_op jit(solution)/shard_map/ppermute | solution.py:111
  99.9 8.5 %collective-permute-start.29 = (bf16[2,4,64,128]{3,2,1,0:T(8,128)(2,1)S(1)}, bf16[2,4,64,128]{3,2,1,0:T(8,128)(2,1)S(1)}, u32[]{:S(2)}, u32[]{:S(2)}) collective-permute-start(bf16[2,4,64,128]{3,2,1,0:T(8,128)(2,1)S(1)} %fusion.6), channel_id=1, source_target_pairs={{0,1},{1,0},{2,3},{3,2},{4,5},{5,4},{6,7},{7,6},{8,9},{9,8},{10,11... | collective-permute-start | bytes 393224 | tf_op jit(solution)/shard_map/ppermute | solution.py:111
  105.6 10.7 %collective-permute-start.33 = (bf16[2,4,64,128]{3,2,1,0:T(8,128)(2,1)S(1)}, bf16[2,4,64,128]{3,2,1,0:T(8,128)(2,1)S(1)}, u32[]{:S(2)}, u32[]{:S(2)}) collective-permute-start(bf16[2,4,64,128]{3,2,1,0:T(8,128)(2,1)S(1)} %get-tuple-element.127), channel_id=1, source_target_pairs={{0,2},{1,3},{2,0},{3,1},{4,6},{5,7},{6,4},{7,5},{8,10},{9,11},{10,... | collective-permute-start | bytes 393224 | tf_op jit(solution)/shard_map/ppermute | solution.py:111
  106.2 10.1 %collective-permute-start.34 = (bf16[2,4,64,128]{3,2,1,0:T(8,128)(2,1)S(1)}, bf16[2,4,64,128]{3,2,1,0:T(8,128)(2,1)S(1)}, u32[]{:S(2)}, u32[]{:S(2)}) collective-permute-start(bf16[2,4,64,128]{3,2,1,0:T(8,128)(2,1)S(1)} %get-tuple-element.126), channel_id=1, source_target_pairs={{0,3},{1,2},{2,1},{3,0},{4,7},{5,6},{6,5},{7,4},{8,11},{9,10},{10,... | collective-permute-start | bytes 393224 | tf_op jit(solution)/shard_map/ppermute | solution.py:111
  110.8 8.1 %collective-permute-start.36 = (bf16[2,4,64,128]{3,2,1,0:T(8,128)(2,1)S(1)}, bf16[2,4,64,128]{3,2,1,0:T(8,128)(2,1)S(1)}, u32[]{:S(2)}, u32[]{:S(2)}) collective-permute-start(bf16[2,4,64,128]{3,2,1,0:T(8,128)(2,1)S(1)} %fusion.9), channel_id=1, source_target_pairs={{0,1},{1,0},{2,3},{3,2},{4,5},{5,4},{6,7},{7,6},{8,9},{9,8},{10,11... | collective-permute-start | bytes 393224 | tf_op jit(solution)/shard_map/ppermute | solution.py:111
  111.5 7.4 %collective-permute-start.37 = (bf16[2,4,64,128]{3,2,1,0:T(8,128)(2,1)S(1)}, bf16[2,4,64,128]{3,2,1,0:T(8,128)(2,1)S(1)}, u32[]{:S(2)}, u32[]{:S(2)}) collective-permute-start(bf16[2,4,64,128]{3,2,1,0:T(8,128)(2,1)S(1)} %get-tuple-element.85.refs_3_), channel_id=1, source_target_pairs={{0,16},{16,0},{1,17},{17,1},{2,18},{18,2},{3,19},{19,3},{4,20},{20... | collective-permute-start | bytes 393224 | tf_op jit(solution)/shard_map/ppermute | solution.py:111
  113.0 10.4 %collective-permute-start.39 = (bf16[2,4,64,128]{3,2,1,0:T(8,128)(2,1)S(1)}, bf16[2,4,64,128]{3,2,1,0:T(8,128)(2,1)S(1)}, u32[]{:S(2)}, u32[]{:S(2)}) collective-permute-start(bf16[2,4,64,128]{3,2,1,0:T(8,128)(2,1)S(1)} %get-tuple-element.86), channel_id=1, source_target_pairs={{0,1},{1,0},{2,3},{3,2},{4,5},{5,4},{6,7},{7,6},{8,9},{9,8},{10,11... | collective-permute-start | bytes 393224 | tf_op jit(solution)/shard_map/ppermute | solution.py:111
  116.3 12.8 %collective-permute-start.30 = (bf16[2,4,64,128]{3,2,1,0:T(8,128)(2,1)S(1)}, bf16[2,4,64,128]{3,2,1,0:T(8,128)(2,1)S(1)}, u32[]{:S(2)}, u32[]{:S(2)}) collective-permute-start(bf16[2,4,64,128]{3,2,1,0:T(8,128)(2,1)S(1)} %get-tuple-element.79), channel_id=1, source_target_pairs={{0,2},{1,3},{2,0},{3,1},{4,6},{5,7},{6,4},{7,5},{8,10},{9,11},{10,... | collective-permute-start | bytes 393224 | tf_op jit(solution)/shard_map/ppermute | solution.py:111
  116.3 14.8 %collective-permute-start.31 = (bf16[2,4,64,128]{3,2,1,0:T(8,128)(2,1)S(1)}, bf16[2,4,64,128]{3,2,1,0:T(8,128)(2,1)S(1)}, u32[]{:S(2)}, u32[]{:S(2)}) collective-permute-start(bf16[2,4,64,128]{3,2,1,0:T(8,128)(2,1)S(1)} %get-tuple-element.80), channel_id=1, source_target_pairs={{0,3},{1,2},{2,1},{3,0},{4,7},{5,6},{6,5},{7,4},{8,11},{9,10},{10,... | collective-permute-start | bytes 393224 | tf_op jit(solution)/shard_map/ppermute | solution.py:111
  121.2 11.2 %collective-permute-start.38 = (bf16[2,4,64,128]{3,2,1,0:T(8,128)(2,1)S(1)}, bf16[2,4,64,128]{3,2,1,0:T(8,128)(2,1)S(1)}, u32[]{:S(2)}, u32[]{:S(2)}) collective-permute-start(bf16[2,4,64,128]{3,2,1,0:T(8,128)(2,1)S(1)} %get-tuple-element.93), channel_id=1, source_target_pairs={{0,1},{1,0},{2,3},{3,2},{4,5},{5,4},{6,7},{7,6},{8,9},{9,8},{10,11... | collective-permute-start | bytes 393224 | tf_op jit(solution)/shard_map/ppermute | solution.py:111
  123.5 9.6 %collective-permute-start.42 = (bf16[2,4,64,128]{3,2,1,0:T(8,128)(2,1)S(1)}, bf16[2,4,64,128]{3,2,1,0:T(8,128)(2,1)S(1)}, u32[]{:S(2)}, u32[]{:S(2)}) collective-permute-start(bf16[2,4,64,128]{3,2,1,0:T(8,128)(2,1)S(1)} %collective-permute-done.39.refs_2_), channel_id=1, source_target_pairs={{0,16},{16,0},{1,17},{17,1},{2,18},{18,2},{3,19},{19,3},{4,20},{20... | collective-permute-start | bytes 393224 | tf_op jit(solution)/shard_map/ppermute | solution.py:111
  124.5 14.9 %collective-permute-start.43 = (bf16[2,4,64,128]{3,2,1,0:T(8,128)(2,1)S(1)}, bf16[2,4,64,128]{3,2,1,0:T(8,128)(2,1)S(1)}, u32[]{:S(2)}, u32[]{:S(2)}) collective-permute-start(bf16[2,4,64,128]{3,2,1,0:T(8,128)(2,1)S(1)} %get-tuple-element.97), channel_id=1, source_target_pairs={{0,2},{1,3},{2,0},{3,1},{4,6},{5,7},{6,4},{7,5},{8,10},{9,11},{10,... | collective-permute-start | bytes 393224 | tf_op jit(solution)/shard_map/ppermute | solution.py:111
  129.1 11.3 %collective-permute-start.44 = (bf16[2,4,64,128]{3,2,1,0:T(8,128)(2,1)S(1)}, bf16[2,4,64,128]{3,2,1,0:T(8,128)(2,1)S(1)}, u32[]{:S(2)}, u32[]{:S(2)}) collective-permute-start(bf16[2,4,64,128]{3,2,1,0:T(8,128)(2,1)S(1)} %get-tuple-element.98), channel_id=1, source_target_pairs={{0,3},{1,2},{2,1},{3,0},{4,7},{5,6},{6,5},{7,4},{8,11},{9,10},{10,... | collective-permute-start | bytes 393224 | tf_op jit(solution)/shard_map/ppermute | solution.py:111
  131.1 10.3 %collective-permute-start.48 = (bf16[2,4,64,128]{3,2,1,0:T(8,128)(2,1)S(1)}, bf16[2,4,64,128]{3,2,1,0:T(8,128)(2,1)S(1)}, u32[]{:S(2)}, u32[]{:S(2)}) collective-permute-start(bf16[2,4,64,128]{3,2,1,0:T(8,128)(2,1)S(1)} %get-tuple-element.100.refs_11_), channel_id=1, source_target_pairs={{0,16},{16,0},{1,17},{17,1},{2,18},{18,2},{3,19},{19,3},{4,20},{20... | collective-permute-start | bytes 393224 | tf_op jit(solution)/shard_map/ppermute | solution.py:111
  132.4 9.9 %collective-permute-start.40 = (bf16[2,4,64,128]{3,2,1,0:T(8,128)(2,1)S(1)}, bf16[2,4,64,128]{3,2,1,0:T(8,128)(2,1)S(1)}, u32[]{:S(2)}, u32[]{:S(2)}) collective-permute-start(bf16[2,4,64,128]{3,2,1,0:T(8,128)(2,1)S(1)} %collective-permute-done.30.refs_0_), channel_id=1, source_target_pairs={{0,16},{16,0},{1,17},{17,1},{2,18},{18,2},{3,19},{19,3},{4,20},{20... | collective-permute-start | bytes 393224 | tf_op jit(solution)/shard_map/ppermute | solution.py:111
  133.1 9.3 %collective-permute-start.41 = (bf16[2,4,64,128]{3,2,1,0:T(8,128)(2,1)S(1)}, bf16[2,4,64,128]{3,2,1,0:T(8,128)(2,1)S(1)}, u32[]{:S(2)}, u32[]{:S(2)}) collective-permute-start(bf16[2,4,64,128]{3,2,1,0:T(8,128)(2,1)S(1)} %collective-permute-done.31.refs_1_), channel_id=1, source_target_pairs={{0,16},{16,0},{1,17},{17,1},{2,18},{18,2},{3,19},{19,3},{4,20},{20... | collective-permute-start | bytes 393224 | tf_op jit(solution)/shard_map/ppermute | solution.py:111
  139.3 6.3 %collective-permute-start.45 = (bf16[2,4,64,128]{3,2,1,0:T(8,128)(2,1)S(1)}, bf16[2,4,64,128]{3,2,1,0:T(8,128)(2,1)S(1)}, u32[]{:S(2)}, u32[]{:S(2)}) collective-permute-start(bf16[2,4,64,128]{3,2,1,0:T(8,128)(2,1)S(1)} %collective-permute-done.43.refs_8_), channel_id=1, source_target_pairs={{0,16},{16,0},{1,17},{17,1},{2,18},{18,2},{3,19},{19,3},{4,20},{20... | collective-permute-start | bytes 393224 | tf_op jit(solution)/shard_map/ppermute | solution.py:111
  140.3 7.5 %collective-permute-start.46 = (bf16[2,4,64,128]{3,2,1,0:T(8,128)(2,1)S(1)}, bf16[2,4,64,128]{3,2,1,0:T(8,128)(2,1)S(1)}, u32[]{:S(2)}, u32[]{:S(2)}) collective-permute-start(bf16[2,4,64,128]{3,2,1,0:T(8,128)(2,1)S(1)} %collective-permute-done.44.refs_9_), channel_id=1, source_target_pairs={{0,16},{16,0},{1,17},{17,1},{2,18},{18,2},{3,19},{19,3},{4,20},{20... | collective-permute-start | bytes 393224 | tf_op jit(solution)/shard_map/ppermute | solution.py:111
  141.4 7.9 %collective-permute-start.47 = (bf16[2,4,64,128]{3,2,1,0:T(8,128)(2,1)S(1)}, bf16[2,4,64,128]{3,2,1,0:T(8,128)(2,1)S(1)}, u32[]{:S(2)}, u32[]{:S(2)}) collective-permute-start(bf16[2,4,64,128]{3,2,1,0:T(8,128)(2,1)S(1)} %collective-permute-done.38.refs_10_), channel_id=1, source_target_pairs={{0,16},{16,0},{1,17},{17,1},{2,18},{18,2},{3,19},{19,3},{4,20},{20... | collective-permute-start | bytes 393224 | tf_op jit(solution)/shard_map/ppermute | solution.py:111
  155.3 8.4 %collective-permute-start.50 = (bf16[4,2,2,64,128]{4,3,2,1,0:T(8,128)(2,1)S(1)}, bf16[4,2,2,64,128]{4,3,2,1,0:T(8,128)(2,1)S(1)}, u32[]{:S(2)}, u32[]{:S(2)}) collective-permute-start(bf16[4,2,2,64,128]{4,3,2,1,0:T(8,128)(2,1)S(1)} %fusion.3), channel_id=1, source_target_pairs={{0,8},{4,12},{8,0},{12,4},{1,9},{5,13},{9,1},{13,5},{2,10},{6,14},... | collective-permute-start | bytes 786440 | tf_op jit(solution)/shard_map/ppermute | solution.py:111
  163.9 8.7 %collective-permute-start.51 = (bf16[2,2,64,128]{3,2,1,0:T(8,128)(2,1)S(1)}, bf16[2,2,64,128]{3,2,1,0:T(8,128)(2,1)S(1)}, u32[]{:S(2)}, u32[]{:S(2)}) collective-permute-start(bf16[2,2,64,128]{3,2,1,0:T(8,128)(2,1)S(1)} %get-tuple-element.132), channel_id=1, source_target_pairs={{0,1},{1,0},{2,3},{3,2},{4,5},{5,4},{6,7},{7,6},{8,9},{9,8},{10,11... | collective-permute-start | bytes 196616 | tf_op jit(solution)/shard_map/ppermute | solution.py:111
  170.2 7.0 %collective-permute-start.52 = (bf16[2,2,64,128]{3,2,1,0:T(8,128)(2,1)S(1)}, bf16[2,2,64,128]{3,2,1,0:T(8,128)(2,1)S(1)}, u32[]{:S(2)}, u32[]{:S(2)}) collective-permute-start(bf16[2,2,64,128]{3,2,1,0:T(8,128)(2,1)S(1)} %get-tuple-element.131), channel_id=1, source_target_pairs={{0,2},{1,3},{2,0},{3,1},{4,6},{5,7},{6,4},{7,5},{8,10},{9,11},{10,... | collective-permute-start | bytes 196616 | tf_op jit(solution)/shard_map/ppermute | solution.py:111
  170.2 7.0 %collective-permute-start.53 = (bf16[2,2,64,128]{3,2,1,0:T(8,128)(2,1)S(1)}, bf16[2,2,64,128]{3,2,1,0:T(8,128)(2,1)S(1)}, u32[]{:S(2)}, u32[]{:S(2)}) collective-permute-start(bf16[2,2,64,128]{3,2,1,0:T(8,128)(2,1)S(1)} %get-tuple-element.130), channel_id=1, source_target_pairs={{0,3},{1,2},{2,1},{3,0},{4,7},{5,6},{6,5},{7,4},{8,11},{9,10},{10,... | collective-permute-start | bytes 196616 | tf_op jit(solution)/shard_map/ppermute | solution.py:111
  178.9 5.1 %collective-permute-start.54 = (bf16[2,2,64,128]{3,2,1,0:T(8,128)(2,1)S(1)}, bf16[2,2,64,128]{3,2,1,0:T(8,128)(2,1)S(1)}, u32[]{:S(2)}, u32[]{:S(2)}) collective-permute-start(bf16[2,2,64,128]{3,2,1,0:T(8,128)(2,1)S(1)} %get-tuple-element.104), channel_id=1, source_target_pairs={{0,1},{1,0},{2,3},{3,2},{4,5},{5,4},{6,7},{7,6},{8,9},{9,8},{10,11... | collective-permute-start | bytes 196616 | tf_op jit(solution)/shard_map/ppermute | solution.py:111
  180.4 7.6 %collective-permute-start.55 = (bf16[2,2,64,128]{3,2,1,0:T(8,128)(2,1)S(1)}, bf16[2,2,64,128]{3,2,1,0:T(8,128)(2,1)S(1)}, u32[]{:S(2)}, u32[]{:S(2)}) collective-permute-start(bf16[2,2,64,128]{3,2,1,0:T(8,128)(2,1)S(1)} %get-tuple-element.105), channel_id=1, source_target_pairs={{0,2},{1,3},{2,0},{3,1},{4,6},{5,7},{6,4},{7,5},{8,10},{9,11},{10,... | collective-permute-start | bytes 196616 | tf_op jit(solution)/shard_map/ppermute | solution.py:111
  181.1 7.0 %collective-permute-start.56 = (bf16[2,2,64,128]{3,2,1,0:T(8,128)(2,1)S(1)}, bf16[2,2,64,128]{3,2,1,0:T(8,128)(2,1)S(1)}, u32[]{:S(2)}, u32[]{:S(2)}) collective-permute-start(bf16[2,2,64,128]{3,2,1,0:T(8,128)(2,1)S(1)} %get-tuple-element.106), channel_id=1, source_target_pairs={{0,3},{1,2},{2,1},{3,0},{4,7},{5,6},{6,5},{7,4},{8,11},{9,10},{10,... | collective-permute-start | bytes 196616 | tf_op jit(solution)/shard_map/ppermute | solution.py:111
  183.3 5.3 %collective-permute-start.57 = (bf16[2,2,64,128]{3,2,1,0:T(8,128)(2,1)S(1)}, bf16[2,2,64,128]{3,2,1,0:T(8,128)(2,1)S(1)}, u32[]{:S(2)}, u32[]{:S(2)}) collective-permute-start(bf16[2,2,64,128]{3,2,1,0:T(8,128)(2,1)S(1)} %get-tuple-element.103.refs_0_), channel_id=1, source_target_pairs={{0,4},{4,0},{8,12},{12,8},{1,5},{5,1},{9,13},{13,9},{2,6},{6,2},{1... | collective-permute-start | bytes 196616 | tf_op jit(solution)/shard_map/ppermute | solution.py:111
  183.3 6.7 %collective-permute-start.61 = (bf16[2,2,64,128]{3,2,1,0:T(8,128)(2,1)S(1)}, bf16[2,2,64,128]{3,2,1,0:T(8,128)(2,1)S(1)}, u32[]{:S(2)}, u32[]{:S(2)}) collective-permute-start(bf16[2,2,64,128]{3,2,1,0:T(8,128)(2,1)S(1)} %get-tuple-element.103.refs_0_), channel_id=1, source_target_pairs={{0,8},{4,12},{8,0},{12,4},{1,9},{5,13},{9,1},{13,5},{2,10},{6,14},... | collective-permute-start | bytes 196616 | tf_op jit(solution)/shard_map/ppermute | solution.py:111
  183.9 6.8 %collective-permute-start.58 = (bf16[2,2,64,128]{3,2,1,0:T(8,128)(2,1)S(1)}, bf16[2,2,64,128]{3,2,1,0:T(8,128)(2,1)S(1)}, u32[]{:S(2)}, u32[]{:S(2)}) collective-permute-start(bf16[2,2,64,128]{3,2,1,0:T(8,128)(2,1)S(1)} %collective-permute-done.54.refs_1_), channel_id=1, source_target_pairs={{0,4},{4,0},{8,12},{12,8},{1,5},{5,1},{9,13},{13,9},{2,6},{6,2},{1... | collective-permute-start | bytes 196616 | tf_op jit(solution)/shard_map/ppermute | solution.py:111
  188.7 5.6 %collective-permute-start.63 = (bf16[2,2,64,128]{3,2,1,0:T(8,128)(2,1)S(1)}, bf16[2,2,64,128]{3,2,1,0:T(8,128)(2,1)S(1)}, u32[]{:S(2)}, u32[]{:S(2)}) collective-permute-start(bf16[2,2,64,128]{3,2,1,0:T(8,128)(2,1)S(1)} %collective-permute-done.55.refs_2_), channel_id=1, source_target_pairs={{0,8},{4,12},{8,0},{12,4},{1,9},{5,13},{9,1},{13,5},{2,10},{6,14},... | collective-permute-start | bytes 196616 | tf_op jit(solution)/shard_map/ppermute | solution.py:111
  190.0 5.3 %collective-permute-start.64 = (bf16[2,2,64,128]{3,2,1,0:T(8,128)(2,1)S(1)}, bf16[2,2,64,128]{3,2,1,0:T(8,128)(2,1)S(1)}, u32[]{:S(2)}, u32[]{:S(2)}) collective-permute-start(bf16[2,2,64,128]{3,2,1,0:T(8,128)(2,1)S(1)} %collective-permute-done.56.refs_3_), channel_id=1, source_target_pairs={{0,8},{4,12},{8,0},{12,4},{1,9},{5,13},{9,1},{13,5},{2,10},{6,14},... | collective-permute-start | bytes 196616 | tf_op jit(solution)/shard_map/ppermute | solution.py:111
  200.6 9.2 %collective-permute-start.69 = (bf16[2,2,4,64,128]{4,3,2,1,0:T(8,128)(2,1)S(1)}, bf16[2,2,4,64,128]{4,3,2,1,0:T(8,128)(2,1)S(1)}, u32[]{:S(2)}, u32[]{:S(2)}) collective-permute-start(bf16[2,2,4,64,128]{4,3,2,1,0:T(8,128)(2,1)S(1)} %get-tuple-element.108), channel_id=1, source_target_pairs={{0,16},{16,0},{1,17},{17,1},{2,18},{18,2},{3,19},{19,3},{4,20},{20... | collective-permute-start | bytes 786440 | tf_op jit(solution)/shard_map/ppermute | solution.py:111
  202.3 13.1 %collective-permute-start.72 = (bf16[2,2,4,64,128]{4,3,2,1,0:T(8,128)(2,1)S(1)}, bf16[2,2,4,64,128]{4,3,2,1,0:T(8,128)(2,1)S(1)}, u32[]{:S(2)}, u32[]{:S(2)}) collective-permute-start(bf16[2,2,4,64,128]{4,3,2,1,0:T(8,128)(2,1)S(1)} %get-tuple-element.110), channel_id=1, source_target_pairs={{0,16},{16,0},{1,17},{17,1},{2,18},{18,2},{3,19},{19,3},{4,20},{20... | collective-permute-start | bytes 786440 | tf_op jit(solution)/shard_map/ppermute | solution.py:111
  202.6 18.4 %collective-permute-start.75 = (bf16[2,2,4,64,128]{4,3,2,1,0:T(8,128)(2,1)S(1)}, bf16[2,2,4,64,128]{4,3,2,1,0:T(8,128)(2,1)S(1)}, u32[]{:S(2)}, u32[]{:S(2)}) collective-permute-start(bf16[2,2,4,64,128]{4,3,2,1,0:T(8,128)(2,1)S(1)} %get-tuple-element.112), channel_id=1, source_target_pairs={{0,16},{16,0},{1,17},{17,1},{2,18},{18,2},{3,19},{19,3},{4,20},{20... | collective-permute-start | bytes 786440 | tf_op jit(solution)/shard_map/ppermute | solution.py:111
  204.3 21.7 %collective-permute-start.78 = (bf16[2,2,4,64,128]{4,3,2,1,0:T(8,128)(2,1)S(1)}, bf16[2,2,4,64,128]{4,3,2,1,0:T(8,128)(2,1)S(1)}, u32[]{:S(2)}, u32[]{:S(2)}) collective-permute-start(bf16[2,2,4,64,128]{4,3,2,1,0:T(8,128)(2,1)S(1)} %get-tuple-element.114), channel_id=1, source_target_pairs={{0,16},{16,0},{1,17},{17,1},{2,18},{18,2},{3,19},{19,3},{4,20},{20... | collective-permute-start | bytes 786440 | tf_op jit(solution)/shard_map/ppermute | solution.py:111
  209.8 11.5 %collective-permute-start.70 = (bf16[2,4,64,128]{3,2,1,0:T(8,128)(2,1)S(1)}, bf16[2,4,64,128]{3,2,1,0:T(8,128)(2,1)S(1)}, u32[]{:S(2)}, u32[]{:S(2)}) collective-permute-start(bf16[2,4,64,128]{3,2,1,0:T(8,128)(2,1)S(1)} %get-tuple-element.125), channel_id=1, source_target_pairs={{0,2},{1,3},{2,0},{3,1},{4,6},{5,7},{6,4},{7,5},{8,10},{9,11},{10,... | collective-permute-start | bytes 393224 | tf_op jit(solution)/shard_map/ppermute | solution.py:111
  210.1 13.6 %collective-permute-start.71 = (bf16[2,4,64,128]{3,2,1,0:T(8,128)(2,1)S(1)}, bf16[2,4,64,128]{3,2,1,0:T(8,128)(2,1)S(1)}, u32[]{:S(2)}, u32[]{:S(2)}) collective-permute-start(bf16[2,4,64,128]{3,2,1,0:T(8,128)(2,1)S(1)} %get-tuple-element.124), channel_id=1, source_target_pairs={{0,3},{1,2},{2,1},{3,0},{4,7},{5,6},{6,5},{7,4},{8,11},{9,10},{10,... | collective-permute-start | bytes 393224 | tf_op jit(solution)/shard_map/ppermute | solution.py:111
  215.4 8.3 %collective-permute-start.73 = (bf16[2,4,64,128]{3,2,1,0:T(8,128)(2,1)S(1)}, bf16[2,4,64,128]{3,2,1,0:T(8,128)(2,1)S(1)}, u32[]{:S(2)}, u32[]{:S(2)}) collective-permute-start(bf16[2,4,64,128]{3,2,1,0:T(8,128)(2,1)S(1)} %fusion.12), channel_id=1, source_target_pairs={{0,1},{1,0},{2,3},{3,2},{4,5},{5,4},{6,7},{7,6},{8,9},{9,8},{10,11... | collective-permute-start | bytes 393224 | tf_op jit(solution)/shard_map/ppermute | solution.py:111
  221.1 10.5 %collective-permute-start.76 = (bf16[2,4,64,128]{3,2,1,0:T(8,128)(2,1)S(1)}, bf16[2,4,64,128]{3,2,1,0:T(8,128)(2,1)S(1)}, u32[]{:S(2)}, u32[]{:S(2)}) collective-permute-start(bf16[2,4,64,128]{3,2,1,0:T(8,128)(2,1)S(1)} %get-tuple-element.123), channel_id=1, source_target_pairs={{0,2},{1,3},{2,0},{3,1},{4,6},{5,7},{6,4},{7,5},{8,10},{9,11},{10,... | collective-permute-start | bytes 393224 | tf_op jit(solution)/shard_map/ppermute | solution.py:111
  221.4 10.2 %collective-permute-start.77 = (bf16[2,4,64,128]{3,2,1,0:T(8,128)(2,1)S(1)}, bf16[2,4,64,128]{3,2,1,0:T(8,128)(2,1)S(1)}, u32[]{:S(2)}, u32[]{:S(2)}) collective-permute-start(bf16[2,4,64,128]{3,2,1,0:T(8,128)(2,1)S(1)} %get-tuple-element.122), channel_id=1, source_target_pairs={{0,3},{1,2},{2,1},{3,0},{4,7},{5,6},{6,5},{7,4},{8,11},{9,10},{10,... | collective-permute-start | bytes 393224 | tf_op jit(solution)/shard_map/ppermute | solution.py:111
  226.1 8.1 %collective-permute-start.79 = (bf16[2,4,64,128]{3,2,1,0:T(8,128)(2,1)S(1)}, bf16[2,4,64,128]{3,2,1,0:T(8,128)(2,1)S(1)}, u32[]{:S(2)}, u32[]{:S(2)}) collective-permute-start(bf16[2,4,64,128]{3,2,1,0:T(8,128)(2,1)S(1)} %fusion.15), channel_id=1, source_target_pairs={{0,1},{1,0},{2,3},{3,2},{4,5},{5,4},{6,7},{7,6},{8,9},{9,8},{10,11... | collective-permute-start | bytes 393224 | tf_op jit(solution)/shard_map/ppermute | solution.py:111
  227.0 11.1 %collective-permute-start.82 = (bf16[4,2,2,64,128]{4,3,2,1,0:T(8,128)(2,1)S(1)}, bf16[4,2,2,64,128]{4,3,2,1,0:T(8,128)(2,1)}, u32[]{:S(2)}, u32[]{:S(2)}) collective-permute-start(bf16[4,2,2,64,128]{4,3,2,1,0:T(8,128)(2,1)S(1)} %get-tuple-element.121.refs_0_), channel_id=1, source_target_pairs={{0,8},{4,12},{8,0},{12,4},{1,9},{5,13},{9,1},{13,5},{2,10},{6,14},... | collective-permute-start | bytes 786440 | tf_op jit(solution)/shard_map/ppermute | solution.py:111
  227.7 21.4 %collective-permute-start.74 = (bf16[2,4,4,64,128]{4,3,2,1,0:T(8,128)(2,1)S(1)}, bf16[2,4,4,64,128]{4,3,2,1,0:T(8,128)(2,1)S(1)}, u32[]{:S(2)}, u32[]{:S(2)}) collective-permute-start(bf16[2,4,4,64,128]{4,3,2,1,0:T(8,128)(2,1)S(1)} %mute_receiver.6.refs_0_), channel_id=1, source_target_pairs={{0,16},{16,0},{1,17},{17,1},{2,18},{18,2},{3,19},{19,3},{4,20},{20... | collective-permute-start | bytes 1572872 | tf_op jit(solution)/shard_map/ppermute | solution.py:111
  236.4 14.9 %collective-permute-start.80 = (bf16[2,4,4,64,128]{4,3,2,1,0:T(8,128)(2,1)S(1)}, bf16[2,4,4,64,128]{4,3,2,1,0:T(8,128)(2,1)}, u32[]{:S(2)}, u32[]{:S(2)}) collective-permute-start(bf16[2,4,4,64,128]{4,3,2,1,0:T(8,128)(2,1)S(1)} %mute_receiver.7.refs_1_), channel_id=1, source_target_pairs={{0,16},{16,0},{1,17},{17,1},{2,18},{18,2},{3,19},{19,3},{4,20},{20... | collective-permute-start | bytes 1572872 | tf_op jit(solution)/shard_map/ppermute | solution.py:111
  (24 other events, 156.0 us)

commit v4 on v3

--- a/solution.py
+++ b/solution.py
@@ -14,6 +14,7 @@
 LANES = 128
 BLOCK_W = 16
 HALVES = 2
+GROUP_ORDER = (4, 3, 15, 5, 12, 2, 6, 9, 7, 14, 11, 1, 10, 13, 0, 8)
 F32 = jnp.float32
 BF16 = jnp.bfloat16
 VMEM_BYTES = 24 * 1024 * 1024
@@ -286,7 +287,7 @@
 
 
 def correlate_kernel(pieces, ids, refl_ref, *refs):
-    ins = [refs[j * pieces : (j + 1) * pieces] for j in range(4)]
+    ins = [[refs[GROUP_ORDER.index(j * pieces + k)] for k in range(pieces)] for j in range(4)]
     outs = refs[4 * pieces : -2]
     hold, result = refs[-2:]
     half, me = ids[0], ids[1]
@@ -356,7 +357,7 @@
         [out] * (2 * count),
         2 * freq * rows * 256 * 256,
         freq * (2 * sources * 512 + rows * 768),
-        (ids, reflection, *[v for group in groups for v in group]),
+        (ids, reflection, *[groups[i // pieces][i % pieces] for i in GROUP_ORDER]),
         [
             pltpu.VMEM((2, rows // 2 * BLOCK_W, LANES), F32),
             pltpu.VMEM((2, rows * BLOCK_W, LANES), F32),
@@ -578,6 +579,10 @@
 
     def to_y(value):
         return swap(value, "rcv", 2, rcv_count)
+
+    def spread(value):
+        across = to_y(value)
+        return [value, to_core(value), across, to_core(across)]
 
     direct = [None] * foc_count
     direct[2] = split_wave(ids, direct_wave, 2, foc_count, False)
@@ -632,21 +637,26 @@
                 renewed.append(fresh)
                 continue
             moved = [to_foc(fresh[k], k) for k in (2, 3, 1, 0)]
-            if q == 0 and not last:
+            if q == 0:
                 before, early = moved, [to_src(moved[3])]
                 continue
-            before[:2], moved[2] = lax.optimization_barrier((before[:2], moved[2]))
-            crossed = [to_src(before[0]), to_src(before[1]), to_src(before[2])] + early
-            after = [to_src(moved[3]), to_src(moved[2])]
+            after = [to_src(moved[3])]
+            before[:2], moved[2], after = lax.optimization_barrier(
+                (before[:2], moved[2], after)
+            )
+            crossed = [to_src(value) for value in before[:3]] + early
+            after.append(to_src(moved[2]))
             after = [to_src(moved[0]), to_src(moved[1]), after[1], after[0]]
             arrays = before + crossed + moved + after
-            plan = [(kind, k, start * count) for start in range(2) for kind in ("own", "other") for k in (2, 3, 1, 0)]
+            plan = [
+                (kind, k, start * count)
+                for start in range(2)
+                for kind in ("own", "other")
+                for k in (2, 3, 1, 0)
+            ]
         if last:
             crossed = [to_src(value) for value in renewed]
-            mine = returned[-1]
-            across = to_y(mine)
-            groups = [mine, to_core(mine), across, to_core(across)]
-            muted_trace = trace_source(ids, onset_source, rows, groups)
+            muted_trace = trace_source(ids, onset_source, rows, spread(returned[-1]))
             partly = join_halves(ids, renewed, 0)
             return join_halves(ids, crossed, 1, partly), muted_trace
 

time: 255 us -> 250 us (0.980)
  waiting for transfers between devices: 117 us -> 103 us
  starting transfers between devices: 86.6 us -> 95.4 us
    ppermute x84, waiting for transfers between devices: 117 us -> 103 us  [swap(): return lax.ppermute(value, axis, [(i, i ^ mask) for i in range(count)])]
    ppermute x84, starting transfers between devices: 86.6 us -> 95.4 us  [swap(): return lax.ppermute(value, axis, [(i, i ^ mask) for i in range(count)])]
  transfers between devices with their start and end apart: 84 -> 84, of which waited for: 41 -> 40; matrix products, arithmetic and copies ran while one was open for 0% -> 0% of each run, Pallas kernels for 10% -> 10%
where the time goes in v4:
time: 250 us
  waiting for transfers between devices  103 us (41%)
  starting transfers between devices  95.4 us (38%)
  Pallas kernels  47.8 us (19%)
    ppermute x84, waiting for transfers between devices, swap(): return lax.ppermute(value, axis, [(i, i ^ mask) for i in range(count)])  103 us
    ppermute x84, starting transfers between devices, swap(): return lax.ppermute(value, axis, [(i, i ^ mask) for i in range(count)])  95.4 us
    pallas_call x11, Pallas kernels, call(): pl.pallas_call(kernel, name=name, out_shape=out_shape, in_specs=[SMEM_SPE...  32.5 us
    pallas_call x1, Pallas kernels, trace_source(): pl.pallas_call(trace_kernel, name='trace_source', out_shape=jax.ShapeDtyp...  6.27 us
    pallas_call x2, Pallas kernels, join_halves(): pl.pallas_call(join_kernel, name='join_halves', out_shape=jax.ShapeDtypeS...  5.85 us
  transfers between devices with their start and end apart: 84, of which 40 were waited for; matrix products, arithmetic and copies ran while one was open for 0% of the time, Pallas kernels for 10%

profile of v4, /device:TPU:0, one launch (start us, length us, event | category | flops | bytes accessed | tf_op | source)
XLA Modules:
  0.0 249.6 jit_solution(5342830631492544033)
XLA Ops:
  0.7 1.6 copy-done.1
  3.1 4.1 %collective-permute-start = (bf16[2,8,64,128]{3,2,1,0:T(8,128)(2,1)S(1)}, bf16[2,8,64,128]{3,2,1,0:T(8,128)(2,1)S(1)}, u32[]{:S(2)}, u32[]{:S(2)}) collective-permute-start(bf16[2,8,64,128]{3,2,1,0:T(8,128)(2,1)S(1)} %split_wave.6.refs_7_), channel_id=1, source_target_pairs={{0,2},{1,3},{2,0},{3,1},{4,6},{5,7},{6,4},{7,5},{8,10},{9,11},{10,... | collective-permute-start | bytes 786440 | tf_op jit(solution)/shard_map/ppermute | solution.py:112
  7.2 4.1 %basis.1 = (bf16[512,1024]{1,0:T(8,128)(2,1)S(1)}, bf16[1024,512]{1,0:T(8,128)(2,1)S(1)}) custom-call(s32[3]{0:T(128)S(1)} %pad_add_fusion.ids), custom_call_target="tpu_custom_call" | custom-call | flops 20971520 | bytes 2097152 | tf_op jit(solution)/shard_map/basis/pallas_call | solution.py:117
  14.7 10.9 %collective-permute-done.refs_1_ = bf16[2,8,64,128]{3,2,1,0:T(8,128)(2,1)S(1)} collective-permute-done((bf16[2,8,64,128]{3,2,1,0:T(8,128)(2,1)S(1)}, bf16[2,8,64,128]{3,2,1,0:T(8,128)(2,1)S(1)}, u32[]{:S(2)}, u32[]{:S(2)}) %collective-permute-start) | collective-permute-done | bytes 262176 | tf_op jit(solution)/shard_map/ppermute | solution.py:112
  25.6 1.8 collective-permute-start.1
  28.5 6.3 %collective-permute-done.1.refs_2_ = bf16[2,8,64,128]{3,2,1,0:T(8,128)(2,1)S(1)} collective-permute-done((bf16[2,8,64,128]{3,2,1,0:T(8,128)(2,1)S(1)}, bf16[2,8,64,128]{3,2,1,0:T(8,128)(2,1)S(1)}, u32[]{:S(2)}, u32[]{:S(2)}) %collective-permute-start.1) | collective-permute-done | bytes 262176 | tf_op jit(solution)/shard_map/ppermute | solution.py:112
  34.8 3.0 %collective-permute-done.3.refs_4_ = bf16[2,8,64,128]{3,2,1,0:T(8,128)(2,1)S(1)} collective-permute-done((bf16[2,8,64,128]{3,2,1,0:T(8,128)(2,1)S(1)}, bf16[2,8,64,128]{3,2,1,0:T(8,128)(2,1)S(1)}, u32[]{:S(2)}, u32[]{:S(2)}) %collective-permute-start.3) | collective-permute-done | bytes 262176 | tf_op jit(solution)/shard_map/ppermute | solution.py:112
  37.9 4.0 %convolve.2 = (bf16[2,4,2,2,64,128]{5,4,3,2,1,0:T(8,128)(2,1)S(1)}, bf16[2,4,2,2,64,128]{5,4,3,2,1,0:T(8,128)(2,1)S(1)}) custom-call(s32[3]{0:T(128)S(1)} %pad_add_fusion.ids, bf16[2,64,128,256]{3,2,1,0:T(8,128)(2,1)S(1)} %copy-done, bf16[2,2,8,64,128]{4,3,2,1,0:T(8,128)(2,1)S(1)} %split_wave.5.refs_0_.refs_5_, ...), custom_call_target="tpu_custom_call" | custom-call | flops 536870912 | bytes 11534336 | tf_op jit(solution)/shard_map/convolve/pallas_call | solution.py:117
  42.0 1.9 collective-permute-done.5
  45.4 7.1 %collective-permute-done.6 = bf16[4,2,2,64,128]{4,3,2,1,0:T(8,128)(2,1)S(1)} collective-permute-done((bf16[4,2,2,64,128]{4,3,2,1,0:T(8,128)(2,1)S(1)}, bf16[4,2,2,64,128]{4,3,2,1,0:T(8,128)(2,1)S(1)}, u32[]{:S(2)}, u32[]{:S(2)}) %collective-permute-start.6) | collective-permute-done | bytes 262176 | tf_op jit(solution)/shard_map/ppermute | solution.py:112
  52.6 1.5 collective-permute-start.7
  54.1 3.4 %collective-permute-start.8 = (bf16[2,2,64,128]{3,2,1,0:T(8,128)(2,1)S(1)}, bf16[2,2,64,128]{3,2,1,0:T(8,128)(2,1)S(1)}, u32[]{:S(2)}, u32[]{:S(2)}) collective-permute-start(bf16[2,2,64,128]{3,2,1,0:T(8,128)(2,1)S(1)} %get-tuple-element.137), channel_id=1, source_target_pairs={{0,2},{1,3},{2,0},{3,1},{4,6},{5,7},{6,4},{7,5},{8,10},{9,11},{10,... | collective-permute-start | bytes 196616 | tf_op jit(solution)/shard_map/ppermute | solution.py:112
  57.5 4.1 %collective-permute-done.8.refs_2_ = bf16[2,2,64,128]{3,2,1,0:T(8,128)(2,1)S(1)} collective-permute-done((bf16[2,2,64,128]{3,2,1,0:T(8,128)(2,1)S(1)}, bf16[2,2,64,128]{3,2,1,0:T(8,128)(2,1)S(1)}, u32[]{:S(2)}, u32[]{:S(2)}) %collective-permute-start.8) | collective-permute-done | bytes 65568 | tf_op jit(solution)/shard_map/ppermute | solution.py:112
  61.6 1.9 collective-permute-done.9.refs_3_
  63.5 1.7 mute_source.2
  68.6 2.7 %collective-permute-start.18 = (bf16[2,2,64,128]{3,2,1,0:T(8,128)(2,1)S(1)}, bf16[2,2,64,128]{3,2,1,0:T(8,128)(2,1)S(1)}, u32[]{:S(2)}, u32[]{:S(2)}) collective-permute-start(bf16[2,2,64,128]{3,2,1,0:T(8,128)(2,1)S(1)} %get-tuple-element.75), channel_id=1, source_target_pairs={{0,2},{1,3},{2,0},{3,1},{4,6},{5,7},{6,4},{7,5},{8,10},{9,11},{10,... | collective-permute-start | bytes 196616 | tf_op jit(solution)/shard_map/ppermute | solution.py:112
  71.5 1.5 collective-permute-start.12
  74.2 1.5 collective-permute-start.20
  76.4 1.9 collective-permute-done.22.refs_12_
  80.2 3.9 %correlate.2 = (bf16[2,2,4,64,128]{4,3,2,1,0:T(8,128)(2,1)S(1)}, bf16[2,2,4,64,128]{4,3,2,1,0:T(8,128)(2,1)S(1)}, bf16[2,2,4,64,128]{4,3,2,1,0:T(8,128)(2,1)S(1)...) custom-call(s32[3]{0:T(128)S(1)} %pad_add_fusion.ids, ...), custom_call_target="tpu_custom_call" | custom-call | flops 536870912 | bytes 11534336 | tf_op jit(solution)/shard_map/correlate/pallas_call | solution.py:117
  84.2 1.6 collective-permute-start.25
  88.3 5.1 %collective-permute-done.25 = bf16[2,2,4,64,128]{4,3,2,1,0:T(8,128)(2,1)S(1)} collective-permute-done((bf16[2,2,4,64,128]{4,3,2,1,0:T(8,128)(2,1)S(1)}, bf16[2,2,4,64,128]{4,3,2,1,0:T(8,128)(2,1)S(1)}, u32[]{:S(2)}, u32[]{:S(2)}) %collective-permute-start.25) | collective-permute-done | bytes 262176 | tf_op jit(solution)/shard_map/ppermute | solution.py:112
  93.5 2.4 collective-permute-start.26
  97.3 1.7 collective-permute-done.28.refs_4_
  100.5 4.1 %collective-permute-done.32 = bf16[2,2,4,64,128]{4,3,2,1,0:T(8,128)(2,1)S(1)} collective-permute-done((bf16[2,2,4,64,128]{4,3,2,1,0:T(8,128)(2,1)S(1)}, bf16[2,2,4,64,128]{4,3,2,1,0:T(8,128)(2,1)S(1)}, u32[]{:S(2)}, u32[]{:S(2)}) %collective-permute-start.32) | collective-permute-done | bytes 262176 | tf_op jit(solution)/shard_map/ppermute | solution.py:112
  104.7 2.4 collective-permute-start.33
  108.5 2.3 mute_receiver.4
  110.9 1.5 collective-permute-start.37
  112.5 2.9 %collective-permute-start.30 = (bf16[2,4,64,128]{3,2,1,0:T(8,128)(2,1)S(1)}, bf16[2,4,64,128]{3,2,1,0:T(8,128)(2,1)S(1)}, u32[]{:S(2)}, u32[]{:S(2)}) collective-permute-start(bf16[2,4,64,128]{3,2,1,0:T(8,128)(2,1)S(1)} %get-tuple-element.80), channel_id=1, source_target_pairs={{0,2},{1,3},{2,0},{3,1},{4,6},{5,7},{6,4},{7,5},{8,10},{9,11},{10,... | collective-permute-start | bytes 393224 | tf_op jit(solution)/shard_map/ppermute | solution.py:112
  116.7 6.2 %collective-permute-start.31 = (bf16[2,4,64,128]{3,2,1,0:T(8,128)(2,1)S(1)}, bf16[2,4,64,128]{3,2,1,0:T(8,128)(2,1)S(1)}, u32[]{:S(2)}, u32[]{:S(2)}) collective-permute-start(bf16[2,4,64,128]{3,2,1,0:T(8,128)(2,1)S(1)} %get-tuple-element.81), channel_id=1, source_target_pairs={{0,3},{1,2},{2,1},{3,0},{4,7},{5,6},{6,5},{7,4},{8,11},{9,10},{10,... | collective-permute-start | bytes 393224 | tf_op jit(solution)/shard_map/ppermute | solution.py:112
  123.9 2.2 mute_receiver.5
  127.2 1.6 collective-permute-start.39
  133.6 1.6 collective-permute-start.41
  135.6 3.5 %collective-permute-done.44.refs_8_ = bf16[2,4,64,128]{3,2,1,0:T(8,128)(2,1)S(1)} collective-permute-done((bf16[2,4,64,128]{3,2,1,0:T(8,128)(2,1)S(1)}, bf16[2,4,64,128]{3,2,1,0:T(8,128)(2,1)S(1)}, u32[]{:S(2)}, u32[]{:S(2)}) %collective-permute-start.44) | collective-permute-done | bytes 131104 | tf_op jit(solution)/shard_map/ppermute | solution.py:112
  142.3 3.2 %collective-permute-done.46.refs_12_ = bf16[2,4,64,128]{3,2,1,0:T(8,128)(2,1)S(1)} collective-permute-done((bf16[2,4,64,128]{3,2,1,0:T(8,128)(2,1)S(1)}, bf16[2,4,64,128]{3,2,1,0:T(8,128)(2,1)S(1)}, u32[]{:S(2)}, u32[]{:S(2)}) %collective-permute-start.46) | collective-permute-done | bytes 131104 | tf_op jit(solution)/shard_map/ppermute | solution.py:112
  145.6 1.6 collective-permute-done.47.refs_13_
  148.6 4.0 %convolve.3 = (bf16[2,4,2,2,64,128]{5,4,3,2,1,0:T(8,128)(2,1)S(1)}, bf16[2,4,2,2,64,128]{5,4,3,2,1,0:T(8,128)(2,1)S(1)}) custom-call(s32[3]{0:T(128)S(1)} %pad_add_fusion.ids, bf16[2,64,128,256]{3,2,1,0:T(8,128)(2,1)S(1)} %copy-done, bf16[2,4,64,128]{3,2,1,0:T(8,128)(2,1)S(1)} %collective-permute-done.30.refs_0_, ...), custom_call_target="tpu_custom_call" | custom-call | flops 536870912 | bytes 11534336 | tf_op jit(solution)/shard_map/convolve/pallas_call | solution.py:117
  152.6 1.9 collective-permute-done.49
  155.7 7.3 %collective-permute-done.50 = bf16[4,2,2,64,128]{4,3,2,1,0:T(8,128)(2,1)S(1)} collective-permute-done((bf16[4,2,2,64,128]{4,3,2,1,0:T(8,128)(2,1)S(1)}, bf16[4,2,2,64,128]{4,3,2,1,0:T(8,128)(2,1)S(1)}, u32[]{:S(2)}, u32[]{:S(2)}) %collective-permute-start.50) | collective-permute-done | bytes 262176 | tf_op jit(solution)/shard_map/ppermute | solution.py:112
  163.2 2.5 collective-permute-start.51
  168.3 4.8 %collective-permute-done.52.refs_2_ = bf16[2,2,64,128]{3,2,1,0:T(8,128)(2,1)S(1)} collective-permute-done((bf16[2,2,64,128]{3,2,1,0:T(8,128)(2,1)S(1)}, bf16[2,2,64,128]{3,2,1,0:T(8,128)(2,1)S(1)}, u32[]{:S(2)}, u32[]{:S(2)}) %collective-permute-start.52) | collective-permute-done | bytes 65568 | tf_op jit(solution)/shard_map/ppermute | solution.py:112
  173.1 1.7 mute_source.3
  174.8 2.4 collective-permute-start.55
  178.5 1.6 collective-permute-start.62
  186.3 1.6 collective-permute-done.66.refs_12_
  190.4 4.0 %correlate.3 = (bf16[2,2,4,64,128]{4,3,2,1,0:T(8,128)(2,1)S(1)}, bf16[2,2,4,64,128]{4,3,2,1,0:T(8,128)(2,1)S(1)}, bf16[2,2,4,64,128]{4,3,2,1,0:T(8,128)(2,1)S(1)...) custom-call(s32[3]{0:T(128)S(1)} %pad_add_fusion.ids, ...), custom_call_target="tpu_custom_call" | custom-call | flops 536870912 | bytes 11534336 | tf_op jit(solution)/shard_map/correlate/pallas_call | solution.py:117
  194.3 1.7 collective-permute-start.69
  196.4 1.7 collective-permute-start.75
  198.5 5.1 %collective-permute-done.69 = bf16[2,2,4,64,128]{4,3,2,1,0:T(8,128)(2,1)S(1)} collective-permute-done((bf16[2,2,4,64,128]{4,3,2,1,0:T(8,128)(2,1)S(1)}, bf16[2,2,4,64,128]{4,3,2,1,0:T(8,128)(2,1)S(1)}, u32[]{:S(2)}, u32[]{:S(2)}) %collective-permute-start.69) | collective-permute-done | bytes 262176 | tf_op jit(solution)/shard_map/ppermute | solution.py:112
  203.6 1.7 collective-permute-start.70
  205.4 2.4 collective-permute-start.71
  209.2 1.7 collective-permute-start.73
  211.0 3.8 %collective-permute-done.75 = bf16[2,2,4,64,128]{4,3,2,1,0:T(8,128)(2,1)S(1)} collective-permute-done((bf16[2,2,4,64,128]{4,3,2,1,0:T(8,128)(2,1)S(1)}, bf16[2,2,4,64,128]{4,3,2,1,0:T(8,128)(2,1)S(1)}, u32[]{:S(2)}, u32[]{:S(2)}) %collective-permute-start.75) | collective-permute-done | bytes 262176 | tf_op jit(solution)/shard_map/ppermute | solution.py:112
  214.9 1.7 collective-permute-start.76
  216.6 2.4 collective-permute-start.77
  219.0 2.2 mute_receiver.6.refs_0_
  222.3 1.6 collective-permute-start.74
  223.8 2.9 %collective-permute-done.76.refs_0_ = bf16[2,4,64,128]{3,2,1,0:T(8,128)(2,1)S(1)} collective-permute-done((bf16[2,4,64,128]{3,2,1,0:T(8,128)(2,1)S(1)}, bf16[2,4,64,128]{3,2,1,0:T(8,128)(2,1)S(1)}, u32[]{:S(2)}, u32[]{:S(2)}) %collective-permute-start.76) | collective-permute-done | bytes 131104 | tf_op jit(solution)/shard_map/ppermute | solution.py:112
  227.8 2.2 mute_receiver.7.refs_1_
  230.1 1.7 collective-permute-start.80
  234.1 6.3 %trace_source.1 = bf16[8,128,1024]{2,1,0:T(8,128)(2,1)} custom-call(s32[3]{0:T(128)S(1)} %pad_add_fusion.ids, s32[8,128,1]{2,1,0:T(8,128)S(1)} %copy.7.onset_ref, bf16[512,1024]{1,0:T(8,128)(2,1)S(1)} %get-tuple-element.65.rows_ref, bf16[4,2,2,64,128]{4,3,2,1,0:T(8,128)(2,1)S(1)} %get-tuple-element.123.refs_0_, ...), custom_call_target="tpu_custom_call" | custom-call | flops 1073741824 | bytes 5242880 | tf_op jit(solution)/shard_map/trace_source/pallas_call | solution.py:441
  240.3 2.4 join_halves.2.refs_2_
  242.7 3.4 %collective-permute-done.80.refs_1_ = bf16[2,4,4,64,128]{4,3,2,1,0:T(8,128)(2,1)} collective-permute-done((bf16[2,4,4,64,128]{4,3,2,1,0:T(8,128)(2,1)S(1)}, bf16[2,4,4,64,128]{4,3,2,1,0:T(8,128)(2,1)}, u32[]{:S(2)}, u32[]{:S(2)}) %collective-permute-start.80) | collective-permute-done | bytes 524320 | tf_op jit(solution)/shard_map/ppermute | solution.py:112
  246.2 3.4 %join_halves.3 = bf16[2,256,8,256]{3,2,1,0:T(8,128)(2,1)} custom-call(s32[3]{0:T(128)S(1)} %pad_add_fusion.ids, bf16[2,4,4,64,128]{4,3,2,1,0:T(8,128)(2,1)S(1)} %collective-permute-done.74.refs_0_, bf16[2,4,4,64,128]{4,3,2,1,0:T(8,128)(2,1)} %collective-permute-done.80.refs_1_, ...), custom_call_target="tpu_custom_call", output_to_operand_aliasing={{}: (3, {})} | custom-call | bytes 2097152 | tf_op jit(solution)/shard_map/join_halves/pallas_call | solution.py:538
  (146 shorter events, 54.9 us)
Async XLA Ops:
  3.1 22.5 %collective-permute-start = (bf16[2,8,64,128]{3,2,1,0:T(8,128)(2,1)S(1)}, bf16[2,8,64,128]{3,2,1,0:T(8,128)(2,1)S(1)}, u32[]{:S(2)}, u32[]{:S(2)}) collective-permute-start(bf16[2,8,64,128]{3,2,1,0:T(8,128)(2,1)S(1)} %split_wave.6.refs_7_), channel_id=1, source_target_pairs={{0,2},{1,3},{2,0},{3,1},{4,6},{5,7},{6,4},{7,5},{8,10},{9,11},{10,... | collective-permute-start | bytes 786440 | tf_op jit(solution)/shard_map/ppermute | solution.py:112
  12.1 15.3 %collective-permute-start.2 = (bf16[2,8,64,128]{3,2,1,0:T(8,128)(2,1)S(1)}, bf16[2,8,64,128]{3,2,1,0:T(8,128)(2,1)S(1)}, u32[]{:S(2)}, u32[]{:S(2)}) collective-permute-start(bf16[2,8,64,128]{3,2,1,0:T(8,128)(2,1)S(1)} %split_wave.4.refs_8_), channel_id=1, source_target_pairs={{0,3},{1,2},{2,1},{3,0},{4,7},{5,6},{6,5},{7,4},{8,11},{9,10},{10,... | collective-permute-start | bytes 786440 | tf_op jit(solution)/shard_map/ppermute | solution.py:112
  14.4 23.5 %collective-permute-start.4 = (bf16[2,2,8,64,128]{4,3,2,1,0:T(8,128)(2,1)S(1)}, bf16[2,2,8,64,128]{4,3,2,1,0:T(8,128)(2,1)S(1)}, u32[]{:S(2)}, u32[]{:S(2)}) collective-permute-start(bf16[2,2,8,64,128]{4,3,2,1,0:T(8,128)(2,1)S(1)} %split_wave.7.refs_6_), channel_id=1, source_target_pairs={{0,1},{1,0},{2,3},{3,2},{4,5},{5,4},{6,7},{7,6},{8,9},{9,8},{10,11... | collective-permute-start | bytes 1572872 | tf_op jit(solution)/shard_map/ppermute | solution.py:112
  25.6 9.2 %collective-permute-start.1 = (bf16[2,8,64,128]{3,2,1,0:T(8,128)(2,1)S(1)}, bf16[2,8,64,128]{3,2,1,0:T(8,128)(2,1)S(1)}, u32[]{:S(2)}, u32[]{:S(2)}) collective-permute-start(bf16[2,8,64,128]{3,2,1,0:T(8,128)(2,1)S(1)} %collective-permute-done.refs_1_), channel_id=1, source_target_pairs={{0,16},{16,0},{1,17},{17,1},{2,18},{18,2},{3,19},{19,3},{4,20},{20... | collective-permute-start | bytes 786440 | tf_op jit(solution)/shard_map/ppermute | solution.py:112
  27.4 10.4 %collective-permute-start.3 = (bf16[2,8,64,128]{3,2,1,0:T(8,128)(2,1)S(1)}, bf16[2,8,64,128]{3,2,1,0:T(8,128)(2,1)S(1)}, u32[]{:S(2)}, u32[]{:S(2)}) collective-permute-start(bf16[2,8,64,128]{3,2,1,0:T(8,128)(2,1)S(1)} %collective-permute-done.2.refs_3_), channel_id=1, source_target_pairs={{0,16},{16,0},{1,17},{17,1},{2,18},{18,2},{3,19},{19,3},{4,20},{20... | collective-permute-start | bytes 786440 | tf_op jit(solution)/shard_map/ppermute | solution.py:112
  44.0 8.4 %collective-permute-start.6 = (bf16[4,2,2,64,128]{4,3,2,1,0:T(8,128)(2,1)S(1)}, bf16[4,2,2,64,128]{4,3,2,1,0:T(8,128)(2,1)S(1)}, u32[]{:S(2)}, u32[]{:S(2)}) collective-permute-start(bf16[4,2,2,64,128]{4,3,2,1,0:T(8,128)(2,1)S(1)} %fusion.2), channel_id=1, source_target_pairs={{0,8},{4,12},{8,0},{12,4},{1,9},{5,13},{9,1},{13,5},{2,10},{6,14},... | collective-permute-start | bytes 786440 | tf_op jit(solution)/shard_map/ppermute | solution.py:112
  52.6 4.9 %collective-permute-start.7 = (bf16[2,2,64,128]{3,2,1,0:T(8,128)(2,1)S(1)}, bf16[2,2,64,128]{3,2,1,0:T(8,128)(2,1)S(1)}, u32[]{:S(2)}, u32[]{:S(2)}) collective-permute-start(bf16[2,2,64,128]{3,2,1,0:T(8,128)(2,1)S(1)} %get-tuple-element.138), channel_id=1, source_target_pairs={{0,1},{1,0},{2,3},{3,2},{4,5},{5,4},{6,7},{7,6},{8,9},{9,8},{10,11... | collective-permute-start | bytes 196616 | tf_op jit(solution)/shard_map/ppermute | solution.py:112
  54.1 7.5 %collective-permute-start.8 = (bf16[2,2,64,128]{3,2,1,0:T(8,128)(2,1)S(1)}, bf16[2,2,64,128]{3,2,1,0:T(8,128)(2,1)S(1)}, u32[]{:S(2)}, u32[]{:S(2)}) collective-permute-start(bf16[2,2,64,128]{3,2,1,0:T(8,128)(2,1)S(1)} %get-tuple-element.137), channel_id=1, source_target_pairs={{0,2},{1,3},{2,0},{3,1},{4,6},{5,7},{6,4},{7,5},{8,10},{9,11},{10,... | collective-permute-start | bytes 196616 | tf_op jit(solution)/shard_map/ppermute | solution.py:112
  57.5 6.1 %collective-permute-start.9 = (bf16[2,2,64,128]{3,2,1,0:T(8,128)(2,1)S(1)}, bf16[2,2,64,128]{3,2,1,0:T(8,128)(2,1)S(1)}, u32[]{:S(2)}, u32[]{:S(2)}) collective-permute-start(bf16[2,2,64,128]{3,2,1,0:T(8,128)(2,1)S(1)} %get-tuple-element.136), channel_id=1, source_target_pairs={{0,3},{1,2},{2,1},{3,0},{4,7},{5,6},{6,5},{7,4},{8,11},{9,10},{10,... | collective-permute-start | bytes 196616 | tf_op jit(solution)/shard_map/ppermute | solution.py:112
  65.2 6.2 %collective-permute-start.11 = (bf16[2,2,64,128]{3,2,1,0:T(8,128)(2,1)S(1)}, bf16[2,2,64,128]{3,2,1,0:T(8,128)(2,1)S(1)}, u32[]{:S(2)}, u32[]{:S(2)}) collective-permute-start(bf16[2,2,64,128]{3,2,1,0:T(8,128)(2,1)S(1)} %get-tuple-element.73), channel_id=1, source_target_pairs={{0,3},{1,2},{2,1},{3,0},{4,7},{5,6},{6,5},{7,4},{8,11},{9,10},{10,... | collective-permute-start | bytes 196616 | tf_op jit(solution)/shard_map/ppermute | solution.py:112
  66.7 6.3 %collective-permute-start.14 = (bf16[2,2,64,128]{3,2,1,0:T(8,128)(2,1)S(1)}, bf16[2,2,64,128]{3,2,1,0:T(8,128)(2,1)S(1)}, u32[]{:S(2)}, u32[]{:S(2)}) collective-permute-start(bf16[2,2,64,128]{3,2,1,0:T(8,128)(2,1)S(1)} %get-tuple-element.74), channel_id=1, source_target_pairs={{0,1},{1,0},{2,3},{3,2},{4,5},{5,4},{6,7},{7,6},{8,9},{9,8},{10,11... | collective-permute-start | bytes 196616 | tf_op jit(solution)/shard_map/ppermute | solution.py:112
  67.0 6.0 %collective-permute-start.16 = (bf16[2,2,64,128]{3,2,1,0:T(8,128)(2,1)S(1)}, bf16[2,2,64,128]{3,2,1,0:T(8,128)(2,1)S(1)}, u32[]{:S(2)}, u32[]{:S(2)}) collective-permute-start(bf16[2,2,64,128]{3,2,1,0:T(8,128)(2,1)S(1)} %get-tuple-element.72.refs_14_), channel_id=1, source_target_pairs={{0,8},{4,12},{8,0},{12,4},{1,9},{5,13},{9,1},{13,5},{2,10},{6,14},... | collective-permute-start | bytes 196616 | tf_op jit(solution)/shard_map/ppermute | solution.py:112
  68.6 5.2 %collective-permute-start.18 = (bf16[2,2,64,128]{3,2,1,0:T(8,128)(2,1)S(1)}, bf16[2,2,64,128]{3,2,1,0:T(8,128)(2,1)S(1)}, u32[]{:S(2)}, u32[]{:S(2)}) collective-permute-start(bf16[2,2,64,128]{3,2,1,0:T(8,128)(2,1)S(1)} %get-tuple-element.75), channel_id=1, source_target_pairs={{0,2},{1,3},{2,0},{3,1},{4,6},{5,7},{6,4},{7,5},{8,10},{9,11},{10,... | collective-permute-start | bytes 196616 | tf_op jit(solution)/shard_map/ppermute | solution.py:112
  71.5 4.3 %collective-permute-start.12 = (bf16[2,2,64,128]{3,2,1,0:T(8,128)(2,1)S(1)}, bf16[2,2,64,128]{3,2,1,0:T(8,128)(2,1)S(1)}, u32[]{:S(2)}, u32[]{:S(2)}) collective-permute-start(bf16[2,2,64,128]{3,2,1,0:T(8,128)(2,1)S(1)} %collective-permute-done.11.refs_1_), channel_id=1, source_target_pairs={{0,8},{4,12},{8,0},{12,4},{1,9},{5,13},{9,1},{13,5},{2,10},{6,14},... | collective-permute-start | bytes 196616 | tf_op jit(solution)/shard_map/ppermute | solution.py:112
  73.7 4.6 %collective-permute-start.22 = (bf16[2,2,64,128]{3,2,1,0:T(8,128)(2,1)S(1)}, bf16[2,2,64,128]{3,2,1,0:T(8,128)(2,1)S(1)}, u32[]{:S(2)}, u32[]{:S(2)}) collective-permute-start(bf16[2,2,64,128]{3,2,1,0:T(8,128)(2,1)S(1)} %collective-permute-done.18.refs_5_), channel_id=1, source_target_pairs={{0,8},{4,12},{8,0},{12,4},{1,9},{5,13},{9,1},{13,5},{2,10},{6,14},... | collective-permute-start | bytes 196616 | tf_op jit(solution)/shard_map/ppermute | solution.py:112
  74.2 4.8 %collective-permute-start.20 = (bf16[2,2,64,128]{3,2,1,0:T(8,128)(2,1)S(1)}, bf16[2,2,64,128]{3,2,1,0:T(8,128)(2,1)S(1)}, u32[]{:S(2)}, u32[]{:S(2)}) collective-permute-start(bf16[2,2,64,128]{3,2,1,0:T(8,128)(2,1)S(1)} %collective-permute-done.14.refs_11_), channel_id=1, source_target_pairs={{0,8},{4,12},{8,0},{12,4},{1,9},{5,13},{9,1},{13,5},{2,10},{6,14},... | collective-permute-start | bytes 196616 | tf_op jit(solution)/shard_map/ppermute | solution.py:112
  84.2 9.2 %collective-permute-start.25 = (bf16[2,2,4,64,128]{4,3,2,1,0:T(8,128)(2,1)S(1)}, bf16[2,2,4,64,128]{4,3,2,1,0:T(8,128)(2,1)S(1)}, u32[]{:S(2)}, u32[]{:S(2)}) collective-permute-start(bf16[2,2,4,64,128]{4,3,2,1,0:T(8,128)(2,1)S(1)} %get-tuple-element.77), channel_id=1, source_target_pairs={{0,16},{16,0},{1,17},{17,1},{2,18},{18,2},{3,19},{19,3},{4,20},{20... | collective-permute-start | bytes 786440 | tf_op jit(solution)/shard_map/ppermute | solution.py:112
  85.7 13.3 %collective-permute-start.28 = (bf16[2,2,4,64,128]{4,3,2,1,0:T(8,128)(2,1)S(1)}, bf16[2,2,4,64,128]{4,3,2,1,0:T(8,128)(2,1)S(1)}, u32[]{:S(2)}, u32[]{:S(2)}) collective-permute-start(bf16[2,2,4,64,128]{4,3,2,1,0:T(8,128)(2,1)S(1)} %get-tuple-element.79), channel_id=1, source_target_pairs={{0,16},{16,0},{1,17},{17,1},{2,18},{18,2},{3,19},{19,3},{4,20},{20... | collective-permute-start | bytes 786440 | tf_op jit(solution)/shard_map/ppermute | solution.py:112
  86.3 18.4 %collective-permute-start.32 = (bf16[2,2,4,64,128]{4,3,2,1,0:T(8,128)(2,1)S(1)}, bf16[2,2,4,64,128]{4,3,2,1,0:T(8,128)(2,1)S(1)}, u32[]{:S(2)}, u32[]{:S(2)}) collective-permute-start(bf16[2,2,4,64,128]{4,3,2,1,0:T(8,128)(2,1)S(1)} %get-tuple-element.83), channel_id=1, source_target_pairs={{0,16},{16,0},{1,17},{17,1},{2,18},{18,2},{3,19},{19,3},{4,20},{20... | collective-permute-start | bytes 786440 | tf_op jit(solution)/shard_map/ppermute | solution.py:112
  87.8 23.0 %collective-permute-start.35 = (bf16[2,2,4,64,128]{4,3,2,1,0:T(8,128)(2,1)S(1)}, bf16[2,2,4,64,128]{4,3,2,1,0:T(8,128)(2,1)S(1)}, u32[]{:S(2)}, u32[]{:S(2)}) collective-permute-start(bf16[2,2,4,64,128]{4,3,2,1,0:T(8,128)(2,1)S(1)} %get-tuple-element.85), channel_id=1, source_target_pairs={{0,16},{16,0},{1,17},{17,1},{2,18},{18,2},{3,19},{19,3},{4,20},{20... | collective-permute-start | bytes 786440 | tf_op jit(solution)/shard_map/ppermute | solution.py:112
  93.5 13.7 %collective-permute-start.26 = (bf16[2,4,64,128]{3,2,1,0:T(8,128)(2,1)S(1)}, bf16[2,4,64,128]{3,2,1,0:T(8,128)(2,1)S(1)}, u32[]{:S(2)}, u32[]{:S(2)}) collective-permute-start(bf16[2,4,64,128]{3,2,1,0:T(8,128)(2,1)S(1)} %get-tuple-element.131), channel_id=1, source_target_pairs={{0,2},{1,3},{2,0},{3,1},{4,6},{5,7},{6,4},{7,5},{8,10},{9,11},{10,... | collective-permute-start | bytes 393224 | tf_op jit(solution)/shard_map/ppermute | solution.py:112
  95.9 12.6 %collective-permute-start.27 = (bf16[2,4,64,128]{3,2,1,0:T(8,128)(2,1)S(1)}, bf16[2,4,64,128]{3,2,1,0:T(8,128)(2,1)S(1)}, u32[]{:S(2)}, u32[]{:S(2)}) collective-permute-start(bf16[2,4,64,128]{3,2,1,0:T(8,128)(2,1)S(1)} %get-tuple-element.130), channel_id=1, source_target_pairs={{0,3},{1,2},{2,1},{3,0},{4,7},{5,6},{6,5},{7,4},{8,11},{9,10},{10,... | collective-permute-start | bytes 393224 | tf_op jit(solution)/shard_map/ppermute | solution.py:112
  99.1 9.5 %collective-permute-start.29 = (bf16[2,4,64,128]{3,2,1,0:T(8,128)(2,1)S(1)}, bf16[2,4,64,128]{3,2,1,0:T(8,128)(2,1)S(1)}, u32[]{:S(2)}, u32[]{:S(2)}) collective-permute-start(bf16[2,4,64,128]{3,2,1,0:T(8,128)(2,1)S(1)} %fusion.6), channel_id=1, source_target_pairs={{0,1},{1,0},{2,3},{3,2},{4,5},{5,4},{6,7},{7,6},{8,9},{9,8},{10,11... | collective-permute-start | bytes 393224 | tf_op jit(solution)/shard_map/ppermute | solution.py:112
  104.7 12.0 %collective-permute-start.33 = (bf16[2,4,64,128]{3,2,1,0:T(8,128)(2,1)S(1)}, bf16[2,4,64,128]{3,2,1,0:T(8,128)(2,1)S(1)}, u32[]{:S(2)}, u32[]{:S(2)}) collective-permute-start(bf16[2,4,64,128]{3,2,1,0:T(8,128)(2,1)S(1)} %get-tuple-element.129), channel_id=1, source_target_pairs={{0,2},{1,3},{2,0},{3,1},{4,6},{5,7},{6,4},{7,5},{8,10},{9,11},{10,... | collective-permute-start | bytes 393224 | tf_op jit(solution)/shard_map/ppermute | solution.py:112
  107.1 15.7 %collective-permute-start.34 = (bf16[2,4,64,128]{3,2,1,0:T(8,128)(2,1)S(1)}, bf16[2,4,64,128]{3,2,1,0:T(8,128)(2,1)S(1)}, u32[]{:S(2)}, u32[]{:S(2)}) collective-permute-start(bf16[2,4,64,128]{3,2,1,0:T(8,128)(2,1)S(1)} %get-tuple-element.128), channel_id=1, source_target_pairs={{0,3},{1,2},{2,1},{3,0},{4,7},{5,6},{6,5},{7,4},{8,11},{9,10},{10,... | collective-permute-start | bytes 393224 | tf_op jit(solution)/shard_map/ppermute | solution.py:112
  110.8 13.1 %collective-permute-start.36 = (bf16[2,4,64,128]{3,2,1,0:T(8,128)(2,1)S(1)}, bf16[2,4,64,128]{3,2,1,0:T(8,128)(2,1)S(1)}, u32[]{:S(2)}, u32[]{:S(2)}) collective-permute-start(bf16[2,4,64,128]{3,2,1,0:T(8,128)(2,1)S(1)} %fusion.9), channel_id=1, source_target_pairs={{0,1},{1,0},{2,3},{3,2},{4,5},{5,4},{6,7},{7,6},{8,9},{9,8},{10,11... | collective-permute-start | bytes 393224 | tf_op jit(solution)/shard_map/ppermute | solution.py:112
  110.9 13.0 %collective-permute-start.37 = (bf16[2,4,64,128]{3,2,1,0:T(8,128)(2,1)S(1)}, bf16[2,4,64,128]{3,2,1,0:T(8,128)(2,1)S(1)}, u32[]{:S(2)}, u32[]{:S(2)}) collective-permute-start(bf16[2,4,64,128]{3,2,1,0:T(8,128)(2,1)S(1)} %get-tuple-element.86.refs_3_), channel_id=1, source_target_pairs={{0,16},{16,0},{1,17},{17,1},{2,18},{18,2},{3,19},{19,3},{4,20},{20... | collective-permute-start | bytes 393224 | tf_op jit(solution)/shard_map/ppermute | solution.py:112
  112.5 17.0 %collective-permute-start.30 = (bf16[2,4,64,128]{3,2,1,0:T(8,128)(2,1)S(1)}, bf16[2,4,64,128]{3,2,1,0:T(8,128)(2,1)S(1)}, u32[]{:S(2)}, u32[]{:S(2)}) collective-permute-start(bf16[2,4,64,128]{3,2,1,0:T(8,128)(2,1)S(1)} %get-tuple-element.80), channel_id=1, source_target_pairs={{0,2},{1,3},{2,0},{3,1},{4,6},{5,7},{6,4},{7,5},{8,10},{9,11},{10,... | collective-permute-start | bytes 393224 | tf_op jit(solution)/shard_map/ppermute | solution.py:112
  116.7 13.9 %collective-permute-start.31 = (bf16[2,4,64,128]{3,2,1,0:T(8,128)(2,1)S(1)}, bf16[2,4,64,128]{3,2,1,0:T(8,128)(2,1)S(1)}, u32[]{:S(2)}, u32[]{:S(2)}) collective-permute-start(bf16[2,4,64,128]{3,2,1,0:T(8,128)(2,1)S(1)} %get-tuple-element.81), channel_id=1, source_target_pairs={{0,3},{1,2},{2,1},{3,0},{4,7},{5,6},{6,5},{7,4},{8,11},{9,10},{10,... | collective-permute-start | bytes 393224 | tf_op jit(solution)/shard_map/ppermute | solution.py:112
  122.9 9.2 %collective-permute-start.40 = (bf16[2,4,64,128]{3,2,1,0:T(8,128)(2,1)S(1)}, bf16[2,4,64,128]{3,2,1,0:T(8,128)(2,1)S(1)}, u32[]{:S(2)}, u32[]{:S(2)}) collective-permute-start(bf16[2,4,64,128]{3,2,1,0:T(8,128)(2,1)S(1)} %get-tuple-element.87), channel_id=1, source_target_pairs={{0,1},{1,0},{2,3},{3,2},{4,5},{5,4},{6,7},{7,6},{8,9},{9,8},{10,11... | collective-permute-start | bytes 393224 | tf_op jit(solution)/shard_map/ppermute | solution.py:112
  126.2 6.9 %collective-permute-start.38 = (bf16[2,4,64,128]{3,2,1,0:T(8,128)(2,1)S(1)}, bf16[2,4,64,128]{3,2,1,0:T(8,128)(2,1)S(1)}, u32[]{:S(2)}, u32[]{:S(2)}) collective-permute-start(bf16[2,4,64,128]{3,2,1,0:T(8,128)(2,1)S(1)} %get-tuple-element.94), channel_id=1, source_target_pairs={{0,1},{1,0},{2,3},{3,2},{4,5},{5,4},{6,7},{7,6},{8,9},{9,8},{10,11... | collective-permute-start | bytes 393224 | tf_op jit(solution)/shard_map/ppermute | solution.py:112
  127.2 6.3 %collective-permute-start.39 = (bf16[2,4,64,128]{3,2,1,0:T(8,128)(2,1)S(1)}, bf16[2,4,64,128]{3,2,1,0:T(8,128)(2,1)S(1)}, u32[]{:S(2)}, u32[]{:S(2)}) collective-permute-start(bf16[2,4,64,128]{3,2,1,0:T(8,128)(2,1)S(1)} %get-tuple-element.95.refs_11_), channel_id=1, source_target_pairs={{0,16},{16,0},{1,17},{17,1},{2,18},{18,2},{3,19},{19,3},{4,20},{20... | collective-permute-start | bytes 393224 | tf_op jit(solution)/shard_map/ppermute | solution.py:112
  129.5 9.6 %collective-permute-start.44 = (bf16[2,4,64,128]{3,2,1,0:T(8,128)(2,1)S(1)}, bf16[2,4,64,128]{3,2,1,0:T(8,128)(2,1)S(1)}, u32[]{:S(2)}, u32[]{:S(2)}) collective-permute-start(bf16[2,4,64,128]{3,2,1,0:T(8,128)(2,1)S(1)} %get-tuple-element.99), channel_id=1, source_target_pairs={{0,2},{1,3},{2,0},{3,1},{4,6},{5,7},{6,4},{7,5},{8,10},{9,11},{10,... | collective-permute-start | bytes 393224 | tf_op jit(solution)/shard_map/ppermute | solution.py:112
  130.6 9.7 %collective-permute-start.45 = (bf16[2,4,64,128]{3,2,1,0:T(8,128)(2,1)S(1)}, bf16[2,4,64,128]{3,2,1,0:T(8,128)(2,1)S(1)}, u32[]{:S(2)}, u32[]{:S(2)}) collective-permute-start(bf16[2,4,64,128]{3,2,1,0:T(8,128)(2,1)S(1)} %get-tuple-element.100), channel_id=1, source_target_pairs={{0,3},{1,2},{2,1},{3,0},{4,7},{5,6},{6,5},{7,4},{8,11},{9,10},{10,... | collective-permute-start | bytes 393224 | tf_op jit(solution)/shard_map/ppermute | solution.py:112
  132.1 9.0 %collective-permute-start.43 = (bf16[2,4,64,128]{3,2,1,0:T(8,128)(2,1)S(1)}, bf16[2,4,64,128]{3,2,1,0:T(8,128)(2,1)S(1)}, u32[]{:S(2)}, u32[]{:S(2)}) collective-permute-start(bf16[2,4,64,128]{3,2,1,0:T(8,128)(2,1)S(1)} %collective-permute-done.40.refs_2_), channel_id=1, source_target_pairs={{0,16},{16,0},{1,17},{17,1},{2,18},{18,2},{3,19},{19,3},{4,20},{20... | collective-permute-start | bytes 393224 | tf_op jit(solution)/shard_map/ppermute | solution.py:112
  133.6 8.8 %collective-permute-start.41 = (bf16[2,4,64,128]{3,2,1,0:T(8,128)(2,1)S(1)}, bf16[2,4,64,128]{3,2,1,0:T(8,128)(2,1)S(1)}, u32[]{:S(2)}, u32[]{:S(2)}) collective-permute-start(bf16[2,4,64,128]{3,2,1,0:T(8,128)(2,1)S(1)} %collective-permute-done.30.refs_0_), channel_id=1, source_target_pairs={{0,16},{16,0},{1,17},{17,1},{2,18},{18,2},{3,19},{19,3},{4,20},{20... | collective-permute-start | bytes 393224 | tf_op jit(solution)/shard_map/ppermute | solution.py:112
  135.2 7.2 %collective-permute-start.42 = (bf16[2,4,64,128]{3,2,1,0:T(8,128)(2,1)S(1)}, bf16[2,4,64,128]{3,2,1,0:T(8,128)(2,1)S(1)}, u32[]{:S(2)}, u32[]{:S(2)}) collective-permute-start(bf16[2,4,64,128]{3,2,1,0:T(8,128)(2,1)S(1)} %collective-permute-done.31.refs_1_), channel_id=1, source_target_pairs={{0,16},{16,0},{1,17},{17,1},{2,18},{18,2},{3,19},{19,3},{4,20},{20... | collective-permute-start | bytes 393224 | tf_op jit(solution)/shard_map/ppermute | solution.py:112
  139.1 6.4 %collective-permute-start.46 = (bf16[2,4,64,128]{3,2,1,0:T(8,128)(2,1)S(1)}, bf16[2,4,64,128]{3,2,1,0:T(8,128)(2,1)S(1)}, u32[]{:S(2)}, u32[]{:S(2)}) collective-permute-start(bf16[2,4,64,128]{3,2,1,0:T(8,128)(2,1)S(1)} %collective-permute-done.44.refs_8_), channel_id=1, source_target_pairs={{0,16},{16,0},{1,17},{17,1},{2,18},{18,2},{3,19},{19,3},{4,20},{20... | collective-permute-start | bytes 393224 | tf_op jit(solution)/shard_map/ppermute | solution.py:112
  140.3 6.8 %collective-permute-start.47 = (bf16[2,4,64,128]{3,2,1,0:T(8,128)(2,1)S(1)}, bf16[2,4,64,128]{3,2,1,0:T(8,128)(2,1)S(1)}, u32[]{:S(2)}, u32[]{:S(2)}) collective-permute-start(bf16[2,4,64,128]{3,2,1,0:T(8,128)(2,1)S(1)} %collective-permute-done.45.refs_9_), channel_id=1, source_target_pairs={{0,16},{16,0},{1,17},{17,1},{2,18},{18,2},{3,19},{19,3},{4,20},{20... | collective-permute-start | bytes 393224 | tf_op jit(solution)/shard_map/ppermute | solution.py:112
  141.2 7.4 %collective-permute-start.48 = (bf16[2,4,64,128]{3,2,1,0:T(8,128)(2,1)S(1)}, bf16[2,4,64,128]{3,2,1,0:T(8,128)(2,1)S(1)}, u32[]{:S(2)}, u32[]{:S(2)}) collective-permute-start(bf16[2,4,64,128]{3,2,1,0:T(8,128)(2,1)S(1)} %collective-permute-done.38.refs_10_), channel_id=1, source_target_pairs={{0,16},{16,0},{1,17},{17,1},{2,18},{18,2},{3,19},{19,3},{4,20},{20... | collective-permute-start | bytes 393224 | tf_op jit(solution)/shard_map/ppermute | solution.py:112
  154.6 8.4 %collective-permute-start.50 = (bf16[4,2,2,64,128]{4,3,2,1,0:T(8,128)(2,1)S(1)}, bf16[4,2,2,64,128]{4,3,2,1,0:T(8,128)(2,1)S(1)}, u32[]{:S(2)}, u32[]{:S(2)}) collective-permute-start(bf16[4,2,2,64,128]{4,3,2,1,0:T(8,128)(2,1)S(1)} %fusion.3), channel_id=1, source_target_pairs={{0,8},{4,12},{8,0},{12,4},{1,9},{5,13},{9,1},{13,5},{2,10},{6,14},... | collective-permute-start | bytes 786440 | tf_op jit(solution)/shard_map/ppermute | solution.py:112
  163.2 5.1 %collective-permute-start.51 = (bf16[2,2,64,128]{3,2,1,0:T(8,128)(2,1)S(1)}, bf16[2,2,64,128]{3,2,1,0:T(8,128)(2,1)S(1)}, u32[]{:S(2)}, u32[]{:S(2)}) collective-permute-start(bf16[2,2,64,128]{3,2,1,0:T(8,128)(2,1)S(1)} %get-tuple-element.134), channel_id=1, source_target_pairs={{0,1},{1,0},{2,3},{3,2},{4,5},{5,4},{6,7},{7,6},{8,9},{9,8},{10,11... | collective-permute-start | bytes 196616 | tf_op jit(solution)/shard_map/ppermute | solution.py:112
  165.6 7.5 %collective-permute-start.52 = (bf16[2,2,64,128]{3,2,1,0:T(8,128)(2,1)S(1)}, bf16[2,2,64,128]{3,2,1,0:T(8,128)(2,1)S(1)}, u32[]{:S(2)}, u32[]{:S(2)}) collective-permute-start(bf16[2,2,64,128]{3,2,1,0:T(8,128)(2,1)S(1)} %get-tuple-element.133), channel_id=1, source_target_pairs={{0,2},{1,3},{2,0},{3,1},{4,6},{5,7},{6,4},{7,5},{8,10},{9,11},{10,... | collective-permute-start | bytes 196616 | tf_op jit(solution)/shard_map/ppermute | solution.py:112
  166.9 6.2 %collective-permute-start.53 = (bf16[2,2,64,128]{3,2,1,0:T(8,128)(2,1)S(1)}, bf16[2,2,64,128]{3,2,1,0:T(8,128)(2,1)S(1)}, u32[]{:S(2)}, u32[]{:S(2)}) collective-permute-start(bf16[2,2,64,128]{3,2,1,0:T(8,128)(2,1)S(1)} %get-tuple-element.132), channel_id=1, source_target_pairs={{0,3},{1,2},{2,1},{3,0},{4,7},{5,6},{6,5},{7,4},{8,11},{9,10},{10,... | collective-permute-start | bytes 196616 | tf_op jit(solution)/shard_map/ppermute | solution.py:112
  174.8 6.6 %collective-permute-start.55 = (bf16[2,2,64,128]{3,2,1,0:T(8,128)(2,1)S(1)}, bf16[2,2,64,128]{3,2,1,0:T(8,128)(2,1)S(1)}, u32[]{:S(2)}, u32[]{:S(2)}) collective-permute-start(bf16[2,2,64,128]{3,2,1,0:T(8,128)(2,1)S(1)} %get-tuple-element.106), channel_id=1, source_target_pairs={{0,3},{1,2},{2,1},{3,0},{4,7},{5,6},{6,5},{7,4},{8,11},{9,10},{10,... | collective-permute-start | bytes 196616 | tf_op jit(solution)/shard_map/ppermute | solution.py:112
  177.3 5.3 %collective-permute-start.58 = (bf16[2,2,64,128]{3,2,1,0:T(8,128)(2,1)S(1)}, bf16[2,2,64,128]{3,2,1,0:T(8,128)(2,1)S(1)}, u32[]{:S(2)}, u32[]{:S(2)}) collective-permute-start(bf16[2,2,64,128]{3,2,1,0:T(8,128)(2,1)S(1)} %get-tuple-element.107), channel_id=1, source_target_pairs={{0,1},{1,0},{2,3},{3,2},{4,5},{5,4},{6,7},{7,6},{8,9},{9,8},{10,11... | collective-permute-start | bytes 196616 | tf_op jit(solution)/shard_map/ppermute | solution.py:112
  177.6 5.0 %collective-permute-start.60 = (bf16[2,2,64,128]{3,2,1,0:T(8,128)(2,1)S(1)}, bf16[2,2,64,128]{3,2,1,0:T(8,128)(2,1)S(1)}, u32[]{:S(2)}, u32[]{:S(2)}) collective-permute-start(bf16[2,2,64,128]{3,2,1,0:T(8,128)(2,1)S(1)} %get-tuple-element.105.refs_14_), channel_id=1, source_target_pairs={{0,8},{4,12},{8,0},{12,4},{1,9},{5,13},{9,1},{13,5},{2,10},{6,14},... | collective-permute-start | bytes 196616 | tf_op jit(solution)/shard_map/ppermute | solution.py:112
  178.5 5.2 %collective-permute-start.62 = (bf16[2,2,64,128]{3,2,1,0:T(8,128)(2,1)S(1)}, bf16[2,2,64,128]{3,2,1,0:T(8,128)(2,1)S(1)}, u32[]{:S(2)}, u32[]{:S(2)}) collective-permute-start(bf16[2,2,64,128]{3,2,1,0:T(8,128)(2,1)S(1)} %get-tuple-element.108), channel_id=1, source_target_pairs={{0,2},{1,3},{2,0},{3,1},{4,6},{5,7},{6,4},{7,5},{8,10},{9,11},{10,... | collective-permute-start | bytes 196616 | tf_op jit(solution)/shard_map/ppermute | solution.py:112
  180.1 4.7 %collective-permute-start.54 = (bf16[2,2,64,128]{3,2,1,0:T(8,128)(2,1)S(1)}, bf16[2,2,64,128]{3,2,1,0:T(8,128)(2,1)S(1)}, u32[]{:S(2)}, u32[]{:S(2)}) collective-permute-start(bf16[2,2,64,128]{3,2,1,0:T(8,128)(2,1)S(1)} %get-tuple-element.105.refs_14_), channel_id=1, source_target_pairs={{0,4},{4,0},{8,12},{12,8},{1,5},{5,1},{9,13},{13,9},{2,6},{6,2},{1... | collective-permute-start | bytes 196616 | tf_op jit(solution)/shard_map/ppermute | solution.py:112
  181.4 4.3 %collective-permute-start.56 = (bf16[2,2,64,128]{3,2,1,0:T(8,128)(2,1)S(1)}, bf16[2,2,64,128]{3,2,1,0:T(8,128)(2,1)S(1)}, u32[]{:S(2)}, u32[]{:S(2)}) collective-permute-start(bf16[2,2,64,128]{3,2,1,0:T(8,128)(2,1)S(1)} %collective-permute-done.55.refs_1_), channel_id=1, source_target_pairs={{0,8},{4,12},{8,0},{12,4},{1,9},{5,13},{9,1},{13,5},{2,10},{6,14},... | collective-permute-start | bytes 196616 | tf_op jit(solution)/shard_map/ppermute | solution.py:112
  184.8 4.3 %collective-permute-start.64 = (bf16[2,2,64,128]{3,2,1,0:T(8,128)(2,1)S(1)}, bf16[2,2,64,128]{3,2,1,0:T(8,128)(2,1)S(1)}, u32[]{:S(2)}, u32[]{:S(2)}) collective-permute-start(bf16[2,2,64,128]{3,2,1,0:T(8,128)(2,1)S(1)} %collective-permute-done.58.refs_11_), channel_id=1, source_target_pairs={{0,8},{4,12},{8,0},{12,4},{1,9},{5,13},{9,1},{13,5},{2,10},{6,14},... | collective-permute-start | bytes 196616 | tf_op jit(solution)/shard_map/ppermute | solution.py:112
  194.3 9.2 %collective-permute-start.69 = (bf16[2,2,4,64,128]{4,3,2,1,0:T(8,128)(2,1)S(1)}, bf16[2,2,4,64,128]{4,3,2,1,0:T(8,128)(2,1)S(1)}, u32[]{:S(2)}, u32[]{:S(2)}) collective-permute-start(bf16[2,2,4,64,128]{4,3,2,1,0:T(8,128)(2,1)S(1)} %get-tuple-element.110), channel_id=1, source_target_pairs={{0,16},{16,0},{1,17},{17,1},{2,18},{18,2},{3,19},{19,3},{4,20},{20... | collective-permute-start | bytes 786440 | tf_op jit(solution)/shard_map/ppermute | solution.py:112
  196.1 13.1 %collective-permute-start.72 = (bf16[2,2,4,64,128]{4,3,2,1,0:T(8,128)(2,1)S(1)}, bf16[2,2,4,64,128]{4,3,2,1,0:T(8,128)(2,1)S(1)}, u32[]{:S(2)}, u32[]{:S(2)}) collective-permute-start(bf16[2,2,4,64,128]{4,3,2,1,0:T(8,128)(2,1)S(1)} %get-tuple-element.112), channel_id=1, source_target_pairs={{0,16},{16,0},{1,17},{17,1},{2,18},{18,2},{3,19},{19,3},{4,20},{20... | collective-permute-start | bytes 786440 | tf_op jit(solution)/shard_map/ppermute | solution.py:112
  196.4 18.4 %collective-permute-start.75 = (bf16[2,2,4,64,128]{4,3,2,1,0:T(8,128)(2,1)S(1)}, bf16[2,2,4,64,128]{4,3,2,1,0:T(8,128)(2,1)S(1)}, u32[]{:S(2)}, u32[]{:S(2)}) collective-permute-start(bf16[2,2,4,64,128]{4,3,2,1,0:T(8,128)(2,1)S(1)} %get-tuple-element.114), channel_id=1, source_target_pairs={{0,16},{16,0},{1,17},{17,1},{2,18},{18,2},{3,19},{19,3},{4,20},{20... | collective-permute-start | bytes 786440 | tf_op jit(solution)/shard_map/ppermute | solution.py:112
  198.1 23.1 %collective-permute-start.78 = (bf16[2,2,4,64,128]{4,3,2,1,0:T(8,128)(2,1)S(1)}, bf16[2,2,4,64,128]{4,3,2,1,0:T(8,128)(2,1)S(1)}, u32[]{:S(2)}, u32[]{:S(2)}) collective-permute-start(bf16[2,2,4,64,128]{4,3,2,1,0:T(8,128)(2,1)S(1)} %get-tuple-element.116), channel_id=1, source_target_pairs={{0,16},{16,0},{1,17},{17,1},{2,18},{18,2},{3,19},{19,3},{4,20},{20... | collective-permute-start | bytes 786440 | tf_op jit(solution)/shard_map/ppermute | solution.py:112
  203.6 12.9 %collective-permute-start.70 = (bf16[2,4,64,128]{3,2,1,0:T(8,128)(2,1)S(1)}, bf16[2,4,64,128]{3,2,1,0:T(8,128)(2,1)S(1)}, u32[]{:S(2)}, u32[]{:S(2)}) collective-permute-start(bf16[2,4,64,128]{3,2,1,0:T(8,128)(2,1)S(1)} %get-tuple-element.127), channel_id=1, source_target_pairs={{0,2},{1,3},{2,0},{3,1},{4,6},{5,7},{6,4},{7,5},{8,10},{9,11},{10,... | collective-permute-start | bytes 393224 | tf_op jit(solution)/shard_map/ppermute | solution.py:112
  205.4 13.6 %collective-permute-start.71 = (bf16[2,4,64,128]{3,2,1,0:T(8,128)(2,1)S(1)}, bf16[2,4,64,128]{3,2,1,0:T(8,128)(2,1)S(1)}, u32[]{:S(2)}, u32[]{:S(2)}) collective-permute-start(bf16[2,4,64,128]{3,2,1,0:T(8,128)(2,1)S(1)} %get-tuple-element.126), channel_id=1, source_target_pairs={{0,3},{1,2},{2,1},{3,0},{4,7},{5,6},{6,5},{7,4},{8,11},{9,10},{10,... | collective-permute-start | bytes 393224 | tf_op jit(solution)/shard_map/ppermute | solution.py:112
  209.2 9.8 %collective-permute-start.73 = (bf16[2,4,64,128]{3,2,1,0:T(8,128)(2,1)S(1)}, bf16[2,4,64,128]{3,2,1,0:T(8,128)(2,1)S(1)}, u32[]{:S(2)}, u32[]{:S(2)}) collective-permute-start(bf16[2,4,64,128]{3,2,1,0:T(8,128)(2,1)S(1)} %fusion.12), channel_id=1, source_target_pairs={{0,1},{1,0},{2,3},{3,2},{4,5},{5,4},{6,7},{7,6},{8,9},{9,8},{10,11... | collective-permute-start | bytes 393224 | tf_op jit(solution)/shard_map/ppermute | solution.py:112
  214.9 11.8 %collective-permute-start.76 = (bf16[2,4,64,128]{3,2,1,0:T(8,128)(2,1)S(1)}, bf16[2,4,64,128]{3,2,1,0:T(8,128)(2,1)S(1)}, u32[]{:S(2)}, u32[]{:S(2)}) collective-permute-start(bf16[2,4,64,128]{3,2,1,0:T(8,128)(2,1)S(1)} %get-tuple-element.125), channel_id=1, source_target_pairs={{0,2},{1,3},{2,0},{3,1},{4,6},{5,7},{6,4},{7,5},{8,10},{9,11},{10,... | collective-permute-start | bytes 393224 | tf_op jit(solution)/shard_map/ppermute | solution.py:112
  216.6 10.1 %collective-permute-start.77 = (bf16[2,4,64,128]{3,2,1,0:T(8,128)(2,1)S(1)}, bf16[2,4,64,128]{3,2,1,0:T(8,128)(2,1)S(1)}, u32[]{:S(2)}, u32[]{:S(2)}) collective-permute-start(bf16[2,4,64,128]{3,2,1,0:T(8,128)(2,1)S(1)} %get-tuple-element.124), channel_id=1, source_target_pairs={{0,3},{1,2},{2,1},{3,0},{4,7},{5,6},{6,5},{7,4},{8,11},{9,10},{10,... | collective-permute-start | bytes 393224 | tf_op jit(solution)/shard_map/ppermute | solution.py:112
  221.3 6.5 %collective-permute-start.79 = (bf16[2,4,64,128]{3,2,1,0:T(8,128)(2,1)S(1)}, bf16[2,4,64,128]{3,2,1,0:T(8,128)(2,1)S(1)}, u32[]{:S(2)}, u32[]{:S(2)}) collective-permute-start(bf16[2,4,64,128]{3,2,1,0:T(8,128)(2,1)S(1)} %fusion.15), channel_id=1, source_target_pairs={{0,1},{1,0},{2,3},{3,2},{4,5},{5,4},{6,7},{7,6},{8,9},{9,8},{10,11... | collective-permute-start | bytes 393224 | tf_op jit(solution)/shard_map/ppermute | solution.py:112
  221.4 10.4 %collective-permute-start.82 = (bf16[4,2,2,64,128]{4,3,2,1,0:T(8,128)(2,1)S(1)}, bf16[4,2,2,64,128]{4,3,2,1,0:T(8,128)(2,1)}, u32[]{:S(2)}, u32[]{:S(2)}) collective-permute-start(bf16[4,2,2,64,128]{4,3,2,1,0:T(8,128)(2,1)S(1)} %get-tuple-element.123.refs_0_), channel_id=1, source_target_pairs={{0,8},{4,12},{8,0},{12,4},{1,9},{5,13},{9,1},{13,5},{2,10},{6,14},... | collective-permute-start | bytes 786440 | tf_op jit(solution)/shard_map/ppermute | solution.py:112
  222.3 20.5 %collective-permute-start.74 = (bf16[2,4,4,64,128]{4,3,2,1,0:T(8,128)(2,1)S(1)}, bf16[2,4,4,64,128]{4,3,2,1,0:T(8,128)(2,1)S(1)}, u32[]{:S(2)}, u32[]{:S(2)}) collective-permute-start(bf16[2,4,4,64,128]{4,3,2,1,0:T(8,128)(2,1)S(1)} %mute_receiver.6.refs_0_), channel_id=1, source_target_pairs={{0,16},{16,0},{1,17},{17,1},{2,18},{18,2},{3,19},{19,3},{4,20},{20... | collective-permute-start | bytes 1572872 | tf_op jit(solution)/shard_map/ppermute | solution.py:112
  230.1 16.1 %collective-permute-start.80 = (bf16[2,4,4,64,128]{4,3,2,1,0:T(8,128)(2,1)S(1)}, bf16[2,4,4,64,128]{4,3,2,1,0:T(8,128)(2,1)}, u32[]{:S(2)}, u32[]{:S(2)}) collective-permute-start(bf16[2,4,4,64,128]{4,3,2,1,0:T(8,128)(2,1)S(1)} %mute_receiver.7.refs_1_), channel_id=1, source_target_pairs={{0,16},{16,0},{1,17},{17,1},{2,18},{18,2},{3,19},{19,3},{4,20},{20... | collective-permute-start | bytes 1572872 | tf_op jit(solution)/shard_map/ppermute | solution.py:112
  (24 other events, 150.9 us)

commit v5 on v4

--- a/solution.py
+++ b/solution.py
@@ -13,6 +13,7 @@
 ITERS = 2
 LANES = 128
 BLOCK_W = 16
+PITCH = 24
 HALVES = 2
 GROUP_ORDER = (4, 3, 15, 5, 12, 2, 6, 9, 7, 14, 11, 1, 10, 13, 0, 8)
 F32 = jnp.float32
@@ -226,9 +227,9 @@
         window = pl.ds(first, BLOCK_W)
 
         def put(place, k, c, start, value):
-            size = value.shape[0] * BLOCK_W
-            at = ((k * 2 + c) * focal + start) * BLOCK_W
-            hold[place, at : at + size, :] = value.astype(F32).reshape(size, LANES)
+            for p in range(value.shape[0]):
+                at = ((k * 2 + c) * focal + start + p) * PITCH
+                hold[place, at : at + BLOCK_W, :] = value[p].astype(F32)
 
         for ref, (kind, k, start) in zip(ins, plan):
             for c in range(2):
@@ -240,7 +241,7 @@
                 else:
                     put(1 - half, k, c, start, ref[c, :, window, :])
         for w in range(BLOCK_W):
-            step = pl.ds(w, rows, stride=BLOCK_W)
+            step = pl.ds(w, rows, stride=PITCH)
             left = jnp.concatenate([hold[0, step, :], hold[1, step, :]], 1).astype(BF16)
             right = refl_ref[:, first + w].reshape(2 * sources, 2 * LANES)
             both = lax.dot_general(
@@ -252,17 +253,15 @@
                 [by_real[:, 0] - by_imag[:, 1], by_real[:, 1] + by_imag[:, 0]], 1
             )
             result[step, :] = value.reshape(rows, LANES)
-        size = share * BLOCK_W
         for place, out in ((0, keep_ref), (1, send_ref)):
             for y in range(2):
                 group = (2 * y + place) ^ me
                 for k in range(pieces):
                     for c in range(2):
-                        start = ((k * 2 + c) * focal + group * share) * BLOCK_W
-                        part = result[pl.ds(pl.multiple_of(start, size), size), :]
-                        out[y, k, c, :, window, :] = part.reshape(
-                            share, BLOCK_W, LANES
-                        ).astype(BF16)
+                        for p in range(share):
+                            start = ((k * 2 + c) * focal + group * share + p) * PITCH
+                            part = result[pl.ds(pl.multiple_of(start, 8), BLOCK_W), :]
+                            out[y, k, c, p, window, :] = part.astype(BF16)
         return carry
 
     lax.fori_loop(0, refl_ref.shape[1] // BLOCK_W, block, 0)
@@ -280,8 +279,8 @@
         freq * (2 * sources * 512 + rows * 768),
         (ids, reflection, *arrays),
         [
-            pltpu.VMEM((2, rows * BLOCK_W, LANES), F32),
-            pltpu.VMEM((rows * BLOCK_W, LANES), F32),
+            pltpu.VMEM((2, rows * PITCH, LANES), F32),
+            pltpu.VMEM((rows * PITCH, LANES), F32),
         ],
     )
 
@@ -300,16 +299,16 @@
     def block(b, carry):
         first = pl.multiple_of(b * BLOCK_W, BLOCK_W)
         window = pl.ds(first, BLOCK_W)
-        size = share * BLOCK_W
         for j in range(4):
             group = j ^ me
             for k in range(pieces):
-                start = pl.multiple_of((k * focal + group * share) * BLOCK_W, size)
-                for c in range(2):
-                    value = ins[j][k][c, :, window, :].astype(F32).reshape(size, LANES)
-                    hold[c, pl.ds(start, size), :] = value
+                for p in range(share):
+                    start = pl.multiple_of((k * focal + group * share + p) * PITCH, 8)
+                    for c in range(2):
+                        value = ins[j][k][c, p, window, :].astype(F32)
+                        hold[c, pl.ds(start, BLOCK_W), :] = value
         for w in range(BLOCK_W):
-            step = pl.ds(w, rows, stride=BLOCK_W)
+            step = pl.ds(w, rows, stride=PITCH)
             real = hold[0, step, :].astype(BF16)
             imag = hold[1, step, :].astype(BF16)
             left = jnp.concatenate(
@@ -319,21 +318,19 @@
             value = lax.dot_general(
                 left, right, (((1,), (0,)), ((), ())), preferred_element_type=F32
             )
-            step = pl.ds(w, 2 * rows, stride=BLOCK_W)
+            step = pl.ds(w, 2 * rows, stride=PITCH)
             result[0, step, :] = value[:, :LANES]
             result[1, step, :] = value[:, LANES:]
-        size = part_size * BLOCK_W
         index = 0
         for place in (half, 1 - half):
             for q in range(HALVES):
                 for group in PAIRS:
                     for i, k in enumerate(group):
                         for c in range(2):
-                            at = ((c * pieces + k) * focal + q * part_size) * BLOCK_W
-                            part = result[place, at : at + size, :]
-                            outs[index][i, c, :, window, :] = part.reshape(
-                                part_size, BLOCK_W, LANES
-                            ).astype(BF16)
+                            for p in range(part_size):
+                                at = ((c * pieces + k) * focal + q * part_size + p) * PITCH
+                                part = result[place, at : at + BLOCK_W, :]
+                                outs[index][i, c, p, window, :] = part.astype(BF16)
                     index += 1
         return carry
 
@@ -359,8 +356,8 @@
         freq * (2 * sources * 512 + rows * 768),
         (ids, reflection, *[groups[i // pieces][i % pieces] for i in GROUP_ORDER]),
         [
-            pltpu.VMEM((2, rows // 2 * BLOCK_W, LANES), F32),
-            pltpu.VMEM((2, rows * BLOCK_W, LANES), F32),
+            pltpu.VMEM((2, rows // 2 * PITCH, LANES), F32),
+            pltpu.VMEM((2, rows * PITCH, LANES), F32),
         ],
     )
     return results[:count], results[count:]

time: 250 us -> 248 us (level)
  no operation moved by 1% of the time
where the time goes in v5:
time: 248 us
  waiting for transfers between devices  103 us (42%)
  starting transfers between devices  95.3 us (38%)
  Pallas kernels  46 us (19%)
    ppermute x84, waiting for transfers between devices, swap(): return lax.ppermute(value, axis, [(i, i ^ mask) for i in range(count)])  103 us
    ppermute x84, starting transfers between devices, swap(): return lax.ppermute(value, axis, [(i, i ^ mask) for i in range(count)])  95.3 us
    pallas_call x11, Pallas kernels, call(): pl.pallas_call(kernel, name=name, out_shape=out_shape, in_specs=[SMEM_SPE...  30.6 us
    pallas_call x1, Pallas kernels, trace_source(): pl.pallas_call(trace_kernel, name='trace_source', out_shape=jax.ShapeDtyp...  6.28 us
    pallas_call x2, Pallas kernels, join_halves(): pl.pallas_call(join_kernel, name='join_halves', out_shape=jax.ShapeDtypeS...  5.85 us
  transfers between devices with their start and end apart: 84, of which 40 were waited for; matrix products, arithmetic and copies ran while one was open for 0% of the time, Pallas kernels for 10%

profile of v5, /device:TPU:0, one launch (start us, length us, event | category | flops | bytes accessed | tf_op | source)
XLA Modules:
  0.0 247.8 jit_solution(11585799544804824946)
XLA Ops:
  0.7 1.6 copy-done.1
  3.1 4.1 %collective-permute-start = (bf16[2,8,64,128]{3,2,1,0:T(8,128)(2,1)S(1)}, bf16[2,8,64,128]{3,2,1,0:T(8,128)(2,1)S(1)}, u32[]{:S(2)}, u32[]{:S(2)}) collective-permute-start(bf16[2,8,64,128]{3,2,1,0:T(8,128)(2,1)S(1)} %split_wave.6.refs_7_), channel_id=1, source_target_pairs={{0,2},{1,3},{2,0},{3,1},{4,6},{5,7},{6,4},{7,5},{8,10},{9,11},{10,... | collective-permute-start | bytes 786440 | tf_op jit(solution)/shard_map/ppermute | solution.py:113
  7.2 4.1 %basis.1 = (bf16[512,1024]{1,0:T(8,128)(2,1)S(1)}, bf16[1024,512]{1,0:T(8,128)(2,1)S(1)}) custom-call(s32[3]{0:T(128)S(1)} %pad_add_fusion.ids), custom_call_target="tpu_custom_call" | custom-call | flops 20971520 | bytes 2097152 | tf_op jit(solution)/shard_map/basis/pallas_call | solution.py:118
  14.7 10.9 %collective-permute-done.refs_1_ = bf16[2,8,64,128]{3,2,1,0:T(8,128)(2,1)S(1)} collective-permute-done((bf16[2,8,64,128]{3,2,1,0:T(8,128)(2,1)S(1)}, bf16[2,8,64,128]{3,2,1,0:T(8,128)(2,1)S(1)}, u32[]{:S(2)}, u32[]{:S(2)}) %collective-permute-start) | collective-permute-done | bytes 262176 | tf_op jit(solution)/shard_map/ppermute | solution.py:113
  25.6 1.8 collective-permute-start.1
  28.5 6.3 %collective-permute-done.1.refs_2_ = bf16[2,8,64,128]{3,2,1,0:T(8,128)(2,1)S(1)} collective-permute-done((bf16[2,8,64,128]{3,2,1,0:T(8,128)(2,1)S(1)}, bf16[2,8,64,128]{3,2,1,0:T(8,128)(2,1)S(1)}, u32[]{:S(2)}, u32[]{:S(2)}) %collective-permute-start.1) | collective-permute-done | bytes 262176 | tf_op jit(solution)/shard_map/ppermute | solution.py:113
  34.8 3.0 %collective-permute-done.3.refs_4_ = bf16[2,8,64,128]{3,2,1,0:T(8,128)(2,1)S(1)} collective-permute-done((bf16[2,8,64,128]{3,2,1,0:T(8,128)(2,1)S(1)}, bf16[2,8,64,128]{3,2,1,0:T(8,128)(2,1)S(1)}, u32[]{:S(2)}, u32[]{:S(2)}) %collective-permute-start.3) | collective-permute-done | bytes 262176 | tf_op jit(solution)/shard_map/ppermute | solution.py:113
  37.9 3.8 %convolve.2 = (bf16[2,4,2,2,64,128]{5,4,3,2,1,0:T(8,128)(2,1)S(1)}, bf16[2,4,2,2,64,128]{5,4,3,2,1,0:T(8,128)(2,1)S(1)}) custom-call(s32[3]{0:T(128)S(1)} %pad_add_fusion.ids, bf16[2,64,128,256]{3,2,1,0:T(8,128)(2,1)S(1)} %copy-done, bf16[2,2,8,64,128]{4,3,2,1,0:T(8,128)(2,1)S(1)} %split_wave.5.refs_0_.refs_5_, ...), custom_call_target="tpu_custom_call" | custom-call | flops 536870912 | bytes 11534336 | tf_op jit(solution)/shard_map/convolve/pallas_call | solution.py:118
  41.8 1.9 collective-permute-done.5
  45.1 7.1 %collective-permute-done.6 = bf16[4,2,2,64,128]{4,3,2,1,0:T(8,128)(2,1)S(1)} collective-permute-done((bf16[4,2,2,64,128]{4,3,2,1,0:T(8,128)(2,1)S(1)}, bf16[4,2,2,64,128]{4,3,2,1,0:T(8,128)(2,1)S(1)}, u32[]{:S(2)}, u32[]{:S(2)}) %collective-permute-start.6) | collective-permute-done | bytes 262176 | tf_op jit(solution)/shard_map/ppermute | solution.py:113
  52.4 1.5 collective-permute-start.7
  53.9 3.4 %collective-permute-start.8 = (bf16[2,2,64,128]{3,2,1,0:T(8,128)(2,1)S(1)}, bf16[2,2,64,128]{3,2,1,0:T(8,128)(2,1)S(1)}, u32[]{:S(2)}, u32[]{:S(2)}) collective-permute-start(bf16[2,2,64,128]{3,2,1,0:T(8,128)(2,1)S(1)} %get-tuple-element.137), channel_id=1, source_target_pairs={{0,2},{1,3},{2,0},{3,1},{4,6},{5,7},{6,4},{7,5},{8,10},{9,11},{10,... | collective-permute-start | bytes 196616 | tf_op jit(solution)/shard_map/ppermute | solution.py:113
  57.3 4.1 %collective-permute-done.8.refs_2_ = bf16[2,2,64,128]{3,2,1,0:T(8,128)(2,1)S(1)} collective-permute-done((bf16[2,2,64,128]{3,2,1,0:T(8,128)(2,1)S(1)}, bf16[2,2,64,128]{3,2,1,0:T(8,128)(2,1)S(1)}, u32[]{:S(2)}, u32[]{:S(2)}) %collective-permute-start.8) | collective-permute-done | bytes 65568 | tf_op jit(solution)/shard_map/ppermute | solution.py:113
  61.4 1.9 collective-permute-done.9.refs_3_
  63.3 1.7 mute_source.2
  66.8 1.5 collective-permute-start.16
  68.3 2.6 %collective-permute-start.18 = (bf16[2,2,64,128]{3,2,1,0:T(8,128)(2,1)S(1)}, bf16[2,2,64,128]{3,2,1,0:T(8,128)(2,1)S(1)}, u32[]{:S(2)}, u32[]{:S(2)}) collective-permute-start(bf16[2,2,64,128]{3,2,1,0:T(8,128)(2,1)S(1)} %get-tuple-element.75), channel_id=1, source_target_pairs={{0,2},{1,3},{2,0},{3,1},{4,6},{5,7},{6,4},{7,5},{8,10},{9,11},{10,... | collective-permute-start | bytes 196616 | tf_op jit(solution)/shard_map/ppermute | solution.py:113
  74.0 1.5 collective-permute-start.20
  76.1 1.9 collective-permute-done.22.refs_12_
  80.0 3.2 %correlate.2 = (bf16[2,2,4,64,128]{4,3,2,1,0:T(8,128)(2,1)S(1)}, bf16[2,2,4,64,128]{4,3,2,1,0:T(8,128)(2,1)S(1)}, bf16[2,2,4,64,128]{4,3,2,1,0:T(8,128)(2,1)S(1)...) custom-call(s32[3]{0:T(128)S(1)} %pad_add_fusion.ids, ...), custom_call_target="tpu_custom_call" | custom-call | flops 536870912 | bytes 11534336 | tf_op jit(solution)/shard_map/correlate/pallas_call | solution.py:118
  83.2 1.6 collective-permute-start.25
  87.3 5.1 %collective-permute-done.25 = bf16[2,2,4,64,128]{4,3,2,1,0:T(8,128)(2,1)S(1)} collective-permute-done((bf16[2,2,4,64,128]{4,3,2,1,0:T(8,128)(2,1)S(1)}, bf16[2,2,4,64,128]{4,3,2,1,0:T(8,128)(2,1)S(1)}, u32[]{:S(2)}, u32[]{:S(2)}) %collective-permute-start.25) | collective-permute-done | bytes 262176 | tf_op jit(solution)/shard_map/ppermute | solution.py:113
  92.5 2.4 collective-permute-start.26
  96.3 1.7 collective-permute-done.28.refs_4_
  99.5 4.1 %collective-permute-done.32 = bf16[2,2,4,64,128]{4,3,2,1,0:T(8,128)(2,1)S(1)} collective-permute-done((bf16[2,2,4,64,128]{4,3,2,1,0:T(8,128)(2,1)S(1)}, bf16[2,2,4,64,128]{4,3,2,1,0:T(8,128)(2,1)S(1)}, u32[]{:S(2)}, u32[]{:S(2)}) %collective-permute-start.32) | collective-permute-done | bytes 262176 | tf_op jit(solution)/shard_map/ppermute | solution.py:113
  103.8 2.4 collective-permute-start.33
  107.6 2.3 mute_receiver.4
  110.0 1.5 collective-permute-start.37
  111.5 2.9 %collective-permute-start.30 = (bf16[2,4,64,128]{3,2,1,0:T(8,128)(2,1)S(1)}, bf16[2,4,64,128]{3,2,1,0:T(8,128)(2,1)S(1)}, u32[]{:S(2)}, u32[]{:S(2)}) collective-permute-start(bf16[2,4,64,128]{3,2,1,0:T(8,128)(2,1)S(1)} %get-tuple-element.80), channel_id=1, source_target_pairs={{0,2},{1,3},{2,0},{3,1},{4,6},{5,7},{6,4},{7,5},{8,10},{9,11},{10,... | collective-permute-start | bytes 393224 | tf_op jit(solution)/shard_map/ppermute | solution.py:113
  115.7 6.2 %collective-permute-start.31 = (bf16[2,4,64,128]{3,2,1,0:T(8,128)(2,1)S(1)}, bf16[2,4,64,128]{3,2,1,0:T(8,128)(2,1)S(1)}, u32[]{:S(2)}, u32[]{:S(2)}) collective-permute-start(bf16[2,4,64,128]{3,2,1,0:T(8,128)(2,1)S(1)} %get-tuple-element.81), channel_id=1, source_target_pairs={{0,3},{1,2},{2,1},{3,0},{4,7},{5,6},{6,5},{7,4},{8,11},{9,10},{10,... | collective-permute-start | bytes 393224 | tf_op jit(solution)/shard_map/ppermute | solution.py:113
  123.0 2.2 mute_receiver.5
  126.3 1.6 collective-permute-start.39
  132.6 1.6 collective-permute-start.41
  134.7 3.5 %collective-permute-done.44.refs_8_ = bf16[2,4,64,128]{3,2,1,0:T(8,128)(2,1)S(1)} collective-permute-done((bf16[2,4,64,128]{3,2,1,0:T(8,128)(2,1)S(1)}, bf16[2,4,64,128]{3,2,1,0:T(8,128)(2,1)S(1)}, u32[]{:S(2)}, u32[]{:S(2)}) %collective-permute-start.44) | collective-permute-done | bytes 131104 | tf_op jit(solution)/shard_map/ppermute | solution.py:113
  141.4 3.2 %collective-permute-done.46.refs_12_ = bf16[2,4,64,128]{3,2,1,0:T(8,128)(2,1)S(1)} collective-permute-done((bf16[2,4,64,128]{3,2,1,0:T(8,128)(2,1)S(1)}, bf16[2,4,64,128]{3,2,1,0:T(8,128)(2,1)S(1)}, u32[]{:S(2)}, u32[]{:S(2)}) %collective-permute-start.46) | collective-permute-done | bytes 131104 | tf_op jit(solution)/shard_map/ppermute | solution.py:113
  144.6 1.6 collective-permute-done.47.refs_13_
  147.6 3.8 %convolve.3 = (bf16[2,4,2,2,64,128]{5,4,3,2,1,0:T(8,128)(2,1)S(1)}, bf16[2,4,2,2,64,128]{5,4,3,2,1,0:T(8,128)(2,1)S(1)}) custom-call(s32[3]{0:T(128)S(1)} %pad_add_fusion.ids, bf16[2,64,128,256]{3,2,1,0:T(8,128)(2,1)S(1)} %copy-done, bf16[2,4,64,128]{3,2,1,0:T(8,128)(2,1)S(1)} %collective-permute-done.30.refs_0_, ...), custom_call_target="tpu_custom_call" | custom-call | flops 536870912 | bytes 11534336 | tf_op jit(solution)/shard_map/convolve/pallas_call | solution.py:118
  151.5 1.9 collective-permute-done.49
  154.5 7.4 %collective-permute-done.50 = bf16[4,2,2,64,128]{4,3,2,1,0:T(8,128)(2,1)S(1)} collective-permute-done((bf16[4,2,2,64,128]{4,3,2,1,0:T(8,128)(2,1)S(1)}, bf16[4,2,2,64,128]{4,3,2,1,0:T(8,128)(2,1)S(1)}, u32[]{:S(2)}, u32[]{:S(2)}) %collective-permute-start.50) | collective-permute-done | bytes 262176 | tf_op jit(solution)/shard_map/ppermute | solution.py:113
  162.1 2.4 collective-permute-start.51
  167.2 4.8 %collective-permute-done.52.refs_2_ = bf16[2,2,64,128]{3,2,1,0:T(8,128)(2,1)S(1)} collective-permute-done((bf16[2,2,64,128]{3,2,1,0:T(8,128)(2,1)S(1)}, bf16[2,2,64,128]{3,2,1,0:T(8,128)(2,1)S(1)}, u32[]{:S(2)}, u32[]{:S(2)}) %collective-permute-start.52) | collective-permute-done | bytes 65568 | tf_op jit(solution)/shard_map/ppermute | solution.py:113
  172.0 1.7 mute_source.3
  173.7 2.4 collective-permute-start.55
  177.4 1.6 collective-permute-start.62
  185.2 1.6 collective-permute-done.66.refs_12_
  189.2 3.2 %correlate.3 = (bf16[2,2,4,64,128]{4,3,2,1,0:T(8,128)(2,1)S(1)}, bf16[2,2,4,64,128]{4,3,2,1,0:T(8,128)(2,1)S(1)}, bf16[2,2,4,64,128]{4,3,2,1,0:T(8,128)(2,1)S(1)...) custom-call(s32[3]{0:T(128)S(1)} %pad_add_fusion.ids, ...), custom_call_target="tpu_custom_call" | custom-call | flops 536870912 | bytes 11534336 | tf_op jit(solution)/shard_map/correlate/pallas_call | solution.py:118
  192.5 1.7 collective-permute-start.69
  194.6 1.7 collective-permute-start.75
  196.6 5.1 %collective-permute-done.69 = bf16[2,2,4,64,128]{4,3,2,1,0:T(8,128)(2,1)S(1)} collective-permute-done((bf16[2,2,4,64,128]{4,3,2,1,0:T(8,128)(2,1)S(1)}, bf16[2,2,4,64,128]{4,3,2,1,0:T(8,128)(2,1)S(1)}, u32[]{:S(2)}, u32[]{:S(2)}) %collective-permute-start.69) | collective-permute-done | bytes 262176 | tf_op jit(solution)/shard_map/ppermute | solution.py:113
  201.8 1.7 collective-permute-start.70
  203.5 2.4 collective-permute-start.71
  207.3 1.7 collective-permute-start.73
  209.1 3.8 %collective-permute-done.75 = bf16[2,2,4,64,128]{4,3,2,1,0:T(8,128)(2,1)S(1)} collective-permute-done((bf16[2,2,4,64,128]{4,3,2,1,0:T(8,128)(2,1)S(1)}, bf16[2,2,4,64,128]{4,3,2,1,0:T(8,128)(2,1)S(1)}, u32[]{:S(2)}, u32[]{:S(2)}) %collective-permute-start.75) | collective-permute-done | bytes 262176 | tf_op jit(solution)/shard_map/ppermute | solution.py:113
  213.0 1.7 collective-permute-start.76
  214.7 2.4 collective-permute-start.77
  217.1 2.2 mute_receiver.6.refs_0_
  220.4 1.5 collective-permute-start.74
  222.0 2.9 %collective-permute-done.76.refs_0_ = bf16[2,4,64,128]{3,2,1,0:T(8,128)(2,1)S(1)} collective-permute-done((bf16[2,4,64,128]{3,2,1,0:T(8,128)(2,1)S(1)}, bf16[2,4,64,128]{3,2,1,0:T(8,128)(2,1)S(1)}, u32[]{:S(2)}, u32[]{:S(2)}) %collective-permute-start.76) | collective-permute-done | bytes 131104 | tf_op jit(solution)/shard_map/ppermute | solution.py:113
  225.9 2.2 mute_receiver.7.refs_1_
  228.2 1.7 collective-permute-start.80
  232.2 6.3 %trace_source.1 = bf16[8,128,1024]{2,1,0:T(8,128)(2,1)} custom-call(s32[3]{0:T(128)S(1)} %pad_add_fusion.ids, s32[8,128,1]{2,1,0:T(8,128)S(1)} %copy.7.onset_ref, bf16[512,1024]{1,0:T(8,128)(2,1)S(1)} %get-tuple-element.65.rows_ref, bf16[4,2,2,64,128]{4,3,2,1,0:T(8,128)(2,1)S(1)} %get-tuple-element.123.refs_0_, ...), custom_call_target="tpu_custom_call" | custom-call | flops 1073741824 | bytes 5242880 | tf_op jit(solution)/shard_map/trace_source/pallas_call | solution.py:438
  238.5 2.4 join_halves.2.refs_2_
  240.9 3.4 %collective-permute-done.80.refs_1_ = bf16[2,4,4,64,128]{4,3,2,1,0:T(8,128)(2,1)} collective-permute-done((bf16[2,4,4,64,128]{4,3,2,1,0:T(8,128)(2,1)S(1)}, bf16[2,4,4,64,128]{4,3,2,1,0:T(8,128)(2,1)}, u32[]{:S(2)}, u32[]{:S(2)}) %collective-permute-start.80) | collective-permute-done | bytes 524320 | tf_op jit(solution)/shard_map/ppermute | solution.py:113
  244.3 3.4 %join_halves.3 = bf16[2,256,8,256]{3,2,1,0:T(8,128)(2,1)} custom-call(s32[3]{0:T(128)S(1)} %pad_add_fusion.ids, bf16[2,4,4,64,128]{4,3,2,1,0:T(8,128)(2,1)S(1)} %collective-permute-done.74.refs_0_, bf16[2,4,4,64,128]{4,3,2,1,0:T(8,128)(2,1)} %collective-permute-done.80.refs_1_, ...), custom_call_target="tpu_custom_call", output_to_operand_aliasing={{}: (3, {})} | custom-call | bytes 2097152 | tf_op jit(solution)/shard_map/join_halves/pallas_call | solution.py:535
  (146 shorter events, 55.0 us)
Async XLA Ops:
  3.1 22.5 %collective-permute-start = (bf16[2,8,64,128]{3,2,1,0:T(8,128)(2,1)S(1)}, bf16[2,8,64,128]{3,2,1,0:T(8,128)(2,1)S(1)}, u32[]{:S(2)}, u32[]{:S(2)}) collective-permute-start(bf16[2,8,64,128]{3,2,1,0:T(8,128)(2,1)S(1)} %split_wave.6.refs_7_), channel_id=1, source_target_pairs={{0,2},{1,3},{2,0},{3,1},{4,6},{5,7},{6,4},{7,5},{8,10},{9,11},{10,... | collective-permute-start | bytes 786440 | tf_op jit(solution)/shard_map/ppermute | solution.py:113
  12.1 15.3 %collective-permute-start.2 = (bf16[2,8,64,128]{3,2,1,0:T(8,128)(2,1)S(1)}, bf16[2,8,64,128]{3,2,1,0:T(8,128)(2,1)S(1)}, u32[]{:S(2)}, u32[]{:S(2)}) collective-permute-start(bf16[2,8,64,128]{3,2,1,0:T(8,128)(2,1)S(1)} %split_wave.4.refs_8_), channel_id=1, source_target_pairs={{0,3},{1,2},{2,1},{3,0},{4,7},{5,6},{6,5},{7,4},{8,11},{9,10},{10,... | collective-permute-start | bytes 786440 | tf_op jit(solution)/shard_map/ppermute | solution.py:113
  14.4 23.5 %collective-permute-start.4 = (bf16[2,2,8,64,128]{4,3,2,1,0:T(8,128)(2,1)S(1)}, bf16[2,2,8,64,128]{4,3,2,1,0:T(8,128)(2,1)S(1)}, u32[]{:S(2)}, u32[]{:S(2)}) collective-permute-start(bf16[2,2,8,64,128]{4,3,2,1,0:T(8,128)(2,1)S(1)} %split_wave.7.refs_6_), channel_id=1, source_target_pairs={{0,1},{1,0},{2,3},{3,2},{4,5},{5,4},{6,7},{7,6},{8,9},{9,8},{10,11... | collective-permute-start | bytes 1572872 | tf_op jit(solution)/shard_map/ppermute | solution.py:113
  25.6 9.2 %collective-permute-start.1 = (bf16[2,8,64,128]{3,2,1,0:T(8,128)(2,1)S(1)}, bf16[2,8,64,128]{3,2,1,0:T(8,128)(2,1)S(1)}, u32[]{:S(2)}, u32[]{:S(2)}) collective-permute-start(bf16[2,8,64,128]{3,2,1,0:T(8,128)(2,1)S(1)} %collective-permute-done.refs_1_), channel_id=1, source_target_pairs={{0,16},{16,0},{1,17},{17,1},{2,18},{18,2},{3,19},{19,3},{4,20},{20... | collective-permute-start | bytes 786440 | tf_op jit(solution)/shard_map/ppermute | solution.py:113
  27.4 10.4 %collective-permute-start.3 = (bf16[2,8,64,128]{3,2,1,0:T(8,128)(2,1)S(1)}, bf16[2,8,64,128]{3,2,1,0:T(8,128)(2,1)S(1)}, u32[]{:S(2)}, u32[]{:S(2)}) collective-permute-start(bf16[2,8,64,128]{3,2,1,0:T(8,128)(2,1)S(1)} %collective-permute-done.2.refs_3_), channel_id=1, source_target_pairs={{0,16},{16,0},{1,17},{17,1},{2,18},{18,2},{3,19},{19,3},{4,20},{20... | collective-permute-start | bytes 786440 | tf_op jit(solution)/shard_map/ppermute | solution.py:113
  43.8 8.4 %collective-permute-start.6 = (bf16[4,2,2,64,128]{4,3,2,1,0:T(8,128)(2,1)S(1)}, bf16[4,2,2,64,128]{4,3,2,1,0:T(8,128)(2,1)S(1)}, u32[]{:S(2)}, u32[]{:S(2)}) collective-permute-start(bf16[4,2,2,64,128]{4,3,2,1,0:T(8,128)(2,1)S(1)} %fusion.2), channel_id=1, source_target_pairs={{0,8},{4,12},{8,0},{12,4},{1,9},{5,13},{9,1},{13,5},{2,10},{6,14},... | collective-permute-start | bytes 786440 | tf_op jit(solution)/shard_map/ppermute | solution.py:113
  52.4 4.9 %collective-permute-start.7 = (bf16[2,2,64,128]{3,2,1,0:T(8,128)(2,1)S(1)}, bf16[2,2,64,128]{3,2,1,0:T(8,128)(2,1)S(1)}, u32[]{:S(2)}, u32[]{:S(2)}) collective-permute-start(bf16[2,2,64,128]{3,2,1,0:T(8,128)(2,1)S(1)} %get-tuple-element.138), channel_id=1, source_target_pairs={{0,1},{1,0},{2,3},{3,2},{4,5},{5,4},{6,7},{7,6},{8,9},{9,8},{10,11... | collective-permute-start | bytes 196616 | tf_op jit(solution)/shard_map/ppermute | solution.py:113
  53.9 7.5 %collective-permute-start.8 = (bf16[2,2,64,128]{3,2,1,0:T(8,128)(2,1)S(1)}, bf16[2,2,64,128]{3,2,1,0:T(8,128)(2,1)S(1)}, u32[]{:S(2)}, u32[]{:S(2)}) collective-permute-start(bf16[2,2,64,128]{3,2,1,0:T(8,128)(2,1)S(1)} %get-tuple-element.137), channel_id=1, source_target_pairs={{0,2},{1,3},{2,0},{3,1},{4,6},{5,7},{6,4},{7,5},{8,10},{9,11},{10,... | collective-permute-start | bytes 196616 | tf_op jit(solution)/shard_map/ppermute | solution.py:113
  57.3 6.1 %collective-permute-start.9 = (bf16[2,2,64,128]{3,2,1,0:T(8,128)(2,1)S(1)}, bf16[2,2,64,128]{3,2,1,0:T(8,128)(2,1)S(1)}, u32[]{:S(2)}, u32[]{:S(2)}) collective-permute-start(bf16[2,2,64,128]{3,2,1,0:T(8,128)(2,1)S(1)} %get-tuple-element.136), channel_id=1, source_target_pairs={{0,3},{1,2},{2,1},{3,0},{4,7},{5,6},{6,5},{7,4},{8,11},{9,10},{10,... | collective-permute-start | bytes 196616 | tf_op jit(solution)/shard_map/ppermute | solution.py:113
  65.0 6.2 %collective-permute-start.11 = (bf16[2,2,64,128]{3,2,1,0:T(8,128)(2,1)S(1)}, bf16[2,2,64,128]{3,2,1,0:T(8,128)(2,1)S(1)}, u32[]{:S(2)}, u32[]{:S(2)}) collective-permute-start(bf16[2,2,64,128]{3,2,1,0:T(8,128)(2,1)S(1)} %get-tuple-element.73), channel_id=1, source_target_pairs={{0,3},{1,2},{2,1},{3,0},{4,7},{5,6},{6,5},{7,4},{8,11},{9,10},{10,... | collective-permute-start | bytes 196616 | tf_op jit(solution)/shard_map/ppermute | solution.py:113
  66.5 6.3 %collective-permute-start.14 = (bf16[2,2,64,128]{3,2,1,0:T(8,128)(2,1)S(1)}, bf16[2,2,64,128]{3,2,1,0:T(8,128)(2,1)S(1)}, u32[]{:S(2)}, u32[]{:S(2)}) collective-permute-start(bf16[2,2,64,128]{3,2,1,0:T(8,128)(2,1)S(1)} %get-tuple-element.74), channel_id=1, source_target_pairs={{0,1},{1,0},{2,3},{3,2},{4,5},{5,4},{6,7},{7,6},{8,9},{9,8},{10,11... | collective-permute-start | bytes 196616 | tf_op jit(solution)/shard_map/ppermute | solution.py:113
  66.8 6.0 %collective-permute-start.16 = (bf16[2,2,64,128]{3,2,1,0:T(8,128)(2,1)S(1)}, bf16[2,2,64,128]{3,2,1,0:T(8,128)(2,1)S(1)}, u32[]{:S(2)}, u32[]{:S(2)}) collective-permute-start(bf16[2,2,64,128]{3,2,1,0:T(8,128)(2,1)S(1)} %get-tuple-element.72.refs_14_), channel_id=1, source_target_pairs={{0,8},{4,12},{8,0},{12,4},{1,9},{5,13},{9,1},{13,5},{2,10},{6,14},... | collective-permute-start | bytes 196616 | tf_op jit(solution)/shard_map/ppermute | solution.py:113
  68.3 5.2 %collective-permute-start.18 = (bf16[2,2,64,128]{3,2,1,0:T(8,128)(2,1)S(1)}, bf16[2,2,64,128]{3,2,1,0:T(8,128)(2,1)S(1)}, u32[]{:S(2)}, u32[]{:S(2)}) collective-permute-start(bf16[2,2,64,128]{3,2,1,0:T(8,128)(2,1)S(1)} %get-tuple-element.75), channel_id=1, source_target_pairs={{0,2},{1,3},{2,0},{3,1},{4,6},{5,7},{6,4},{7,5},{8,10},{9,11},{10,... | collective-permute-start | bytes 196616 | tf_op jit(solution)/shard_map/ppermute | solution.py:113
  71.3 4.3 %collective-permute-start.12 = (bf16[2,2,64,128]{3,2,1,0:T(8,128)(2,1)S(1)}, bf16[2,2,64,128]{3,2,1,0:T(8,128)(2,1)S(1)}, u32[]{:S(2)}, u32[]{:S(2)}) collective-permute-start(bf16[2,2,64,128]{3,2,1,0:T(8,128)(2,1)S(1)} %collective-permute-done.11.refs_1_), channel_id=1, source_target_pairs={{0,8},{4,12},{8,0},{12,4},{1,9},{5,13},{9,1},{13,5},{2,10},{6,14},... | collective-permute-start | bytes 196616 | tf_op jit(solution)/shard_map/ppermute | solution.py:113
  73.5 4.6 %collective-permute-start.22 = (bf16[2,2,64,128]{3,2,1,0:T(8,128)(2,1)S(1)}, bf16[2,2,64,128]{3,2,1,0:T(8,128)(2,1)S(1)}, u32[]{:S(2)}, u32[]{:S(2)}) collective-permute-start(bf16[2,2,64,128]{3,2,1,0:T(8,128)(2,1)S(1)} %collective-permute-done.18.refs_5_), channel_id=1, source_target_pairs={{0,8},{4,12},{8,0},{12,4},{1,9},{5,13},{9,1},{13,5},{2,10},{6,14},... | collective-permute-start | bytes 196616 | tf_op jit(solution)/shard_map/ppermute | solution.py:113
  74.0 4.7 %collective-permute-start.20 = (bf16[2,2,64,128]{3,2,1,0:T(8,128)(2,1)S(1)}, bf16[2,2,64,128]{3,2,1,0:T(8,128)(2,1)S(1)}, u32[]{:S(2)}, u32[]{:S(2)}) collective-permute-start(bf16[2,2,64,128]{3,2,1,0:T(8,128)(2,1)S(1)} %collective-permute-done.14.refs_11_), channel_id=1, source_target_pairs={{0,8},{4,12},{8,0},{12,4},{1,9},{5,13},{9,1},{13,5},{2,10},{6,14},... | collective-permute-start | bytes 196616 | tf_op jit(solution)/shard_map/ppermute | solution.py:113
  83.2 9.2 %collective-permute-start.25 = (bf16[2,2,4,64,128]{4,3,2,1,0:T(8,128)(2,1)S(1)}, bf16[2,2,4,64,128]{4,3,2,1,0:T(8,128)(2,1)S(1)}, u32[]{:S(2)}, u32[]{:S(2)}) collective-permute-start(bf16[2,2,4,64,128]{4,3,2,1,0:T(8,128)(2,1)S(1)} %get-tuple-element.77), channel_id=1, source_target_pairs={{0,16},{16,0},{1,17},{17,1},{2,18},{18,2},{3,19},{19,3},{4,20},{20... | collective-permute-start | bytes 786440 | tf_op jit(solution)/shard_map/ppermute | solution.py:113
  84.8 13.3 %collective-permute-start.28 = (bf16[2,2,4,64,128]{4,3,2,1,0:T(8,128)(2,1)S(1)}, bf16[2,2,4,64,128]{4,3,2,1,0:T(8,128)(2,1)S(1)}, u32[]{:S(2)}, u32[]{:S(2)}) collective-permute-start(bf16[2,2,4,64,128]{4,3,2,1,0:T(8,128)(2,1)S(1)} %get-tuple-element.79), channel_id=1, source_target_pairs={{0,16},{16,0},{1,17},{17,1},{2,18},{18,2},{3,19},{19,3},{4,20},{20... | collective-permute-start | bytes 786440 | tf_op jit(solution)/shard_map/ppermute | solution.py:113
  85.3 18.4 %collective-permute-start.32 = (bf16[2,2,4,64,128]{4,3,2,1,0:T(8,128)(2,1)S(1)}, bf16[2,2,4,64,128]{4,3,2,1,0:T(8,128)(2,1)S(1)}, u32[]{:S(2)}, u32[]{:S(2)}) collective-permute-start(bf16[2,2,4,64,128]{4,3,2,1,0:T(8,128)(2,1)S(1)} %get-tuple-element.83), channel_id=1, source_target_pairs={{0,16},{16,0},{1,17},{17,1},{2,18},{18,2},{3,19},{19,3},{4,20},{20... | collective-permute-start | bytes 786440 | tf_op jit(solution)/shard_map/ppermute | solution.py:113
  86.8 23.0 %collective-permute-start.35 = (bf16[2,2,4,64,128]{4,3,2,1,0:T(8,128)(2,1)S(1)}, bf16[2,2,4,64,128]{4,3,2,1,0:T(8,128)(2,1)S(1)}, u32[]{:S(2)}, u32[]{:S(2)}) collective-permute-start(bf16[2,2,4,64,128]{4,3,2,1,0:T(8,128)(2,1)S(1)} %get-tuple-element.85), channel_id=1, source_target_pairs={{0,16},{16,0},{1,17},{17,1},{2,18},{18,2},{3,19},{19,3},{4,20},{20... | collective-permute-start | bytes 786440 | tf_op jit(solution)/shard_map/ppermute | solution.py:113
  92.5 13.7 %collective-permute-start.26 = (bf16[2,4,64,128]{3,2,1,0:T(8,128)(2,1)S(1)}, bf16[2,4,64,128]{3,2,1,0:T(8,128)(2,1)S(1)}, u32[]{:S(2)}, u32[]{:S(2)}) collective-permute-start(bf16[2,4,64,128]{3,2,1,0:T(8,128)(2,1)S(1)} %get-tuple-element.131), channel_id=1, source_target_pairs={{0,2},{1,3},{2,0},{3,1},{4,6},{5,7},{6,4},{7,5},{8,10},{9,11},{10,... | collective-permute-start | bytes 393224 | tf_op jit(solution)/shard_map/ppermute | solution.py:113
  94.9 12.6 %collective-permute-start.27 = (bf16[2,4,64,128]{3,2,1,0:T(8,128)(2,1)S(1)}, bf16[2,4,64,128]{3,2,1,0:T(8,128)(2,1)S(1)}, u32[]{:S(2)}, u32[]{:S(2)}) collective-permute-start(bf16[2,4,64,128]{3,2,1,0:T(8,128)(2,1)S(1)} %get-tuple-element.130), channel_id=1, source_target_pairs={{0,3},{1,2},{2,1},{3,0},{4,7},{5,6},{6,5},{7,4},{8,11},{9,10},{10,... | collective-permute-start | bytes 393224 | tf_op jit(solution)/shard_map/ppermute | solution.py:113
  98.1 9.5 %collective-permute-start.29 = (bf16[2,4,64,128]{3,2,1,0:T(8,128)(2,1)S(1)}, bf16[2,4,64,128]{3,2,1,0:T(8,128)(2,1)S(1)}, u32[]{:S(2)}, u32[]{:S(2)}) collective-permute-start(bf16[2,4,64,128]{3,2,1,0:T(8,128)(2,1)S(1)} %fusion.6), channel_id=1, source_target_pairs={{0,1},{1,0},{2,3},{3,2},{4,5},{5,4},{6,7},{7,6},{8,9},{9,8},{10,11... | collective-permute-start | bytes 393224 | tf_op jit(solution)/shard_map/ppermute | solution.py:113
  103.8 12.0 %collective-permute-start.33 = (bf16[2,4,64,128]{3,2,1,0:T(8,128)(2,1)S(1)}, bf16[2,4,64,128]{3,2,1,0:T(8,128)(2,1)S(1)}, u32[]{:S(2)}, u32[]{:S(2)}) collective-permute-start(bf16[2,4,64,128]{3,2,1,0:T(8,128)(2,1)S(1)} %get-tuple-element.129), channel_id=1, source_target_pairs={{0,2},{1,3},{2,0},{3,1},{4,6},{5,7},{6,4},{7,5},{8,10},{9,11},{10,... | collective-permute-start | bytes 393224 | tf_op jit(solution)/shard_map/ppermute | solution.py:113
  106.2 15.8 %collective-permute-start.34 = (bf16[2,4,64,128]{3,2,1,0:T(8,128)(2,1)S(1)}, bf16[2,4,64,128]{3,2,1,0:T(8,128)(2,1)S(1)}, u32[]{:S(2)}, u32[]{:S(2)}) collective-permute-start(bf16[2,4,64,128]{3,2,1,0:T(8,128)(2,1)S(1)} %get-tuple-element.128), channel_id=1, source_target_pairs={{0,3},{1,2},{2,1},{3,0},{4,7},{5,6},{6,5},{7,4},{8,11},{9,10},{10,... | collective-permute-start | bytes 393224 | tf_op jit(solution)/shard_map/ppermute | solution.py:113
  109.9 13.1 %collective-permute-start.36 = (bf16[2,4,64,128]{3,2,1,0:T(8,128)(2,1)S(1)}, bf16[2,4,64,128]{3,2,1,0:T(8,128)(2,1)S(1)}, u32[]{:S(2)}, u32[]{:S(2)}) collective-permute-start(bf16[2,4,64,128]{3,2,1,0:T(8,128)(2,1)S(1)} %fusion.9), channel_id=1, source_target_pairs={{0,1},{1,0},{2,3},{3,2},{4,5},{5,4},{6,7},{7,6},{8,9},{9,8},{10,11... | collective-permute-start | bytes 393224 | tf_op jit(solution)/shard_map/ppermute | solution.py:113
  110.0 13.0 %collective-permute-start.37 = (bf16[2,4,64,128]{3,2,1,0:T(8,128)(2,1)S(1)}, bf16[2,4,64,128]{3,2,1,0:T(8,128)(2,1)S(1)}, u32[]{:S(2)}, u32[]{:S(2)}) collective-permute-start(bf16[2,4,64,128]{3,2,1,0:T(8,128)(2,1)S(1)} %get-tuple-element.86.refs_3_), channel_id=1, source_target_pairs={{0,16},{16,0},{1,17},{17,1},{2,18},{18,2},{3,19},{19,3},{4,20},{20... | collective-permute-start | bytes 393224 | tf_op jit(solution)/shard_map/ppermute | solution.py:113
  111.5 17.0 %collective-permute-start.30 = (bf16[2,4,64,128]{3,2,1,0:T(8,128)(2,1)S(1)}, bf16[2,4,64,128]{3,2,1,0:T(8,128)(2,1)S(1)}, u32[]{:S(2)}, u32[]{:S(2)}) collective-permute-start(bf16[2,4,64,128]{3,2,1,0:T(8,128)(2,1)S(1)} %get-tuple-element.80), channel_id=1, source_target_pairs={{0,2},{1,3},{2,0},{3,1},{4,6},{5,7},{6,4},{7,5},{8,10},{9,11},{10,... | collective-permute-start | bytes 393224 | tf_op jit(solution)/shard_map/ppermute | solution.py:113
  115.7 13.9 %collective-permute-start.31 = (bf16[2,4,64,128]{3,2,1,0:T(8,128)(2,1)S(1)}, bf16[2,4,64,128]{3,2,1,0:T(8,128)(2,1)S(1)}, u32[]{:S(2)}, u32[]{:S(2)}) collective-permute-start(bf16[2,4,64,128]{3,2,1,0:T(8,128)(2,1)S(1)} %get-tuple-element.81), channel_id=1, source_target_pairs={{0,3},{1,2},{2,1},{3,0},{4,7},{5,6},{6,5},{7,4},{8,11},{9,10},{10,... | collective-permute-start | bytes 393224 | tf_op jit(solution)/shard_map/ppermute | solution.py:113
  121.9 9.2 %collective-permute-start.40 = (bf16[2,4,64,128]{3,2,1,0:T(8,128)(2,1)S(1)}, bf16[2,4,64,128]{3,2,1,0:T(8,128)(2,1)S(1)}, u32[]{:S(2)}, u32[]{:S(2)}) collective-permute-start(bf16[2,4,64,128]{3,2,1,0:T(8,128)(2,1)S(1)} %get-tuple-element.87), channel_id=1, source_target_pairs={{0,1},{1,0},{2,3},{3,2},{4,5},{5,4},{6,7},{7,6},{8,9},{9,8},{10,11... | collective-permute-start | bytes 393224 | tf_op jit(solution)/shard_map/ppermute | solution.py:113
  125.2 6.9 %collective-permute-start.38 = (bf16[2,4,64,128]{3,2,1,0:T(8,128)(2,1)S(1)}, bf16[2,4,64,128]{3,2,1,0:T(8,128)(2,1)S(1)}, u32[]{:S(2)}, u32[]{:S(2)}) collective-permute-start(bf16[2,4,64,128]{3,2,1,0:T(8,128)(2,1)S(1)} %get-tuple-element.94), channel_id=1, source_target_pairs={{0,1},{1,0},{2,3},{3,2},{4,5},{5,4},{6,7},{7,6},{8,9},{9,8},{10,11... | collective-permute-start | bytes 393224 | tf_op jit(solution)/shard_map/ppermute | solution.py:113
  126.3 6.3 %collective-permute-start.39 = (bf16[2,4,64,128]{3,2,1,0:T(8,128)(2,1)S(1)}, bf16[2,4,64,128]{3,2,1,0:T(8,128)(2,1)S(1)}, u32[]{:S(2)}, u32[]{:S(2)}) collective-permute-start(bf16[2,4,64,128]{3,2,1,0:T(8,128)(2,1)S(1)} %get-tuple-element.95.refs_11_), channel_id=1, source_target_pairs={{0,16},{16,0},{1,17},{17,1},{2,18},{18,2},{3,19},{19,3},{4,20},{20... | collective-permute-start | bytes 393224 | tf_op jit(solution)/shard_map/ppermute | solution.py:113
  128.5 9.6 %collective-permute-start.44 = (bf16[2,4,64,128]{3,2,1,0:T(8,128)(2,1)S(1)}, bf16[2,4,64,128]{3,2,1,0:T(8,128)(2,1)S(1)}, u32[]{:S(2)}, u32[]{:S(2)}) collective-permute-start(bf16[2,4,64,128]{3,2,1,0:T(8,128)(2,1)S(1)} %get-tuple-element.99), channel_id=1, source_target_pairs={{0,2},{1,3},{2,0},{3,1},{4,6},{5,7},{6,4},{7,5},{8,10},{9,11},{10,... | collective-permute-start | bytes 393224 | tf_op jit(solution)/shard_map/ppermute | solution.py:113
  129.7 9.6 %collective-permute-start.45 = (bf16[2,4,64,128]{3,2,1,0:T(8,128)(2,1)S(1)}, bf16[2,4,64,128]{3,2,1,0:T(8,128)(2,1)S(1)}, u32[]{:S(2)}, u32[]{:S(2)}) collective-permute-start(bf16[2,4,64,128]{3,2,1,0:T(8,128)(2,1)S(1)} %get-tuple-element.100), channel_id=1, source_target_pairs={{0,3},{1,2},{2,1},{3,0},{4,7},{5,6},{6,5},{7,4},{8,11},{9,10},{10,... | collective-permute-start | bytes 393224 | tf_op jit(solution)/shard_map/ppermute | solution.py:113
  131.2 9.0 %collective-permute-start.43 = (bf16[2,4,64,128]{3,2,1,0:T(8,128)(2,1)S(1)}, bf16[2,4,64,128]{3,2,1,0:T(8,128)(2,1)S(1)}, u32[]{:S(2)}, u32[]{:S(2)}) collective-permute-start(bf16[2,4,64,128]{3,2,1,0:T(8,128)(2,1)S(1)} %collective-permute-done.40.refs_2_), channel_id=1, source_target_pairs={{0,16},{16,0},{1,17},{17,1},{2,18},{18,2},{3,19},{19,3},{4,20},{20... | collective-permute-start | bytes 393224 | tf_op jit(solution)/shard_map/ppermute | solution.py:113
  132.6 8.7 %collective-permute-start.41 = (bf16[2,4,64,128]{3,2,1,0:T(8,128)(2,1)S(1)}, bf16[2,4,64,128]{3,2,1,0:T(8,128)(2,1)S(1)}, u32[]{:S(2)}, u32[]{:S(2)}) collective-permute-start(bf16[2,4,64,128]{3,2,1,0:T(8,128)(2,1)S(1)} %collective-permute-done.30.refs_0_), channel_id=1, source_target_pairs={{0,16},{16,0},{1,17},{17,1},{2,18},{18,2},{3,19},{19,3},{4,20},{20... | collective-permute-start | bytes 393224 | tf_op jit(solution)/shard_map/ppermute | solution.py:113
  134.2 7.2 %collective-permute-start.42 = (bf16[2,4,64,128]{3,2,1,0:T(8,128)(2,1)S(1)}, bf16[2,4,64,128]{3,2,1,0:T(8,128)(2,1)S(1)}, u32[]{:S(2)}, u32[]{:S(2)}) collective-permute-start(bf16[2,4,64,128]{3,2,1,0:T(8,128)(2,1)S(1)} %collective-permute-done.31.refs_1_), channel_id=1, source_target_pairs={{0,16},{16,0},{1,17},{17,1},{2,18},{18,2},{3,19},{19,3},{4,20},{20... | collective-permute-start | bytes 393224 | tf_op jit(solution)/shard_map/ppermute | solution.py:113
  138.2 6.4 %collective-permute-start.46 = (bf16[2,4,64,128]{3,2,1,0:T(8,128)(2,1)S(1)}, bf16[2,4,64,128]{3,2,1,0:T(8,128)(2,1)S(1)}, u32[]{:S(2)}, u32[]{:S(2)}) collective-permute-start(bf16[2,4,64,128]{3,2,1,0:T(8,128)(2,1)S(1)} %collective-permute-done.44.refs_8_), channel_id=1, source_target_pairs={{0,16},{16,0},{1,17},{17,1},{2,18},{18,2},{3,19},{19,3},{4,20},{20... | collective-permute-start | bytes 393224 | tf_op jit(solution)/shard_map/ppermute | solution.py:113
  139.3 6.9 %collective-permute-start.47 = (bf16[2,4,64,128]{3,2,1,0:T(8,128)(2,1)S(1)}, bf16[2,4,64,128]{3,2,1,0:T(8,128)(2,1)S(1)}, u32[]{:S(2)}, u32[]{:S(2)}) collective-permute-start(bf16[2,4,64,128]{3,2,1,0:T(8,128)(2,1)S(1)} %collective-permute-done.45.refs_9_), channel_id=1, source_target_pairs={{0,16},{16,0},{1,17},{17,1},{2,18},{18,2},{3,19},{19,3},{4,20},{20... | collective-permute-start | bytes 393224 | tf_op jit(solution)/shard_map/ppermute | solution.py:113
  140.2 7.4 %collective-permute-start.48 = (bf16[2,4,64,128]{3,2,1,0:T(8,128)(2,1)S(1)}, bf16[2,4,64,128]{3,2,1,0:T(8,128)(2,1)S(1)}, u32[]{:S(2)}, u32[]{:S(2)}) collective-permute-start(bf16[2,4,64,128]{3,2,1,0:T(8,128)(2,1)S(1)} %collective-permute-done.38.refs_10_), channel_id=1, source_target_pairs={{0,16},{16,0},{1,17},{17,1},{2,18},{18,2},{3,19},{19,3},{4,20},{20... | collective-permute-start | bytes 393224 | tf_op jit(solution)/shard_map/ppermute | solution.py:113
  153.5 8.4 %collective-permute-start.50 = (bf16[4,2,2,64,128]{4,3,2,1,0:T(8,128)(2,1)S(1)}, bf16[4,2,2,64,128]{4,3,2,1,0:T(8,128)(2,1)S(1)}, u32[]{:S(2)}, u32[]{:S(2)}) collective-permute-start(bf16[4,2,2,64,128]{4,3,2,1,0:T(8,128)(2,1)S(1)} %fusion.3), channel_id=1, source_target_pairs={{0,8},{4,12},{8,0},{12,4},{1,9},{5,13},{9,1},{13,5},{2,10},{6,14},... | collective-permute-start | bytes 786440 | tf_op jit(solution)/shard_map/ppermute | solution.py:113
  162.1 5.1 %collective-permute-start.51 = (bf16[2,2,64,128]{3,2,1,0:T(8,128)(2,1)S(1)}, bf16[2,2,64,128]{3,2,1,0:T(8,128)(2,1)S(1)}, u32[]{:S(2)}, u32[]{:S(2)}) collective-permute-start(bf16[2,2,64,128]{3,2,1,0:T(8,128)(2,1)S(1)} %get-tuple-element.134), channel_id=1, source_target_pairs={{0,1},{1,0},{2,3},{3,2},{4,5},{5,4},{6,7},{7,6},{8,9},{9,8},{10,11... | collective-permute-start | bytes 196616 | tf_op jit(solution)/shard_map/ppermute | solution.py:113
  164.5 7.5 %collective-permute-start.52 = (bf16[2,2,64,128]{3,2,1,0:T(8,128)(2,1)S(1)}, bf16[2,2,64,128]{3,2,1,0:T(8,128)(2,1)S(1)}, u32[]{:S(2)}, u32[]{:S(2)}) collective-permute-start(bf16[2,2,64,128]{3,2,1,0:T(8,128)(2,1)S(1)} %get-tuple-element.133), channel_id=1, source_target_pairs={{0,2},{1,3},{2,0},{3,1},{4,6},{5,7},{6,4},{7,5},{8,10},{9,11},{10,... | collective-permute-start | bytes 196616 | tf_op jit(solution)/shard_map/ppermute | solution.py:113
  165.8 6.2 %collective-permute-start.53 = (bf16[2,2,64,128]{3,2,1,0:T(8,128)(2,1)S(1)}, bf16[2,2,64,128]{3,2,1,0:T(8,128)(2,1)S(1)}, u32[]{:S(2)}, u32[]{:S(2)}) collective-permute-start(bf16[2,2,64,128]{3,2,1,0:T(8,128)(2,1)S(1)} %get-tuple-element.132), channel_id=1, source_target_pairs={{0,3},{1,2},{2,1},{3,0},{4,7},{5,6},{6,5},{7,4},{8,11},{9,10},{10,... | collective-permute-start | bytes 196616 | tf_op jit(solution)/shard_map/ppermute | solution.py:113
  173.7 6.6 %collective-permute-start.55 = (bf16[2,2,64,128]{3,2,1,0:T(8,128)(2,1)S(1)}, bf16[2,2,64,128]{3,2,1,0:T(8,128)(2,1)S(1)}, u32[]{:S(2)}, u32[]{:S(2)}) collective-permute-start(bf16[2,2,64,128]{3,2,1,0:T(8,128)(2,1)S(1)} %get-tuple-element.106), channel_id=1, source_target_pairs={{0,3},{1,2},{2,1},{3,0},{4,7},{5,6},{6,5},{7,4},{8,11},{9,10},{10,... | collective-permute-start | bytes 196616 | tf_op jit(solution)/shard_map/ppermute | solution.py:113
  176.2 5.3 %collective-permute-start.58 = (bf16[2,2,64,128]{3,2,1,0:T(8,128)(2,1)S(1)}, bf16[2,2,64,128]{3,2,1,0:T(8,128)(2,1)S(1)}, u32[]{:S(2)}, u32[]{:S(2)}) collective-permute-start(bf16[2,2,64,128]{3,2,1,0:T(8,128)(2,1)S(1)} %get-tuple-element.107), channel_id=1, source_target_pairs={{0,1},{1,0},{2,3},{3,2},{4,5},{5,4},{6,7},{7,6},{8,9},{9,8},{10,11... | collective-permute-start | bytes 196616 | tf_op jit(solution)/shard_map/ppermute | solution.py:113
  176.5 4.9 %collective-permute-start.60 = (bf16[2,2,64,128]{3,2,1,0:T(8,128)(2,1)S(1)}, bf16[2,2,64,128]{3,2,1,0:T(8,128)(2,1)S(1)}, u32[]{:S(2)}, u32[]{:S(2)}) collective-permute-start(bf16[2,2,64,128]{3,2,1,0:T(8,128)(2,1)S(1)} %get-tuple-element.105.refs_14_), channel_id=1, source_target_pairs={{0,8},{4,12},{8,0},{12,4},{1,9},{5,13},{9,1},{13,5},{2,10},{6,14},... | collective-permute-start | bytes 196616 | tf_op jit(solution)/shard_map/ppermute | solution.py:113
  177.4 5.2 %collective-permute-start.62 = (bf16[2,2,64,128]{3,2,1,0:T(8,128)(2,1)S(1)}, bf16[2,2,64,128]{3,2,1,0:T(8,128)(2,1)S(1)}, u32[]{:S(2)}, u32[]{:S(2)}) collective-permute-start(bf16[2,2,64,128]{3,2,1,0:T(8,128)(2,1)S(1)} %get-tuple-element.108), channel_id=1, source_target_pairs={{0,2},{1,3},{2,0},{3,1},{4,6},{5,7},{6,4},{7,5},{8,10},{9,11},{10,... | collective-permute-start | bytes 196616 | tf_op jit(solution)/shard_map/ppermute | solution.py:113
  179.0 4.7 %collective-permute-start.54 = (bf16[2,2,64,128]{3,2,1,0:T(8,128)(2,1)S(1)}, bf16[2,2,64,128]{3,2,1,0:T(8,128)(2,1)S(1)}, u32[]{:S(2)}, u32[]{:S(2)}) collective-permute-start(bf16[2,2,64,128]{3,2,1,0:T(8,128)(2,1)S(1)} %get-tuple-element.105.refs_14_), channel_id=1, source_target_pairs={{0,4},{4,0},{8,12},{12,8},{1,5},{5,1},{9,13},{13,9},{2,6},{6,2},{1... | collective-permute-start | bytes 196616 | tf_op jit(solution)/shard_map/ppermute | solution.py:113
  182.5 4.3 %collective-permute-start.66 = (bf16[2,2,64,128]{3,2,1,0:T(8,128)(2,1)S(1)}, bf16[2,2,64,128]{3,2,1,0:T(8,128)(2,1)S(1)}, u32[]{:S(2)}, u32[]{:S(2)}) collective-permute-start(bf16[2,2,64,128]{3,2,1,0:T(8,128)(2,1)S(1)} %collective-permute-done.62.refs_5_), channel_id=1, source_target_pairs={{0,8},{4,12},{8,0},{12,4},{1,9},{5,13},{9,1},{13,5},{2,10},{6,14},... | collective-permute-start | bytes 196616 | tf_op jit(solution)/shard_map/ppermute | solution.py:113
  183.7 4.3 %collective-permute-start.64 = (bf16[2,2,64,128]{3,2,1,0:T(8,128)(2,1)S(1)}, bf16[2,2,64,128]{3,2,1,0:T(8,128)(2,1)S(1)}, u32[]{:S(2)}, u32[]{:S(2)}) collective-permute-start(bf16[2,2,64,128]{3,2,1,0:T(8,128)(2,1)S(1)} %collective-permute-done.58.refs_11_), channel_id=1, source_target_pairs={{0,8},{4,12},{8,0},{12,4},{1,9},{5,13},{9,1},{13,5},{2,10},{6,14},... | collective-permute-start | bytes 196616 | tf_op jit(solution)/shard_map/ppermute | solution.py:113
  192.5 9.2 %collective-permute-start.69 = (bf16[2,2,4,64,128]{4,3,2,1,0:T(8,128)(2,1)S(1)}, bf16[2,2,4,64,128]{4,3,2,1,0:T(8,128)(2,1)S(1)}, u32[]{:S(2)}, u32[]{:S(2)}) collective-permute-start(bf16[2,2,4,64,128]{4,3,2,1,0:T(8,128)(2,1)S(1)} %get-tuple-element.110), channel_id=1, source_target_pairs={{0,16},{16,0},{1,17},{17,1},{2,18},{18,2},{3,19},{19,3},{4,20},{20... | collective-permute-start | bytes 786440 | tf_op jit(solution)/shard_map/ppermute | solution.py:113
  194.2 13.1 %collective-permute-start.72 = (bf16[2,2,4,64,128]{4,3,2,1,0:T(8,128)(2,1)S(1)}, bf16[2,2,4,64,128]{4,3,2,1,0:T(8,128)(2,1)S(1)}, u32[]{:S(2)}, u32[]{:S(2)}) collective-permute-start(bf16[2,2,4,64,128]{4,3,2,1,0:T(8,128)(2,1)S(1)} %get-tuple-element.112), channel_id=1, source_target_pairs={{0,16},{16,0},{1,17},{17,1},{2,18},{18,2},{3,19},{19,3},{4,20},{20... | collective-permute-start | bytes 786440 | tf_op jit(solution)/shard_map/ppermute | solution.py:113
  194.6 18.4 %collective-permute-start.75 = (bf16[2,2,4,64,128]{4,3,2,1,0:T(8,128)(2,1)S(1)}, bf16[2,2,4,64,128]{4,3,2,1,0:T(8,128)(2,1)S(1)}, u32[]{:S(2)}, u32[]{:S(2)}) collective-permute-start(bf16[2,2,4,64,128]{4,3,2,1,0:T(8,128)(2,1)S(1)} %get-tuple-element.114), channel_id=1, source_target_pairs={{0,16},{16,0},{1,17},{17,1},{2,18},{18,2},{3,19},{19,3},{4,20},{20... | collective-permute-start | bytes 786440 | tf_op jit(solution)/shard_map/ppermute | solution.py:113
  196.2 23.1 %collective-permute-start.78 = (bf16[2,2,4,64,128]{4,3,2,1,0:T(8,128)(2,1)S(1)}, bf16[2,2,4,64,128]{4,3,2,1,0:T(8,128)(2,1)S(1)}, u32[]{:S(2)}, u32[]{:S(2)}) collective-permute-start(bf16[2,2,4,64,128]{4,3,2,1,0:T(8,128)(2,1)S(1)} %get-tuple-element.116), channel_id=1, source_target_pairs={{0,16},{16,0},{1,17},{17,1},{2,18},{18,2},{3,19},{19,3},{4,20},{20... | collective-permute-start | bytes 786440 | tf_op jit(solution)/shard_map/ppermute | solution.py:113
  201.8 13.0 %collective-permute-start.70 = (bf16[2,4,64,128]{3,2,1,0:T(8,128)(2,1)S(1)}, bf16[2,4,64,128]{3,2,1,0:T(8,128)(2,1)S(1)}, u32[]{:S(2)}, u32[]{:S(2)}) collective-permute-start(bf16[2,4,64,128]{3,2,1,0:T(8,128)(2,1)S(1)} %get-tuple-element.127), channel_id=1, source_target_pairs={{0,2},{1,3},{2,0},{3,1},{4,6},{5,7},{6,4},{7,5},{8,10},{9,11},{10,... | collective-permute-start | bytes 393224 | tf_op jit(solution)/shard_map/ppermute | solution.py:113
  203.5 13.6 %collective-permute-start.71 = (bf16[2,4,64,128]{3,2,1,0:T(8,128)(2,1)S(1)}, bf16[2,4,64,128]{3,2,1,0:T(8,128)(2,1)S(1)}, u32[]{:S(2)}, u32[]{:S(2)}) collective-permute-start(bf16[2,4,64,128]{3,2,1,0:T(8,128)(2,1)S(1)} %get-tuple-element.126), channel_id=1, source_target_pairs={{0,3},{1,2},{2,1},{3,0},{4,7},{5,6},{6,5},{7,4},{8,11},{9,10},{10,... | collective-permute-start | bytes 393224 | tf_op jit(solution)/shard_map/ppermute | solution.py:113
  207.3 9.8 %collective-permute-start.73 = (bf16[2,4,64,128]{3,2,1,0:T(8,128)(2,1)S(1)}, bf16[2,4,64,128]{3,2,1,0:T(8,128)(2,1)S(1)}, u32[]{:S(2)}, u32[]{:S(2)}) collective-permute-start(bf16[2,4,64,128]{3,2,1,0:T(8,128)(2,1)S(1)} %fusion.12), channel_id=1, source_target_pairs={{0,1},{1,0},{2,3},{3,2},{4,5},{5,4},{6,7},{7,6},{8,9},{9,8},{10,11... | collective-permute-start | bytes 393224 | tf_op jit(solution)/shard_map/ppermute | solution.py:113
  213.0 11.8 %collective-permute-start.76 = (bf16[2,4,64,128]{3,2,1,0:T(8,128)(2,1)S(1)}, bf16[2,4,64,128]{3,2,1,0:T(8,128)(2,1)S(1)}, u32[]{:S(2)}, u32[]{:S(2)}) collective-permute-start(bf16[2,4,64,128]{3,2,1,0:T(8,128)(2,1)S(1)} %get-tuple-element.125), channel_id=1, source_target_pairs={{0,2},{1,3},{2,0},{3,1},{4,6},{5,7},{6,4},{7,5},{8,10},{9,11},{10,... | collective-permute-start | bytes 393224 | tf_op jit(solution)/shard_map/ppermute | solution.py:113
  214.7 10.1 %collective-permute-start.77 = (bf16[2,4,64,128]{3,2,1,0:T(8,128)(2,1)S(1)}, bf16[2,4,64,128]{3,2,1,0:T(8,128)(2,1)S(1)}, u32[]{:S(2)}, u32[]{:S(2)}) collective-permute-start(bf16[2,4,64,128]{3,2,1,0:T(8,128)(2,1)S(1)} %get-tuple-element.124), channel_id=1, source_target_pairs={{0,3},{1,2},{2,1},{3,0},{4,7},{5,6},{6,5},{7,4},{8,11},{9,10},{10,... | collective-permute-start | bytes 393224 | tf_op jit(solution)/shard_map/ppermute | solution.py:113
  219.4 6.5 %collective-permute-start.79 = (bf16[2,4,64,128]{3,2,1,0:T(8,128)(2,1)S(1)}, bf16[2,4,64,128]{3,2,1,0:T(8,128)(2,1)S(1)}, u32[]{:S(2)}, u32[]{:S(2)}) collective-permute-start(bf16[2,4,64,128]{3,2,1,0:T(8,128)(2,1)S(1)} %fusion.15), channel_id=1, source_target_pairs={{0,1},{1,0},{2,3},{3,2},{4,5},{5,4},{6,7},{7,6},{8,9},{9,8},{10,11... | collective-permute-start | bytes 393224 | tf_op jit(solution)/shard_map/ppermute | solution.py:113
  219.5 10.4 %collective-permute-start.82 = (bf16[4,2,2,64,128]{4,3,2,1,0:T(8,128)(2,1)S(1)}, bf16[4,2,2,64,128]{4,3,2,1,0:T(8,128)(2,1)}, u32[]{:S(2)}, u32[]{:S(2)}) collective-permute-start(bf16[4,2,2,64,128]{4,3,2,1,0:T(8,128)(2,1)S(1)} %get-tuple-element.123.refs_0_), channel_id=1, source_target_pairs={{0,8},{4,12},{8,0},{12,4},{1,9},{5,13},{9,1},{13,5},{2,10},{6,14},... | collective-permute-start | bytes 786440 | tf_op jit(solution)/shard_map/ppermute | solution.py:113
  220.4 20.5 %collective-permute-start.74 = (bf16[2,4,4,64,128]{4,3,2,1,0:T(8,128)(2,1)S(1)}, bf16[2,4,4,64,128]{4,3,2,1,0:T(8,128)(2,1)S(1)}, u32[]{:S(2)}, u32[]{:S(2)}) collective-permute-start(bf16[2,4,4,64,128]{4,3,2,1,0:T(8,128)(2,1)S(1)} %mute_receiver.6.refs_0_), channel_id=1, source_target_pairs={{0,16},{16,0},{1,17},{17,1},{2,18},{18,2},{3,19},{19,3},{4,20},{20... | collective-permute-start | bytes 1572872 | tf_op jit(solution)/shard_map/ppermute | solution.py:113
  228.2 16.1 %collective-permute-start.80 = (bf16[2,4,4,64,128]{4,3,2,1,0:T(8,128)(2,1)S(1)}, bf16[2,4,4,64,128]{4,3,2,1,0:T(8,128)(2,1)}, u32[]{:S(2)}, u32[]{:S(2)}) collective-permute-start(bf16[2,4,4,64,128]{4,3,2,1,0:T(8,128)(2,1)S(1)} %mute_receiver.7.refs_1_), channel_id=1, source_target_pairs={{0,16},{16,0},{1,17},{17,1},{2,18},{18,2},{3,19},{19,3},{4,20},{20... | collective-permute-start | bytes 1572872 | tf_op jit(solution)/shard_map/ppermute | solution.py:113
  (24 other events, 150.2 us)

commit v6 on v5

--- a/solution.py
+++ b/solution.py
@@ -211,7 +211,7 @@
         cost_estimate=pl.CostEstimate(
             flops=0, bytes_accessed=8 * focal * freq * LANES, transcendentals=0
         ),
-    )(ids, wave)
+    )(ids, pltpu.with_memory_space_constraint(wave, pltpu.HBM))
 
 
 def convolve_kernel(plan, pieces, focal, ids, refl_ref, *refs):

time: 248 us -> 247 us (level)
  Pallas kernels: 46 us -> 49.7 us
  waiting for transfers between devices: 103 us -> 99.9 us
    pallas_call x4, Pallas kernels: 3.25 us -> 7.04 us  [split_wave(): pl.pallas_call(functools.partial(split_kernel, both), name='split_wave',...]
    ppermute x84, waiting for transfers between devices: 103 us -> 99.9 us  [swap(): return lax.ppermute(value, axis, [(i, i ^ mask) for i in range(count)])]
  transfers between devices with their start and end apart: 84 -> 84, of which waited for: 40 -> 41; matrix products, arithmetic and copies ran while one was open for 0% -> 0% of each run, Pallas kernels for 10% -> 11%
where the time goes in v6:
time: 247 us
  waiting for transfers between devices  99.9 us (40%)
  starting transfers between devices  95.4 us (39%)
  Pallas kernels  49.7 us (20%)
    ppermute x84, waiting for transfers between devices, swap(): return lax.ppermute(value, axis, [(i, i ^ mask) for i in range(count)])  99.9 us
    ppermute x84, starting transfers between devices, swap(): return lax.ppermute(value, axis, [(i, i ^ mask) for i in range(count)])  95.4 us
    pallas_call x11, Pallas kernels, call(): pl.pallas_call(kernel, name=name, out_shape=out_shape, in_specs=[SMEM_SPE...  30.6 us
    pallas_call x4, Pallas kernels, split_wave(): pl.pallas_call(functools.partial(split_kernel, both), name='split_wave',...  7.04 us
    pallas_call x1, Pallas kernels, trace_source(): pl.pallas_call(trace_kernel, name='trace_source', out_shape=jax.ShapeDtyp...  6.28 us
    pallas_call x2, Pallas kernels, join_halves(): pl.pallas_call(join_kernel, name='join_halves', out_shape=jax.ShapeDtypeS...  5.85 us
  transfers between devices with their start and end apart: 84, of which 41 were waited for; matrix products, arithmetic and copies ran while one was open for 0% of the time, Pallas kernels for 11%

profile of v6, /device:TPU:0, one launch (start us, length us, event | category | flops | bytes accessed | tf_op | source)
XLA Modules:
  0.0 247.2 jit_solution(16834412174845567209)
XLA Ops:
  0.7 1.8 split_wave.6.refs_7_
  2.6 4.1 %collective-permute-start = (bf16[2,8,64,128]{3,2,1,0:T(8,128)(2,1)S(1)}, bf16[2,8,64,128]{3,2,1,0:T(8,128)(2,1)S(1)}, u32[]{:S(2)}, u32[]{:S(2)}) collective-permute-start(bf16[2,8,64,128]{3,2,1,0:T(8,128)(2,1)S(1)} %split_wave.6.refs_7_), channel_id=1, source_target_pairs={{0,2},{1,3},{2,0},{3,1},{4,6},{5,7},{6,4},{7,5},{8,10},{9,11},{10,... | collective-permute-start | bytes 786440 | tf_op jit(solution)/shard_map/ppermute | solution.py:113
  6.7 4.1 %basis.1 = (bf16[512,1024]{1,0:T(8,128)(2,1)S(1)}, bf16[1024,512]{1,0:T(8,128)(2,1)S(1)}) custom-call(s32[3]{0:T(128)S(1)} %pad_add_fusion.ids), custom_call_target="tpu_custom_call" | custom-call | flops 20971520 | bytes 2097152 | tf_op jit(solution)/shard_map/basis/pallas_call | solution.py:118
  10.8 1.6 split_wave.4.refs_8_
  13.8 1.8 split_wave.7.refs_6_
  15.9 9.1 %collective-permute-done.refs_1_ = bf16[2,8,64,128]{3,2,1,0:T(8,128)(2,1)S(1)} collective-permute-done((bf16[2,8,64,128]{3,2,1,0:T(8,128)(2,1)S(1)}, bf16[2,8,64,128]{3,2,1,0:T(8,128)(2,1)S(1)}, u32[]{:S(2)}, u32[]{:S(2)}) %collective-permute-start) | collective-permute-done | bytes 262176 | tf_op jit(solution)/shard_map/ppermute | solution.py:113
  25.1 1.8 collective-permute-start.1
  27.1 1.8 split_wave.5.refs_0_.refs_5_
  28.9 5.4 %collective-permute-done.1.refs_2_ = bf16[2,8,64,128]{3,2,1,0:T(8,128)(2,1)S(1)} collective-permute-done((bf16[2,8,64,128]{3,2,1,0:T(8,128)(2,1)S(1)}, bf16[2,8,64,128]{3,2,1,0:T(8,128)(2,1)S(1)}, u32[]{:S(2)}, u32[]{:S(2)}) %collective-permute-start.1) | collective-permute-done | bytes 262176 | tf_op jit(solution)/shard_map/ppermute | solution.py:113
  34.3 2.9 %collective-permute-done.3.refs_4_ = bf16[2,8,64,128]{3,2,1,0:T(8,128)(2,1)S(1)} collective-permute-done((bf16[2,8,64,128]{3,2,1,0:T(8,128)(2,1)S(1)}, bf16[2,8,64,128]{3,2,1,0:T(8,128)(2,1)S(1)}, u32[]{:S(2)}, u32[]{:S(2)}) %collective-permute-start.3) | collective-permute-done | bytes 262176 | tf_op jit(solution)/shard_map/ppermute | solution.py:113
  37.2 3.8 %convolve.2 = (bf16[2,4,2,2,64,128]{5,4,3,2,1,0:T(8,128)(2,1)S(1)}, bf16[2,4,2,2,64,128]{5,4,3,2,1,0:T(8,128)(2,1)S(1)}) custom-call(s32[3]{0:T(128)S(1)} %pad_add_fusion.ids, bf16[2,64,128,256]{3,2,1,0:T(8,128)(2,1)S(1)} %copy-done, bf16[2,2,8,64,128]{4,3,2,1,0:T(8,128)(2,1)S(1)} %split_wave.5.refs_0_.refs_5_, ...), custom_call_target="tpu_custom_call" | custom-call | flops 536870912 | bytes 11534336 | tf_op jit(solution)/shard_map/convolve/pallas_call | solution.py:118
  41.2 1.9 collective-permute-done.5
  44.2 7.3 %collective-permute-done.6 = bf16[4,2,2,64,128]{4,3,2,1,0:T(8,128)(2,1)S(1)} collective-permute-done((bf16[4,2,2,64,128]{4,3,2,1,0:T(8,128)(2,1)S(1)}, bf16[4,2,2,64,128]{4,3,2,1,0:T(8,128)(2,1)S(1)}, u32[]{:S(2)}, u32[]{:S(2)}) %collective-permute-start.6) | collective-permute-done | bytes 262176 | tf_op jit(solution)/shard_map/ppermute | solution.py:113
  51.7 1.7 collective-permute-start.7
  53.3 3.4 %collective-permute-start.8 = (bf16[2,2,64,128]{3,2,1,0:T(8,128)(2,1)S(1)}, bf16[2,2,64,128]{3,2,1,0:T(8,128)(2,1)S(1)}, u32[]{:S(2)}, u32[]{:S(2)}) collective-permute-start(bf16[2,2,64,128]{3,2,1,0:T(8,128)(2,1)S(1)} %get-tuple-element.137), channel_id=1, source_target_pairs={{0,2},{1,3},{2,0},{3,1},{4,6},{5,7},{6,4},{7,5},{8,10},{9,11},{10,... | collective-permute-start | bytes 196616 | tf_op jit(solution)/shard_map/ppermute | solution.py:113
  56.7 4.1 %collective-permute-done.8.refs_2_ = bf16[2,2,64,128]{3,2,1,0:T(8,128)(2,1)S(1)} collective-permute-done((bf16[2,2,64,128]{3,2,1,0:T(8,128)(2,1)S(1)}, bf16[2,2,64,128]{3,2,1,0:T(8,128)(2,1)S(1)}, u32[]{:S(2)}, u32[]{:S(2)}) %collective-permute-start.8) | collective-permute-done | bytes 65568 | tf_op jit(solution)/shard_map/ppermute | solution.py:113
  60.9 1.9 collective-permute-done.9.refs_3_
  62.8 1.7 mute_source.2
  67.8 2.7 %collective-permute-start.18 = (bf16[2,2,64,128]{3,2,1,0:T(8,128)(2,1)S(1)}, bf16[2,2,64,128]{3,2,1,0:T(8,128)(2,1)S(1)}, u32[]{:S(2)}, u32[]{:S(2)}) collective-permute-start(bf16[2,2,64,128]{3,2,1,0:T(8,128)(2,1)S(1)} %get-tuple-element.75), channel_id=1, source_target_pairs={{0,2},{1,3},{2,0},{3,1},{4,6},{5,7},{6,4},{7,5},{8,10},{9,11},{10,... | collective-permute-start | bytes 196616 | tf_op jit(solution)/shard_map/ppermute | solution.py:113
  70.7 1.5 collective-permute-start.12
  73.5 1.5 collective-permute-start.20
  75.6 1.9 collective-permute-done.22.refs_12_
  79.5 3.2 %correlate.2 = (bf16[2,2,4,64,128]{4,3,2,1,0:T(8,128)(2,1)S(1)}, bf16[2,2,4,64,128]{4,3,2,1,0:T(8,128)(2,1)S(1)}, bf16[2,2,4,64,128]{4,3,2,1,0:T(8,128)(2,1)S(1)...) custom-call(s32[3]{0:T(128)S(1)} %pad_add_fusion.ids, ...), custom_call_target="tpu_custom_call" | custom-call | flops 536870912 | bytes 11534336 | tf_op jit(solution)/shard_map/correlate/pallas_call | solution.py:118
  82.7 1.6 collective-permute-start.25
  86.8 5.1 %collective-permute-done.25 = bf16[2,2,4,64,128]{4,3,2,1,0:T(8,128)(2,1)S(1)} collective-permute-done((bf16[2,2,4,64,128]{4,3,2,1,0:T(8,128)(2,1)S(1)}, bf16[2,2,4,64,128]{4,3,2,1,0:T(8,128)(2,1)S(1)}, u32[]{:S(2)}, u32[]{:S(2)}) %collective-permute-start.25) | collective-permute-done | bytes 262176 | tf_op jit(solution)/shard_map/ppermute | solution.py:113
  92.0 2.4 collective-permute-start.26
  95.8 1.7 collective-permute-done.28.refs_4_
  99.0 4.1 %collective-permute-done.32 = bf16[2,2,4,64,128]{4,3,2,1,0:T(8,128)(2,1)S(1)} collective-permute-done((bf16[2,2,4,64,128]{4,3,2,1,0:T(8,128)(2,1)S(1)}, bf16[2,2,4,64,128]{4,3,2,1,0:T(8,128)(2,1)S(1)}, u32[]{:S(2)}, u32[]{:S(2)}) %collective-permute-start.32) | collective-permute-done | bytes 262176 | tf_op jit(solution)/shard_map/ppermute | solution.py:113
  103.2 2.4 collective-permute-start.33
  107.0 2.3 mute_receiver.4
  109.5 1.5 collective-permute-start.37
  111.0 2.9 %collective-permute-start.30 = (bf16[2,4,64,128]{3,2,1,0:T(8,128)(2,1)S(1)}, bf16[2,4,64,128]{3,2,1,0:T(8,128)(2,1)S(1)}, u32[]{:S(2)}, u32[]{:S(2)}) collective-permute-start(bf16[2,4,64,128]{3,2,1,0:T(8,128)(2,1)S(1)} %get-tuple-element.80), channel_id=1, source_target_pairs={{0,2},{1,3},{2,0},{3,1},{4,6},{5,7},{6,4},{7,5},{8,10},{9,11},{10,... | collective-permute-start | bytes 393224 | tf_op jit(solution)/shard_map/ppermute | solution.py:113
  115.2 6.2 %collective-permute-start.31 = (bf16[2,4,64,128]{3,2,1,0:T(8,128)(2,1)S(1)}, bf16[2,4,64,128]{3,2,1,0:T(8,128)(2,1)S(1)}, u32[]{:S(2)}, u32[]{:S(2)}) collective-permute-start(bf16[2,4,64,128]{3,2,1,0:T(8,128)(2,1)S(1)} %get-tuple-element.81), channel_id=1, source_target_pairs={{0,3},{1,2},{2,1},{3,0},{4,7},{5,6},{6,5},{7,4},{8,11},{9,10},{10,... | collective-permute-start | bytes 393224 | tf_op jit(solution)/shard_map/ppermute | solution.py:113
  122.4 2.2 mute_receiver.5
  134.1 3.5 %collective-permute-done.44.refs_8_ = bf16[2,4,64,128]{3,2,1,0:T(8,128)(2,1)S(1)} collective-permute-done((bf16[2,4,64,128]{3,2,1,0:T(8,128)(2,1)S(1)}, bf16[2,4,64,128]{3,2,1,0:T(8,128)(2,1)S(1)}, u32[]{:S(2)}, u32[]{:S(2)}) %collective-permute-start.44) | collective-permute-done | bytes 131104 | tf_op jit(solution)/shard_map/ppermute | solution.py:113
  140.8 3.2 %collective-permute-done.46.refs_12_ = bf16[2,4,64,128]{3,2,1,0:T(8,128)(2,1)S(1)} collective-permute-done((bf16[2,4,64,128]{3,2,1,0:T(8,128)(2,1)S(1)}, bf16[2,4,64,128]{3,2,1,0:T(8,128)(2,1)S(1)}, u32[]{:S(2)}, u32[]{:S(2)}) %collective-permute-start.46) | collective-permute-done | bytes 131104 | tf_op jit(solution)/shard_map/ppermute | solution.py:113
  146.9 3.8 %convolve.3 = (bf16[2,4,2,2,64,128]{5,4,3,2,1,0:T(8,128)(2,1)S(1)}, bf16[2,4,2,2,64,128]{5,4,3,2,1,0:T(8,128)(2,1)S(1)}) custom-call(s32[3]{0:T(128)S(1)} %pad_add_fusion.ids, bf16[2,64,128,256]{3,2,1,0:T(8,128)(2,1)S(1)} %copy-done, bf16[2,4,64,128]{3,2,1,0:T(8,128)(2,1)S(1)} %collective-permute-done.30.refs_0_, ...), custom_call_target="tpu_custom_call" | custom-call | flops 536870912 | bytes 11534336 | tf_op jit(solution)/shard_map/convolve/pallas_call | solution.py:118
  150.9 1.9 collective-permute-done.49
  154.0 7.2 %collective-permute-done.50 = bf16[4,2,2,64,128]{4,3,2,1,0:T(8,128)(2,1)S(1)} collective-permute-done((bf16[4,2,2,64,128]{4,3,2,1,0:T(8,128)(2,1)S(1)}, bf16[4,2,2,64,128]{4,3,2,1,0:T(8,128)(2,1)S(1)}, u32[]{:S(2)}, u32[]{:S(2)}) %collective-permute-start.50) | collective-permute-done | bytes 262176 | tf_op jit(solution)/shard_map/ppermute | solution.py:113
  161.4 2.6 %collective-permute-start.51 = (bf16[2,2,64,128]{3,2,1,0:T(8,128)(2,1)S(1)}, bf16[2,2,64,128]{3,2,1,0:T(8,128)(2,1)S(1)}, u32[]{:S(2)}, u32[]{:S(2)}) collective-permute-start(bf16[2,2,64,128]{3,2,1,0:T(8,128)(2,1)S(1)} %get-tuple-element.134), channel_id=1, source_target_pairs={{0,1},{1,0},{2,3},{3,2},{4,5},{5,4},{6,7},{7,6},{8,9},{9,8},{10,11... | collective-permute-start | bytes 196616 | tf_op jit(solution)/shard_map/ppermute | solution.py:113
  166.6 4.8 %collective-permute-done.52.refs_2_ = bf16[2,2,64,128]{3,2,1,0:T(8,128)(2,1)S(1)} collective-permute-done((bf16[2,2,64,128]{3,2,1,0:T(8,128)(2,1)S(1)}, bf16[2,2,64,128]{3,2,1,0:T(8,128)(2,1)S(1)}, u32[]{:S(2)}, u32[]{:S(2)}) %collective-permute-start.52) | collective-permute-done | bytes 65568 | tf_op jit(solution)/shard_map/ppermute | solution.py:113
  171.5 1.7 mute_source.3
  173.2 2.4 collective-permute-start.55
  176.8 1.6 collective-permute-start.62
  184.6 1.6 collective-permute-done.66.refs_12_
  188.7 3.2 %correlate.3 = (bf16[2,2,4,64,128]{4,3,2,1,0:T(8,128)(2,1)S(1)}, bf16[2,2,4,64,128]{4,3,2,1,0:T(8,128)(2,1)S(1)}, bf16[2,2,4,64,128]{4,3,2,1,0:T(8,128)(2,1)S(1)...) custom-call(s32[3]{0:T(128)S(1)} %pad_add_fusion.ids, ...), custom_call_target="tpu_custom_call" | custom-call | flops 536870912 | bytes 11534336 | tf_op jit(solution)/shard_map/correlate/pallas_call | solution.py:118
  191.9 1.7 collective-permute-start.69
  194.0 1.7 collective-permute-start.75
  196.1 5.1 %collective-permute-done.69 = bf16[2,2,4,64,128]{4,3,2,1,0:T(8,128)(2,1)S(1)} collective-permute-done((bf16[2,2,4,64,128]{4,3,2,1,0:T(8,128)(2,1)S(1)}, bf16[2,2,4,64,128]{4,3,2,1,0:T(8,128)(2,1)S(1)}, u32[]{:S(2)}, u32[]{:S(2)}) %collective-permute-start.69) | collective-permute-done | bytes 262176 | tf_op jit(solution)/shard_map/ppermute | solution.py:113
  201.2 1.7 collective-permute-start.70
  202.9 2.4 collective-permute-start.71
  206.8 1.7 collective-permute-start.73
  208.5 3.8 %collective-permute-done.75 = bf16[2,2,4,64,128]{4,3,2,1,0:T(8,128)(2,1)S(1)} collective-permute-done((bf16[2,2,4,64,128]{4,3,2,1,0:T(8,128)(2,1)S(1)}, bf16[2,2,4,64,128]{4,3,2,1,0:T(8,128)(2,1)S(1)}, u32[]{:S(2)}, u32[]{:S(2)}) %collective-permute-start.75) | collective-permute-done | bytes 262176 | tf_op jit(solution)/shard_map/ppermute | solution.py:113
  212.5 1.7 collective-permute-start.76
  214.2 2.4 collective-permute-start.77
  216.6 2.2 mute_receiver.6.refs_0_
  219.9 1.5 collective-permute-start.74
  221.4 2.9 %collective-permute-done.76.refs_0_ = bf16[2,4,64,128]{3,2,1,0:T(8,128)(2,1)S(1)} collective-permute-done((bf16[2,4,64,128]{3,2,1,0:T(8,128)(2,1)S(1)}, bf16[2,4,64,128]{3,2,1,0:T(8,128)(2,1)S(1)}, u32[]{:S(2)}, u32[]{:S(2)}) %collective-permute-start.76) | collective-permute-done | bytes 131104 | tf_op jit(solution)/shard_map/ppermute | solution.py:113
  225.4 2.2 mute_receiver.7.refs_1_
  227.7 1.7 collective-permute-start.80
  231.7 6.3 %trace_source.1 = bf16[8,128,1024]{2,1,0:T(8,128)(2,1)} custom-call(s32[3]{0:T(128)S(1)} %pad_add_fusion.ids, s32[8,128,1]{2,1,0:T(8,128)S(1)} %copy.7.onset_ref, bf16[512,1024]{1,0:T(8,128)(2,1)S(1)} %get-tuple-element.65.rows_ref, bf16[4,2,2,64,128]{4,3,2,1,0:T(8,128)(2,1)S(1)} %get-tuple-element.123.refs_0_, ...), custom_call_target="tpu_custom_call" | custom-call | flops 1073741824 | bytes 5242880 | tf_op jit(solution)/shard_map/trace_source/pallas_call | solution.py:438
  237.9 2.4 join_halves.2.refs_2_
  240.3 3.5 %collective-permute-done.80.refs_1_ = bf16[2,4,4,64,128]{4,3,2,1,0:T(8,128)(2,1)} collective-permute-done((bf16[2,4,4,64,128]{4,3,2,1,0:T(8,128)(2,1)S(1)}, bf16[2,4,4,64,128]{4,3,2,1,0:T(8,128)(2,1)}, u32[]{:S(2)}, u32[]{:S(2)}) %collective-permute-start.80) | collective-permute-done | bytes 524320 | tf_op jit(solution)/shard_map/ppermute | solution.py:113
  243.8 3.4 %join_halves.3 = bf16[2,256,8,256]{3,2,1,0:T(8,128)(2,1)} custom-call(s32[3]{0:T(128)S(1)} %pad_add_fusion.ids, bf16[2,4,4,64,128]{4,3,2,1,0:T(8,128)(2,1)S(1)} %collective-permute-done.74.refs_0_, bf16[2,4,4,64,128]{4,3,2,1,0:T(8,128)(2,1)} %collective-permute-done.80.refs_1_, ...), custom_call_target="tpu_custom_call", output_to_operand_aliasing={{}: (3, {})} | custom-call | bytes 2097152 | tf_op jit(solution)/shard_map/join_halves/pallas_call | solution.py:535
  (144 shorter events, 56.2 us)
Async XLA Ops:
  2.6 22.5 %collective-permute-start = (bf16[2,8,64,128]{3,2,1,0:T(8,128)(2,1)S(1)}, bf16[2,8,64,128]{3,2,1,0:T(8,128)(2,1)S(1)}, u32[]{:S(2)}, u32[]{:S(2)}) collective-permute-start(bf16[2,8,64,128]{3,2,1,0:T(8,128)(2,1)S(1)} %split_wave.6.refs_7_), channel_id=1, source_target_pairs={{0,2},{1,3},{2,0},{3,1},{4,6},{5,7},{6,4},{7,5},{8,10},{9,11},{10,... | collective-permute-start | bytes 786440 | tf_op jit(solution)/shard_map/ppermute | solution.py:113
  12.4 14.5 %collective-permute-start.2 = (bf16[2,8,64,128]{3,2,1,0:T(8,128)(2,1)S(1)}, bf16[2,8,64,128]{3,2,1,0:T(8,128)(2,1)S(1)}, u32[]{:S(2)}, u32[]{:S(2)}) collective-permute-start(bf16[2,8,64,128]{3,2,1,0:T(8,128)(2,1)S(1)} %split_wave.4.refs_8_), channel_id=1, source_target_pairs={{0,3},{1,2},{2,1},{3,0},{4,7},{5,6},{6,5},{7,4},{8,11},{9,10},{10,... | collective-permute-start | bytes 786440 | tf_op jit(solution)/shard_map/ppermute | solution.py:113
  15.6 21.6 %collective-permute-start.4 = (bf16[2,2,8,64,128]{4,3,2,1,0:T(8,128)(2,1)S(1)}, bf16[2,2,8,64,128]{4,3,2,1,0:T(8,128)(2,1)S(1)}, u32[]{:S(2)}, u32[]{:S(2)}) collective-permute-start(bf16[2,2,8,64,128]{4,3,2,1,0:T(8,128)(2,1)S(1)} %split_wave.7.refs_6_), channel_id=1, source_target_pairs={{0,1},{1,0},{2,3},{3,2},{4,5},{5,4},{6,7},{7,6},{8,9},{9,8},{10,11... | collective-permute-start | bytes 1572872 | tf_op jit(solution)/shard_map/ppermute | solution.py:113
  25.1 9.2 %collective-permute-start.1 = (bf16[2,8,64,128]{3,2,1,0:T(8,128)(2,1)S(1)}, bf16[2,8,64,128]{3,2,1,0:T(8,128)(2,1)S(1)}, u32[]{:S(2)}, u32[]{:S(2)}) collective-permute-start(bf16[2,8,64,128]{3,2,1,0:T(8,128)(2,1)S(1)} %collective-permute-done.refs_1_), channel_id=1, source_target_pairs={{0,16},{16,0},{1,17},{17,1},{2,18},{18,2},{3,19},{19,3},{4,20},{20... | collective-permute-start | bytes 786440 | tf_op jit(solution)/shard_map/ppermute | solution.py:113
  26.9 10.3 %collective-permute-start.3 = (bf16[2,8,64,128]{3,2,1,0:T(8,128)(2,1)S(1)}, bf16[2,8,64,128]{3,2,1,0:T(8,128)(2,1)S(1)}, u32[]{:S(2)}, u32[]{:S(2)}) collective-permute-start(bf16[2,8,64,128]{3,2,1,0:T(8,128)(2,1)S(1)} %collective-permute-done.2.refs_3_), channel_id=1, source_target_pairs={{0,16},{16,0},{1,17},{17,1},{2,18},{18,2},{3,19},{19,3},{4,20},{20... | collective-permute-start | bytes 786440 | tf_op jit(solution)/shard_map/ppermute | solution.py:113
  43.1 8.4 %collective-permute-start.6 = (bf16[4,2,2,64,128]{4,3,2,1,0:T(8,128)(2,1)S(1)}, bf16[4,2,2,64,128]{4,3,2,1,0:T(8,128)(2,1)S(1)}, u32[]{:S(2)}, u32[]{:S(2)}) collective-permute-start(bf16[4,2,2,64,128]{4,3,2,1,0:T(8,128)(2,1)S(1)} %fusion.2), channel_id=1, source_target_pairs={{0,8},{4,12},{8,0},{12,4},{1,9},{5,13},{9,1},{13,5},{2,10},{6,14},... | collective-permute-start | bytes 786440 | tf_op jit(solution)/shard_map/ppermute | solution.py:113
  51.7 5.0 %collective-permute-start.7 = (bf16[2,2,64,128]{3,2,1,0:T(8,128)(2,1)S(1)}, bf16[2,2,64,128]{3,2,1,0:T(8,128)(2,1)S(1)}, u32[]{:S(2)}, u32[]{:S(2)}) collective-permute-start(bf16[2,2,64,128]{3,2,1,0:T(8,128)(2,1)S(1)} %get-tuple-element.138), channel_id=1, source_target_pairs={{0,1},{1,0},{2,3},{3,2},{4,5},{5,4},{6,7},{7,6},{8,9},{9,8},{10,11... | collective-permute-start | bytes 196616 | tf_op jit(solution)/shard_map/ppermute | solution.py:113
  53.3 7.5 %collective-permute-start.8 = (bf16[2,2,64,128]{3,2,1,0:T(8,128)(2,1)S(1)}, bf16[2,2,64,128]{3,2,1,0:T(8,128)(2,1)S(1)}, u32[]{:S(2)}, u32[]{:S(2)}) collective-permute-start(bf16[2,2,64,128]{3,2,1,0:T(8,128)(2,1)S(1)} %get-tuple-element.137), channel_id=1, source_target_pairs={{0,2},{1,3},{2,0},{3,1},{4,6},{5,7},{6,4},{7,5},{8,10},{9,11},{10,... | collective-permute-start | bytes 196616 | tf_op jit(solution)/shard_map/ppermute | solution.py:113
  56.7 6.1 %collective-permute-start.9 = (bf16[2,2,64,128]{3,2,1,0:T(8,128)(2,1)S(1)}, bf16[2,2,64,128]{3,2,1,0:T(8,128)(2,1)S(1)}, u32[]{:S(2)}, u32[]{:S(2)}) collective-permute-start(bf16[2,2,64,128]{3,2,1,0:T(8,128)(2,1)S(1)} %get-tuple-element.136), channel_id=1, source_target_pairs={{0,3},{1,2},{2,1},{3,0},{4,7},{5,6},{6,5},{7,4},{8,11},{9,10},{10,... | collective-permute-start | bytes 196616 | tf_op jit(solution)/shard_map/ppermute | solution.py:113
  64.5 6.2 %collective-permute-start.11 = (bf16[2,2,64,128]{3,2,1,0:T(8,128)(2,1)S(1)}, bf16[2,2,64,128]{3,2,1,0:T(8,128)(2,1)S(1)}, u32[]{:S(2)}, u32[]{:S(2)}) collective-permute-start(bf16[2,2,64,128]{3,2,1,0:T(8,128)(2,1)S(1)} %get-tuple-element.73), channel_id=1, source_target_pairs={{0,3},{1,2},{2,1},{3,0},{4,7},{5,6},{6,5},{7,4},{8,11},{9,10},{10,... | collective-permute-start | bytes 196616 | tf_op jit(solution)/shard_map/ppermute | solution.py:113
  65.9 6.3 %collective-permute-start.14 = (bf16[2,2,64,128]{3,2,1,0:T(8,128)(2,1)S(1)}, bf16[2,2,64,128]{3,2,1,0:T(8,128)(2,1)S(1)}, u32[]{:S(2)}, u32[]{:S(2)}) collective-permute-start(bf16[2,2,64,128]{3,2,1,0:T(8,128)(2,1)S(1)} %get-tuple-element.74), channel_id=1, source_target_pairs={{0,1},{1,0},{2,3},{3,2},{4,5},{5,4},{6,7},{7,6},{8,9},{9,8},{10,11... | collective-permute-start | bytes 196616 | tf_op jit(solution)/shard_map/ppermute | solution.py:113
  66.3 6.0 %collective-permute-start.16 = (bf16[2,2,64,128]{3,2,1,0:T(8,128)(2,1)S(1)}, bf16[2,2,64,128]{3,2,1,0:T(8,128)(2,1)S(1)}, u32[]{:S(2)}, u32[]{:S(2)}) collective-permute-start(bf16[2,2,64,128]{3,2,1,0:T(8,128)(2,1)S(1)} %get-tuple-element.72.refs_14_), channel_id=1, source_target_pairs={{0,8},{4,12},{8,0},{12,4},{1,9},{5,13},{9,1},{13,5},{2,10},{6,14},... | collective-permute-start | bytes 196616 | tf_op jit(solution)/shard_map/ppermute | solution.py:113
  67.8 5.2 %collective-permute-start.18 = (bf16[2,2,64,128]{3,2,1,0:T(8,128)(2,1)S(1)}, bf16[2,2,64,128]{3,2,1,0:T(8,128)(2,1)S(1)}, u32[]{:S(2)}, u32[]{:S(2)}) collective-permute-start(bf16[2,2,64,128]{3,2,1,0:T(8,128)(2,1)S(1)} %get-tuple-element.75), channel_id=1, source_target_pairs={{0,2},{1,3},{2,0},{3,1},{4,6},{5,7},{6,4},{7,5},{8,10},{9,11},{10,... | collective-permute-start | bytes 196616 | tf_op jit(solution)/shard_map/ppermute | solution.py:113
  70.7 4.3 %collective-permute-start.12 = (bf16[2,2,64,128]{3,2,1,0:T(8,128)(2,1)S(1)}, bf16[2,2,64,128]{3,2,1,0:T(8,128)(2,1)S(1)}, u32[]{:S(2)}, u32[]{:S(2)}) collective-permute-start(bf16[2,2,64,128]{3,2,1,0:T(8,128)(2,1)S(1)} %collective-permute-done.11.refs_1_), channel_id=1, source_target_pairs={{0,8},{4,12},{8,0},{12,4},{1,9},{5,13},{9,1},{13,5},{2,10},{6,14},... | collective-permute-start | bytes 196616 | tf_op jit(solution)/shard_map/ppermute | solution.py:113
  73.0 4.6 %collective-permute-start.22 = (bf16[2,2,64,128]{3,2,1,0:T(8,128)(2,1)S(1)}, bf16[2,2,64,128]{3,2,1,0:T(8,128)(2,1)S(1)}, u32[]{:S(2)}, u32[]{:S(2)}) collective-permute-start(bf16[2,2,64,128]{3,2,1,0:T(8,128)(2,1)S(1)} %collective-permute-done.18.refs_5_), channel_id=1, source_target_pairs={{0,8},{4,12},{8,0},{12,4},{1,9},{5,13},{9,1},{13,5},{2,10},{6,14},... | collective-permute-start | bytes 196616 | tf_op jit(solution)/shard_map/ppermute | solution.py:113
  73.5 4.7 %collective-permute-start.20 = (bf16[2,2,64,128]{3,2,1,0:T(8,128)(2,1)S(1)}, bf16[2,2,64,128]{3,2,1,0:T(8,128)(2,1)S(1)}, u32[]{:S(2)}, u32[]{:S(2)}) collective-permute-start(bf16[2,2,64,128]{3,2,1,0:T(8,128)(2,1)S(1)} %collective-permute-done.14.refs_11_), channel_id=1, source_target_pairs={{0,8},{4,12},{8,0},{12,4},{1,9},{5,13},{9,1},{13,5},{2,10},{6,14},... | collective-permute-start | bytes 196616 | tf_op jit(solution)/shard_map/ppermute | solution.py:113
  82.7 9.2 %collective-permute-start.25 = (bf16[2,2,4,64,128]{4,3,2,1,0:T(8,128)(2,1)S(1)}, bf16[2,2,4,64,128]{4,3,2,1,0:T(8,128)(2,1)S(1)}, u32[]{:S(2)}, u32[]{:S(2)}) collective-permute-start(bf16[2,2,4,64,128]{4,3,2,1,0:T(8,128)(2,1)S(1)} %get-tuple-element.77), channel_id=1, source_target_pairs={{0,16},{16,0},{1,17},{17,1},{2,18},{18,2},{3,19},{19,3},{4,20},{20... | collective-permute-start | bytes 786440 | tf_op jit(solution)/shard_map/ppermute | solution.py:113
  84.2 13.3 %collective-permute-start.28 = (bf16[2,2,4,64,128]{4,3,2,1,0:T(8,128)(2,1)S(1)}, bf16[2,2,4,64,128]{4,3,2,1,0:T(8,128)(2,1)S(1)}, u32[]{:S(2)}, u32[]{:S(2)}) collective-permute-start(bf16[2,2,4,64,128]{4,3,2,1,0:T(8,128)(2,1)S(1)} %get-tuple-element.79), channel_id=1, source_target_pairs={{0,16},{16,0},{1,17},{17,1},{2,18},{18,2},{3,19},{19,3},{4,20},{20... | collective-permute-start | bytes 786440 | tf_op jit(solution)/shard_map/ppermute | solution.py:113
  84.8 18.4 %collective-permute-start.32 = (bf16[2,2,4,64,128]{4,3,2,1,0:T(8,128)(2,1)S(1)}, bf16[2,2,4,64,128]{4,3,2,1,0:T(8,128)(2,1)S(1)}, u32[]{:S(2)}, u32[]{:S(2)}) collective-permute-start(bf16[2,2,4,64,128]{4,3,2,1,0:T(8,128)(2,1)S(1)} %get-tuple-element.83), channel_id=1, source_target_pairs={{0,16},{16,0},{1,17},{17,1},{2,18},{18,2},{3,19},{19,3},{4,20},{20... | collective-permute-start | bytes 786440 | tf_op jit(solution)/shard_map/ppermute | solution.py:113
  86.3 23.0 %collective-permute-start.35 = (bf16[2,2,4,64,128]{4,3,2,1,0:T(8,128)(2,1)S(1)}, bf16[2,2,4,64,128]{4,3,2,1,0:T(8,128)(2,1)S(1)}, u32[]{:S(2)}, u32[]{:S(2)}) collective-permute-start(bf16[2,2,4,64,128]{4,3,2,1,0:T(8,128)(2,1)S(1)} %get-tuple-element.85), channel_id=1, source_target_pairs={{0,16},{16,0},{1,17},{17,1},{2,18},{18,2},{3,19},{19,3},{4,20},{20... | collective-permute-start | bytes 786440 | tf_op jit(solution)/shard_map/ppermute | solution.py:113
  92.0 13.7 %collective-permute-start.26 = (bf16[2,4,64,128]{3,2,1,0:T(8,128)(2,1)S(1)}, bf16[2,4,64,128]{3,2,1,0:T(8,128)(2,1)S(1)}, u32[]{:S(2)}, u32[]{:S(2)}) collective-permute-start(bf16[2,4,64,128]{3,2,1,0:T(8,128)(2,1)S(1)} %get-tuple-element.131), channel_id=1, source_target_pairs={{0,2},{1,3},{2,0},{3,1},{4,6},{5,7},{6,4},{7,5},{8,10},{9,11},{10,... | collective-permute-start | bytes 393224 | tf_op jit(solution)/shard_map/ppermute | solution.py:113
  94.4 12.6 %collective-permute-start.27 = (bf16[2,4,64,128]{3,2,1,0:T(8,128)(2,1)S(1)}, bf16[2,4,64,128]{3,2,1,0:T(8,128)(2,1)S(1)}, u32[]{:S(2)}, u32[]{:S(2)}) collective-permute-start(bf16[2,4,64,128]{3,2,1,0:T(8,128)(2,1)S(1)} %get-tuple-element.130), channel_id=1, source_target_pairs={{0,3},{1,2},{2,1},{3,0},{4,7},{5,6},{6,5},{7,4},{8,11},{9,10},{10,... | collective-permute-start | bytes 393224 | tf_op jit(solution)/shard_map/ppermute | solution.py:113
  97.6 9.5 %collective-permute-start.29 = (bf16[2,4,64,128]{3,2,1,0:T(8,128)(2,1)S(1)}, bf16[2,4,64,128]{3,2,1,0:T(8,128)(2,1)S(1)}, u32[]{:S(2)}, u32[]{:S(2)}) collective-permute-start(bf16[2,4,64,128]{3,2,1,0:T(8,128)(2,1)S(1)} %fusion.6), channel_id=1, source_target_pairs={{0,1},{1,0},{2,3},{3,2},{4,5},{5,4},{6,7},{7,6},{8,9},{9,8},{10,11... | collective-permute-start | bytes 393224 | tf_op jit(solution)/shard_map/ppermute | solution.py:113
  103.2 12.0 %collective-permute-start.33 = (bf16[2,4,64,128]{3,2,1,0:T(8,128)(2,1)S(1)}, bf16[2,4,64,128]{3,2,1,0:T(8,128)(2,1)S(1)}, u32[]{:S(2)}, u32[]{:S(2)}) collective-permute-start(bf16[2,4,64,128]{3,2,1,0:T(8,128)(2,1)S(1)} %get-tuple-element.129), channel_id=1, source_target_pairs={{0,2},{1,3},{2,0},{3,1},{4,6},{5,7},{6,4},{7,5},{8,10},{9,11},{10,... | collective-permute-start | bytes 393224 | tf_op jit(solution)/shard_map/ppermute | solution.py:113
  105.6 15.8 %collective-permute-start.34 = (bf16[2,4,64,128]{3,2,1,0:T(8,128)(2,1)S(1)}, bf16[2,4,64,128]{3,2,1,0:T(8,128)(2,1)S(1)}, u32[]{:S(2)}, u32[]{:S(2)}) collective-permute-start(bf16[2,4,64,128]{3,2,1,0:T(8,128)(2,1)S(1)} %get-tuple-element.128), channel_id=1, source_target_pairs={{0,3},{1,2},{2,1},{3,0},{4,7},{5,6},{6,5},{7,4},{8,11},{9,10},{10,... | collective-permute-start | bytes 393224 | tf_op jit(solution)/shard_map/ppermute | solution.py:113
  109.4 13.1 %collective-permute-start.36 = (bf16[2,4,64,128]{3,2,1,0:T(8,128)(2,1)S(1)}, bf16[2,4,64,128]{3,2,1,0:T(8,128)(2,1)S(1)}, u32[]{:S(2)}, u32[]{:S(2)}) collective-permute-start(bf16[2,4,64,128]{3,2,1,0:T(8,128)(2,1)S(1)} %fusion.9), channel_id=1, source_target_pairs={{0,1},{1,0},{2,3},{3,2},{4,5},{5,4},{6,7},{7,6},{8,9},{9,8},{10,11... | collective-permute-start | bytes 393224 | tf_op jit(solution)/shard_map/ppermute | solution.py:113
  109.5 13.0 %collective-permute-start.37 = (bf16[2,4,64,128]{3,2,1,0:T(8,128)(2,1)S(1)}, bf16[2,4,64,128]{3,2,1,0:T(8,128)(2,1)S(1)}, u32[]{:S(2)}, u32[]{:S(2)}) collective-permute-start(bf16[2,4,64,128]{3,2,1,0:T(8,128)(2,1)S(1)} %get-tuple-element.86.refs_3_), channel_id=1, source_target_pairs={{0,16},{16,0},{1,17},{17,1},{2,18},{18,2},{3,19},{19,3},{4,20},{20... | collective-permute-start | bytes 393224 | tf_op jit(solution)/shard_map/ppermute | solution.py:113
  111.0 17.0 %collective-permute-start.30 = (bf16[2,4,64,128]{3,2,1,0:T(8,128)(2,1)S(1)}, bf16[2,4,64,128]{3,2,1,0:T(8,128)(2,1)S(1)}, u32[]{:S(2)}, u32[]{:S(2)}) collective-permute-start(bf16[2,4,64,128]{3,2,1,0:T(8,128)(2,1)S(1)} %get-tuple-element.80), channel_id=1, source_target_pairs={{0,2},{1,3},{2,0},{3,1},{4,6},{5,7},{6,4},{7,5},{8,10},{9,11},{10,... | collective-permute-start | bytes 393224 | tf_op jit(solution)/shard_map/ppermute | solution.py:113
  115.2 13.9 %collective-permute-start.31 = (bf16[2,4,64,128]{3,2,1,0:T(8,128)(2,1)S(1)}, bf16[2,4,64,128]{3,2,1,0:T(8,128)(2,1)S(1)}, u32[]{:S(2)}, u32[]{:S(2)}) collective-permute-start(bf16[2,4,64,128]{3,2,1,0:T(8,128)(2,1)S(1)} %get-tuple-element.81), channel_id=1, source_target_pairs={{0,3},{1,2},{2,1},{3,0},{4,7},{5,6},{6,5},{7,4},{8,11},{9,10},{10,... | collective-permute-start | bytes 393224 | tf_op jit(solution)/shard_map/ppermute | solution.py:113
  121.4 9.2 %collective-permute-start.40 = (bf16[2,4,64,128]{3,2,1,0:T(8,128)(2,1)S(1)}, bf16[2,4,64,128]{3,2,1,0:T(8,128)(2,1)S(1)}, u32[]{:S(2)}, u32[]{:S(2)}) collective-permute-start(bf16[2,4,64,128]{3,2,1,0:T(8,128)(2,1)S(1)} %get-tuple-element.87), channel_id=1, source_target_pairs={{0,1},{1,0},{2,3},{3,2},{4,5},{5,4},{6,7},{7,6},{8,9},{9,8},{10,11... | collective-permute-start | bytes 393224 | tf_op jit(solution)/shard_map/ppermute | solution.py:113
  124.7 6.9 %collective-permute-start.38 = (bf16[2,4,64,128]{3,2,1,0:T(8,128)(2,1)S(1)}, bf16[2,4,64,128]{3,2,1,0:T(8,128)(2,1)S(1)}, u32[]{:S(2)}, u32[]{:S(2)}) collective-permute-start(bf16[2,4,64,128]{3,2,1,0:T(8,128)(2,1)S(1)} %get-tuple-element.94), channel_id=1, source_target_pairs={{0,1},{1,0},{2,3},{3,2},{4,5},{5,4},{6,7},{7,6},{8,9},{9,8},{10,11... | collective-permute-start | bytes 393224 | tf_op jit(solution)/shard_map/ppermute | solution.py:113
  125.8 6.3 %collective-permute-start.39 = (bf16[2,4,64,128]{3,2,1,0:T(8,128)(2,1)S(1)}, bf16[2,4,64,128]{3,2,1,0:T(8,128)(2,1)S(1)}, u32[]{:S(2)}, u32[]{:S(2)}) collective-permute-start(bf16[2,4,64,128]{3,2,1,0:T(8,128)(2,1)S(1)} %get-tuple-element.95.refs_11_), channel_id=1, source_target_pairs={{0,16},{16,0},{1,17},{17,1},{2,18},{18,2},{3,19},{19,3},{4,20},{20... | collective-permute-start | bytes 393224 | tf_op jit(solution)/shard_map/ppermute | solution.py:113
  128.0 9.6 %collective-permute-start.44 = (bf16[2,4,64,128]{3,2,1,0:T(8,128)(2,1)S(1)}, bf16[2,4,64,128]{3,2,1,0:T(8,128)(2,1)S(1)}, u32[]{:S(2)}, u32[]{:S(2)}) collective-permute-start(bf16[2,4,64,128]{3,2,1,0:T(8,128)(2,1)S(1)} %get-tuple-element.99), channel_id=1, source_target_pairs={{0,2},{1,3},{2,0},{3,1},{4,6},{5,7},{6,4},{7,5},{8,10},{9,11},{10,... | collective-permute-start | bytes 393224 | tf_op jit(solution)/shard_map/ppermute | solution.py:113
  129.2 9.6 %collective-permute-start.45 = (bf16[2,4,64,128]{3,2,1,0:T(8,128)(2,1)S(1)}, bf16[2,4,64,128]{3,2,1,0:T(8,128)(2,1)S(1)}, u32[]{:S(2)}, u32[]{:S(2)}) collective-permute-start(bf16[2,4,64,128]{3,2,1,0:T(8,128)(2,1)S(1)} %get-tuple-element.100), channel_id=1, source_target_pairs={{0,3},{1,2},{2,1},{3,0},{4,7},{5,6},{6,5},{7,4},{8,11},{9,10},{10,... | collective-permute-start | bytes 393224 | tf_op jit(solution)/shard_map/ppermute | solution.py:113
  130.6 9.0 %collective-permute-start.43 = (bf16[2,4,64,128]{3,2,1,0:T(8,128)(2,1)S(1)}, bf16[2,4,64,128]{3,2,1,0:T(8,128)(2,1)S(1)}, u32[]{:S(2)}, u32[]{:S(2)}) collective-permute-start(bf16[2,4,64,128]{3,2,1,0:T(8,128)(2,1)S(1)} %collective-permute-done.40.refs_2_), channel_id=1, source_target_pairs={{0,16},{16,0},{1,17},{17,1},{2,18},{18,2},{3,19},{19,3},{4,20},{20... | collective-permute-start | bytes 393224 | tf_op jit(solution)/shard_map/ppermute | solution.py:113
  132.1 8.7 %collective-permute-start.41 = (bf16[2,4,64,128]{3,2,1,0:T(8,128)(2,1)S(1)}, bf16[2,4,64,128]{3,2,1,0:T(8,128)(2,1)S(1)}, u32[]{:S(2)}, u32[]{:S(2)}) collective-permute-start(bf16[2,4,64,128]{3,2,1,0:T(8,128)(2,1)S(1)} %collective-permute-done.30.refs_0_), channel_id=1, source_target_pairs={{0,16},{16,0},{1,17},{17,1},{2,18},{18,2},{3,19},{19,3},{4,20},{20... | collective-permute-start | bytes 393224 | tf_op jit(solution)/shard_map/ppermute | solution.py:113
  133.5 7.3 %collective-permute-start.42 = (bf16[2,4,64,128]{3,2,1,0:T(8,128)(2,1)S(1)}, bf16[2,4,64,128]{3,2,1,0:T(8,128)(2,1)S(1)}, u32[]{:S(2)}, u32[]{:S(2)}) collective-permute-start(bf16[2,4,64,128]{3,2,1,0:T(8,128)(2,1)S(1)} %collective-permute-done.31.refs_1_), channel_id=1, source_target_pairs={{0,16},{16,0},{1,17},{17,1},{2,18},{18,2},{3,19},{19,3},{4,20},{20... | collective-permute-start | bytes 393224 | tf_op jit(solution)/shard_map/ppermute | solution.py:113
  137.6 6.4 %collective-permute-start.46 = (bf16[2,4,64,128]{3,2,1,0:T(8,128)(2,1)S(1)}, bf16[2,4,64,128]{3,2,1,0:T(8,128)(2,1)S(1)}, u32[]{:S(2)}, u32[]{:S(2)}) collective-permute-start(bf16[2,4,64,128]{3,2,1,0:T(8,128)(2,1)S(1)} %collective-permute-done.44.refs_8_), channel_id=1, source_target_pairs={{0,16},{16,0},{1,17},{17,1},{2,18},{18,2},{3,19},{19,3},{4,20},{20... | collective-permute-start | bytes 393224 | tf_op jit(solution)/shard_map/ppermute | solution.py:113
  138.8 6.7 %collective-permute-start.47 = (bf16[2,4,64,128]{3,2,1,0:T(8,128)(2,1)S(1)}, bf16[2,4,64,128]{3,2,1,0:T(8,128)(2,1)S(1)}, u32[]{:S(2)}, u32[]{:S(2)}) collective-permute-start(bf16[2,4,64,128]{3,2,1,0:T(8,128)(2,1)S(1)} %collective-permute-done.45.refs_9_), channel_id=1, source_target_pairs={{0,16},{16,0},{1,17},{17,1},{2,18},{18,2},{3,19},{19,3},{4,20},{20... | collective-permute-start | bytes 393224 | tf_op jit(solution)/shard_map/ppermute | solution.py:113
  139.7 7.3 %collective-permute-start.48 = (bf16[2,4,64,128]{3,2,1,0:T(8,128)(2,1)S(1)}, bf16[2,4,64,128]{3,2,1,0:T(8,128)(2,1)S(1)}, u32[]{:S(2)}, u32[]{:S(2)}) collective-permute-start(bf16[2,4,64,128]{3,2,1,0:T(8,128)(2,1)S(1)} %collective-permute-done.38.refs_10_), channel_id=1, source_target_pairs={{0,16},{16,0},{1,17},{17,1},{2,18},{18,2},{3,19},{19,3},{4,20},{20... | collective-permute-start | bytes 393224 | tf_op jit(solution)/shard_map/ppermute | solution.py:113
  152.8 8.4 %collective-permute-start.50 = (bf16[4,2,2,64,128]{4,3,2,1,0:T(8,128)(2,1)S(1)}, bf16[4,2,2,64,128]{4,3,2,1,0:T(8,128)(2,1)S(1)}, u32[]{:S(2)}, u32[]{:S(2)}) collective-permute-start(bf16[4,2,2,64,128]{4,3,2,1,0:T(8,128)(2,1)S(1)} %fusion.3), channel_id=1, source_target_pairs={{0,8},{4,12},{8,0},{12,4},{1,9},{5,13},{9,1},{13,5},{2,10},{6,14},... | collective-permute-start | bytes 786440 | tf_op jit(solution)/shard_map/ppermute | solution.py:113
  161.4 5.2 %collective-permute-start.51 = (bf16[2,2,64,128]{3,2,1,0:T(8,128)(2,1)S(1)}, bf16[2,2,64,128]{3,2,1,0:T(8,128)(2,1)S(1)}, u32[]{:S(2)}, u32[]{:S(2)}) collective-permute-start(bf16[2,2,64,128]{3,2,1,0:T(8,128)(2,1)S(1)} %get-tuple-element.134), channel_id=1, source_target_pairs={{0,1},{1,0},{2,3},{3,2},{4,5},{5,4},{6,7},{7,6},{8,9},{9,8},{10,11... | collective-permute-start | bytes 196616 | tf_op jit(solution)/shard_map/ppermute | solution.py:113
  164.0 7.5 %collective-permute-start.52 = (bf16[2,2,64,128]{3,2,1,0:T(8,128)(2,1)S(1)}, bf16[2,2,64,128]{3,2,1,0:T(8,128)(2,1)S(1)}, u32[]{:S(2)}, u32[]{:S(2)}) collective-permute-start(bf16[2,2,64,128]{3,2,1,0:T(8,128)(2,1)S(1)} %get-tuple-element.133), channel_id=1, source_target_pairs={{0,2},{1,3},{2,0},{3,1},{4,6},{5,7},{6,4},{7,5},{8,10},{9,11},{10,... | collective-permute-start | bytes 196616 | tf_op jit(solution)/shard_map/ppermute | solution.py:113
  165.2 6.2 %collective-permute-start.53 = (bf16[2,2,64,128]{3,2,1,0:T(8,128)(2,1)S(1)}, bf16[2,2,64,128]{3,2,1,0:T(8,128)(2,1)S(1)}, u32[]{:S(2)}, u32[]{:S(2)}) collective-permute-start(bf16[2,2,64,128]{3,2,1,0:T(8,128)(2,1)S(1)} %get-tuple-element.132), channel_id=1, source_target_pairs={{0,3},{1,2},{2,1},{3,0},{4,7},{5,6},{6,5},{7,4},{8,11},{9,10},{10,... | collective-permute-start | bytes 196616 | tf_op jit(solution)/shard_map/ppermute | solution.py:113
  173.2 6.6 %collective-permute-start.55 = (bf16[2,2,64,128]{3,2,1,0:T(8,128)(2,1)S(1)}, bf16[2,2,64,128]{3,2,1,0:T(8,128)(2,1)S(1)}, u32[]{:S(2)}, u32[]{:S(2)}) collective-permute-start(bf16[2,2,64,128]{3,2,1,0:T(8,128)(2,1)S(1)} %get-tuple-element.106), channel_id=1, source_target_pairs={{0,3},{1,2},{2,1},{3,0},{4,7},{5,6},{6,5},{7,4},{8,11},{9,10},{10,... | collective-permute-start | bytes 196616 | tf_op jit(solution)/shard_map/ppermute | solution.py:113
  175.6 5.3 %collective-permute-start.58 = (bf16[2,2,64,128]{3,2,1,0:T(8,128)(2,1)S(1)}, bf16[2,2,64,128]{3,2,1,0:T(8,128)(2,1)S(1)}, u32[]{:S(2)}, u32[]{:S(2)}) collective-permute-start(bf16[2,2,64,128]{3,2,1,0:T(8,128)(2,1)S(1)} %get-tuple-element.107), channel_id=1, source_target_pairs={{0,1},{1,0},{2,3},{3,2},{4,5},{5,4},{6,7},{7,6},{8,9},{9,8},{10,11... | collective-permute-start | bytes 196616 | tf_op jit(solution)/shard_map/ppermute | solution.py:113
  176.0 4.9 %collective-permute-start.60 = (bf16[2,2,64,128]{3,2,1,0:T(8,128)(2,1)S(1)}, bf16[2,2,64,128]{3,2,1,0:T(8,128)(2,1)S(1)}, u32[]{:S(2)}, u32[]{:S(2)}) collective-permute-start(bf16[2,2,64,128]{3,2,1,0:T(8,128)(2,1)S(1)} %get-tuple-element.105.refs_14_), channel_id=1, source_target_pairs={{0,8},{4,12},{8,0},{12,4},{1,9},{5,13},{9,1},{13,5},{2,10},{6,14},... | collective-permute-start | bytes 196616 | tf_op jit(solution)/shard_map/ppermute | solution.py:113
  176.8 5.2 %collective-permute-start.62 = (bf16[2,2,64,128]{3,2,1,0:T(8,128)(2,1)S(1)}, bf16[2,2,64,128]{3,2,1,0:T(8,128)(2,1)S(1)}, u32[]{:S(2)}, u32[]{:S(2)}) collective-permute-start(bf16[2,2,64,128]{3,2,1,0:T(8,128)(2,1)S(1)} %get-tuple-element.108), channel_id=1, source_target_pairs={{0,2},{1,3},{2,0},{3,1},{4,6},{5,7},{6,4},{7,5},{8,10},{9,11},{10,... | collective-permute-start | bytes 196616 | tf_op jit(solution)/shard_map/ppermute | solution.py:113
  178.5 4.7 %collective-permute-start.54 = (bf16[2,2,64,128]{3,2,1,0:T(8,128)(2,1)S(1)}, bf16[2,2,64,128]{3,2,1,0:T(8,128)(2,1)S(1)}, u32[]{:S(2)}, u32[]{:S(2)}) collective-permute-start(bf16[2,2,64,128]{3,2,1,0:T(8,128)(2,1)S(1)} %get-tuple-element.105.refs_14_), channel_id=1, source_target_pairs={{0,4},{4,0},{8,12},{12,8},{1,5},{5,1},{9,13},{13,9},{2,6},{6,2},{1... | collective-permute-start | bytes 196616 | tf_op jit(solution)/shard_map/ppermute | solution.py:113
  179.8 4.3 %collective-permute-start.56 = (bf16[2,2,64,128]{3,2,1,0:T(8,128)(2,1)S(1)}, bf16[2,2,64,128]{3,2,1,0:T(8,128)(2,1)S(1)}, u32[]{:S(2)}, u32[]{:S(2)}) collective-permute-start(bf16[2,2,64,128]{3,2,1,0:T(8,128)(2,1)S(1)} %collective-permute-done.55.refs_1_), channel_id=1, source_target_pairs={{0,8},{4,12},{8,0},{12,4},{1,9},{5,13},{9,1},{13,5},{2,10},{6,14},... | collective-permute-start | bytes 196616 | tf_op jit(solution)/shard_map/ppermute | solution.py:113
  183.2 4.3 %collective-permute-start.64 = (bf16[2,2,64,128]{3,2,1,0:T(8,128)(2,1)S(1)}, bf16[2,2,64,128]{3,2,1,0:T(8,128)(2,1)S(1)}, u32[]{:S(2)}, u32[]{:S(2)}) collective-permute-start(bf16[2,2,64,128]{3,2,1,0:T(8,128)(2,1)S(1)} %collective-permute-done.58.refs_11_), channel_id=1, source_target_pairs={{0,8},{4,12},{8,0},{12,4},{1,9},{5,13},{9,1},{13,5},{2,10},{6,14},... | collective-permute-start | bytes 196616 | tf_op jit(solution)/shard_map/ppermute | solution.py:113
  191.9 9.2 %collective-permute-start.69 = (bf16[2,2,4,64,128]{4,3,2,1,0:T(8,128)(2,1)S(1)}, bf16[2,2,4,64,128]{4,3,2,1,0:T(8,128)(2,1)S(1)}, u32[]{:S(2)}, u32[]{:S(2)}) collective-permute-start(bf16[2,2,4,64,128]{4,3,2,1,0:T(8,128)(2,1)S(1)} %get-tuple-element.110), channel_id=1, source_target_pairs={{0,16},{16,0},{1,17},{17,1},{2,18},{18,2},{3,19},{19,3},{4,20},{20... | collective-permute-start | bytes 786440 | tf_op jit(solution)/shard_map/ppermute | solution.py:113
  193.7 13.1 %collective-permute-start.72 = (bf16[2,2,4,64,128]{4,3,2,1,0:T(8,128)(2,1)S(1)}, bf16[2,2,4,64,128]{4,3,2,1,0:T(8,128)(2,1)S(1)}, u32[]{:S(2)}, u32[]{:S(2)}) collective-permute-start(bf16[2,2,4,64,128]{4,3,2,1,0:T(8,128)(2,1)S(1)} %get-tuple-element.112), channel_id=1, source_target_pairs={{0,16},{16,0},{1,17},{17,1},{2,18},{18,2},{3,19},{19,3},{4,20},{20... | collective-permute-start | bytes 786440 | tf_op jit(solution)/shard_map/ppermute | solution.py:113
  194.0 18.4 %collective-permute-start.75 = (bf16[2,2,4,64,128]{4,3,2,1,0:T(8,128)(2,1)S(1)}, bf16[2,2,4,64,128]{4,3,2,1,0:T(8,128)(2,1)S(1)}, u32[]{:S(2)}, u32[]{:S(2)}) collective-permute-start(bf16[2,2,4,64,128]{4,3,2,1,0:T(8,128)(2,1)S(1)} %get-tuple-element.114), channel_id=1, source_target_pairs={{0,16},{16,0},{1,17},{17,1},{2,18},{18,2},{3,19},{19,3},{4,20},{20... | collective-permute-start | bytes 786440 | tf_op jit(solution)/shard_map/ppermute | solution.py:113
  195.7 23.1 %collective-permute-start.78 = (bf16[2,2,4,64,128]{4,3,2,1,0:T(8,128)(2,1)S(1)}, bf16[2,2,4,64,128]{4,3,2,1,0:T(8,128)(2,1)S(1)}, u32[]{:S(2)}, u32[]{:S(2)}) collective-permute-start(bf16[2,2,4,64,128]{4,3,2,1,0:T(8,128)(2,1)S(1)} %get-tuple-element.116), channel_id=1, source_target_pairs={{0,16},{16,0},{1,17},{17,1},{2,18},{18,2},{3,19},{19,3},{4,20},{20... | collective-permute-start | bytes 786440 | tf_op jit(solution)/shard_map/ppermute | solution.py:113
  201.2 13.0 %collective-permute-start.70 = (bf16[2,4,64,128]{3,2,1,0:T(8,128)(2,1)S(1)}, bf16[2,4,64,128]{3,2,1,0:T(8,128)(2,1)S(1)}, u32[]{:S(2)}, u32[]{:S(2)}) collective-permute-start(bf16[2,4,64,128]{3,2,1,0:T(8,128)(2,1)S(1)} %get-tuple-element.127), channel_id=1, source_target_pairs={{0,2},{1,3},{2,0},{3,1},{4,6},{5,7},{6,4},{7,5},{8,10},{9,11},{10,... | collective-permute-start | bytes 393224 | tf_op jit(solution)/shard_map/ppermute | solution.py:113
  202.9 13.6 %collective-permute-start.71 = (bf16[2,4,64,128]{3,2,1,0:T(8,128)(2,1)S(1)}, bf16[2,4,64,128]{3,2,1,0:T(8,128)(2,1)S(1)}, u32[]{:S(2)}, u32[]{:S(2)}) collective-permute-start(bf16[2,4,64,128]{3,2,1,0:T(8,128)(2,1)S(1)} %get-tuple-element.126), channel_id=1, source_target_pairs={{0,3},{1,2},{2,1},{3,0},{4,7},{5,6},{6,5},{7,4},{8,11},{9,10},{10,... | collective-permute-start | bytes 393224 | tf_op jit(solution)/shard_map/ppermute | solution.py:113
  206.8 9.8 %collective-permute-start.73 = (bf16[2,4,64,128]{3,2,1,0:T(8,128)(2,1)S(1)}, bf16[2,4,64,128]{3,2,1,0:T(8,128)(2,1)S(1)}, u32[]{:S(2)}, u32[]{:S(2)}) collective-permute-start(bf16[2,4,64,128]{3,2,1,0:T(8,128)(2,1)S(1)} %fusion.12), channel_id=1, source_target_pairs={{0,1},{1,0},{2,3},{3,2},{4,5},{5,4},{6,7},{7,6},{8,9},{9,8},{10,11... | collective-permute-start | bytes 393224 | tf_op jit(solution)/shard_map/ppermute | solution.py:113
  212.5 11.8 %collective-permute-start.76 = (bf16[2,4,64,128]{3,2,1,0:T(8,128)(2,1)S(1)}, bf16[2,4,64,128]{3,2,1,0:T(8,128)(2,1)S(1)}, u32[]{:S(2)}, u32[]{:S(2)}) collective-permute-start(bf16[2,4,64,128]{3,2,1,0:T(8,128)(2,1)S(1)} %get-tuple-element.125), channel_id=1, source_target_pairs={{0,2},{1,3},{2,0},{3,1},{4,6},{5,7},{6,4},{7,5},{8,10},{9,11},{10,... | collective-permute-start | bytes 393224 | tf_op jit(solution)/shard_map/ppermute | solution.py:113
  214.2 10.1 %collective-permute-start.77 = (bf16[2,4,64,128]{3,2,1,0:T(8,128)(2,1)S(1)}, bf16[2,4,64,128]{3,2,1,0:T(8,128)(2,1)S(1)}, u32[]{:S(2)}, u32[]{:S(2)}) collective-permute-start(bf16[2,4,64,128]{3,2,1,0:T(8,128)(2,1)S(1)} %get-tuple-element.124), channel_id=1, source_target_pairs={{0,3},{1,2},{2,1},{3,0},{4,7},{5,6},{6,5},{7,4},{8,11},{9,10},{10,... | collective-permute-start | bytes 393224 | tf_op jit(solution)/shard_map/ppermute | solution.py:113
  218.9 6.5 %collective-permute-start.79 = (bf16[2,4,64,128]{3,2,1,0:T(8,128)(2,1)S(1)}, bf16[2,4,64,128]{3,2,1,0:T(8,128)(2,1)S(1)}, u32[]{:S(2)}, u32[]{:S(2)}) collective-permute-start(bf16[2,4,64,128]{3,2,1,0:T(8,128)(2,1)S(1)} %fusion.15), channel_id=1, source_target_pairs={{0,1},{1,0},{2,3},{3,2},{4,5},{5,4},{6,7},{7,6},{8,9},{9,8},{10,11... | collective-permute-start | bytes 393224 | tf_op jit(solution)/shard_map/ppermute | solution.py:113
  219.0 10.4 %collective-permute-start.82 = (bf16[4,2,2,64,128]{4,3,2,1,0:T(8,128)(2,1)S(1)}, bf16[4,2,2,64,128]{4,3,2,1,0:T(8,128)(2,1)}, u32[]{:S(2)}, u32[]{:S(2)}) collective-permute-start(bf16[4,2,2,64,128]{4,3,2,1,0:T(8,128)(2,1)S(1)} %get-tuple-element.123.refs_0_), channel_id=1, source_target_pairs={{0,8},{4,12},{8,0},{12,4},{1,9},{5,13},{9,1},{13,5},{2,10},{6,14},... | collective-permute-start | bytes 786440 | tf_op jit(solution)/shard_map/ppermute | solution.py:113
  219.9 20.4 %collective-permute-start.74 = (bf16[2,4,4,64,128]{4,3,2,1,0:T(8,128)(2,1)S(1)}, bf16[2,4,4,64,128]{4,3,2,1,0:T(8,128)(2,1)S(1)}, u32[]{:S(2)}, u32[]{:S(2)}) collective-permute-start(bf16[2,4,4,64,128]{4,3,2,1,0:T(8,128)(2,1)S(1)} %mute_receiver.6.refs_0_), channel_id=1, source_target_pairs={{0,16},{16,0},{1,17},{17,1},{2,18},{18,2},{3,19},{19,3},{4,20},{20... | collective-permute-start | bytes 1572872 | tf_op jit(solution)/shard_map/ppermute | solution.py:113
  227.7 16.1 %collective-permute-start.80 = (bf16[2,4,4,64,128]{4,3,2,1,0:T(8,128)(2,1)S(1)}, bf16[2,4,4,64,128]{4,3,2,1,0:T(8,128)(2,1)}, u32[]{:S(2)}, u32[]{:S(2)}) collective-permute-start(bf16[2,4,4,64,128]{4,3,2,1,0:T(8,128)(2,1)S(1)} %mute_receiver.7.refs_1_), channel_id=1, source_target_pairs={{0,16},{16,0},{1,17},{17,1},{2,18},{18,2},{3,19},{19,3},{4,20},{20... | collective-permute-start | bytes 1572872 | tf_op jit(solution)/shard_map/ppermute | solution.py:113
  (23 other events, 149.6 us)

commit v7 on v6

--- a/solution.py
+++ b/solution.py
@@ -264,7 +264,7 @@
                             out[y, k, c, p, window, :] = part.astype(BF16)
         return carry
 
-    lax.fori_loop(0, refl_ref.shape[1] // BLOCK_W, block, 0)
+    lax.fori_loop(0, refl_ref.shape[1] // BLOCK_W, block, 0, unroll=2)
 
 
 def convolve_pieces(ids, reflection, plan, arrays, pieces, focal):
@@ -334,7 +334,7 @@
                     index += 1
         return carry
 
-    lax.fori_loop(0, refl_ref.shape[1] // BLOCK_W, block, 0)
+    lax.fori_loop(0, refl_ref.shape[1] // BLOCK_W, block, 0, unroll=2)
 
 
 PAIRS = ((2, 3), (1, 0))

time: 247 us -> 247 us (level)
  transfers between devices with their start and end apart: 84 -> 84, of which waited for: 41 -> 42; matrix products, arithmetic and copies ran while one was open for 0% -> 0% of each run, Pallas kernels for 11% -> 11%
where the time goes in v7:
time: 247 us
  waiting for transfers between devices  99.9 us (40%)
  starting transfers between devices  95.4 us (39%)
  Pallas kernels  49.2 us (20%)
    ppermute x84, waiting for transfers between devices, swap(): return lax.ppermute(value, axis, [(i, i ^ mask) for i in range(count)])  99.9 us
    ppermute x84, starting transfers between devices, swap(): return lax.ppermute(value, axis, [(i, i ^ mask) for i in range(count)])  95.4 us
    pallas_call x11, Pallas kernels, call(): pl.pallas_call(kernel, name=name, out_shape=out_shape, in_specs=[SMEM_SPE...  30.1 us
    pallas_call x4, Pallas kernels, split_wave(): pl.pallas_call(functools.partial(split_kernel, both), name='split_wave',...  7.04 us
    pallas_call x1, Pallas kernels, trace_source(): pl.pallas_call(trace_kernel, name='trace_source', out_shape=jax.ShapeDtyp...  6.27 us
    pallas_call x2, Pallas kernels, join_halves(): pl.pallas_call(join_kernel, name='join_halves', out_shape=jax.ShapeDtypeS...  5.85 us
  transfers between devices with their start and end apart: 84, of which 42 were waited for; matrix products, arithmetic and copies ran while one was open for 0% of the time, Pallas kernels for 11%

profile of v7, /device:TPU:0, one launch (start us, length us, event | category | flops | bytes accessed | tf_op | source)
XLA Modules:
  0.0 246.7 jit_solution(3506166100209197068)
XLA Ops:
  0.7 1.8 split_wave.6.refs_7_
  2.6 4.1 %collective-permute-start = (bf16[2,8,64,128]{3,2,1,0:T(8,128)(2,1)S(1)}, bf16[2,8,64,128]{3,2,1,0:T(8,128)(2,1)S(1)}, u32[]{:S(2)}, u32[]{:S(2)}) collective-permute-start(bf16[2,8,64,128]{3,2,1,0:T(8,128)(2,1)S(1)} %split_wave.6.refs_7_), channel_id=1, source_target_pairs={{0,2},{1,3},{2,0},{3,1},{4,6},{5,7},{6,4},{7,5},{8,10},{9,11},{10,... | collective-permute-start | bytes 786440 | tf_op jit(solution)/shard_map/ppermute | solution.py:113
  6.7 4.1 %basis.1 = (bf16[512,1024]{1,0:T(8,128)(2,1)S(1)}, bf16[1024,512]{1,0:T(8,128)(2,1)S(1)}) custom-call(s32[3]{0:T(128)S(1)} %pad_add_fusion.ids), custom_call_target="tpu_custom_call" | custom-call | flops 20971520 | bytes 2097152 | tf_op jit(solution)/shard_map/basis/pallas_call | solution.py:118
  10.8 1.6 split_wave.4.refs_8_
  13.8 1.8 split_wave.7.refs_6_
  15.9 9.1 %collective-permute-done.refs_1_ = bf16[2,8,64,128]{3,2,1,0:T(8,128)(2,1)S(1)} collective-permute-done((bf16[2,8,64,128]{3,2,1,0:T(8,128)(2,1)S(1)}, bf16[2,8,64,128]{3,2,1,0:T(8,128)(2,1)S(1)}, u32[]{:S(2)}, u32[]{:S(2)}) %collective-permute-start) | collective-permute-done | bytes 262176 | tf_op jit(solution)/shard_map/ppermute | solution.py:113
  25.1 1.8 collective-permute-start.1
  27.1 1.8 split_wave.5.refs_0_.refs_5_
  28.9 5.4 %collective-permute-done.1.refs_2_ = bf16[2,8,64,128]{3,2,1,0:T(8,128)(2,1)S(1)} collective-permute-done((bf16[2,8,64,128]{3,2,1,0:T(8,128)(2,1)S(1)}, bf16[2,8,64,128]{3,2,1,0:T(8,128)(2,1)S(1)}, u32[]{:S(2)}, u32[]{:S(2)}) %collective-permute-start.1) | collective-permute-done | bytes 262176 | tf_op jit(solution)/shard_map/ppermute | solution.py:113
  34.3 2.9 %collective-permute-done.3.refs_4_ = bf16[2,8,64,128]{3,2,1,0:T(8,128)(2,1)S(1)} collective-permute-done((bf16[2,8,64,128]{3,2,1,0:T(8,128)(2,1)S(1)}, bf16[2,8,64,128]{3,2,1,0:T(8,128)(2,1)S(1)}, u32[]{:S(2)}, u32[]{:S(2)}) %collective-permute-start.3) | collective-permute-done | bytes 262176 | tf_op jit(solution)/shard_map/ppermute | solution.py:113
  37.2 3.7 %convolve.2 = (bf16[2,4,2,2,64,128]{5,4,3,2,1,0:T(8,128)(2,1)S(1)}, bf16[2,4,2,2,64,128]{5,4,3,2,1,0:T(8,128)(2,1)S(1)}) custom-call(s32[3]{0:T(128)S(1)} %pad_add_fusion.ids, bf16[2,64,128,256]{3,2,1,0:T(8,128)(2,1)S(1)} %copy-done, bf16[2,2,8,64,128]{4,3,2,1,0:T(8,128)(2,1)S(1)} %split_wave.5.refs_0_.refs_5_, ...), custom_call_target="tpu_custom_call" | custom-call | flops 536870912 | bytes 11534336 | tf_op jit(solution)/shard_map/convolve/pallas_call | solution.py:118
  41.0 1.9 collective-permute-done.5
  44.1 7.3 %collective-permute-done.6 = bf16[4,2,2,64,128]{4,3,2,1,0:T(8,128)(2,1)S(1)} collective-permute-done((bf16[4,2,2,64,128]{4,3,2,1,0:T(8,128)(2,1)S(1)}, bf16[4,2,2,64,128]{4,3,2,1,0:T(8,128)(2,1)S(1)}, u32[]{:S(2)}, u32[]{:S(2)}) %collective-permute-start.6) | collective-permute-done | bytes 262176 | tf_op jit(solution)/shard_map/ppermute | solution.py:113
  51.5 1.7 collective-permute-start.7
  53.2 3.4 %collective-permute-start.8 = (bf16[2,2,64,128]{3,2,1,0:T(8,128)(2,1)S(1)}, bf16[2,2,64,128]{3,2,1,0:T(8,128)(2,1)S(1)}, u32[]{:S(2)}, u32[]{:S(2)}) collective-permute-start(bf16[2,2,64,128]{3,2,1,0:T(8,128)(2,1)S(1)} %get-tuple-element.137), channel_id=1, source_target_pairs={{0,2},{1,3},{2,0},{3,1},{4,6},{5,7},{6,4},{7,5},{8,10},{9,11},{10,... | collective-permute-start | bytes 196616 | tf_op jit(solution)/shard_map/ppermute | solution.py:113
  56.6 4.1 %collective-permute-done.8.refs_2_ = bf16[2,2,64,128]{3,2,1,0:T(8,128)(2,1)S(1)} collective-permute-done((bf16[2,2,64,128]{3,2,1,0:T(8,128)(2,1)S(1)}, bf16[2,2,64,128]{3,2,1,0:T(8,128)(2,1)S(1)}, u32[]{:S(2)}, u32[]{:S(2)}) %collective-permute-start.8) | collective-permute-done | bytes 65568 | tf_op jit(solution)/shard_map/ppermute | solution.py:113
  60.7 1.9 collective-permute-done.9.refs_3_
  62.6 1.7 mute_source.2
  67.7 2.6 %collective-permute-start.18 = (bf16[2,2,64,128]{3,2,1,0:T(8,128)(2,1)S(1)}, bf16[2,2,64,128]{3,2,1,0:T(8,128)(2,1)S(1)}, u32[]{:S(2)}, u32[]{:S(2)}) collective-permute-start(bf16[2,2,64,128]{3,2,1,0:T(8,128)(2,1)S(1)} %get-tuple-element.75), channel_id=1, source_target_pairs={{0,2},{1,3},{2,0},{3,1},{4,6},{5,7},{6,4},{7,5},{8,10},{9,11},{10,... | collective-permute-start | bytes 196616 | tf_op jit(solution)/shard_map/ppermute | solution.py:113
  73.3 1.5 collective-permute-start.20
  75.5 1.9 collective-permute-done.22.refs_12_
  79.3 3.0 %correlate.2 = (bf16[2,2,4,64,128]{4,3,2,1,0:T(8,128)(2,1)S(1)}, bf16[2,2,4,64,128]{4,3,2,1,0:T(8,128)(2,1)S(1)}, bf16[2,2,4,64,128]{4,3,2,1,0:T(8,128)(2,1)S(1)...) custom-call(s32[3]{0:T(128)S(1)} %pad_add_fusion.ids, ...), custom_call_target="tpu_custom_call" | custom-call | flops 536870912 | bytes 11534336 | tf_op jit(solution)/shard_map/correlate/pallas_call | solution.py:118
  82.4 1.6 collective-permute-start.25
  84.5 1.5 collective-permute-start.32
  86.5 5.1 %collective-permute-done.25 = bf16[2,2,4,64,128]{4,3,2,1,0:T(8,128)(2,1)S(1)} collective-permute-done((bf16[2,2,4,64,128]{4,3,2,1,0:T(8,128)(2,1)S(1)}, bf16[2,2,4,64,128]{4,3,2,1,0:T(8,128)(2,1)S(1)}, u32[]{:S(2)}, u32[]{:S(2)}) %collective-permute-start.25) | collective-permute-done | bytes 262176 | tf_op jit(solution)/shard_map/ppermute | solution.py:113
  91.7 2.4 collective-permute-start.26
  95.5 1.7 collective-permute-done.28.refs_4_
  98.7 4.1 %collective-permute-done.32 = bf16[2,2,4,64,128]{4,3,2,1,0:T(8,128)(2,1)S(1)} collective-permute-done((bf16[2,2,4,64,128]{4,3,2,1,0:T(8,128)(2,1)S(1)}, bf16[2,2,4,64,128]{4,3,2,1,0:T(8,128)(2,1)S(1)}, u32[]{:S(2)}, u32[]{:S(2)}) %collective-permute-start.32) | collective-permute-done | bytes 262176 | tf_op jit(solution)/shard_map/ppermute | solution.py:113
  102.9 2.4 collective-permute-start.33
  106.8 2.3 mute_receiver.4
  109.2 1.5 collective-permute-start.37
  110.7 3.0 %collective-permute-start.30 = (bf16[2,4,64,128]{3,2,1,0:T(8,128)(2,1)S(1)}, bf16[2,4,64,128]{3,2,1,0:T(8,128)(2,1)S(1)}, u32[]{:S(2)}, u32[]{:S(2)}) collective-permute-start(bf16[2,4,64,128]{3,2,1,0:T(8,128)(2,1)S(1)} %get-tuple-element.80), channel_id=1, source_target_pairs={{0,2},{1,3},{2,0},{3,1},{4,6},{5,7},{6,4},{7,5},{8,10},{9,11},{10,... | collective-permute-start | bytes 393224 | tf_op jit(solution)/shard_map/ppermute | solution.py:113
  115.0 6.1 %collective-permute-start.31 = (bf16[2,4,64,128]{3,2,1,0:T(8,128)(2,1)S(1)}, bf16[2,4,64,128]{3,2,1,0:T(8,128)(2,1)S(1)}, u32[]{:S(2)}, u32[]{:S(2)}) collective-permute-start(bf16[2,4,64,128]{3,2,1,0:T(8,128)(2,1)S(1)} %get-tuple-element.81), channel_id=1, source_target_pairs={{0,3},{1,2},{2,1},{3,0},{4,7},{5,6},{6,5},{7,4},{8,11},{9,10},{10,... | collective-permute-start | bytes 393224 | tf_op jit(solution)/shard_map/ppermute | solution.py:113
  122.1 2.2 mute_receiver.5
  128.8 1.6 collective-permute-start.45
  133.8 3.5 %collective-permute-done.44.refs_8_ = bf16[2,4,64,128]{3,2,1,0:T(8,128)(2,1)S(1)} collective-permute-done((bf16[2,4,64,128]{3,2,1,0:T(8,128)(2,1)S(1)}, bf16[2,4,64,128]{3,2,1,0:T(8,128)(2,1)S(1)}, u32[]{:S(2)}, u32[]{:S(2)}) %collective-permute-start.44) | collective-permute-done | bytes 131104 | tf_op jit(solution)/shard_map/ppermute | solution.py:113
  140.6 3.2 %collective-permute-done.46.refs_12_ = bf16[2,4,64,128]{3,2,1,0:T(8,128)(2,1)S(1)} collective-permute-done((bf16[2,4,64,128]{3,2,1,0:T(8,128)(2,1)S(1)}, bf16[2,4,64,128]{3,2,1,0:T(8,128)(2,1)S(1)}, u32[]{:S(2)}, u32[]{:S(2)}) %collective-permute-start.46) | collective-permute-done | bytes 131104 | tf_op jit(solution)/shard_map/ppermute | solution.py:113
  146.6 3.7 %convolve.3 = (bf16[2,4,2,2,64,128]{5,4,3,2,1,0:T(8,128)(2,1)S(1)}, bf16[2,4,2,2,64,128]{5,4,3,2,1,0:T(8,128)(2,1)S(1)}) custom-call(s32[3]{0:T(128)S(1)} %pad_add_fusion.ids, bf16[2,64,128,256]{3,2,1,0:T(8,128)(2,1)S(1)} %copy-done, bf16[2,4,64,128]{3,2,1,0:T(8,128)(2,1)S(1)} %collective-permute-done.30.refs_0_, ...), custom_call_target="tpu_custom_call" | custom-call | flops 536870912 | bytes 11534336 | tf_op jit(solution)/shard_map/convolve/pallas_call | solution.py:118
  150.4 1.9 collective-permute-done.49
  153.6 7.2 %collective-permute-done.50 = bf16[4,2,2,64,128]{4,3,2,1,0:T(8,128)(2,1)S(1)} collective-permute-done((bf16[4,2,2,64,128]{4,3,2,1,0:T(8,128)(2,1)S(1)}, bf16[4,2,2,64,128]{4,3,2,1,0:T(8,128)(2,1)S(1)}, u32[]{:S(2)}, u32[]{:S(2)}) %collective-permute-start.50) | collective-permute-done | bytes 262176 | tf_op jit(solution)/shard_map/ppermute | solution.py:113
  161.0 2.5 %collective-permute-start.51 = (bf16[2,2,64,128]{3,2,1,0:T(8,128)(2,1)S(1)}, bf16[2,2,64,128]{3,2,1,0:T(8,128)(2,1)S(1)}, u32[]{:S(2)}, u32[]{:S(2)}) collective-permute-start(bf16[2,2,64,128]{3,2,1,0:T(8,128)(2,1)S(1)} %get-tuple-element.134), channel_id=1, source_target_pairs={{0,1},{1,0},{2,3},{3,2},{4,5},{5,4},{6,7},{7,6},{8,9},{9,8},{10,11... | collective-permute-start | bytes 196616 | tf_op jit(solution)/shard_map/ppermute | solution.py:113
  166.1 4.8 %collective-permute-done.52.refs_2_ = bf16[2,2,64,128]{3,2,1,0:T(8,128)(2,1)S(1)} collective-permute-done((bf16[2,2,64,128]{3,2,1,0:T(8,128)(2,1)S(1)}, bf16[2,2,64,128]{3,2,1,0:T(8,128)(2,1)S(1)}, u32[]{:S(2)}, u32[]{:S(2)}) %collective-permute-start.52) | collective-permute-done | bytes 65568 | tf_op jit(solution)/shard_map/ppermute | solution.py:113
  171.0 1.7 mute_source.3
  172.7 2.4 collective-permute-start.55
  176.4 1.6 collective-permute-start.62
  184.2 1.6 collective-permute-done.66.refs_12_
  188.2 3.1 %correlate.3 = (bf16[2,2,4,64,128]{4,3,2,1,0:T(8,128)(2,1)S(1)}, bf16[2,2,4,64,128]{4,3,2,1,0:T(8,128)(2,1)S(1)}, bf16[2,2,4,64,128]{4,3,2,1,0:T(8,128)(2,1)S(1)...) custom-call(s32[3]{0:T(128)S(1)} %pad_add_fusion.ids, ...), custom_call_target="tpu_custom_call" | custom-call | flops 536870912 | bytes 11534336 | tf_op jit(solution)/shard_map/correlate/pallas_call | solution.py:118
  191.3 1.7 collective-permute-start.69
  193.4 1.6 collective-permute-start.75
  195.4 5.1 %collective-permute-done.69 = bf16[2,2,4,64,128]{4,3,2,1,0:T(8,128)(2,1)S(1)} collective-permute-done((bf16[2,2,4,64,128]{4,3,2,1,0:T(8,128)(2,1)S(1)}, bf16[2,2,4,64,128]{4,3,2,1,0:T(8,128)(2,1)S(1)}, u32[]{:S(2)}, u32[]{:S(2)}) %collective-permute-start.69) | collective-permute-done | bytes 262176 | tf_op jit(solution)/shard_map/ppermute | solution.py:113
  200.6 1.7 collective-permute-start.70
  202.3 2.4 collective-permute-start.71
  206.2 1.7 collective-permute-start.73
  207.9 3.8 %collective-permute-done.75 = bf16[2,2,4,64,128]{4,3,2,1,0:T(8,128)(2,1)S(1)} collective-permute-done((bf16[2,2,4,64,128]{4,3,2,1,0:T(8,128)(2,1)S(1)}, bf16[2,2,4,64,128]{4,3,2,1,0:T(8,128)(2,1)S(1)}, u32[]{:S(2)}, u32[]{:S(2)}) %collective-permute-start.75) | collective-permute-done | bytes 262176 | tf_op jit(solution)/shard_map/ppermute | solution.py:113
  211.9 1.7 collective-permute-start.76
  213.6 2.4 collective-permute-start.77
  216.0 2.2 mute_receiver.6.refs_0_
  220.8 2.9 %collective-permute-done.76.refs_0_ = bf16[2,4,64,128]{3,2,1,0:T(8,128)(2,1)S(1)} collective-permute-done((bf16[2,4,64,128]{3,2,1,0:T(8,128)(2,1)S(1)}, bf16[2,4,64,128]{3,2,1,0:T(8,128)(2,1)S(1)}, u32[]{:S(2)}, u32[]{:S(2)}) %collective-permute-start.76) | collective-permute-done | bytes 131104 | tf_op jit(solution)/shard_map/ppermute | solution.py:113
  224.8 2.2 mute_receiver.7.refs_1_
  227.0 1.7 collective-permute-start.80
  231.0 6.3 %trace_source.1 = bf16[8,128,1024]{2,1,0:T(8,128)(2,1)} custom-call(s32[3]{0:T(128)S(1)} %pad_add_fusion.ids, s32[8,128,1]{2,1,0:T(8,128)S(1)} %copy.7.onset_ref, bf16[512,1024]{1,0:T(8,128)(2,1)S(1)} %get-tuple-element.65.rows_ref, bf16[4,2,2,64,128]{4,3,2,1,0:T(8,128)(2,1)S(1)} %get-tuple-element.123.refs_0_, ...), custom_call_target="tpu_custom_call" | custom-call | flops 1073741824 | bytes 5242880 | tf_op jit(solution)/shard_map/trace_source/pallas_call | solution.py:438
  237.3 2.4 join_halves.2.refs_2_
  239.7 3.5 %collective-permute-done.80.refs_1_ = bf16[2,4,4,64,128]{4,3,2,1,0:T(8,128)(2,1)} collective-permute-done((bf16[2,4,4,64,128]{4,3,2,1,0:T(8,128)(2,1)S(1)}, bf16[2,4,4,64,128]{4,3,2,1,0:T(8,128)(2,1)}, u32[]{:S(2)}, u32[]{:S(2)}) %collective-permute-start.80) | collective-permute-done | bytes 524320 | tf_op jit(solution)/shard_map/ppermute | solution.py:113
  243.2 3.4 %join_halves.3 = bf16[2,256,8,256]{3,2,1,0:T(8,128)(2,1)} custom-call(s32[3]{0:T(128)S(1)} %pad_add_fusion.ids, bf16[2,4,4,64,128]{4,3,2,1,0:T(8,128)(2,1)S(1)} %collective-permute-done.74.refs_0_, bf16[2,4,4,64,128]{4,3,2,1,0:T(8,128)(2,1)} %collective-permute-done.80.refs_1_, ...), custom_call_target="tpu_custom_call", output_to_operand_aliasing={{}: (3, {})} | custom-call | bytes 2097152 | tf_op jit(solution)/shard_map/join_halves/pallas_call | solution.py:535
  (144 shorter events, 56.3 us)
Async XLA Ops:
  2.6 22.5 %collective-permute-start = (bf16[2,8,64,128]{3,2,1,0:T(8,128)(2,1)S(1)}, bf16[2,8,64,128]{3,2,1,0:T(8,128)(2,1)S(1)}, u32[]{:S(2)}, u32[]{:S(2)}) collective-permute-start(bf16[2,8,64,128]{3,2,1,0:T(8,128)(2,1)S(1)} %split_wave.6.refs_7_), channel_id=1, source_target_pairs={{0,2},{1,3},{2,0},{3,1},{4,6},{5,7},{6,4},{7,5},{8,10},{9,11},{10,... | collective-permute-start | bytes 786440 | tf_op jit(solution)/shard_map/ppermute | solution.py:113
  12.4 14.5 %collective-permute-start.2 = (bf16[2,8,64,128]{3,2,1,0:T(8,128)(2,1)S(1)}, bf16[2,8,64,128]{3,2,1,0:T(8,128)(2,1)S(1)}, u32[]{:S(2)}, u32[]{:S(2)}) collective-permute-start(bf16[2,8,64,128]{3,2,1,0:T(8,128)(2,1)S(1)} %split_wave.4.refs_8_), channel_id=1, source_target_pairs={{0,3},{1,2},{2,1},{3,0},{4,7},{5,6},{6,5},{7,4},{8,11},{9,10},{10,... | collective-permute-start | bytes 786440 | tf_op jit(solution)/shard_map/ppermute | solution.py:113
  15.6 21.6 %collective-permute-start.4 = (bf16[2,2,8,64,128]{4,3,2,1,0:T(8,128)(2,1)S(1)}, bf16[2,2,8,64,128]{4,3,2,1,0:T(8,128)(2,1)S(1)}, u32[]{:S(2)}, u32[]{:S(2)}) collective-permute-start(bf16[2,2,8,64,128]{4,3,2,1,0:T(8,128)(2,1)S(1)} %split_wave.7.refs_6_), channel_id=1, source_target_pairs={{0,1},{1,0},{2,3},{3,2},{4,5},{5,4},{6,7},{7,6},{8,9},{9,8},{10,11... | collective-permute-start | bytes 1572872 | tf_op jit(solution)/shard_map/ppermute | solution.py:113
  25.1 9.2 %collective-permute-start.1 = (bf16[2,8,64,128]{3,2,1,0:T(8,128)(2,1)S(1)}, bf16[2,8,64,128]{3,2,1,0:T(8,128)(2,1)S(1)}, u32[]{:S(2)}, u32[]{:S(2)}) collective-permute-start(bf16[2,8,64,128]{3,2,1,0:T(8,128)(2,1)S(1)} %collective-permute-done.refs_1_), channel_id=1, source_target_pairs={{0,16},{16,0},{1,17},{17,1},{2,18},{18,2},{3,19},{19,3},{4,20},{20... | collective-permute-start | bytes 786440 | tf_op jit(solution)/shard_map/ppermute | solution.py:113
  26.9 10.3 %collective-permute-start.3 = (bf16[2,8,64,128]{3,2,1,0:T(8,128)(2,1)S(1)}, bf16[2,8,64,128]{3,2,1,0:T(8,128)(2,1)S(1)}, u32[]{:S(2)}, u32[]{:S(2)}) collective-permute-start(bf16[2,8,64,128]{3,2,1,0:T(8,128)(2,1)S(1)} %collective-permute-done.2.refs_3_), channel_id=1, source_target_pairs={{0,16},{16,0},{1,17},{17,1},{2,18},{18,2},{3,19},{19,3},{4,20},{20... | collective-permute-start | bytes 786440 | tf_op jit(solution)/shard_map/ppermute | solution.py:113
  43.0 8.4 %collective-permute-start.6 = (bf16[4,2,2,64,128]{4,3,2,1,0:T(8,128)(2,1)S(1)}, bf16[4,2,2,64,128]{4,3,2,1,0:T(8,128)(2,1)S(1)}, u32[]{:S(2)}, u32[]{:S(2)}) collective-permute-start(bf16[4,2,2,64,128]{4,3,2,1,0:T(8,128)(2,1)S(1)} %fusion.2), channel_id=1, source_target_pairs={{0,8},{4,12},{8,0},{12,4},{1,9},{5,13},{9,1},{13,5},{2,10},{6,14},... | collective-permute-start | bytes 786440 | tf_op jit(solution)/shard_map/ppermute | solution.py:113
  51.5 5.1 %collective-permute-start.7 = (bf16[2,2,64,128]{3,2,1,0:T(8,128)(2,1)S(1)}, bf16[2,2,64,128]{3,2,1,0:T(8,128)(2,1)S(1)}, u32[]{:S(2)}, u32[]{:S(2)}) collective-permute-start(bf16[2,2,64,128]{3,2,1,0:T(8,128)(2,1)S(1)} %get-tuple-element.138), channel_id=1, source_target_pairs={{0,1},{1,0},{2,3},{3,2},{4,5},{5,4},{6,7},{7,6},{8,9},{9,8},{10,11... | collective-permute-start | bytes 196616 | tf_op jit(solution)/shard_map/ppermute | solution.py:113
  53.2 7.5 %collective-permute-start.8 = (bf16[2,2,64,128]{3,2,1,0:T(8,128)(2,1)S(1)}, bf16[2,2,64,128]{3,2,1,0:T(8,128)(2,1)S(1)}, u32[]{:S(2)}, u32[]{:S(2)}) collective-permute-start(bf16[2,2,64,128]{3,2,1,0:T(8,128)(2,1)S(1)} %get-tuple-element.137), channel_id=1, source_target_pairs={{0,2},{1,3},{2,0},{3,1},{4,6},{5,7},{6,4},{7,5},{8,10},{9,11},{10,... | collective-permute-start | bytes 196616 | tf_op jit(solution)/shard_map/ppermute | solution.py:113
  56.6 6.1 %collective-permute-start.9 = (bf16[2,2,64,128]{3,2,1,0:T(8,128)(2,1)S(1)}, bf16[2,2,64,128]{3,2,1,0:T(8,128)(2,1)S(1)}, u32[]{:S(2)}, u32[]{:S(2)}) collective-permute-start(bf16[2,2,64,128]{3,2,1,0:T(8,128)(2,1)S(1)} %get-tuple-element.136), channel_id=1, source_target_pairs={{0,3},{1,2},{2,1},{3,0},{4,7},{5,6},{6,5},{7,4},{8,11},{9,10},{10,... | collective-permute-start | bytes 196616 | tf_op jit(solution)/shard_map/ppermute | solution.py:113
  64.3 6.2 %collective-permute-start.11 = (bf16[2,2,64,128]{3,2,1,0:T(8,128)(2,1)S(1)}, bf16[2,2,64,128]{3,2,1,0:T(8,128)(2,1)S(1)}, u32[]{:S(2)}, u32[]{:S(2)}) collective-permute-start(bf16[2,2,64,128]{3,2,1,0:T(8,128)(2,1)S(1)} %get-tuple-element.73), channel_id=1, source_target_pairs={{0,3},{1,2},{2,1},{3,0},{4,7},{5,6},{6,5},{7,4},{8,11},{9,10},{10,... | collective-permute-start | bytes 196616 | tf_op jit(solution)/shard_map/ppermute | solution.py:113
  65.8 6.3 %collective-permute-start.14 = (bf16[2,2,64,128]{3,2,1,0:T(8,128)(2,1)S(1)}, bf16[2,2,64,128]{3,2,1,0:T(8,128)(2,1)S(1)}, u32[]{:S(2)}, u32[]{:S(2)}) collective-permute-start(bf16[2,2,64,128]{3,2,1,0:T(8,128)(2,1)S(1)} %get-tuple-element.74), channel_id=1, source_target_pairs={{0,1},{1,0},{2,3},{3,2},{4,5},{5,4},{6,7},{7,6},{8,9},{9,8},{10,11... | collective-permute-start | bytes 196616 | tf_op jit(solution)/shard_map/ppermute | solution.py:113
  66.2 6.0 %collective-permute-start.16 = (bf16[2,2,64,128]{3,2,1,0:T(8,128)(2,1)S(1)}, bf16[2,2,64,128]{3,2,1,0:T(8,128)(2,1)S(1)}, u32[]{:S(2)}, u32[]{:S(2)}) collective-permute-start(bf16[2,2,64,128]{3,2,1,0:T(8,128)(2,1)S(1)} %get-tuple-element.72.refs_14_), channel_id=1, source_target_pairs={{0,8},{4,12},{8,0},{12,4},{1,9},{5,13},{9,1},{13,5},{2,10},{6,14},... | collective-permute-start | bytes 196616 | tf_op jit(solution)/shard_map/ppermute | solution.py:113
  67.7 5.2 %collective-permute-start.18 = (bf16[2,2,64,128]{3,2,1,0:T(8,128)(2,1)S(1)}, bf16[2,2,64,128]{3,2,1,0:T(8,128)(2,1)S(1)}, u32[]{:S(2)}, u32[]{:S(2)}) collective-permute-start(bf16[2,2,64,128]{3,2,1,0:T(8,128)(2,1)S(1)} %get-tuple-element.75), channel_id=1, source_target_pairs={{0,2},{1,3},{2,0},{3,1},{4,6},{5,7},{6,4},{7,5},{8,10},{9,11},{10,... | collective-permute-start | bytes 196616 | tf_op jit(solution)/shard_map/ppermute | solution.py:113
  70.6 4.3 %collective-permute-start.12 = (bf16[2,2,64,128]{3,2,1,0:T(8,128)(2,1)S(1)}, bf16[2,2,64,128]{3,2,1,0:T(8,128)(2,1)S(1)}, u32[]{:S(2)}, u32[]{:S(2)}) collective-permute-start(bf16[2,2,64,128]{3,2,1,0:T(8,128)(2,1)S(1)} %collective-permute-done.11.refs_1_), channel_id=1, source_target_pairs={{0,8},{4,12},{8,0},{12,4},{1,9},{5,13},{9,1},{13,5},{2,10},{6,14},... | collective-permute-start | bytes 196616 | tf_op jit(solution)/shard_map/ppermute | solution.py:113
  72.8 4.5 %collective-permute-start.22 = (bf16[2,2,64,128]{3,2,1,0:T(8,128)(2,1)S(1)}, bf16[2,2,64,128]{3,2,1,0:T(8,128)(2,1)S(1)}, u32[]{:S(2)}, u32[]{:S(2)}) collective-permute-start(bf16[2,2,64,128]{3,2,1,0:T(8,128)(2,1)S(1)} %collective-permute-done.18.refs_5_), channel_id=1, source_target_pairs={{0,8},{4,12},{8,0},{12,4},{1,9},{5,13},{9,1},{13,5},{2,10},{6,14},... | collective-permute-start | bytes 196616 | tf_op jit(solution)/shard_map/ppermute | solution.py:113
  73.3 4.7 %collective-permute-start.20 = (bf16[2,2,64,128]{3,2,1,0:T(8,128)(2,1)S(1)}, bf16[2,2,64,128]{3,2,1,0:T(8,128)(2,1)S(1)}, u32[]{:S(2)}, u32[]{:S(2)}) collective-permute-start(bf16[2,2,64,128]{3,2,1,0:T(8,128)(2,1)S(1)} %collective-permute-done.14.refs_11_), channel_id=1, source_target_pairs={{0,8},{4,12},{8,0},{12,4},{1,9},{5,13},{9,1},{13,5},{2,10},{6,14},... | collective-permute-start | bytes 196616 | tf_op jit(solution)/shard_map/ppermute | solution.py:113
  82.4 9.2 %collective-permute-start.25 = (bf16[2,2,4,64,128]{4,3,2,1,0:T(8,128)(2,1)S(1)}, bf16[2,2,4,64,128]{4,3,2,1,0:T(8,128)(2,1)S(1)}, u32[]{:S(2)}, u32[]{:S(2)}) collective-permute-start(bf16[2,2,4,64,128]{4,3,2,1,0:T(8,128)(2,1)S(1)} %get-tuple-element.77), channel_id=1, source_target_pairs={{0,16},{16,0},{1,17},{17,1},{2,18},{18,2},{3,19},{19,3},{4,20},{20... | collective-permute-start | bytes 786440 | tf_op jit(solution)/shard_map/ppermute | solution.py:113
  84.0 13.2 %collective-permute-start.28 = (bf16[2,2,4,64,128]{4,3,2,1,0:T(8,128)(2,1)S(1)}, bf16[2,2,4,64,128]{4,3,2,1,0:T(8,128)(2,1)S(1)}, u32[]{:S(2)}, u32[]{:S(2)}) collective-permute-start(bf16[2,2,4,64,128]{4,3,2,1,0:T(8,128)(2,1)S(1)} %get-tuple-element.79), channel_id=1, source_target_pairs={{0,16},{16,0},{1,17},{17,1},{2,18},{18,2},{3,19},{19,3},{4,20},{20... | collective-permute-start | bytes 786440 | tf_op jit(solution)/shard_map/ppermute | solution.py:113
  84.5 18.4 %collective-permute-start.32 = (bf16[2,2,4,64,128]{4,3,2,1,0:T(8,128)(2,1)S(1)}, bf16[2,2,4,64,128]{4,3,2,1,0:T(8,128)(2,1)S(1)}, u32[]{:S(2)}, u32[]{:S(2)}) collective-permute-start(bf16[2,2,4,64,128]{4,3,2,1,0:T(8,128)(2,1)S(1)} %get-tuple-element.83), channel_id=1, source_target_pairs={{0,16},{16,0},{1,17},{17,1},{2,18},{18,2},{3,19},{19,3},{4,20},{20... | collective-permute-start | bytes 786440 | tf_op jit(solution)/shard_map/ppermute | solution.py:113
  86.0 23.0 %collective-permute-start.35 = (bf16[2,2,4,64,128]{4,3,2,1,0:T(8,128)(2,1)S(1)}, bf16[2,2,4,64,128]{4,3,2,1,0:T(8,128)(2,1)S(1)}, u32[]{:S(2)}, u32[]{:S(2)}) collective-permute-start(bf16[2,2,4,64,128]{4,3,2,1,0:T(8,128)(2,1)S(1)} %get-tuple-element.85), channel_id=1, source_target_pairs={{0,16},{16,0},{1,17},{17,1},{2,18},{18,2},{3,19},{19,3},{4,20},{20... | collective-permute-start | bytes 786440 | tf_op jit(solution)/shard_map/ppermute | solution.py:113
  91.7 13.7 %collective-permute-start.26 = (bf16[2,4,64,128]{3,2,1,0:T(8,128)(2,1)S(1)}, bf16[2,4,64,128]{3,2,1,0:T(8,128)(2,1)S(1)}, u32[]{:S(2)}, u32[]{:S(2)}) collective-permute-start(bf16[2,4,64,128]{3,2,1,0:T(8,128)(2,1)S(1)} %get-tuple-element.131), channel_id=1, source_target_pairs={{0,2},{1,3},{2,0},{3,1},{4,6},{5,7},{6,4},{7,5},{8,10},{9,11},{10,... | collective-permute-start | bytes 393224 | tf_op jit(solution)/shard_map/ppermute | solution.py:113
  94.1 12.6 %collective-permute-start.27 = (bf16[2,4,64,128]{3,2,1,0:T(8,128)(2,1)S(1)}, bf16[2,4,64,128]{3,2,1,0:T(8,128)(2,1)S(1)}, u32[]{:S(2)}, u32[]{:S(2)}) collective-permute-start(bf16[2,4,64,128]{3,2,1,0:T(8,128)(2,1)S(1)} %get-tuple-element.130), channel_id=1, source_target_pairs={{0,3},{1,2},{2,1},{3,0},{4,7},{5,6},{6,5},{7,4},{8,11},{9,10},{10,... | collective-permute-start | bytes 393224 | tf_op jit(solution)/shard_map/ppermute | solution.py:113
  97.3 9.5 %collective-permute-start.29 = (bf16[2,4,64,128]{3,2,1,0:T(8,128)(2,1)S(1)}, bf16[2,4,64,128]{3,2,1,0:T(8,128)(2,1)S(1)}, u32[]{:S(2)}, u32[]{:S(2)}) collective-permute-start(bf16[2,4,64,128]{3,2,1,0:T(8,128)(2,1)S(1)} %fusion.6), channel_id=1, source_target_pairs={{0,1},{1,0},{2,3},{3,2},{4,5},{5,4},{6,7},{7,6},{8,9},{9,8},{10,11... | collective-permute-start | bytes 393224 | tf_op jit(solution)/shard_map/ppermute | solution.py:113
  102.9 12.0 %collective-permute-start.33 = (bf16[2,4,64,128]{3,2,1,0:T(8,128)(2,1)S(1)}, bf16[2,4,64,128]{3,2,1,0:T(8,128)(2,1)S(1)}, u32[]{:S(2)}, u32[]{:S(2)}) collective-permute-start(bf16[2,4,64,128]{3,2,1,0:T(8,128)(2,1)S(1)} %get-tuple-element.129), channel_id=1, source_target_pairs={{0,2},{1,3},{2,0},{3,1},{4,6},{5,7},{6,4},{7,5},{8,10},{9,11},{10,... | collective-permute-start | bytes 393224 | tf_op jit(solution)/shard_map/ppermute | solution.py:113
  105.4 15.7 %collective-permute-start.34 = (bf16[2,4,64,128]{3,2,1,0:T(8,128)(2,1)S(1)}, bf16[2,4,64,128]{3,2,1,0:T(8,128)(2,1)S(1)}, u32[]{:S(2)}, u32[]{:S(2)}) collective-permute-start(bf16[2,4,64,128]{3,2,1,0:T(8,128)(2,1)S(1)} %get-tuple-element.128), channel_id=1, source_target_pairs={{0,3},{1,2},{2,1},{3,0},{4,7},{5,6},{6,5},{7,4},{8,11},{9,10},{10,... | collective-permute-start | bytes 393224 | tf_op jit(solution)/shard_map/ppermute | solution.py:113
  109.1 13.0 %collective-permute-start.36 = (bf16[2,4,64,128]{3,2,1,0:T(8,128)(2,1)S(1)}, bf16[2,4,64,128]{3,2,1,0:T(8,128)(2,1)S(1)}, u32[]{:S(2)}, u32[]{:S(2)}) collective-permute-start(bf16[2,4,64,128]{3,2,1,0:T(8,128)(2,1)S(1)} %fusion.9), channel_id=1, source_target_pairs={{0,1},{1,0},{2,3},{3,2},{4,5},{5,4},{6,7},{7,6},{8,9},{9,8},{10,11... | collective-permute-start | bytes 393224 | tf_op jit(solution)/shard_map/ppermute | solution.py:113
  109.2 13.0 %collective-permute-start.37 = (bf16[2,4,64,128]{3,2,1,0:T(8,128)(2,1)S(1)}, bf16[2,4,64,128]{3,2,1,0:T(8,128)(2,1)S(1)}, u32[]{:S(2)}, u32[]{:S(2)}) collective-permute-start(bf16[2,4,64,128]{3,2,1,0:T(8,128)(2,1)S(1)} %get-tuple-element.86.refs_3_), channel_id=1, source_target_pairs={{0,16},{16,0},{1,17},{17,1},{2,18},{18,2},{3,19},{19,3},{4,20},{20... | collective-permute-start | bytes 393224 | tf_op jit(solution)/shard_map/ppermute | solution.py:113
  110.7 17.0 %collective-permute-start.30 = (bf16[2,4,64,128]{3,2,1,0:T(8,128)(2,1)S(1)}, bf16[2,4,64,128]{3,2,1,0:T(8,128)(2,1)S(1)}, u32[]{:S(2)}, u32[]{:S(2)}) collective-permute-start(bf16[2,4,64,128]{3,2,1,0:T(8,128)(2,1)S(1)} %get-tuple-element.80), channel_id=1, source_target_pairs={{0,2},{1,3},{2,0},{3,1},{4,6},{5,7},{6,4},{7,5},{8,10},{9,11},{10,... | collective-permute-start | bytes 393224 | tf_op jit(solution)/shard_map/ppermute | solution.py:113
  115.0 13.8 %collective-permute-start.31 = (bf16[2,4,64,128]{3,2,1,0:T(8,128)(2,1)S(1)}, bf16[2,4,64,128]{3,2,1,0:T(8,128)(2,1)S(1)}, u32[]{:S(2)}, u32[]{:S(2)}) collective-permute-start(bf16[2,4,64,128]{3,2,1,0:T(8,128)(2,1)S(1)} %get-tuple-element.81), channel_id=1, source_target_pairs={{0,3},{1,2},{2,1},{3,0},{4,7},{5,6},{6,5},{7,4},{8,11},{9,10},{10,... | collective-permute-start | bytes 393224 | tf_op jit(solution)/shard_map/ppermute | solution.py:113
  121.1 9.3 %collective-permute-start.40 = (bf16[2,4,64,128]{3,2,1,0:T(8,128)(2,1)S(1)}, bf16[2,4,64,128]{3,2,1,0:T(8,128)(2,1)S(1)}, u32[]{:S(2)}, u32[]{:S(2)}) collective-permute-start(bf16[2,4,64,128]{3,2,1,0:T(8,128)(2,1)S(1)} %get-tuple-element.87), channel_id=1, source_target_pairs={{0,1},{1,0},{2,3},{3,2},{4,5},{5,4},{6,7},{7,6},{8,9},{9,8},{10,11... | collective-permute-start | bytes 393224 | tf_op jit(solution)/shard_map/ppermute | solution.py:113
  124.4 6.9 %collective-permute-start.38 = (bf16[2,4,64,128]{3,2,1,0:T(8,128)(2,1)S(1)}, bf16[2,4,64,128]{3,2,1,0:T(8,128)(2,1)S(1)}, u32[]{:S(2)}, u32[]{:S(2)}) collective-permute-start(bf16[2,4,64,128]{3,2,1,0:T(8,128)(2,1)S(1)} %get-tuple-element.94), channel_id=1, source_target_pairs={{0,1},{1,0},{2,3},{3,2},{4,5},{5,4},{6,7},{7,6},{8,9},{9,8},{10,11... | collective-permute-start | bytes 393224 | tf_op jit(solution)/shard_map/ppermute | solution.py:113
  125.4 6.4 %collective-permute-start.39 = (bf16[2,4,64,128]{3,2,1,0:T(8,128)(2,1)S(1)}, bf16[2,4,64,128]{3,2,1,0:T(8,128)(2,1)S(1)}, u32[]{:S(2)}, u32[]{:S(2)}) collective-permute-start(bf16[2,4,64,128]{3,2,1,0:T(8,128)(2,1)S(1)} %get-tuple-element.95.refs_11_), channel_id=1, source_target_pairs={{0,16},{16,0},{1,17},{17,1},{2,18},{18,2},{3,19},{19,3},{4,20},{20... | collective-permute-start | bytes 393224 | tf_op jit(solution)/shard_map/ppermute | solution.py:113
  127.7 9.6 %collective-permute-start.44 = (bf16[2,4,64,128]{3,2,1,0:T(8,128)(2,1)S(1)}, bf16[2,4,64,128]{3,2,1,0:T(8,128)(2,1)S(1)}, u32[]{:S(2)}, u32[]{:S(2)}) collective-permute-start(bf16[2,4,64,128]{3,2,1,0:T(8,128)(2,1)S(1)} %get-tuple-element.99), channel_id=1, source_target_pairs={{0,2},{1,3},{2,0},{3,1},{4,6},{5,7},{6,4},{7,5},{8,10},{9,11},{10,... | collective-permute-start | bytes 393224 | tf_op jit(solution)/shard_map/ppermute | solution.py:113
  128.8 9.7 %collective-permute-start.45 = (bf16[2,4,64,128]{3,2,1,0:T(8,128)(2,1)S(1)}, bf16[2,4,64,128]{3,2,1,0:T(8,128)(2,1)S(1)}, u32[]{:S(2)}, u32[]{:S(2)}) collective-permute-start(bf16[2,4,64,128]{3,2,1,0:T(8,128)(2,1)S(1)} %get-tuple-element.100), channel_id=1, source_target_pairs={{0,3},{1,2},{2,1},{3,0},{4,7},{5,6},{6,5},{7,4},{8,11},{9,10},{10,... | collective-permute-start | bytes 393224 | tf_op jit(solution)/shard_map/ppermute | solution.py:113
  130.4 9.0 %collective-permute-start.43 = (bf16[2,4,64,128]{3,2,1,0:T(8,128)(2,1)S(1)}, bf16[2,4,64,128]{3,2,1,0:T(8,128)(2,1)S(1)}, u32[]{:S(2)}, u32[]{:S(2)}) collective-permute-start(bf16[2,4,64,128]{3,2,1,0:T(8,128)(2,1)S(1)} %collective-permute-done.40.refs_2_), channel_id=1, source_target_pairs={{0,16},{16,0},{1,17},{17,1},{2,18},{18,2},{3,19},{19,3},{4,20},{20... | collective-permute-start | bytes 393224 | tf_op jit(solution)/shard_map/ppermute | solution.py:113
  131.8 8.8 %collective-permute-start.41 = (bf16[2,4,64,128]{3,2,1,0:T(8,128)(2,1)S(1)}, bf16[2,4,64,128]{3,2,1,0:T(8,128)(2,1)S(1)}, u32[]{:S(2)}, u32[]{:S(2)}) collective-permute-start(bf16[2,4,64,128]{3,2,1,0:T(8,128)(2,1)S(1)} %collective-permute-done.30.refs_0_), channel_id=1, source_target_pairs={{0,16},{16,0},{1,17},{17,1},{2,18},{18,2},{3,19},{19,3},{4,20},{20... | collective-permute-start | bytes 393224 | tf_op jit(solution)/shard_map/ppermute | solution.py:113
  133.2 7.4 %collective-permute-start.42 = (bf16[2,4,64,128]{3,2,1,0:T(8,128)(2,1)S(1)}, bf16[2,4,64,128]{3,2,1,0:T(8,128)(2,1)S(1)}, u32[]{:S(2)}, u32[]{:S(2)}) collective-permute-start(bf16[2,4,64,128]{3,2,1,0:T(8,128)(2,1)S(1)} %collective-permute-done.31.refs_1_), channel_id=1, source_target_pairs={{0,16},{16,0},{1,17},{17,1},{2,18},{18,2},{3,19},{19,3},{4,20},{20... | collective-permute-start | bytes 393224 | tf_op jit(solution)/shard_map/ppermute | solution.py:113
  137.3 6.4 %collective-permute-start.46 = (bf16[2,4,64,128]{3,2,1,0:T(8,128)(2,1)S(1)}, bf16[2,4,64,128]{3,2,1,0:T(8,128)(2,1)S(1)}, u32[]{:S(2)}, u32[]{:S(2)}) collective-permute-start(bf16[2,4,64,128]{3,2,1,0:T(8,128)(2,1)S(1)} %collective-permute-done.44.refs_8_), channel_id=1, source_target_pairs={{0,16},{16,0},{1,17},{17,1},{2,18},{18,2},{3,19},{19,3},{4,20},{20... | collective-permute-start | bytes 393224 | tf_op jit(solution)/shard_map/ppermute | solution.py:113
  138.6 6.6 %collective-permute-start.47 = (bf16[2,4,64,128]{3,2,1,0:T(8,128)(2,1)S(1)}, bf16[2,4,64,128]{3,2,1,0:T(8,128)(2,1)S(1)}, u32[]{:S(2)}, u32[]{:S(2)}) collective-permute-start(bf16[2,4,64,128]{3,2,1,0:T(8,128)(2,1)S(1)} %collective-permute-done.45.refs_9_), channel_id=1, source_target_pairs={{0,16},{16,0},{1,17},{17,1},{2,18},{18,2},{3,19},{19,3},{4,20},{20... | collective-permute-start | bytes 393224 | tf_op jit(solution)/shard_map/ppermute | solution.py:113
  139.4 7.2 %collective-permute-start.48 = (bf16[2,4,64,128]{3,2,1,0:T(8,128)(2,1)S(1)}, bf16[2,4,64,128]{3,2,1,0:T(8,128)(2,1)S(1)}, u32[]{:S(2)}, u32[]{:S(2)}) collective-permute-start(bf16[2,4,64,128]{3,2,1,0:T(8,128)(2,1)S(1)} %collective-permute-done.38.refs_10_), channel_id=1, source_target_pairs={{0,16},{16,0},{1,17},{17,1},{2,18},{18,2},{3,19},{19,3},{4,20},{20... | collective-permute-start | bytes 393224 | tf_op jit(solution)/shard_map/ppermute | solution.py:113
  152.4 8.4 %collective-permute-start.50 = (bf16[4,2,2,64,128]{4,3,2,1,0:T(8,128)(2,1)S(1)}, bf16[4,2,2,64,128]{4,3,2,1,0:T(8,128)(2,1)S(1)}, u32[]{:S(2)}, u32[]{:S(2)}) collective-permute-start(bf16[4,2,2,64,128]{4,3,2,1,0:T(8,128)(2,1)S(1)} %fusion.3), channel_id=1, source_target_pairs={{0,8},{4,12},{8,0},{12,4},{1,9},{5,13},{9,1},{13,5},{2,10},{6,14},... | collective-permute-start | bytes 786440 | tf_op jit(solution)/shard_map/ppermute | solution.py:113
  161.0 5.2 %collective-permute-start.51 = (bf16[2,2,64,128]{3,2,1,0:T(8,128)(2,1)S(1)}, bf16[2,2,64,128]{3,2,1,0:T(8,128)(2,1)S(1)}, u32[]{:S(2)}, u32[]{:S(2)}) collective-permute-start(bf16[2,2,64,128]{3,2,1,0:T(8,128)(2,1)S(1)} %get-tuple-element.134), channel_id=1, source_target_pairs={{0,1},{1,0},{2,3},{3,2},{4,5},{5,4},{6,7},{7,6},{8,9},{9,8},{10,11... | collective-permute-start | bytes 196616 | tf_op jit(solution)/shard_map/ppermute | solution.py:113
  163.5 7.5 %collective-permute-start.52 = (bf16[2,2,64,128]{3,2,1,0:T(8,128)(2,1)S(1)}, bf16[2,2,64,128]{3,2,1,0:T(8,128)(2,1)S(1)}, u32[]{:S(2)}, u32[]{:S(2)}) collective-permute-start(bf16[2,2,64,128]{3,2,1,0:T(8,128)(2,1)S(1)} %get-tuple-element.133), channel_id=1, source_target_pairs={{0,2},{1,3},{2,0},{3,1},{4,6},{5,7},{6,4},{7,5},{8,10},{9,11},{10,... | collective-permute-start | bytes 196616 | tf_op jit(solution)/shard_map/ppermute | solution.py:113
  164.7 6.2 %collective-permute-start.53 = (bf16[2,2,64,128]{3,2,1,0:T(8,128)(2,1)S(1)}, bf16[2,2,64,128]{3,2,1,0:T(8,128)(2,1)S(1)}, u32[]{:S(2)}, u32[]{:S(2)}) collective-permute-start(bf16[2,2,64,128]{3,2,1,0:T(8,128)(2,1)S(1)} %get-tuple-element.132), channel_id=1, source_target_pairs={{0,3},{1,2},{2,1},{3,0},{4,7},{5,6},{6,5},{7,4},{8,11},{9,10},{10,... | collective-permute-start | bytes 196616 | tf_op jit(solution)/shard_map/ppermute | solution.py:113
  172.7 6.7 %collective-permute-start.55 = (bf16[2,2,64,128]{3,2,1,0:T(8,128)(2,1)S(1)}, bf16[2,2,64,128]{3,2,1,0:T(8,128)(2,1)S(1)}, u32[]{:S(2)}, u32[]{:S(2)}) collective-permute-start(bf16[2,2,64,128]{3,2,1,0:T(8,128)(2,1)S(1)} %get-tuple-element.106), channel_id=1, source_target_pairs={{0,3},{1,2},{2,1},{3,0},{4,7},{5,6},{6,5},{7,4},{8,11},{9,10},{10,... | collective-permute-start | bytes 196616 | tf_op jit(solution)/shard_map/ppermute | solution.py:113
  175.1 5.4 %collective-permute-start.58 = (bf16[2,2,64,128]{3,2,1,0:T(8,128)(2,1)S(1)}, bf16[2,2,64,128]{3,2,1,0:T(8,128)(2,1)S(1)}, u32[]{:S(2)}, u32[]{:S(2)}) collective-permute-start(bf16[2,2,64,128]{3,2,1,0:T(8,128)(2,1)S(1)} %get-tuple-element.107), channel_id=1, source_target_pairs={{0,1},{1,0},{2,3},{3,2},{4,5},{5,4},{6,7},{7,6},{8,9},{9,8},{10,11... | collective-permute-start | bytes 196616 | tf_op jit(solution)/shard_map/ppermute | solution.py:113
  175.5 5.0 %collective-permute-start.60 = (bf16[2,2,64,128]{3,2,1,0:T(8,128)(2,1)S(1)}, bf16[2,2,64,128]{3,2,1,0:T(8,128)(2,1)S(1)}, u32[]{:S(2)}, u32[]{:S(2)}) collective-permute-start(bf16[2,2,64,128]{3,2,1,0:T(8,128)(2,1)S(1)} %get-tuple-element.105.refs_14_), channel_id=1, source_target_pairs={{0,8},{4,12},{8,0},{12,4},{1,9},{5,13},{9,1},{13,5},{2,10},{6,14},... | collective-permute-start | bytes 196616 | tf_op jit(solution)/shard_map/ppermute | solution.py:113
  176.4 5.2 %collective-permute-start.62 = (bf16[2,2,64,128]{3,2,1,0:T(8,128)(2,1)S(1)}, bf16[2,2,64,128]{3,2,1,0:T(8,128)(2,1)S(1)}, u32[]{:S(2)}, u32[]{:S(2)}) collective-permute-start(bf16[2,2,64,128]{3,2,1,0:T(8,128)(2,1)S(1)} %get-tuple-element.108), channel_id=1, source_target_pairs={{0,2},{1,3},{2,0},{3,1},{4,6},{5,7},{6,4},{7,5},{8,10},{9,11},{10,... | collective-permute-start | bytes 196616 | tf_op jit(solution)/shard_map/ppermute | solution.py:113
  178.1 4.6 %collective-permute-start.54 = (bf16[2,2,64,128]{3,2,1,0:T(8,128)(2,1)S(1)}, bf16[2,2,64,128]{3,2,1,0:T(8,128)(2,1)S(1)}, u32[]{:S(2)}, u32[]{:S(2)}) collective-permute-start(bf16[2,2,64,128]{3,2,1,0:T(8,128)(2,1)S(1)} %get-tuple-element.105.refs_14_), channel_id=1, source_target_pairs={{0,4},{4,0},{8,12},{12,8},{1,5},{5,1},{9,13},{13,9},{2,6},{6,2},{1... | collective-permute-start | bytes 196616 | tf_op jit(solution)/shard_map/ppermute | solution.py:113
  179.4 4.3 %collective-permute-start.56 = (bf16[2,2,64,128]{3,2,1,0:T(8,128)(2,1)S(1)}, bf16[2,2,64,128]{3,2,1,0:T(8,128)(2,1)S(1)}, u32[]{:S(2)}, u32[]{:S(2)}) collective-permute-start(bf16[2,2,64,128]{3,2,1,0:T(8,128)(2,1)S(1)} %collective-permute-done.55.refs_1_), channel_id=1, source_target_pairs={{0,8},{4,12},{8,0},{12,4},{1,9},{5,13},{9,1},{13,5},{2,10},{6,14},... | collective-permute-start | bytes 196616 | tf_op jit(solution)/shard_map/ppermute | solution.py:113
  182.7 4.3 %collective-permute-start.64 = (bf16[2,2,64,128]{3,2,1,0:T(8,128)(2,1)S(1)}, bf16[2,2,64,128]{3,2,1,0:T(8,128)(2,1)S(1)}, u32[]{:S(2)}, u32[]{:S(2)}) collective-permute-start(bf16[2,2,64,128]{3,2,1,0:T(8,128)(2,1)S(1)} %collective-permute-done.58.refs_11_), channel_id=1, source_target_pairs={{0,8},{4,12},{8,0},{12,4},{1,9},{5,13},{9,1},{13,5},{2,10},{6,14},... | collective-permute-start | bytes 196616 | tf_op jit(solution)/shard_map/ppermute | solution.py:113
  191.3 9.2 %collective-permute-start.69 = (bf16[2,2,4,64,128]{4,3,2,1,0:T(8,128)(2,1)S(1)}, bf16[2,2,4,64,128]{4,3,2,1,0:T(8,128)(2,1)S(1)}, u32[]{:S(2)}, u32[]{:S(2)}) collective-permute-start(bf16[2,2,4,64,128]{4,3,2,1,0:T(8,128)(2,1)S(1)} %get-tuple-element.110), channel_id=1, source_target_pairs={{0,16},{16,0},{1,17},{17,1},{2,18},{18,2},{3,19},{19,3},{4,20},{20... | collective-permute-start | bytes 786440 | tf_op jit(solution)/shard_map/ppermute | solution.py:113
  193.0 13.1 %collective-permute-start.72 = (bf16[2,2,4,64,128]{4,3,2,1,0:T(8,128)(2,1)S(1)}, bf16[2,2,4,64,128]{4,3,2,1,0:T(8,128)(2,1)S(1)}, u32[]{:S(2)}, u32[]{:S(2)}) collective-permute-start(bf16[2,2,4,64,128]{4,3,2,1,0:T(8,128)(2,1)S(1)} %get-tuple-element.112), channel_id=1, source_target_pairs={{0,16},{16,0},{1,17},{17,1},{2,18},{18,2},{3,19},{19,3},{4,20},{20... | collective-permute-start | bytes 786440 | tf_op jit(solution)/shard_map/ppermute | solution.py:113
  193.4 18.4 %collective-permute-start.75 = (bf16[2,2,4,64,128]{4,3,2,1,0:T(8,128)(2,1)S(1)}, bf16[2,2,4,64,128]{4,3,2,1,0:T(8,128)(2,1)S(1)}, u32[]{:S(2)}, u32[]{:S(2)}) collective-permute-start(bf16[2,2,4,64,128]{4,3,2,1,0:T(8,128)(2,1)S(1)} %get-tuple-element.114), channel_id=1, source_target_pairs={{0,16},{16,0},{1,17},{17,1},{2,18},{18,2},{3,19},{19,3},{4,20},{20... | collective-permute-start | bytes 786440 | tf_op jit(solution)/shard_map/ppermute | solution.py:113
  195.1 23.1 %collective-permute-start.78 = (bf16[2,2,4,64,128]{4,3,2,1,0:T(8,128)(2,1)S(1)}, bf16[2,2,4,64,128]{4,3,2,1,0:T(8,128)(2,1)S(1)}, u32[]{:S(2)}, u32[]{:S(2)}) collective-permute-start(bf16[2,2,4,64,128]{4,3,2,1,0:T(8,128)(2,1)S(1)} %get-tuple-element.116), channel_id=1, source_target_pairs={{0,16},{16,0},{1,17},{17,1},{2,18},{18,2},{3,19},{19,3},{4,20},{20... | collective-permute-start | bytes 786440 | tf_op jit(solution)/shard_map/ppermute | solution.py:113
  200.6 13.0 %collective-permute-start.70 = (bf16[2,4,64,128]{3,2,1,0:T(8,128)(2,1)S(1)}, bf16[2,4,64,128]{3,2,1,0:T(8,128)(2,1)S(1)}, u32[]{:S(2)}, u32[]{:S(2)}) collective-permute-start(bf16[2,4,64,128]{3,2,1,0:T(8,128)(2,1)S(1)} %get-tuple-element.127), channel_id=1, source_target_pairs={{0,2},{1,3},{2,0},{3,1},{4,6},{5,7},{6,4},{7,5},{8,10},{9,11},{10,... | collective-permute-start | bytes 393224 | tf_op jit(solution)/shard_map/ppermute | solution.py:113
  202.3 13.6 %collective-permute-start.71 = (bf16[2,4,64,128]{3,2,1,0:T(8,128)(2,1)S(1)}, bf16[2,4,64,128]{3,2,1,0:T(8,128)(2,1)S(1)}, u32[]{:S(2)}, u32[]{:S(2)}) collective-permute-start(bf16[2,4,64,128]{3,2,1,0:T(8,128)(2,1)S(1)} %get-tuple-element.126), channel_id=1, source_target_pairs={{0,3},{1,2},{2,1},{3,0},{4,7},{5,6},{6,5},{7,4},{8,11},{9,10},{10,... | collective-permute-start | bytes 393224 | tf_op jit(solution)/shard_map/ppermute | solution.py:113
  206.2 9.8 %collective-permute-start.73 = (bf16[2,4,64,128]{3,2,1,0:T(8,128)(2,1)S(1)}, bf16[2,4,64,128]{3,2,1,0:T(8,128)(2,1)S(1)}, u32[]{:S(2)}, u32[]{:S(2)}) collective-permute-start(bf16[2,4,64,128]{3,2,1,0:T(8,128)(2,1)S(1)} %fusion.12), channel_id=1, source_target_pairs={{0,1},{1,0},{2,3},{3,2},{4,5},{5,4},{6,7},{7,6},{8,9},{9,8},{10,11... | collective-permute-start | bytes 393224 | tf_op jit(solution)/shard_map/ppermute | solution.py:113
  211.9 11.8 %collective-permute-start.76 = (bf16[2,4,64,128]{3,2,1,0:T(8,128)(2,1)S(1)}, bf16[2,4,64,128]{3,2,1,0:T(8,128)(2,1)S(1)}, u32[]{:S(2)}, u32[]{:S(2)}) collective-permute-start(bf16[2,4,64,128]{3,2,1,0:T(8,128)(2,1)S(1)} %get-tuple-element.125), channel_id=1, source_target_pairs={{0,2},{1,3},{2,0},{3,1},{4,6},{5,7},{6,4},{7,5},{8,10},{9,11},{10,... | collective-permute-start | bytes 393224 | tf_op jit(solution)/shard_map/ppermute | solution.py:113
  213.6 10.1 %collective-permute-start.77 = (bf16[2,4,64,128]{3,2,1,0:T(8,128)(2,1)S(1)}, bf16[2,4,64,128]{3,2,1,0:T(8,128)(2,1)S(1)}, u32[]{:S(2)}, u32[]{:S(2)}) collective-permute-start(bf16[2,4,64,128]{3,2,1,0:T(8,128)(2,1)S(1)} %get-tuple-element.124), channel_id=1, source_target_pairs={{0,3},{1,2},{2,1},{3,0},{4,7},{5,6},{6,5},{7,4},{8,11},{9,10},{10,... | collective-permute-start | bytes 393224 | tf_op jit(solution)/shard_map/ppermute | solution.py:113
  218.3 6.5 %collective-permute-start.79 = (bf16[2,4,64,128]{3,2,1,0:T(8,128)(2,1)S(1)}, bf16[2,4,64,128]{3,2,1,0:T(8,128)(2,1)S(1)}, u32[]{:S(2)}, u32[]{:S(2)}) collective-permute-start(bf16[2,4,64,128]{3,2,1,0:T(8,128)(2,1)S(1)} %fusion.15), channel_id=1, source_target_pairs={{0,1},{1,0},{2,3},{3,2},{4,5},{5,4},{6,7},{7,6},{8,9},{9,8},{10,11... | collective-permute-start | bytes 393224 | tf_op jit(solution)/shard_map/ppermute | solution.py:113
  218.4 10.4 %collective-permute-start.82 = (bf16[4,2,2,64,128]{4,3,2,1,0:T(8,128)(2,1)S(1)}, bf16[4,2,2,64,128]{4,3,2,1,0:T(8,128)(2,1)}, u32[]{:S(2)}, u32[]{:S(2)}) collective-permute-start(bf16[4,2,2,64,128]{4,3,2,1,0:T(8,128)(2,1)S(1)} %get-tuple-element.123.refs_0_), channel_id=1, source_target_pairs={{0,8},{4,12},{8,0},{12,4},{1,9},{5,13},{9,1},{13,5},{2,10},{6,14},... | collective-permute-start | bytes 786440 | tf_op jit(solution)/shard_map/ppermute | solution.py:113
  219.3 20.3 %collective-permute-start.74 = (bf16[2,4,4,64,128]{4,3,2,1,0:T(8,128)(2,1)S(1)}, bf16[2,4,4,64,128]{4,3,2,1,0:T(8,128)(2,1)S(1)}, u32[]{:S(2)}, u32[]{:S(2)}) collective-permute-start(bf16[2,4,4,64,128]{4,3,2,1,0:T(8,128)(2,1)S(1)} %mute_receiver.6.refs_0_), channel_id=1, source_target_pairs={{0,16},{16,0},{1,17},{17,1},{2,18},{18,2},{3,19},{19,3},{4,20},{20... | collective-permute-start | bytes 1572872 | tf_op jit(solution)/shard_map/ppermute | solution.py:113
  227.0 16.2 %collective-permute-start.80 = (bf16[2,4,4,64,128]{4,3,2,1,0:T(8,128)(2,1)S(1)}, bf16[2,4,4,64,128]{4,3,2,1,0:T(8,128)(2,1)}, u32[]{:S(2)}, u32[]{:S(2)}) collective-permute-start(bf16[2,4,4,64,128]{4,3,2,1,0:T(8,128)(2,1)S(1)} %mute_receiver.7.refs_1_), channel_id=1, source_target_pairs={{0,16},{16,0},{1,17},{17,1},{2,18},{18,2},{3,19},{19,3},{4,20},{20... | collective-permute-start | bytes 1572872 | tf_op jit(solution)/shard_map/ppermute | solution.py:113
  (23 other events, 149.3 us)
